TPU v7x, 32 devices: a whole 2x2x4 slice. The times are simulated.
32 devices in a mesh: ctx: 8 (over z, y), fsdp: 4 (over x, core).
Axes of the slice: x: 2, y: 2, z: 4, core: 2. Of those that a mesh axis runs over, the one named last changes fastest.
Arguments:
- tokens: bfloat16 [4, 1024, 2048], P('fsdp', 'ctx'), may hold values from -6 to 6
- doc_lengths: int32 [4, 8], P('fsdp'), may hold values from 1 to 512, 1024 in all within a row
- cotangent: bfloat16 [4, 1024, 2048], P('fsdp', 'ctx'), may hold values from -6 to 6
- gain_attn: bfloat16 [2048], P(('ctx', 'fsdp')), may hold values from 0.099609375 to 1.8984375
- w_query: bfloat16 [2048, 2048], P(('ctx', 'fsdp')), may hold values from -0.5 to 0.5
- w_key: bfloat16 [2048, 512], P(('ctx', 'fsdp')), may hold values from -0.5 to 0.5
- w_value: bfloat16 [2048, 512], P(('ctx', 'fsdp')), may hold values from -0.125 to 0.125
- w_output: bfloat16 [2048, 2048], P(('ctx', 'fsdp')), may hold values from -3 to 3
- gain_mlp: bfloat16 [2048], P(('ctx', 'fsdp')), may hold values from 0.099609375 to 1.8984375
- w_gate: bfloat16 [2048, 8192], P(('ctx', 'fsdp')), may hold values from -0.125 to 0.125
- w_up: bfloat16 [2048, 8192], P(('ctx', 'fsdp')), may hold values from -0.125 to 0.125
- w_down: bfloat16 [8192, 2048], P(('ctx', 'fsdp')), may hold values from -0.5 to 0.5
Outputs:
- output: bfloat16 [4, 1024, 2048], P('fsdp', 'ctx')
- grad_tokens: float32 [4, 1024, 2048], P('fsdp', 'ctx')
- grad_gain_attn: float32 [2048], P(('ctx', 'fsdp'))
- grad_w_query: float32 [2048, 2048], P(('ctx', 'fsdp'))
- grad_w_key: float32 [2048, 512], P(('ctx', 'fsdp'))
- grad_w_value: float32 [2048, 512], P(('ctx', 'fsdp'))
- grad_w_output: float32 [2048, 2048], P(('ctx', 'fsdp'))
- grad_gain_mlp: float32 [2048], P(('ctx', 'fsdp'))
- grad_w_gate: float32 [2048, 8192], P(('ctx', 'fsdp'))
- grad_w_up: float32 [2048, 8192], P(('ctx', 'fsdp'))
- grad_w_down: float32 [8192, 2048], P(('ctx', 'fsdp'))
Inputs may be any that keep to these rules, and one draw needn't show every extreme that they name: `doc_lengths`: each sequence's 8 lengths sum to 1024, and the longest is 512.
All inputs are finite; a program needn't handle non-finite values.
Results may differ from a plain program's by a relative error of at most 0.022.
Values may be sent and summed in bfloat16 or wider, within the bound.
A program may use at most 640 MiB of HBM per device.

v0:
```python
import math

import jax
import jax.numpy as jnp
from jax import lax
from jax.sharding import PartitionSpec as P

H = 32
KVH = 8
HD = 64
FF = 8192


EPSILON = 1e-05
SCORE_SCALE = 1.0 / 64.0
RESIDUAL_MULT = 0.22
ROPE_BASE = 10000000.0
NEGATIVE = -1e30


def doc_index(positions, starts):
    return jnp.sum((positions[:, None] >= starts[None, :]).astype(jnp.int32), axis=1) - 1


def rope_tables(positions):
    half_size = HD // 2
    frequency = ROPE_BASE ** (-(jnp.arange(half_size, dtype=jnp.float32) * 2.0) / HD)
    angles = positions.astype(jnp.float32)[:, None] * frequency[None, :]
    return (jnp.cos(angles), jnp.sin(angles))


def rotate(tensor, cos_table, sin_table, head_count):
    row_count = tensor.shape[0]
    by_head = tensor.reshape(row_count, head_count, HD)
    half_size = HD // 2
    first_half = by_head[..., :half_size]
    second_half = by_head[..., half_size:]
    cos_rows = cos_table[:, None, :]
    sin_rows = sin_table[:, None, :]
    turned = jnp.concatenate(
        [
            first_half * cos_rows - second_half * sin_rows,
            second_half * cos_rows + first_half * sin_rows,
        ],
        axis=-1,
    )
    return turned.reshape(row_count, head_count * HD)


def dot_plain(left, right):
    return jnp.dot(left, right, preferred_element_type=jnp.float32)


def dot_back(left, right):
    return lax.dot_general(
        left, right, (((1,), (1,)), ((), ())), preferred_element_type=jnp.float32
    )


def dot_outer(left, right):
    return lax.dot_general(
        left, right, (((0,), (0,)), ((), ())), preferred_element_type=jnp.float32
    )


def norm_back(grad_normed, unit_rows, inv_scale, gain_full):
    scaled = grad_normed * gain_full
    return inv_scale * (scaled - unit_rows * jnp.mean(scaled * unit_rows, axis=-1, keepdims=True))


def on_device(
    tokens,
    doc_lengths,
    cotangent,
    gain_attn,
    w_query,
    w_key,
    w_value,
    w_output,
    gain_mlp,
    w_gate,
    w_up,
    w_down,
):
    local_rows = tokens.shape[1]
    ctx_size = lax.axis_size("ctx")
    length = local_rows * ctx_size
    group_size = H // KVH
    offset = lax.axis_index("ctx") * local_rows
    positions = offset + jnp.arange(local_rows, dtype=jnp.int32)
    seq_lengths = doc_lengths[0]
    starts = jnp.cumsum(seq_lengths) - seq_lengths
    doc_ids = doc_index(positions, starts)
    last_pos = offset + local_rows - 1
    first_doc = doc_ids[0]
    cos_table, sin_table = rope_tables(positions)
    gain1, gain2, wq_full, wk_full, wv_full, wo_full = (
        lax.all_gather(gain_attn, ("ctx", "fsdp"), axis=0, tiled=True),
        lax.all_gather(gain_mlp, ("ctx", "fsdp"), axis=0, tiled=True),
        lax.all_gather(w_query, ("ctx", "fsdp"), axis=0, tiled=True),
        lax.all_gather(w_key, ("ctx", "fsdp"), axis=0, tiled=True),
        lax.all_gather(w_value, ("ctx", "fsdp"), axis=0, tiled=True),
        lax.all_gather(w_output, ("ctx", "fsdp"), axis=0, tiled=True),
    )
    gain1_f = gain1.astype(jnp.float32)
    gain2_f = gain2.astype(jnp.float32)
    inputs = tokens[0].astype(jnp.float32)
    inv_one = lax.rsqrt(jnp.mean(inputs * inputs, axis=-1, keepdims=True) + EPSILON)
    unit_one = inputs * inv_one
    normed1 = (unit_one * gain1_f).astype(jnp.bfloat16)
    queries = rotate(dot_plain(normed1, wq_full), cos_table, sin_table, H).astype(jnp.bfloat16)
    key_rot = rotate(dot_plain(normed1, wk_full), cos_table, sin_table, KVH).astype(jnp.bfloat16)
    values = dot_plain(normed1, wv_full).astype(jnp.bfloat16)
    grouped = queries.reshape(local_rows, KVH, group_size, HD)
    start_state = (
        jnp.full((local_rows, KVH, group_size), NEGATIVE, jnp.float32),
        jnp.zeros((local_rows, KVH, group_size), jnp.float32),
        jnp.zeros((local_rows, KVH, group_size, HD), jnp.float32),
    )
    running = start_state
    key_piece = lax.all_gather(key_rot, "ctx", axis=0, tiled=True)
    value_piece = lax.all_gather(values, "ctx", axis=0, tiled=True)
    piece_rows = key_piece.shape[0]
    attend_key_width = math.gcd(piece_rows, 512)
    block_count = piece_rows // attend_key_width

    def one_block(carried, index_block):
        block_start = index_block * attend_key_width
        key_blk = lax.dynamic_slice_in_dim(key_piece, block_start, attend_key_width, 0).reshape(
            attend_key_width, KVH, HD
        )
        value_blk = lax.dynamic_slice_in_dim(value_piece, block_start, attend_key_width, 0).reshape(
            attend_key_width, KVH, HD
        )
        key_pos = block_start + jnp.arange(attend_key_width, dtype=jnp.int32)
        key_docs = doc_index(key_pos, starts)
        skip_block = (block_start > last_pos) | (key_docs[attend_key_width - 1] < first_doc)

        def update(current):
            run_max, run_sum, accumulated = current
            scores = (
                jnp.einsum("qkgd,tkd->qkgt", grouped, key_blk, preferred_element_type=jnp.float32)
                * SCORE_SCALE
            )
            allowed = (key_docs[None, :] == doc_ids[:, None]) & (
                key_pos[None, :] <= positions[:, None]
            )
            allowed = allowed[:, None, None, :]
            masked = jnp.where(allowed, scores, NEGATIVE)
            new_max = jnp.maximum(run_max, jnp.max(masked, axis=-1))
            weights_exp = jnp.where(allowed, jnp.exp(masked - new_max[..., None]), 0.0)
            factor = jnp.exp(run_max - new_max)
            new_sum = run_sum * factor + jnp.sum(weights_exp, axis=-1)
            new_acc = accumulated * factor[..., None] + jnp.einsum(
                "qkgt,tkd->qkgd",
                weights_exp.astype(jnp.bfloat16),
                value_blk,
                preferred_element_type=jnp.float32,
            )
            return (new_max, new_sum, new_acc)

        return (lax.cond(skip_block, lambda unchanged: unchanged, update, carried), None)

    running, _ = lax.scan(one_block, running, jnp.arange(block_count))
    run_max, run_sum, accumulated = running
    attended = accumulated / run_sum[..., None]
    log_sum = run_max + jnp.log(run_sum)
    mixed_heads = attended.reshape(local_rows, H * HD).astype(jnp.bfloat16)
    hidden = inputs + RESIDUAL_MULT * dot_plain(mixed_heads, wo_full)
    inv_two = lax.rsqrt(jnp.mean(hidden * hidden, axis=-1, keepdims=True) + EPSILON)
    unit_two = hidden * inv_two
    normed2 = (unit_two * gain2_f).astype(jnp.bfloat16)
    wg_full, wu_full, wd_full = (
        lax.all_gather(w_gate, ("ctx", "fsdp"), axis=0, tiled=True),
        lax.all_gather(w_up, ("ctx", "fsdp"), axis=0, tiled=True),
        lax.all_gather(w_down, ("ctx", "fsdp"), axis=0, tiled=True),
    )
    gate_pre = dot_plain(normed2, wg_full)
    up_pre = dot_plain(normed2, wu_full)
    sig_gate = jax.nn.sigmoid(gate_pre)
    silu_gate = gate_pre * sig_gate
    activ = (silu_gate * up_pre).astype(jnp.bfloat16)
    result = hidden + RESIDUAL_MULT * dot_plain(activ, wd_full)
    output = result.astype(jnp.bfloat16)[None]
    grad_out = cotangent[0].astype(jnp.float32)
    grad_mlp = (RESIDUAL_MULT * grad_out).astype(jnp.bfloat16)
    silu_slope = sig_gate * (1.0 + gate_pre * (1.0 - sig_gate))
    wg_back, wu_back, wd_back = (
        lax.all_gather(w_gate, ("ctx", "fsdp"), axis=0, tiled=True),
        lax.all_gather(w_up, ("ctx", "fsdp"), axis=0, tiled=True),
        lax.all_gather(w_down, ("ctx", "fsdp"), axis=0, tiled=True),
    )
    grad_act = dot_back(grad_mlp, wd_back)
    grad_gate = (grad_act * up_pre * silu_slope).astype(jnp.bfloat16)
    grad_up = (grad_act * silu_gate).astype(jnp.bfloat16)
    grad_norm2 = dot_back(grad_gate, wg_back) + dot_back(grad_up, wu_back)
    left_cols = normed2
    gate_up_shard = lax.psum_scatter(
        jnp.concatenate([dot_outer(left_cols, grad_gate), dot_outer(left_cols, grad_up)], axis=1),
        ("ctx", "fsdp"),
        scatter_dimension=0,
        tiled=True,
    )
    wg_shard = gate_up_shard[:, :FF]
    wu_shard = gate_up_shard[:, FF:]
    left_cols = activ
    wd_shard = lax.psum_scatter(
        dot_outer(left_cols, grad_mlp), ("ctx", "fsdp"), scatter_dimension=0, tiled=True
    )
    grad_g2 = jnp.sum(grad_norm2 * unit_two, axis=0)
    grad_hidden = grad_out + norm_back(grad_norm2, unit_two, inv_two, gain2_f)
    grad_attn = (RESIDUAL_MULT * grad_hidden).astype(jnp.bfloat16)
    wq_back, wk_back, wv_back, wo_back = (
        lax.all_gather(w_query, ("ctx", "fsdp"), axis=0, tiled=True),
        lax.all_gather(w_key, ("ctx", "fsdp"), axis=0, tiled=True),
        lax.all_gather(w_value, ("ctx", "fsdp"), axis=0, tiled=True),
        lax.all_gather(w_output, ("ctx", "fsdp"), axis=0, tiled=True),
    )
    grad_wo = dot_outer(mixed_heads, grad_attn)
    grad_att = (
        dot_back(grad_attn, wo_back).astype(jnp.bfloat16).reshape(local_rows, KVH, group_size, HD)
    )
    row_delta = jnp.sum(grad_att.astype(jnp.float32) * attended, axis=-1)
    key_all, value_all = (
        lax.all_gather(key_rot, "ctx", axis=0, tiled=True),
        lax.all_gather(values, "ctx", axis=0, tiled=True),
    )
    key_width = math.gcd(length, 512)
    block_count = length // key_width

    def back_block(grad_query, index_block):
        block_start = index_block * key_width
        key_blk = lax.dynamic_slice_in_dim(key_all, block_start, key_width, 0).reshape(
            key_width, KVH, HD
        )
        value_blk = lax.dynamic_slice_in_dim(value_all, block_start, key_width, 0).reshape(
            key_width, KVH, HD
        )
        key_pos = block_start + jnp.arange(key_width, dtype=jnp.int32)
        key_docs = doc_index(key_pos, starts)
        skip_block = (block_start > last_pos) | (key_docs[key_width - 1] < first_doc)

        def compute(current):
            scores = (
                jnp.einsum("qkgd,tkd->qkgt", grouped, key_blk, preferred_element_type=jnp.float32)
                * SCORE_SCALE
            )
            allowed = (key_docs[None, :] == doc_ids[:, None]) & (
                key_pos[None, :] <= positions[:, None]
            )
            allowed = allowed[:, None, None, :]
            probs_blk = jnp.where(
                allowed, jnp.exp(jnp.where(allowed, scores, NEGATIVE) - log_sum[..., None]), 0.0
            )
            grad_probs = jnp.einsum(
                "qkgd,tkd->qkgt", grad_att, value_blk, preferred_element_type=jnp.float32
            )
            grad_scores = (probs_blk * (grad_probs - row_delta[..., None])).astype(jnp.bfloat16)
            new_query = (
                current
                + jnp.einsum(
                    "qkgt,tkd->qkgd", grad_scores, key_blk, preferred_element_type=jnp.float32
                )
                * SCORE_SCALE
            )
            grad_key = (
                jnp.einsum(
                    "qkgt,qkgd->tkd", grad_scores, grouped, preferred_element_type=jnp.float32
                )
                * SCORE_SCALE
            )
            grad_value = jnp.einsum(
                "qkgt,qkgd->tkd",
                probs_blk.astype(jnp.bfloat16),
                grad_att,
                preferred_element_type=jnp.float32,
            )
            return (
                new_query,
                (grad_key.reshape(key_width, KVH * HD), grad_value.reshape(key_width, KVH * HD)),
            )

        def nothing(current):
            zero_rows = jnp.zeros((key_width, KVH * HD), jnp.float32)
            return (current, (zero_rows, zero_rows))

        return lax.cond(skip_block, nothing, compute, grad_query)

    grad_query, key_terms = lax.scan(
        back_block,
        jnp.zeros((local_rows, KVH, group_size, HD), jnp.float32),
        jnp.arange(block_count),
    )
    key_term_all = key_terms[0].reshape(length, KVH * HD)
    value_term_all = key_terms[1].reshape(length, KVH * HD)
    grad_keys, grad_values = (
        lax.psum_scatter(
            key_term_all.astype(jnp.bfloat16), "ctx", scatter_dimension=0, tiled=True
        ).astype(jnp.float32),
        lax.psum_scatter(
            value_term_all.astype(jnp.bfloat16), "ctx", scatter_dimension=0, tiled=True
        ).astype(jnp.float32),
    )
    grad_q_pre = rotate(grad_query.reshape(local_rows, H * HD), cos_table, -sin_table, H).astype(
        jnp.bfloat16
    )
    grad_k_pre = rotate(grad_keys, cos_table, -sin_table, KVH).astype(jnp.bfloat16)
    grad_v_pre = grad_values.astype(jnp.bfloat16)
    grad_norm1 = (
        dot_back(grad_q_pre, wq_back)
        + dot_back(grad_k_pre, wk_back)
        + dot_back(grad_v_pre, wv_back)
    )
    grad_wq = dot_outer(normed1, grad_q_pre)
    grad_wk = dot_outer(normed1, grad_k_pre)
    grad_wv = dot_outer(normed1, grad_v_pre)
    grad_g1 = jnp.sum(grad_norm1 * unit_one, axis=0)
    grad_inputs = grad_hidden + norm_back(grad_norm1, unit_one, inv_one, gain1_f)
    g1_shard, g2_shard, wq_shard, wk_shard, wv_shard, wo_shard = (
        lax.psum_scatter(grad_g1, ("ctx", "fsdp"), scatter_dimension=0, tiled=True),
        lax.psum_scatter(grad_g2, ("ctx", "fsdp"), scatter_dimension=0, tiled=True),
        lax.psum_scatter(grad_wq, ("ctx", "fsdp"), scatter_dimension=0, tiled=True),
        lax.psum_scatter(grad_wk, ("ctx", "fsdp"), scatter_dimension=0, tiled=True),
        lax.psum_scatter(grad_wv, ("ctx", "fsdp"), scatter_dimension=0, tiled=True),
        lax.psum_scatter(grad_wo, ("ctx", "fsdp"), scatter_dimension=0, tiled=True),
    )
    return (
        output,
        grad_inputs[None],
        g1_shard,
        wq_shard,
        wk_shard,
        wv_shard,
        wo_shard,
        g2_shard,
        wg_shard,
        wu_shard,
        wd_shard,
    )


def solution(mesh):
    in_specs = (
        P("fsdp", "ctx", None),
        P("fsdp", None),
        P("fsdp", "ctx", None),
        P(("ctx", "fsdp")),
        P(("ctx", "fsdp"), None),
        P(("ctx", "fsdp"), None),
        P(("ctx", "fsdp"), None),
        P(("ctx", "fsdp"), None),
        P(("ctx", "fsdp")),
        P(("ctx", "fsdp"), None),
        P(("ctx", "fsdp"), None),
        P(("ctx", "fsdp"), None),
    )
    out_specs = (
        P("fsdp", "ctx", None),
        P("fsdp", "ctx", None),
        P(("ctx", "fsdp")),
        P(("ctx", "fsdp"), None),
        P(("ctx", "fsdp"), None),
        P(("ctx", "fsdp"), None),
        P(("ctx", "fsdp"), None),
        P(("ctx", "fsdp")),
        P(("ctx", "fsdp"), None),
        P(("ctx", "fsdp"), None),
        P(("ctx", "fsdp"), None),
    )
    return jax.shard_map(
        on_device, mesh=mesh, in_specs=in_specs, out_specs=out_specs, check_vma=False
    )
```

profile of v0, /device:TPU:0, one launch (start us, length us, event | category | flops | bytes accessed | tf_op | source)
XLA Modules:
  0.0 4451.8 jit_solution(17137574567937606820)
XLA Ops:
  10.4 42.1 all-reduce.6
  52.5 1.2 fusion.52
  53.8 16.1 all-gather.16.cloned.1.call-done
  69.9 2.9 convolution_convert_fusion.1
  74.2 53.6 %all-gather.10.cloned.1.call-done = bf16[2048,512]{1,0:T(8,128)(2,1)} async-done(((bf16[64,512]{1,0:T(8,128)(2,1)}), bf16[2048,512]{1,0:T(8,128)(2,1)}) %all-gather.10.cloned.1.call-update) | async-done | bytes 2097168 | tf_op jit(solution)/shard_map/all_gather | solution.py:101
  127.8 2.9 copy.61
  130.7 1.8 fusion.58
  136.5 33.2 all-gather.18.cloned.1.call-done
  169.7 2.3 copy.63
  171.9 76.2 %all-gather.14.cloned.1.call-done = bf16[2048,2048]{1,0:T(8,128)(2,1)} async-done(((bf16[64,2048]{1,0:T(8,128)(2,1)}), bf16[2048,2048]{1,0:T(8,128)(2,1)}) %all-gather.14.cloned.1.call-update) | async-done | bytes 8388624 | tf_op jit(solution)/shard_map/all_gather | solution.py:100
  248.2 12.3 copy.62
  260.5 5.9 fusion.56
  266.6 22.1 all-gather.12.cloned.1.call-done
  288.8 13.2 while.37
  291.4 7.7 conditional.6
  291.7 1.8 constant_dynamic-slice_fusion
  293.5 1.3 fusion.4
  294.8 2.1 fusion.6
  296.9 2.2 fusion.13
  303.0 64.5 %all-gather.20.cloned.1.call-done = bf16[2048,2048]{1,0:T(8,128)(2,1)} async-done(((bf16[64,2048]{1,0:T(8,128)(2,1)}), bf16[2048,2048]{1,0:T(8,128)(2,1)}) %all-gather.20.cloned.1.call-update) | async-done | bytes 8388624 | tf_op jit(solution)/shard_map/all_gather | solution.py:103
  367.5 5.0 multiply_reduce_fusion.3
  372.7 190.5 %all-gather.22.cloned.1.call-done = bf16[2048,8192]{1,0:T(8,128)(2,1)} async-done(((bf16[64,8192]{1,0:T(8,128)(2,1)}), bf16[2048,8192]{1,0:T(8,128)(2,1)}) %all-gather.22.cloned.1.call-update) | async-done | bytes 33554448 | tf_op jit(solution)/shard_map/all_gather | solution.py:174
  563.2 17.7 fusion.86
  580.9 177.5 %all-gather.24.cloned.1.call-done = bf16[2048,8192]{1,0:T(8,128)(2,1)} async-done(((bf16[64,8192]{1,0:T(8,128)(2,1)}), bf16[2048,8192]{1,0:T(8,128)(2,1)}) %all-gather.24.cloned.1.call-update) | async-done | bytes 33554448 | tf_op jit(solution)/shard_map/all_gather | solution.py:175
  758.4 17.8 fusion.87
  776.2 177.5 %all-gather.26.cloned.1.call-done = bf16[8192,2048]{1,0:T(8,128)(2,1)} async-done(((bf16[256,2048]{1,0:T(8,128)(2,1)}), bf16[8192,2048]{1,0:T(8,128)(2,1)}) %all-gather.26.cloned.1.call-update) | async-done | bytes 33554448 | tf_op jit(solution)/shard_map/all_gather | solution.py:176
  953.6 21.3 multiply_convert_fusion
  974.9 24.9 fusion.91
  999.8 15.9 fusion.88
  1015.7 18.3 multiply_reduce_fusion
  1034.0 1.5 convert_add_fusion
  1036.5 6.3 convolution_convert_fusion
  1043.8 1.3 multiply_reduce_fusion.1
  1045.2 21.4 while.38
  1048.0 12.8 conditional.7
  1048.0 1.8 constant_dynamic-slice_fusion.2
  1049.8 1.3 fusion.85
  1051.3 4.0 fusion.20
  1056.2 1.4 fusion.30
  1057.6 3.1 fusion.25
  1061.2 1.1 constant_dynamic-update-slice_fusion.3
  1065.5 1.1 constant_dynamic-update-slice_fusion.3
  1066.6 25.7 fusion.90
  1092.4 86.8 %pad_maximum_fusion = f32[2048,16384]{1,0:T(8,128)} fusion(f32[2048,8192]{1,0:T(8,128)} %fusion.91, f32[2048,8192]{1,0:T(8,128)} %fusion.90), kind=kLoop, calls=%fused_computation.52 | loop fusion | flops 33554432 | bytes 268435456 | tf_op jit(solution)/shard_map/concatenate | solution.py:199
  1179.4 1.1 copy.67
  1180.6 2.8 fusion.60
  1183.7 24.6 reduce-scatter.10.cloned.1.call-done
  1208.3 3.6 fusion.70
  1212.2 9.4 fusion.62
  1221.7 1.1 copy-done.5
  1223.0 8.3 fusion.69
  1232.4 25.8 fusion.64
  1258.2 6.8 fusion.89
  1265.0 16.1 fusion.38
  1282.0 2.6 fusion.51
  1284.6 41.6 all-reduce.5
  1327.4 1.3 fusion.50
  1328.7 1754.9 %all-reduce.9.cloned.1.call-done = f32[2048,16384]{1,0:T(8,128)} async-done(((f32[2048,16384]{1,0:T(8,128)}), f32[2048,16384]{1,0:T(8,128)}) %all-reduce.9.cloned.1.call-update) | async-done | bytes 134217744
  3083.6 4.9 fusion.84
  3088.5 139.4 %reduce-scatter.14.cloned.1.call-done = f32[64,512]{1,0:T(8,128)} async-done(((f32[2048,512]{1,0:T(8,128)}), f32[64,512]{1,0:T(8,128)}) %reduce-scatter.14.cloned.1.call-update) | async-done | bytes 131088 | tf_op jit(solution)/shard_map/reduce_scatter | solution.py:323
  3227.9 140.9 %reduce-scatter.16.cloned.1.call-done = f32[64,512]{1,0:T(8,128)} async-done(((f32[2048,512]{1,0:T(8,128)}), f32[64,512]{1,0:T(8,128)}) %reduce-scatter.16.cloned.1.call-update) | async-done | bytes 131088 | tf_op jit(solution)/shard_map/reduce_scatter | solution.py:324
  3368.9 181.5 %reduce-scatter.12.cloned.1.call-done = f32[64,2048]{1,0:T(8,128)} async-done(((f32[2048,2048]{1,0:T(8,128)}), f32[64,2048]{1,0:T(8,128)}) %reduce-scatter.12.cloned.1.call-update) | async-done | bytes 524304 | tf_op jit(solution)/shard_map/reduce_scatter | solution.py:322
  3550.4 187.4 %reduce-scatter.18.cloned.1.call-done = f32[64,2048]{1,0:T(8,128)} async-done(((f32[2048,2048]{1,0:T(8,128)}), f32[64,2048]{1,0:T(8,128)}) %reduce-scatter.18.cloned.1.call-update) | async-done | bytes 524304 | tf_op jit(solution)/shard_map/reduce_scatter | solution.py:325
  3737.8 707.1 %reduce-scatter.20.cloned.1.call-done = f32[256,2048]{1,0:T(8,128)} async-done(((f32[8192,2048]{1,0:T(8,128)}), f32[256,2048]{1,0:T(8,128)}) %reduce-scatter.20.cloned.1.call-update) | async-done | bytes 2097168 | tf_op jit(solution)/shard_map/reduce_scatter | solution.py:207
  (169 shorter events, 23.5 us)
Async XLA Ops:
  7.2 129.0 %copy-start.22 = (s32[1,8]{1,0:T(1,128)S(1)}, s32[1,8]{1,0:T(1,128)}, u32[]{:S(2)}) copy-start(s32[1,8]{1,0:T(1,128)} %param.21) | copy-start | bytes 100
  7.2 62.7 %all-gather.16.cloned.1.call-start = ((), (), s32[]{:S(2)}) async-start(), calls=%async_computation.10 | async-start | bytes 2162688 | tf_op jit(solution)/shard_map/all_gather | solution.py:102
  7.9 119.9 %all-gather.10.cloned.1.call-start = ((), (), s32[]{:S(2)}) async-start(), calls=%async_computation.7 | async-start | bytes 2162688 | tf_op jit(solution)/shard_map/all_gather | solution.py:101
  8.7 161.0 %all-gather.18.cloned.1.call-start = ((), (), s32[]{:S(2)}) async-start(), calls=%async_computation.11 | async-start | bytes 1179648 | tf_op jit(solution)/shard_map/all_gather | solution.py:122
  52.5 208.0 %copy-start.13 = (f32[2048]{0:T(1024)}, f32[2048]{0:T(1024)S(1)}, u32[]{:S(2)}) copy-start(f32[2048]{0:T(1024)S(1)} %convert_element_type.177) | copy-start | bytes 24580
  53.8 206.8 %copy-start.20 = (f32[128]{0:T(128)}, f32[128]{0:T(128)S(1)}, u32[]{:S(2)}) copy-start(f32[128]{0:T(128)S(1)} %add_rsqrt_fusion.1) | copy-start | bytes 1540
  72.8 175.4 %all-gather.14.cloned.1.call-start = ((), (), s32[]{:S(2)}) async-start(), calls=%async_computation.9 | async-start | bytes 8650752 | tf_op jit(solution)/shard_map/all_gather | solution.py:100
  73.4 215.3 %all-gather.12.cloned.1.call-start = ((), (), s32[]{:S(2)}) async-start(), calls=%async_computation.8 | async-start | bytes 1179648 | tf_op jit(solution)/shard_map/all_gather | solution.py:121
  74.2 192.2 %copy-start.16 = (f32[128,32]{0,1:T(8,128)}, f32[128,32]{0,1:T(8,128)S(1)}, u32[]{:S(2)}) copy-start(f32[128,32]{0,1:T(8,128)S(1)} %get-tuple-element.960) | copy-start | bytes 49156
  133.3 234.2 %all-gather.20.cloned.1.call-start = ((), (), s32[]{:S(2)}) async-start(), calls=%async_computation.12 | async-start | bytes 8650752 | tf_op jit(solution)/shard_map/all_gather | solution.py:103
  133.9 429.3 %all-gather.22.cloned.1.call-start = ((), (), s32[]{:S(2)}) async-start(), calls=%async_computation.13 | async-start | bytes 34603008 | tf_op jit(solution)/shard_map/all_gather | solution.py:174
  134.6 623.8 %all-gather.24.cloned.1.call-start = ((), (), s32[]{:S(2)}) async-start(), calls=%async_computation.14 | async-start | bytes 34603008 | tf_op jit(solution)/shard_map/all_gather | solution.py:175
  135.4 818.2 %all-gather.26.cloned.1.call-start = ((), (), s32[]{:S(2)}) async-start(), calls=%async_computation.15 | async-start | bytes 34603008 | tf_op jit(solution)/shard_map/all_gather | solution.py:176
  136.1 1043.3 %reduce-scatter.8.cloned.1.call-start = ((), (), s32[]{:S(2)}) async-start(), calls=%async_computation.16 | async-start | bytes 1179648 | tf_op jit(solution)/shard_map/reduce_scatter | solution.py:297
  248.2 12.4 copy-start
  372.4 661.5 %copy-start.2 = (f32[128,2048]{1,0:T(8,128)}, f32[128,2048]{1,0:T(8,128)S(1)}, u32[]{:S(2)}) copy-start(f32[128,2048]{1,0:T(8,128)S(1)} %get-tuple-element.962) | copy-start | bytes 3145732
  372.7 602.3 %copy-start.6 = (bf16[128,2048]{1,0:T(8,128)(2,1)}, bf16[128,2048]{1,0:T(8,128)(2,1)S(1)}, u32[]{:S(2)}) copy-start(bf16[128,2048]{1,0:T(8,128)(2,1)S(1)} %multiply_convert_fusion.4) | copy-start | bytes 1572868
  974.9 24.9 copy-start.8
  1015.7 18.3 copy-start.11
  1035.5 1.0 copy-start.4
  1066.6 141.7 %reduce-scatter.10.cloned.1.call-start = ((), (), s32[]{:S(2)}) async-start(), calls=%async_computation.17 | async-start | bytes 1179648 | tf_op jit(solution)/shard_map/reduce_scatter | solution.py:300
  1092.4 1991.2 %all-reduce.9.cloned.1.call-start = ((), (), s32[]{:S(2)}) async-start(), calls=%async_computation.23 | async-start | bytes 268435456
  1179.3 1.2 copy-start.17
  1179.3 1.2 copy-start.18
  1179.3 1.3 copy-start.1
  1179.3 1.3 copy-start.14
  1179.3 1.3 copy-start.21
  1179.3 2048.6 %reduce-scatter.14.cloned.1.call-start = ((), (), s32[]{:S(2)}) async-start(), calls=%async_computation.19 | async-start | bytes 4325376 | tf_op jit(solution)/shard_map/reduce_scatter | solution.py:323
  1183.4 2185.5 %reduce-scatter.16.cloned.1.call-start = ((), (), s32[]{:S(2)}) async-start(), calls=%async_computation.20 | async-start | bytes 4325376 | tf_op jit(solution)/shard_map/reduce_scatter | solution.py:324
  1212.0 2338.5 %reduce-scatter.12.cloned.1.call-start = ((), (), s32[]{:S(2)}) async-start(), calls=%async_computation.18 | async-start | bytes 17301504 | tf_op jit(solution)/shard_map/reduce_scatter | solution.py:322
  1221.7 1.2 copy-start.5
  1221.7 1.4 copy-start.10
  1221.7 2516.1 %reduce-scatter.18.cloned.1.call-start = ((), (), s32[]{:S(2)}) async-start(), calls=%async_computation.21 | async-start | bytes 17301504 | tf_op jit(solution)/shard_map/reduce_scatter | solution.py:325
  1231.3 1.1 copy-start.12
  1231.4 3213.6 %reduce-scatter.20.cloned.1.call-start = ((), (), s32[]{:S(2)}) async-start(), calls=%async_computation.22 | async-start | bytes 69206016 | tf_op jit(solution)/shard_map/reduce_scatter | solution.py:207
  1258.2 6.8 copy-start.3
  1258.2 6.8 copy-start.7
  1265.0 16.1 copy-start.9
  1265.0 17.0 copy-start.15
  1281.2 3.4 copy-start.19
Sparse Core Ops, SparseCore 0:
  10.9 58.9 all-gather.15
  72.7 55.0 all-gather.9
  130.5 39.1 all-gather.17
  172.4 75.7 all-gather.13
  250.6 38.0 all-gather.11
  291.4 76.0 all-gather.19
  370.3 192.7 all-gather.21
  566.0 192.3 all-gather.23
  761.3 192.3 all-gather.25
  1066.7 74.9 reduce-scatter.7
  1145.1 63.1 reduce-scatter.9
  1214.6 1868.9 all-reduce.8
  3086.5 141.4 reduce-scatter.13
  3230.6 138.1 reduce-scatter.15
  3371.6 178.7 reduce-scatter.11
  3553.1 184.6 reduce-scatter.17
  3740.6 704.3 reduce-scatter.19
where the time goes:
time: 4470 us; the launch traced here: 4450 us
  waiting for transfers between devices  3950 us (88%)
  matrix products  254 us (6%)
  other arithmetic  98.5 us (2%)
  blocking collectives  83.7 us (2%)
    unnamed x18, waiting for transfers between devices  1760 us
    reduce_scatter x1, waiting for transfers between devices, on_device(): lax.psum_scatter(dot_outer(left_cols, grad_mlp), ('ctx', 'fsdp'), scatter...  707 us
    all_gather x1, waiting for transfers between devices, on_device(): lax.all_gather(w_gate, ('ctx', 'fsdp'), axis=0, tiled=True)  191 us
    reduce_scatter x1, waiting for transfers between devices, on_device(): lax.psum_scatter(grad_wo, ('ctx', 'fsdp'), scatter_dimension=0, tiled=True)  187 us
    reduce_scatter x1, waiting for transfers between devices, on_device(): lax.psum_scatter(grad_wq, ('ctx', 'fsdp'), scatter_dimension=0, tiled=True)  182 us
    all_gather x1, waiting for transfers between devices, on_device(): lax.all_gather(w_up, ('ctx', 'fsdp'), axis=0, tiled=True)  177 us
    all_gather x1, waiting for transfers between devices, on_device(): lax.all_gather(w_down, ('ctx', 'fsdp'), axis=0, tiled=True)  177 us
    reduce_scatter x1, waiting for transfers between devices, on_device(): lax.psum_scatter(grad_wv, ('ctx', 'fsdp'), scatter_dimension=0, tiled=True)  141 us
  transfers between devices with their start and end apart: 17, of which 16 were waited for; matrix products, arithmetic and copies ran while one was open for 6% of the time, Pallas kernels for 0%

commit v1 on v0

--- a/solution.py
+++ b/solution.py
@@ -1,8 +1,11 @@
+import functools
 import math
 
 import jax
 import jax.numpy as jnp
 from jax import lax
+from jax.experimental import pallas as pl
+from jax.experimental.pallas import tpu as pltpu
 from jax.sharding import PartitionSpec as P
 
 H = 32
@@ -68,7 +71,7 @@
     return inv_scale * (scaled - unit_rows * jnp.mean(scaled * unit_rows, axis=-1, keepdims=True))
 
 
-def on_device(
+def general_device(
     tokens,
     doc_lengths,
     cotangent,
@@ -339,6 +342,273 @@
     )
 
 
+def rows_of(blocks):
+    return blocks.reshape((-1,) + blocks.shape[2:])
+
+
+def gather_ctx(local):
+    return lax.all_gather(local, "ctx", axis=0, tiled=True)
+
+
+def scatter_ctx(partial):
+    return lax.psum_scatter(partial, "ctx", scatter_dimension=0, tiled=True).astype(jnp.float32)
+
+
+def swap_ctx(blocks):
+    return lax.all_to_all(blocks, "ctx", split_axis=0, concat_axis=0, tiled=True)
+
+
+def spread_columns(blocks):
+    mine = swap_ctx(blocks)
+    full = lax.all_gather(mine[:, None], "fsdp", axis=1, tiled=True)
+    return full.reshape(-1, blocks.shape[-1])
+
+
+def return_columns(grad, ctx_size, fsdp_size):
+    by_owner = grad.reshape(ctx_size, fsdp_size, -1, grad.shape[-1]).transpose(1, 0, 2, 3)
+    mine = lax.psum_scatter(rows_of(rows_of(by_owner)), "fsdp", scatter_dimension=0, tiled=True)
+    return swap_ctx(mine.reshape(ctx_size, -1, grad.shape[-1]))
+
+
+def half_turn(values, sign_table):
+    lane = lax.broadcasted_iota(jnp.int32, values.shape, 1)
+    width = values.shape[1]
+    quarter = HD // 2
+    ahead = pltpu.roll(values, width - quarter, 1)
+    behind = pltpu.roll(values, quarter, 1)
+    return jnp.where(lane % HD < quarter, ahead, behind) * sign_table
+
+
+def turn(values, cos_table, sign_table):
+    copies = values.shape[1] // cos_table.shape[1]
+    if copies > 1:
+        cos_table = jnp.concatenate([cos_table] * copies, axis=1)
+        sign_table = jnp.concatenate([sign_table] * copies, axis=1)
+    return values * cos_table + half_turn(values, sign_table)
+
+
+def attention_forward_kernel(
+    block_rows, qkv_ref, cos_ref, sin_ref, doc_col_ref, doc_row_ref, q_ref, kv_ref, out_ref, lse_ref
+):
+    length = qkv_ref.shape[0]
+    group = H // KVH
+    width = group * HD
+    q_ref[...] = turn(qkv_ref[:, :width], cos_ref[...], sin_ref[...]).astype(jnp.bfloat16)
+    pair = qkv_ref[:, width:]
+    lane = lax.broadcasted_iota(jnp.int32, pair.shape, 1)
+    turned = turn(pair, cos_ref[...], sin_ref[...])
+    kv_ref[...] = jnp.where(lane < HD, turned, pair).astype(jnp.bfloat16)
+    for block in range(length // block_rows):
+        rows = slice(block * block_rows, (block + 1) * block_rows)
+        reach = (block + 1) * block_rows
+        keys = kv_ref[:reach, :HD]
+        values = kv_ref[:reach, HD:]
+        query_at = block * block_rows + lax.broadcasted_iota(jnp.int32, (block_rows, reach), 0)
+        key_at = lax.broadcasted_iota(jnp.int32, (block_rows, reach), 1)
+        allowed = (doc_col_ref[rows, :] == doc_row_ref[:, :reach]) & (key_at <= query_at)
+        for head in range(group):
+            cols = slice(head * HD, (head + 1) * HD)
+            scores = dot_back(q_ref[rows, cols], keys) * SCORE_SCALE
+            masked = jnp.where(allowed, scores, NEGATIVE)
+            top = jnp.max(masked, axis=1, keepdims=True)
+            weights = jnp.where(allowed, jnp.exp(masked - top), 0.0)
+            total = jnp.sum(weights, axis=1, keepdims=True)
+            mixed = dot_plain(weights.astype(jnp.bfloat16), values)
+            out_ref[rows, cols] = (mixed / total).astype(jnp.bfloat16)
+            lse_ref[rows, head : head + 1] = top + jnp.log(total)
+
+
+def attention_backward_kernel(
+    block_rows, q_ref, kv_ref, do_ref, lse_ref, cos_ref, sin_ref, doc_col_ref, doc_row_ref, grad_ref, dq_ref, dkv_ref
+):
+    length = q_ref.shape[0]
+    group = H // KVH
+    width = group * HD
+    dkv_ref[...] = jnp.zeros_like(dkv_ref)
+    for block in range(length // block_rows):
+        rows = slice(block * block_rows, (block + 1) * block_rows)
+        reach = (block + 1) * block_rows
+        keys = kv_ref[:reach, :HD]
+        values = kv_ref[:reach, HD:]
+        query_at = block * block_rows + lax.broadcasted_iota(jnp.int32, (block_rows, reach), 0)
+        key_at = lax.broadcasted_iota(jnp.int32, (block_rows, reach), 1)
+        allowed = (doc_col_ref[rows, :] == doc_row_ref[:, :reach]) & (key_at <= query_at)
+        for head in range(group):
+            cols = slice(head * HD, (head + 1) * HD)
+            query = q_ref[rows, cols]
+            grad_out = do_ref[rows, cols]
+            scores = dot_back(query, keys) * SCORE_SCALE
+            probs = jnp.where(
+                allowed,
+                jnp.exp(jnp.where(allowed, scores, NEGATIVE) - lse_ref[rows, head : head + 1]),
+                0.0,
+            )
+            grad_probs = dot_back(grad_out, values)
+            delta = jnp.sum(probs * grad_probs, axis=1, keepdims=True)
+            grad_scores = (probs * (grad_probs - delta)).astype(jnp.bfloat16)
+            dq_ref[rows, cols] = dot_plain(grad_scores, keys) * SCORE_SCALE
+            dkv_ref[:reach, :HD] += dot_outer(grad_scores, query) * SCORE_SCALE
+            dkv_ref[:reach, HD:] += dot_outer(probs.astype(jnp.bfloat16), grad_out)
+    grad_ref[:, :width] = turn(dq_ref[...], cos_ref[...], -sin_ref[...]).astype(jnp.bfloat16)
+    pair = dkv_ref[...]
+    lane = lax.broadcasted_iota(jnp.int32, pair.shape, 1)
+    turned = turn(pair, cos_ref[...], -sin_ref[...])
+    grad_ref[:, width:] = jnp.where(lane < HD, turned, pair).astype(jnp.bfloat16)
+
+
+def in_vmem(count):
+    return [pl.BlockSpec(memory_space=pltpu.VMEM)] * count
+
+
+def attention_forward(qkv, tables, block_rows):
+    length = qkv.shape[0]
+    width = (H // KVH) * HD
+    return pl.pallas_call(
+        functools.partial(attention_forward_kernel, block_rows),
+        out_shape=(
+            jax.ShapeDtypeStruct((length, width), jnp.bfloat16),
+            jax.ShapeDtypeStruct((length, 2 * HD), jnp.bfloat16),
+            jax.ShapeDtypeStruct((length, width), jnp.bfloat16),
+            jax.ShapeDtypeStruct((length, H // KVH), jnp.float32),
+        ),
+        in_specs=in_vmem(5),
+        out_specs=tuple(in_vmem(4)),
+        compiler_params=pltpu.CompilerParams(vmem_limit_bytes=48 * 2**20),
+        name="attend",
+    )(qkv, *tables)
+
+
+def attention_backward(q, kv, grad_out, lse, tables, block_rows):
+    length, width = q.shape
+    return pl.pallas_call(
+        functools.partial(attention_backward_kernel, block_rows),
+        out_shape=jax.ShapeDtypeStruct((length, width + 2 * HD), jnp.bfloat16),
+        in_specs=in_vmem(8),
+        out_specs=in_vmem(1)[0],
+        scratch_shapes=[
+            pltpu.VMEM((length, width), jnp.float32),
+            pltpu.VMEM((length, 2 * HD), jnp.float32),
+        ],
+        compiler_params=pltpu.CompilerParams(vmem_limit_bytes=48 * 2**20),
+        name="attend_back",
+    )(q, kv, grad_out, lse, *tables)
+
+
+def on_device(
+    tokens,
+    doc_lengths,
+    cotangent,
+    gain_attn,
+    w_query,
+    w_key,
+    w_value,
+    w_output,
+    gain_mlp,
+    w_gate,
+    w_up,
+    w_down,
+):
+    local_rows, model = tokens.shape[1:]
+    ctx_size = lax.axis_size("ctx")
+    fsdp_size = lax.axis_size("fsdp")
+    length = local_rows * ctx_size
+    group_width = (H // KVH) * HD
+    ff_slice = FF // ctx_size
+    held_rows = w_query.shape[0]
+    bf16 = jnp.bfloat16
+
+    positions = jnp.arange(length, dtype=jnp.int32)
+    seq_lengths = doc_lengths[0]
+    starts = jnp.cumsum(seq_lengths) - seq_lengths
+    doc_ids = doc_index(positions, starts)
+    cos_half, sin_half = rope_tables(positions)
+    cos_table = jnp.concatenate([cos_half] * 4, axis=1)
+    sin_table = jnp.concatenate([-sin_half, sin_half] * 2, axis=1)
+    tables = (cos_table, sin_table, doc_ids[:, None], doc_ids[None, :])
+
+    gains = lax.all_gather(jnp.stack([gain_attn, gain_mlp]), ("ctx", "fsdp"), axis=1, tiled=True)
+    gain1 = gains[0].astype(jnp.float32)
+    gain2 = gains[1].astype(jnp.float32)
+
+    def by_slice(weight):
+        return weight.reshape(held_rows, ctx_size, -1)
+
+    qkv_parts = jnp.concatenate([by_slice(w_query), by_slice(w_key), by_slice(w_value)], axis=2)
+    w_qkv = spread_columns(qkv_parts.transpose(1, 0, 2))
+    wo_mine = lax.all_gather(w_output, "fsdp", axis=0, tiled=True)
+    gu_parts = jnp.concatenate([by_slice(w_gate), by_slice(w_up)], axis=2)
+    w_gu = spread_columns(gu_parts.transpose(1, 0, 2))
+    wd_mine = lax.all_gather(w_down, "fsdp", axis=0, tiled=True)
+
+    inputs = tokens[0].astype(jnp.float32)
+    inv_one = lax.rsqrt(jnp.mean(inputs * inputs, axis=-1, keepdims=True) + EPSILON)
+    unit_one = inputs * inv_one
+    normed1 = gather_ctx((unit_one * gain1).astype(bf16))
+    grad_out = cotangent[0].astype(jnp.float32)
+    grad_mlp = gather_ctx((RESIDUAL_MULT * grad_out).astype(bf16))
+
+    block_rows = math.gcd(length, 256)
+    qkv = dot_plain(normed1, w_qkv)
+    q, kv, mixed_heads, log_sum = attention_forward(qkv, tables, block_rows)
+    hidden = inputs + RESIDUAL_MULT * scatter_ctx(dot_plain(mixed_heads, wo_mine).astype(bf16))
+    inv_two = lax.rsqrt(jnp.mean(hidden * hidden, axis=-1, keepdims=True) + EPSILON)
+    unit_two = hidden * inv_two
+    normed2 = gather_ctx((unit_two * gain2).astype(bf16))
+
+    gate_up = dot_plain(normed2, w_gu)
+    gate_pre, up_pre = gate_up[:, :ff_slice], gate_up[:, ff_slice:]
+    sig_gate = jax.nn.sigmoid(gate_pre)
+    silu_gate = gate_pre * sig_gate
+    activ = (silu_gate * up_pre).astype(bf16)
+    branch = scatter_ctx(dot_plain(activ, wd_mine).astype(bf16))
+    output = (hidden + RESIDUAL_MULT * branch).astype(bf16)[None]
+
+    silu_slope = sig_gate * (1.0 + gate_pre * (1.0 - sig_gate))
+    grad_act = dot_back(grad_mlp, wd_mine)
+    grad_gu = jnp.concatenate(
+        [(grad_act * up_pre * silu_slope).astype(bf16), (grad_act * silu_gate).astype(bf16)], axis=1
+    )
+    grad_norm2 = scatter_ctx(dot_back(grad_gu, w_gu).astype(bf16))
+    gu_back = return_columns(dot_outer(normed2, grad_gu).astype(bf16), ctx_size, fsdp_size)
+    wd_back = lax.psum_scatter(
+        dot_outer(activ, grad_mlp).astype(bf16), "fsdp", scatter_dimension=0, tiled=True
+    )
+
+    grad_g2 = jnp.sum(grad_norm2 * unit_two, axis=0)
+    grad_hidden = grad_out + norm_back(grad_norm2, unit_two, inv_two, gain2)
+    grad_attn = gather_ctx((RESIDUAL_MULT * grad_hidden).astype(bf16))
+    grad_mixed = dot_back(grad_attn, wo_mine).astype(bf16)
+    wo_back = lax.psum_scatter(
+        dot_outer(mixed_heads, grad_attn).astype(bf16), "fsdp", scatter_dimension=0, tiled=True
+    )
+    grad_qkv = attention_backward(q, kv, grad_mixed, log_sum, tables, block_rows)
+    grad_norm1 = scatter_ctx(dot_back(grad_qkv, w_qkv).astype(bf16))
+    qkv_back = return_columns(dot_outer(normed1, grad_qkv).astype(bf16), ctx_size, fsdp_size)
+    grad_g1 = jnp.sum(grad_norm1 * unit_one, axis=0)
+    grad_inputs = grad_hidden + norm_back(grad_norm1, unit_one, inv_one, gain1)
+    gain_back = lax.psum_scatter(
+        jnp.stack([grad_g1, grad_g2]), ("ctx", "fsdp"), scatter_dimension=1, tiled=True
+    )
+
+    def joined(parts):
+        return parts.transpose(1, 0, 2).reshape(held_rows, -1).astype(jnp.float32)
+
+    key_end = group_width + HD
+    return (
+        output,
+        grad_inputs[None],
+        gain_back[0],
+        joined(qkv_back[:, :, :group_width]),
+        joined(qkv_back[:, :, group_width:key_end]),
+        joined(qkv_back[:, :, key_end:]),
+        wo_back.astype(jnp.float32),
+        gain_back[1],
+        joined(gu_back[:, :, :ff_slice]),
+        joined(gu_back[:, :, ff_slice:]),
+        wd_back.astype(jnp.float32),
+    )
+
+
 def solution(mesh):
     in_specs = (
         P("fsdp", "ctx", None),
@@ -367,6 +637,7 @@
         P(("ctx", "fsdp"), None),
         P(("ctx", "fsdp"), None),
     )
+    split_heads = mesh.shape["ctx"] == KVH
     return jax.shard_map(
-        on_device, mesh=mesh, in_specs=in_specs, out_specs=out_specs, check_vma=False
-    )
+        on_device if split_heads else general_device, mesh=mesh, in_specs=in_specs, out_specs=out_specs, check_vma=False
+    )

time: 4470 us -> 1270 us (0.28)
  waiting for transfers between devices: 3950 us -> 893 us
  matrix products: 254 us -> 98.2 us
  other arithmetic: 98.5 us -> 24.2 us
  blocking collectives: 83.7 us -> 142 us
    unnamed x18, waiting for transfers between devices: 1760 us -> 137 us
    reduce_scatter x7 -> x8, waiting for transfers between devices: 1380 us -> 406 us  [the longest x4 295 us: scatter_ctx(): lax.psum_scatter(partial, 'ctx', scatter_dimension=0, tiled=True)]
    all_gather x9 -> x8, waiting for transfers between devices: 811 us -> 350 us  [the longest x4 274 us: gather_ctx(): return lax.all_gather(local, 'ctx', axis=0, tiled=True)]
    all_to_all x0 -> x2, blocking collectives: none -> 103 us  [swap_ctx(): lax.all_to_all(blocks, 'ctx', split_axis=0, concat_axis=0, tiled=True)]
    concatenate x3 -> x1, other arithmetic: 87.6 us -> 0.88 us  [on_device(): cos_table = jnp.concatenate([cos_half] * 4, axis=1)]
    unnamed x2 -> x0, blocking collectives: 83.7 us -> none
    dot_general x7 -> x4, matrix products: 101 us -> 31 us  [dot_outer(): lax.dot_general(left, right, (((0,), (0,)), ((), ())), preferred_element_...]
  transfers between devices with their start and end apart: 17 -> 19, of which waited for: 16 -> 15; matrix products, arithmetic and copies ran while one was open for 6% -> 9% of each run, Pallas kernels for 0% -> 1%
where the time goes in v1:
time: 1270 us; the launch traced here: 1260 us
  waiting for transfers between devices  893 us (70%)
  blocking collectives  142 us (11%)
  matrix products  98.2 us (8%)
  local copies, waits for them, and re-layouts  51.2 us (4%)
  other arithmetic  24.2 us (2%)
  Pallas kernels  21.5 us (2%)
  between operations  14.6 us (1%)
    reduce_scatter x4, waiting for transfers between devices, scatter_ctx(): lax.psum_scatter(partial, 'ctx', scatter_dimension=0, tiled=True)  295 us
    all_gather x4, waiting for transfers between devices, gather_ctx(): return lax.all_gather(local, 'ctx', axis=0, tiled=True)  274 us
    unnamed x18, waiting for transfers between devices  137 us
    all_to_all x2, blocking collectives, swap_ctx(): lax.all_to_all(blocks, 'ctx', split_axis=0, concat_axis=0, tiled=True)  103 us
    all_gather x2, waiting for transfers between devices, spread_columns(): full = lax.all_gather(mine[:, None], 'fsdp', axis=1, tiled=True)  53.7 us
    reduce_scatter x2, waiting for transfers between devices, return_columns(): lax.psum_scatter(rows_of(rows_of(by_owner)), 'fsdp', scatter_dimension=0,...  44.3 us
    reduce_scatter x1, waiting for transfers between devices, on_device(): lax.psum_scatter(dot_outer(activ, grad_mlp).astype(bf16), 'fsdp', scatter...  41.3 us
    all_gather x1, blocking collectives, on_device(): lax.all_gather(jnp.stack([gain_attn, gain_mlp]), ('ctx', 'fsdp'), axis=1,...  39.2 us
  transfers between devices with their start and end apart: 19, of which 15 were waited for; matrix products, arithmetic and copies ran while one was open for 9% of the time, Pallas kernels for 1%

profile of v1, /device:TPU:0, one launch (start us, length us, event | category | flops | bytes accessed | tf_op | source)
XLA Modules:
  0.0 1255.3 jit_solution(7160325387825014133)
XLA Ops:
  7.3 1.0 reshape.134
  8.3 1.0 reshape.135
  9.3 1.0 copy.109
  10.5 19.2 %all_to_all.20 = bf16[8,64,384]{2,1,0:T(8,128)(2,1)S(1)} all-to-all(bf16[8,64,384]{2,1,0:T(8,128)(2,1)S(1)} %copy.83), channel_id=1, replica_groups=mesh['ctx'=8,'fsdp'=4] {'ctx'}, dimensions={0} | all-to-all | bytes 786432 | tf_op jit(solution)/shard_map/all_to_all | solution.py:358
  29.6 1.0 copy.84
  30.7 39.2 %all-gather.2 = bf16[32,64,2]{1,2,0:T(2,128)(2,1)S(1)} all-gather(bf16[1,64,2]{1,2,0:T(2,128)(2,1)S(1)} %maximum_bitcast_fusion.2), channel_id=1, replica_groups=mesh['ctx'=8,'fsdp'=4] {'ctx','fsdp'}, dimensions={0}, use_global_device_ids=true | all-gather | bytes 8448 | tf_op jit(solution)/shard_map/all_gather | solution.py:529
  70.3 1.0 fusion.15
  72.6 1.9 fusion.20
  75.4 2.8 copy.85
  78.3 62.1 %all-gather.12.cloned.1.call-done = bf16[1024,2048]{1,0:T(8,128)(2,1)} async-done(((bf16[128,2048]{1,0:T(8,128)(2,1)}), bf16[1024,2048]{1,0:T(8,128)(2,1)}) %all-gather.12.cloned.1.call-update) | async-done | bytes 4194320 | tf_op jit(solution)/shard_map/all_gather | solution.py:350
  140.3 5.0 fusion.24.qkv_ref
  145.3 8.2 attend.1
  154.3 2.9 all-gather.14.cloned.1.call-done
  157.2 4.7 convolution_convert_fusion.3
  161.9 1.8 copy.110
  163.8 1.8 copy.111
  165.8 1.2 copy.88
  166.9 83.8 %all_to_all.21 = bf16[8,64,2048]{2,1,0:T(8,128)(2,1)S(1)} all-to-all(bf16[8,64,2048]{2,1,0:T(8,128)(2,1)S(1)} %copy.88), channel_id=1, replica_groups=mesh['ctx'=8,'fsdp'=4] {'ctx'}, dimensions={0} | all-to-all | bytes 4194304 | tf_op jit(solution)/shard_map/all_to_all | solution.py:358
  250.8 2.5 copy.89
  253.3 35.7 %reduce-scatter.12.cloned.1.call-done = bf16[128,2048]{1,0:T(8,128)(2,1)} async-done(((bf16[1024,2048]{1,0:T(8,128)(2,1)}), bf16[128,2048]{1,0:T(8,128)(2,1)}) %reduce-scatter.12.cloned.1.call-update) | async-done | bytes 524304 | tf_op jit(solution)/shard_map/reduce_scatter | solution.py:354
  289.0 1.3 multiply_reduce_fusion
  290.3 2.1 multiply_convert_fusion.4
  293.2 1.9 fusion.14
  295.2 53.7 %all-gather.26.cloned.1.call-done = bf16[8,256,2048]{2,0,1:T(8,128)(2,1)} async-done(((bf16[8,64,2048]{2,0,1:T(8,128)(2,1)}), bf16[8,256,2048]{2,0,1:T(8,128)(2,1)}) %all-gather.26.cloned.1.call-update) | async-done | bytes 8388624 | tf_op jit(solution)/shard_map/all_gather | solution.py:363
  348.9 11.3 copy.90
  360.3 64.0 %all-gather.16.cloned.1.call-done = bf16[1024,2048]{1,0:T(8,128)(2,1)} async-done(((bf16[128,2048]{1,0:T(8,128)(2,1)}), bf16[1024,2048]{1,0:T(8,128)(2,1)}) %all-gather.16.cloned.1.call-update) | async-done | bytes 4194320 | tf_op jit(solution)/shard_map/all_gather | solution.py:350
  424.3 14.7 %fusion.25 = f32[1024,2048]{1,0:T(8,128)} fusion(bf16[1024,2048]{1,0:T(8,128)(2,1)} %all-gather.16.cloned.1.call-done, bf16[2048,2048]{1,0:T(8,128)(2,1)} %bitcast.121), kind=kOutput, calls=%fused_computation.76 | convolution fusion | flops 8589934592 | bytes 20971520 | tf_op jit(solution)/shard_map/dot_general | solution.py:54
  439.0 19.9 %all-gather.18.cloned.1.call-done = bf16[1024,2048]{1,0:T(8,128)(2,1)} async-done(((bf16[256,2048]{1,0:T(8,128)(2,1)}), bf16[1024,2048]{1,0:T(8,128)(2,1)}) %all-gather.18.cloned.1.call-update) | async-done | bytes 4194320 | tf_op jit(solution)/shard_map/all_gather | solution.py:541
  458.9 75.5 %all-gather.20.cloned.1.call-done = bf16[1024,2048]{1,0:T(8,128)(2,1)} async-done(((bf16[128,2048]{1,0:T(8,128)(2,1)}), bf16[1024,2048]{1,0:T(8,128)(2,1)}) %all-gather.20.cloned.1.call-update) | async-done | bytes 4194320 | tf_op jit(solution)/shard_map/all_gather | solution.py:350
  534.4 13.1 %multiply_convert_fusion.1 = (bf16[1024,1024]{1,0:T(8,128)(2,1)S(1)}, bf16[1024,1024]{1,0:T(8,128)(2,1)S(1)}, bf16[1024,1024]{1,0:T(8,128)(2,1)}) fusion(f32[1024,2048]{1,0:T(8,128)} %fusion.25, bf16[1024,2048]{1,0:T(8,128)(2,1)} %all-gather.20.cloned.1.call-done, bf16[1024,2048]{1,0:T(8,128)(2,1)} %all-gather.18.cloned.1.call-done), kind=kOutput, calls=%fused_computation.3 | convolution fusion | flops 4310695936 | bytes 23068672 | tf_op jit(solution)/shard_map/dot_general | solution.py:58
  547.5 1.3 copy-done.15
  549.5 12.6 %convolution_convert_fusion.2 = bf16[1024,2048]{1,0:T(8,128)(2,1)} fusion(bf16[2048,2048]{1,0:T(8,128)(2,1)} %bitcast.122, bf16[1024,1024]{1,0:T(8,128)(2,1)S(1)} %get-tuple-element.24, bf16[1024,1024]{1,0:T(8,128)(2,1)S(1)} %get-tuple-element.23), kind=kOutput, calls=%fused_computation.8 | convolution fusion | flops 8600420352 | bytes 16777216 | tf_op jit(solution)/shard_map/dot_general | solution.py:58
  562.2 87.0 %reduce-scatter.16.cloned.1.call-done = bf16[128,2048]{1,0:T(8,128)(2,1)} async-done(((bf16[1024,2048]{1,0:T(8,128)(2,1)}), bf16[128,2048]{1,0:T(8,128)(2,1)}) %reduce-scatter.16.cloned.1.call-update) | async-done | bytes 524304 | tf_op jit(solution)/shard_map/reduce_scatter | solution.py:354
  649.2 1.7 fusion.13
  650.9 2.7 multiply_convert_fusion.3
  654.0 72.1 %all-gather.22.cloned.1.call-done = bf16[1024,2048]{1,0:T(8,128)(2,1)} async-done(((bf16[128,2048]{1,0:T(8,128)(2,1)}), bf16[1024,2048]{1,0:T(8,128)(2,1)}) %all-gather.22.cloned.1.call-update) | async-done | bytes 4194320 | tf_op jit(solution)/shard_map/all_gather | solution.py:350
  726.1 3.9 convolution_convert_fusion.8.do_ref
  730.1 1.0 copy-done.1
  731.1 0.9 copy-done.3
  732.1 13.3 %attend_back.1 = bf16[1024,384]{1,0:T(8,128)(2,1)S(1)} custom-call(bf16[1024,256]{1,0:T(8,128)(2,1)S(1)} %get-tuple-element.16.q_ref, bf16[1024,128]{1,0:T(8,128)(2,1)S(1)} %copy-done.3, bf16[1024,256]{1,0:T(8,128)(2,1)S(1)} %convolution_convert_fusion.8.do_ref, f32[1024,4]{1,0:T(8,128)S(1)} %copy-done.1, f32[1024,128]{1,0:T(8,128)S(1)} %get-tuple-element.39.cos_ref, ...), custom_call_target="tpu_custom_call" | custom-call | tf_op jit(solution)/shard_map/attend_back/pallas_call | solution.py:483
  745.4 2.4 convolution_convert_fusion.6
  747.8 1.3 copy.94
  749.2 14.0 %convolution_convert_fusion = bf16[2048,2048]{1,0:T(8,128)(2,1)} fusion(bf16[1024,2048]{1,0:T(8,128)(2,1)} %all-gather.16.cloned.1.call-done, bf16[1024,1024]{1,0:T(8,128)(2,1)} %copy-done.16, bf16[1024,1024]{1,0:T(8,128)(2,1)} %copy-done.15), kind=kOutput, calls=%fused_computation | convolution fusion | flops 8602517504 | bytes 16777216 | tf_op jit(solution)/shard_map/dot_general | solution.py:64
  763.3 8.6 copy.98
  772.1 9.5 convolution_convert_fusion.4
  781.7 4.9 convolution_convert_fusion.7
  786.8 5.1 convolution_convert_fusion.1
  791.9 1.7 copy-done.14
  793.6 8.2 convolution_convert_fusion.5
  801.8 3.6 all-to-all-start.2
  805.4 44.3 %reduce-scatter.24.cloned.1.call-done = bf16[512,2048]{1,0:T(8,128)(2,1)} async-done(((bf16[2048,2048]{1,0:T(8,128)(2,1)}), bf16[512,2048]{1,0:T(8,128)(2,1)}) %reduce-scatter.24.cloned.1.call-update) | async-done | bytes 2097168 | tf_op jit(solution)/shard_map/reduce_scatter | solution.py:369
  849.7 5.5 all-to-all-start.3
  855.6 41.3 %reduce-scatter.26.cloned.1.call-done = bf16[256,2048]{1,0:T(8,128)(2,1)} async-done(((bf16[1024,2048]{1,0:T(8,128)(2,1)}), bf16[256,2048]{1,0:T(8,128)(2,1)}) %reduce-scatter.26.cloned.1.call-update) | async-done | bytes 1048592 | tf_op jit(solution)/shard_map/reduce_scatter | solution.py:573
  896.9 2.8 convert_element_type.197
  899.7 25.0 %reduce-scatter.22.cloned.1.call-done = bf16[64,2048]{1,0:T(8,128)(2,1)} async-done(((bf16[256,2048]{1,0:T(8,128)(2,1)}), bf16[64,2048]{1,0:T(8,128)(2,1)}) %reduce-scatter.22.cloned.1.call-update) | async-done | bytes 262160 | tf_op jit(solution)/shard_map/reduce_scatter | solution.py:581
  924.7 1.8 convert_element_type.188
  929.8 1.5 copy.108
  931.3 1.5 copy.107
  932.7 83.8 %reduce-scatter.18.cloned.1.call-done = bf16[128,2048]{1,0:T(8,128)(2,1)} async-done(((bf16[1024,2048]{1,0:T(8,128)(2,1)}), bf16[128,2048]{1,0:T(8,128)(2,1)}) %reduce-scatter.18.cloned.1.call-update) | async-done | bytes 524304 | tf_op jit(solution)/shard_map/reduce_scatter | solution.py:354
  1016.5 1.5 fusion.17
  1018.0 1.4 copy.102
  1019.4 88.5 %reduce-scatter.14.cloned.1.call-done = bf16[128,2048]{1,0:T(8,128)(2,1)} async-done(((bf16[1024,2048]{1,0:T(8,128)(2,1)}), bf16[128,2048]{1,0:T(8,128)(2,1)}) %reduce-scatter.14.cloned.1.call-update) | async-done | bytes 524304 | tf_op jit(solution)/shard_map/reduce_scatter | solution.py:354
  1108.0 3.2 fusion.10
  1111.2 135.2 %reduce-scatter.28.cloned.1.call-done = f32[64,2]{1,0:T(8,128)} async-done(((f32[2048,2]{1,0:T(8,128)}), f32[64,2]{1,0:T(8,128)}) %reduce-scatter.28.cloned.1.call-update) | async-done | bytes 528
  (100 shorter events, 12.2 us)
Async XLA Ops:
  7.2 23.5 %copy-start.11 = (bf16[64]{0:T(256)(128)(2,1)S(1)}, bf16[64]{0:T(256)(128)(2,1)}, u32[]{:S(2)}) copy-start(bf16[64]{0:T(256)(128)(2,1)} %param.20) | copy-start | bytes 388
  7.2 23.5 %copy-start.12 = (bf16[64]{0:T(256)(128)(2,1)S(1)}, bf16[64]{0:T(256)(128)(2,1)}, u32[]{:S(2)}) copy-start(bf16[64]{0:T(256)(128)(2,1)} %param.15) | copy-start | bytes 388
  7.2 62.9 %copy-start.4 = (bf16[1,128,2048]{2,1,0:T(8,128)(2,1)S(1)}, bf16[1,128,2048]{2,1,0:T(8,128)(2,1)}, u32[]{:S(2)}) copy-start(bf16[1,128,2048]{2,1,0:T(8,128)(2,1)} %param.12) | copy-start | bytes 1572868
  7.2 64.9 %copy-start.13 = (s32[1,8]{1,0:T(1,128)S(1)}, s32[1,8]{1,0:T(1,128)}, u32[]{:S(2)}) copy-start(s32[1,8]{1,0:T(1,128)} %param.13) | copy-start | bytes 100
  7.2 68.2 %all-gather.24.cloned.1.call-start = ((), (), s32[]{:S(2)}) async-start(), calls=%async_computation.27 | async-start | bytes 1966080 | tf_op jit(solution)/shard_map/all_gather | solution.py:363
  30.6 109.7 %all-gather.12.cloned.1.call-start = ((), (), s32[]{:S(2)}) async-start(), calls=%async_computation.13 | async-start | bytes 4718592 | tf_op jit(solution)/shard_map/all_gather | solution.py:350
  71.3 85.9 %all-gather.14.cloned.1.call-start = ((), (), s32[]{:S(2)}) async-start(), calls=%async_computation.14 | async-start | bytes 1310720 | tf_op jit(solution)/shard_map/all_gather | solution.py:538
  72.0 217.0 %reduce-scatter.12.cloned.1.call-start = ((), (), s32[]{:S(2)}) async-start(), calls=%async_computation.15 | async-start | bytes 4718592 | tf_op jit(solution)/shard_map/reduce_scatter | solution.py:354
  153.5 0.8 copy-start
  154.3 7.6 copy-start.2
  161.9 187.0 %all-gather.26.cloned.1.call-start = ((), (), s32[]{:S(2)}) async-start(), calls=%async_computation.28 | async-start | bytes 10485760 | tf_op jit(solution)/shard_map/all_gather | solution.py:363
  253.3 171.0 %all-gather.16.cloned.1.call-start = ((), (), s32[]{:S(2)}) async-start(), calls=%async_computation.16 | async-start | bytes 4718592 | tf_op jit(solution)/shard_map/all_gather | solution.py:350
  292.4 166.4 %all-gather.18.cloned.1.call-start = ((), (), s32[]{:S(2)}) async-start(), calls=%async_computation.17 | async-start | bytes 5242880 | tf_op jit(solution)/shard_map/all_gather | solution.py:541
  293.2 241.2 %all-gather.20.cloned.1.call-start = ((), (), s32[]{:S(2)}) async-start(), calls=%async_computation.19 | async-start | bytes 4718592 | tf_op jit(solution)/shard_map/all_gather | solution.py:350
  295.2 354.0 %reduce-scatter.16.cloned.1.call-start = ((), (), s32[]{:S(2)}) async-start(), calls=%async_computation.20 | async-start | bytes 4718592 | tf_op jit(solution)/shard_map/reduce_scatter | solution.py:354
  547.5 1.3 copy-start.15
  547.5 2.0 copy-start.16
  562.1 164.0 %all-gather.22.cloned.1.call-start = ((), (), s32[]{:S(2)}) async-start(), calls=%async_computation.21 | async-start | bytes 4718592 | tf_op jit(solution)/shard_map/all_gather | solution.py:350
  653.6 148.2 %reduce-scatter.20.cloned.1.call-start = ((), (), s32[]{:S(2)}) async-start(), calls=%async_computation.23 | async-start | bytes 1966080 | tf_op jit(solution)/shard_map/reduce_scatter | solution.py:369
  726.1 19.2 %copy-start.10 = (bf16[1024,2048]{1,0:T(8,128)(2,1)S(1)}, bf16[1024,2048]{1,0:T(8,128)(2,1)}, u32[]{:S(2)}) copy-start(bf16[1024,2048]{1,0:T(8,128)(2,1)} %all-gather.12.cloned.1.call-done) | copy-start | bytes 12582916
  730.1 1.0 copy-start.1
  731.1 0.9 copy-start.3
  749.2 100.6 %reduce-scatter.24.cloned.1.call-start = ((), (), s32[]{:S(2)}) async-start(), calls=%async_computation.25 | async-start | bytes 10485760 | tf_op jit(solution)/shard_map/reduce_scatter | solution.py:369
  771.9 125.0 %reduce-scatter.26.cloned.1.call-start = ((), (), s32[]{:S(2)}) async-start(), calls=%async_computation.26 | async-start | bytes 5242880 | tf_op jit(solution)/shard_map/reduce_scatter | solution.py:573
  781.7 5.1 copy-start.9
  781.7 143.0 %reduce-scatter.22.cloned.1.call-start = ((), (), s32[]{:S(2)}) async-start(), calls=%async_computation.24 | async-start | bytes 1310720 | tf_op jit(solution)/shard_map/reduce_scatter | solution.py:581
  786.7 229.8 %reduce-scatter.18.cloned.1.call-start = ((), (), s32[]{:S(2)}) async-start(), calls=%async_computation.22 | async-start | bytes 4718592 | tf_op jit(solution)/shard_map/reduce_scatter | solution.py:354
  791.8 1.7 copy-start.14
  791.8 316.1 %reduce-scatter.14.cloned.1.call-start = ((), (), s32[]{:S(2)}) async-start(), calls=%async_computation.18 | async-start | bytes 4718592 | tf_op jit(solution)/shard_map/reduce_scatter | solution.py:354
  801.8 47.9 %all-to-all-start.2 = ((bf16[8,64,384]{2,1,0:T(8,128)(2,1)}), bf16[8,64,384]{2,1,0:T(8,128)(2,1)S(1)}, u32[]{:S(2)}, u32[]{:S(2)}) async-start(bf16[8,64,384]{2,1,0:T(8,128)(2,1)} %bitcast.138), calls=%async_computation.7 | async-start | bytes 786432 | tf_op jit(solution)/shard_map/all_to_all | solution.py:358
  849.7 79.6 %all-to-all-start.3 = ((bf16[8,64,2048]{2,1,0:T(8,128)(2,1)}), bf16[8,64,2048]{2,1,0:T(8,128)(2,1)S(1)}, u32[]{:S(2)}, u32[]{:S(2)}) async-start(bf16[8,64,2048]{2,1,0:T(8,128)(2,1)} %bitcast.128), calls=%async_computation.10 | async-start | bytes 4194304 | tf_op jit(solution)/shard_map/all_to_all | solution.py:358
  855.3 391.1 %reduce-scatter.28.cloned.1.call-start = ((), (), s32[]{:S(2)}) async-start(), calls=%async_computation.29 | async-start | bytes 1081344
  929.8 86.7 %copy-start.5 = (bf16[1,128,2048]{2,1,0:T(8,128)(2,1)S(1)}, bf16[1,128,2048]{2,1,0:T(8,128)(2,1)}, u32[]{:S(2)}) copy-start(bf16[1,128,2048]{2,1,0:T(8,128)(2,1)} %param.12) | copy-start | bytes 1572868
  931.3 176.7 %copy-start.6 = (bf16[128,2048]{1,0:T(8,128)(2,1)S(1)}, bf16[128,2048]{1,0:T(8,128)(2,1)}, u32[]{:S(2)}) copy-start(bf16[128,2048]{1,0:T(8,128)(2,1)} %reduce-scatter.12.cloned.1.call-done) | copy-start | bytes 1572868
  931.3 176.7 %copy-start.7 = (bf16[1,128,2048]{2,1,0:T(8,128)(2,1)S(1)}, bf16[1,128,2048]{2,1,0:T(8,128)(2,1)}, u32[]{:S(2)}) copy-start(bf16[1,128,2048]{2,1,0:T(8,128)(2,1)} %param.14) | copy-start | bytes 1572868
  931.3 176.7 %copy-start.8 = (bf16[128,2048]{1,0:T(8,128)(2,1)S(1)}, bf16[128,2048]{1,0:T(8,128)(2,1)}, u32[]{:S(2)}) copy-start(bf16[128,2048]{1,0:T(8,128)(2,1)} %reduce-scatter.16.cloned.1.call-done) | copy-start | bytes 1572868
Sparse Core Ops, SparseCore 0:
  30.7 18.3 all-gather.23
  71.4 68.8 all-gather.11
  141.9 15.2 all-gather.13
  162.0 126.9 reduce-scatter.11
  291.0 57.8 all-gather.25
  351.5 72.7 all-gather.15
  425.9 32.9 all-gather.17
  461.6 72.7 all-gather.19
  562.2 86.8 reduce-scatter.15
  653.7 72.3 all-gather.21
  749.3 26.5 reduce-scatter.19
  778.3 71.3 reduce-scatter.23
  852.3 44.5 reduce-scatter.25
  899.8 24.8 reduce-scatter.21
  928.2 88.2 reduce-scatter.17
  1020.0 87.9 reduce-scatter.13
  1110.0 136.2 reduce-scatter.27

commit v2 on v1

--- a/solution.py
+++ b/solution.py
@@ -19,6 +19,9 @@
 RESIDUAL_MULT = 0.22
 ROPE_BASE = 10000000.0
 NEGATIVE = -1e30
+MESH = pl.DeviceIdType.MESH
+PAIR = 2
+CHUNKS = 2
 
 
 def doc_index(positions, starts):
@@ -346,12 +349,289 @@
     return blocks.reshape((-1,) + blocks.shape[2:])
 
 
+def greet_line(barrier, ctx_at, line_at, line_size):
+    other = ctx_at + 1 - 2 * (ctx_at % PAIR)
+    pl.semaphore_signal(barrier, inc=1, device_id={"ctx": other}, device_id_type=MESH)
+
+    @pl.when(line_at > 0)
+    def _():
+        pl.semaphore_signal(barrier, inc=1, device_id={"ctx": ctx_at - PAIR}, device_id_type=MESH)
+
+    @pl.when(line_at < line_size - 1)
+    def _():
+        pl.semaphore_signal(barrier, inc=1, device_id={"ctx": ctx_at + PAIR}, device_id_type=MESH)
+
+    last = line_size - 1
+    neighbours = 1 + (line_at + last - 1) // last + (2 * last - 1 - line_at) // last
+    pl.semaphore_wait(barrier, neighbours)
+
+
+def gather_kernel(line_size, x_ref, out_ref, send_sem, recv_sem, own_sem):
+    me = lax.axis_index("ctx")
+    line_at, pair_at = me // PAIR, me % PAIR
+    rows = x_ref.shape[0]
+    step = rows // CHUNKS
+    greet_line(pltpu.get_barrier_semaphore(), me, line_at, line_size)
+
+    def piece(block, part):
+        return out_ref.at[pl.ds(pl.multiple_of(block * rows + part * step, step), step), :]
+
+    def copy(block, part, way, own):
+        target = (me + 1 - 2 * pair_at, me + PAIR, me - PAIR)[way]
+        slot = block * CHUNKS + part
+        return pltpu.make_async_remote_copy(
+            src_ref=x_ref.at[pl.ds(part * step, step), :] if own else piece(block, part),
+            dst_ref=piece(block, part),
+            send_sem=send_sem.at[way, slot],
+            recv_sem=recv_sem.at[slot],
+            device_id={"ctx": target},
+            device_id_type=MESH,
+        )
+
+    def pass_on(block, part, upward, downward, own, act):
+        if upward is not None:
+            pl.when(upward)(lambda: act(copy(block, part, 1, own)))
+        if downward is not None:
+            pl.when(downward)(lambda: act(copy(block, part, 2, own)))
+        act(copy(block, part, 0, own))
+
+    def visit(act, arrive):
+        for part in range(CHUNKS):
+            pass_on(me, part, line_at < line_size - 1, line_at > 0, True, act)
+        for distance in range(1, line_size):
+            for part in range(CHUNKS):
+
+                @pl.when(line_at >= distance)
+                def _():
+                    block = me - PAIR * distance
+                    arrive(block, part)
+                    pass_on(block, part, line_at < line_size - 1, None, False, act)
+
+                @pl.when(line_at + distance < line_size)
+                def _():
+                    block = me + PAIR * distance
+                    arrive(block, part)
+                    pass_on(block, part, None, line_at > 0, False, act)
+
+    keep = pltpu.make_async_copy(
+        x_ref, out_ref.at[pl.ds(pl.multiple_of(me * rows, rows), rows), :], own_sem
+    )
+    keep.start()
+    visit(lambda c: c.start(), lambda block, part: copy(block, part, 0, False).wait_recv())
+    for place in range(line_size):
+        for part in range(CHUNKS):
+            copy(place * PAIR + 1 - pair_at, part, 0, False).wait_recv()
+    visit(lambda c: c.wait_send(), lambda block, part: None)
+    keep.wait()
+
+
 def gather_ctx(local):
-    return lax.all_gather(local, "ctx", axis=0, tiled=True)
+    ctx_size = lax.axis_size("ctx")
+    rows, width = local.shape
+    return pl.pallas_call(
+        functools.partial(gather_kernel, ctx_size // PAIR),
+        out_shape=jax.ShapeDtypeStruct((ctx_size * rows, width), local.dtype),
+        in_specs=[pl.BlockSpec(memory_space=pl.ANY)],
+        out_specs=pl.BlockSpec(memory_space=pl.ANY),
+        scratch_shapes=[
+            pltpu.SemaphoreType.DMA((3, ctx_size * CHUNKS)),
+            pltpu.SemaphoreType.DMA((ctx_size * CHUNKS,)),
+            pltpu.SemaphoreType.DMA,
+        ],
+        compiler_params=pltpu.CompilerParams(collective_id=0, has_side_effects=True),
+        name="gather_ctx",
+    )(local)
+
+
+def scatter_kernel(line_size, x_ref, out_ref, near, below, above, send_sem, near_sem, line_sem, line_send):
+    me = lax.axis_index("ctx")
+    line_at, pair_at = me // PAIR, me % PAIR
+    rows = out_ref.shape[0]
+    step = rows // CHUNKS
+    greet_line(pltpu.get_barrier_semaphore(), me, line_at, line_size)
+    half = line_size // 2
+    low = line_at // half
+    last = line_size - 1
+    order = [k + (last - 2 * k) * (1 - low) for k in range(half)]
+    if line_size == 4:
+        order += [line_at + 1 - 2 * (line_at % 2), line_at]
+
+    def near_copy(place, part):
+        start = (place * PAIR + 1 - pair_at) * rows + part * step
+        return pltpu.make_async_remote_copy(
+            src_ref=x_ref.at[pl.ds(pl.multiple_of(start, step), step), :],
+            dst_ref=near.at[place, pl.ds(part * step, step), :],
+            send_sem=send_sem.at[place, part],
+            recv_sem=near_sem.at[place, part],
+            device_id={"ctx": me + 1 - 2 * pair_at},
+            device_id_type=MESH,
+        )
+
+    def line_copy(place, part, up):
+        part_rows = pl.ds(part * step, step)
+        return pltpu.make_async_remote_copy(
+            src_ref=near.at[place, part_rows, :],
+            dst_ref=(below if up else above).at[place, part_rows, :],
+            send_sem=line_send.at[place, part],
+            recv_sem=line_sem.at[0 if up else 1, place, part],
+            device_id={"ctx": me + PAIR if up else me - PAIR},
+            device_id_type=MESH,
+        )
+
+    for place in order:
+        for part in range(CHUNKS):
+            near_copy(place, part).start()
+
+    for place in order[:-1]:
+        for part in range(CHUNKS):
+            part_rows = pl.ds(part * step, step)
+            mine = x_ref.at[pl.ds(pl.multiple_of((place * PAIR + pair_at) * rows + part * step, step), step), :]
+            near_copy(place, part).wait_recv()
+
+            def send(up, waits, arrived):
+                @pl.when(waits)
+                def _():
+                    line_copy(place, part, up).wait_recv()
+                    near[place, part_rows, :] = (
+                        mine[...].astype(jnp.float32)
+                        + near[place, part_rows, :].astype(jnp.float32)
+                        + arrived[place, part_rows, :].astype(jnp.float32)
+                    ).astype(near.dtype)
+
+                @pl.when(jnp.logical_not(waits))
+                def _():
+                    near[place, part_rows, :] = (
+                        mine[...].astype(jnp.float32) + near[place, part_rows, :].astype(jnp.float32)
+                    ).astype(near.dtype)
+
+                line_copy(place, part, up).start()
+
+            @pl.when(place > line_at)
+            def _():
+                send(True, line_at > 0, below)
+
+            @pl.when(place < line_at)
+            def _():
+                send(False, line_at < last, above)
+
+    for part in range(CHUNKS):
+        part_rows = pl.ds(part * step, step)
+        mine = x_ref.at[pl.ds(pl.multiple_of(me * rows + part * step, step), step), :]
+        near_copy(line_at, part).wait_recv()
+        out_ref[part_rows, :] = mine[...].astype(jnp.float32) + near[line_at, part_rows, :].astype(jnp.float32)
+
+        @pl.when(line_at > 0)
+        def _():
+            line_copy(line_at, part, True).wait_recv()
+            out_ref[part_rows, :] += below[line_at, part_rows, :].astype(jnp.float32)
+
+        @pl.when(line_at < last)
+        def _():
+            line_copy(line_at, part, False).wait_recv()
+            out_ref[part_rows, :] += above[line_at, part_rows, :].astype(jnp.float32)
+
+    for place in order:
+        for part in range(CHUNKS):
+            near_copy(place, part).wait_send()
+    for place in order[:-1]:
+        for part in range(CHUNKS):
+            line_copy(place, part, True).wait_send()
 
 
 def scatter_ctx(partial):
-    return lax.psum_scatter(partial, "ctx", scatter_dimension=0, tiled=True).astype(jnp.float32)
+    ctx_size = lax.axis_size("ctx")
+    line_size = ctx_size // PAIR
+    rows, width = partial.shape[0] // ctx_size, partial.shape[1]
+    held = pltpu.VMEM((line_size, rows, width), partial.dtype)
+    return pl.pallas_call(
+        functools.partial(scatter_kernel, line_size),
+        out_shape=jax.ShapeDtypeStruct((rows, width), jnp.float32),
+        in_specs=[pl.BlockSpec(memory_space=pltpu.VMEM)],
+        out_specs=pl.BlockSpec(memory_space=pltpu.VMEM),
+        scratch_shapes=[
+            held, held, held,
+            pltpu.SemaphoreType.DMA((line_size, CHUNKS)),
+            pltpu.SemaphoreType.DMA((line_size, CHUNKS)),
+            pltpu.SemaphoreType.DMA((2, line_size, CHUNKS)),
+            pltpu.SemaphoreType.DMA((line_size, CHUNKS)),
+        ],
+        compiler_params=pltpu.CompilerParams(
+            collective_id=1, has_side_effects=True, vmem_limit_bytes=32 * 2**20
+        ),
+        name="scatter_ctx",
+    )(partial)
+
+
+def exchange_kernel(ctx_size, fsdp_size, x_ref, out_ref, send_sem, recv_sem):
+    count = ctx_size * fsdp_size
+    me = lax.axis_index("ctx") * fsdp_size + lax.axis_index("fsdp")
+    barrier = pltpu.get_barrier_semaphore()
+
+    def device(index):
+        return (index // fsdp_size, index % fsdp_size)
+
+    def greet(k, unused):
+        pl.semaphore_signal(barrier, inc=1, device_id=device((me + k) % count), device_id_type=MESH)
+        return unused
+
+    lax.fori_loop(1, count, greet, 0)
+    pl.semaphore_wait(barrier, count - 1)
+
+    def copy(k):
+        target = (me + k) % count
+        return pltpu.make_async_remote_copy(
+            src_ref=x_ref.at[target], dst_ref=out_ref.at[me],
+            send_sem=send_sem.at[k], recv_sem=recv_sem.at[k],
+            device_id=device(target), device_id_type=MESH,
+        )
+
+    def start(k, unused):
+        copy(k).start()
+        return unused
+
+    def finish(k, unused):
+        source = (me + count - k) % count
+        pltpu.make_async_remote_copy(
+            src_ref=x_ref.at[source], dst_ref=out_ref.at[source],
+            send_sem=send_sem.at[k], recv_sem=recv_sem.at[k],
+            device_id=device(source), device_id_type=MESH,
+        ).wait_recv()
+        copy(k).wait_send()
+        return unused
+
+    lax.fori_loop(1, count, start, 0)
+    out_ref[pl.ds(me, 1)] = x_ref[pl.ds(me, 1)]
+    lax.fori_loop(1, count, finish, 0)
+
+
+def exchange(tiles):
+    ctx_size, fsdp_size = lax.axis_size("ctx"), lax.axis_size("fsdp")
+    count = ctx_size * fsdp_size
+    return pl.pallas_call(
+        functools.partial(exchange_kernel, ctx_size, fsdp_size),
+        out_shape=jax.ShapeDtypeStruct(tiles.shape, tiles.dtype),
+        in_specs=[pl.BlockSpec(memory_space=pltpu.VMEM)],
+        out_specs=pl.BlockSpec(memory_space=pltpu.VMEM),
+        scratch_shapes=[pltpu.SemaphoreType.DMA((count,)), pltpu.SemaphoreType.DMA((count,))],
+        compiler_params=pltpu.CompilerParams(collective_id=2, has_side_effects=True),
+        name="exchange",
+    )(tiles)
+
+
+def padded(rows):
+    return jnp.pad(rows, ((0, 0), (0, 8 - rows.shape[1]), (0, 128 - rows.shape[2])))
+
+
+def gather_rows(rows):
+    count = lax.axis_size("ctx") * lax.axis_size("fsdp")
+    tiles = jnp.broadcast_to(padded(rows[None]), (count, 8, 128))
+    return exchange(tiles)[:, : rows.shape[0], : rows.shape[1]].transpose(1, 0, 2).reshape(rows.shape[0], -1)
+
+
+def scatter_rows(rows):
+    count = lax.axis_size("ctx") * lax.axis_size("fsdp")
+    by_owner = rows.reshape(rows.shape[0], count, -1).transpose(1, 0, 2)
+    return jnp.sum(exchange(padded(by_owner)), axis=0)[: rows.shape[0], : by_owner.shape[2]]
 
 
 def swap_ctx(blocks):
@@ -526,9 +806,7 @@
     sin_table = jnp.concatenate([-sin_half, sin_half] * 2, axis=1)
     tables = (cos_table, sin_table, doc_ids[:, None], doc_ids[None, :])
 
-    gains = lax.all_gather(jnp.stack([gain_attn, gain_mlp]), ("ctx", "fsdp"), axis=1, tiled=True)
-    gain1 = gains[0].astype(jnp.float32)
-    gain2 = gains[1].astype(jnp.float32)
+    gain1, gain2 = gather_rows(jnp.stack([gain_attn, gain_mlp]).astype(jnp.float32))
 
     def by_slice(weight):
         return weight.reshape(held_rows, ctx_size, -1)
@@ -586,9 +864,7 @@
     qkv_back = return_columns(dot_outer(normed1, grad_qkv).astype(bf16), ctx_size, fsdp_size)
     grad_g1 = jnp.sum(grad_norm1 * unit_one, axis=0)
     grad_inputs = grad_hidden + norm_back(grad_norm1, unit_one, inv_one, gain1)
-    gain_back = lax.psum_scatter(
-        jnp.stack([grad_g1, grad_g2]), ("ctx", "fsdp"), scatter_dimension=1, tiled=True
-    )
+    gain_back = scatter_rows(jnp.stack([grad_g1, grad_g2]))
 
     def joined(parts):
         return parts.transpose(1, 0, 2).reshape(held_rows, -1).astype(jnp.float32)
@@ -637,7 +913,7 @@
         P(("ctx", "fsdp"), None),
         P(("ctx", "fsdp"), None),
     )
-    split_heads = mesh.shape["ctx"] == KVH
+    split_heads = mesh.shape["ctx"] == KVH == 4 * PAIR
     return jax.shard_map(
         on_device if split_heads else general_device, mesh=mesh, in_specs=in_specs, out_specs=out_specs, check_vma=False
     )

time: 1270 us -> 756 us (0.60)
  waiting for transfers between devices: 893 us -> 109 us
  Pallas kernels: 21.5 us -> 431 us
  blocking collectives: 142 us -> 13.1 us
    pallas_call x0 -> x10, Pallas kernels: none -> 410 us  [the longest x4 203 us: scatter_ctx(): pl.pallas_call(functools.partial(scatter_kernel, line_size), out_shape=ja...]
    reduce_scatter x4 -> x0, waiting for transfers between devices: 295 us -> none  [scatter_ctx(): lax.psum_scatter(partial, 'ctx', scatter_dimension=0, tiled=True)]
    all_gather x4 -> x0, waiting for transfers between devices: 274 us -> none  [gather_ctx(): return lax.all_gather(local, 'ctx', axis=0, tiled=True)]
    unnamed x18 -> x8, waiting for transfers between devices: 137 us -> 1.32 us
    all_to_all x2 -> x1, blocking collectives: 103 us -> 13.1 us  [swap_ctx(): lax.all_to_all(blocks, 'ctx', split_axis=0, concat_axis=0, tiled=True)]
    all_to_all x2 -> x3, waiting for transfers between devices: 0.01 us -> 56.5 us  [swap_ctx(): lax.all_to_all(blocks, 'ctx', split_axis=0, concat_axis=0, tiled=True)]
    all_gather x2, waiting for transfers between devices: 53.7 us -> 0.04 us  [spread_columns(): full = lax.all_gather(mine[:, None], 'fsdp', axis=1, tiled=True)]
    reduce_scatter x1, waiting for transfers between devices: 41.3 us -> 0.01 us  [on_device(): lax.psum_scatter(dot_outer(activ, grad_mlp).astype(bf16), 'fsdp', scatter...]
  transfers between devices with their start and end apart: 19 -> 11, of which waited for: 15 -> 3; matrix products, arithmetic and copies ran while one was open for 9% -> 15% of each run, Pallas kernels for 1% -> 44%
where the time goes in v2:
time: 756 us; the launch traced here: 750 us
  Pallas kernels  431 us (57%)
  waiting for transfers between devices  109 us (14%)
  matrix products  90.6 us (12%)
  local copies, waits for them, and re-layouts  50.7 us (7%)
  other arithmetic  22.4 us (3%)
  starting transfers between devices  17 us (2%)
  between operations  15 us (2%)
  blocking collectives  13.1 us (2%)
    pallas_call x4, Pallas kernels, scatter_ctx(): pl.pallas_call(functools.partial(scatter_kernel, line_size), out_shape=ja...  203 us
    pallas_call x4, Pallas kernels, gather_ctx(): pl.pallas_call(functools.partial(gather_kernel, ctx_size // PAIR), out_sh...  187 us
    all_to_all x3, waiting for transfers between devices, swap_ctx(): lax.all_to_all(blocks, 'ctx', split_axis=0, concat_axis=0, tiled=True)  56.5 us
    reduce_scatter x2, waiting for transfers between devices, return_columns(): lax.psum_scatter(rows_of(rows_of(by_owner)), 'fsdp', scatter_dimension=0,...  51.3 us
    dot_general x4, matrix products, dot_back(): lax.dot_general(left, right, (((1,), (1,)), ((), ())), preferred_element_...  32.1 us
    dot_general x4, matrix products, dot_outer(): lax.dot_general(left, right, (((0,), (0,)), ((), ())), preferred_element_...  30.2 us
    dot_general x4, matrix products, dot_plain(): return jnp.dot(left, right, preferred_element_type=jnp.float32)  28.3 us
    pallas_call x2, Pallas kernels, exchange(): pl.pallas_call(functools.partial(exchange_kernel, ctx_size, fsdp_size), o...  19.9 us
  transfers between devices with their start and end apart: 11, of which 3 were waited for; matrix products, arithmetic and copies ran while one was open for 15% of the time, Pallas kernels for 44%

profile of v2, /device:TPU:0, one launch (start us, length us, event | category | flops | bytes accessed | tf_op | source)
XLA Modules:
  0.0 749.7 jit_solution(7944151033146057115)
XLA Ops:
  7.2 1.1 reshape.175
  8.3 1.0 reshape.176
  9.2 1.0 copy.100
  10.4 0.8 copy.78
  11.2 7.3 all-to-all-start
  18.5 1.8 copy.101
  21.0 9.2 %all-to-all-done = bf16[8,64,384]{2,1,0:T(8,128)(2,1)S(1)} async-done(((bf16[8,64,384]{2,1,0:T(8,128)(2,1)}), bf16[8,64,384]{2,1,0:T(8,128)(2,1)S(1)}, u32[]{:S(2)}, u32[]{:S(2)}) %all-to-all-start) | async-done | bytes 393248 | tf_op jit(solution)/shard_map/all_to_all | solution.py:638
  30.1 1.0 copy.79
  31.3 2.5 copy.83
  33.8 3.6 all-to-all-start.1
  38.3 47.3 %all-to-all-done.1 = bf16[8,64,2048]{2,1,0:T(8,128)(2,1)S(1)} async-done(((bf16[8,64,2048]{2,1,0:T(8,128)(2,1)}), bf16[8,64,2048]{2,1,0:T(8,128)(2,1)S(1)}, u32[]{:S(2)}, u32[]{:S(2)}) %all-to-all-start.1) | async-done | bytes 2097184 | tf_op jit(solution)/shard_map/all_to_all | solution.py:638
  85.6 2.5 copy.84
  89.4 9.9 %exchange.2 = f32[32,8,128]{2,1,0:T(8,128)} custom-call(f32[32,8,128]{2,1,0:T(8,128)} %broadcast_in_dim.17.x_ref), custom_call_target="tpu_custom_call" | custom-call | tf_op jit(solution)/shard_map/exchange/pallas_call | solution.py:610
  99.4 0.9 slice_bitcast_fusion
  101.1 0.9 fusion.5.x_ref
  102.0 49.2 %gather_ctx.6 = bf16[1024,2048]{1,0:T(8,128)(2,1)} custom-call(bf16[128,2048]{1,0:T(8,128)(2,1)} %fusion.5.x_ref), custom_call_target="tpu_custom_call" | custom-call | tf_op jit(solution)/shard_map/gather_ctx/pallas_call | solution.py:431
  151.4 1.0 fusion.6.x_ref
  152.4 47.8 %gather_ctx.4 = bf16[1024,2048]{1,0:T(8,128)(2,1)} custom-call(bf16[128,2048]{1,0:T(8,128)(2,1)} %fusion.6.x_ref), custom_call_target="tpu_custom_call" | custom-call | tf_op jit(solution)/shard_map/gather_ctx/pallas_call | solution.py:431
  200.2 1.9 fusion.15
  202.1 0.9 pad_maximum_fusion.3
  203.0 1.6 copy.80
  204.7 5.1 fusion.26.qkv_ref
  209.7 8.2 %attend.1 = (bf16[1024,256]{1,0:T(8,128)(2,1)S(1)}, bf16[1024,128]{1,0:T(8,128)(2,1)S(1)}, bf16[1024,256]{1,0:T(8,128)(2,1)S(1)}, f32[1024,4]{1,0:T(8,128)S(1)}) custom-call(f32[1024,384]{1,0:T(8,128)S(1)} %fusion.26.qkv_ref, f32[1024,128]{1,0:T(8,128)S(1)} %get-tuple-element.41.cos_ref, f32[1024,128]{1,0:T(8,128)S(1)} %get-tuple-element.42.sin_ref, ...), custom_call_target="tpu_custom_call" | custom-call | tf_op jit(solution)/shard_map/attend/pallas_call | solution.py:746
  219.6 2.9 convolution_convert_fusion.3.x_ref
  222.4 46.7 %scatter_ctx.4 = f32[128,2048]{1,0:T(8,128)S(1)} custom-call(bf16[1024,2048]{1,0:T(8,128)(2,1)S(1)} %convolution_convert_fusion.3.x_ref), custom_call_target="tpu_custom_call" | custom-call | tf_op jit(solution)/shard_map/scatter_ctx/pallas_call | solution.py:546
  269.4 0.9 copy-done.6
  270.4 0.9 multiply_convert_fusion.4.x_ref
  271.3 46.0 %gather_ctx.5 = bf16[1024,2048]{1,0:T(8,128)(2,1)} custom-call(bf16[128,2048]{1,0:T(8,128)(2,1)} %multiply_convert_fusion.4.x_ref), custom_call_target="tpu_custom_call" | custom-call | tf_op jit(solution)/shard_map/gather_ctx/pallas_call | solution.py:431
  317.4 11.4 %copy.85 = bf16[8,256,2048]{2,1,0:T(8,128)(2,1)} copy(bf16[8,256,2048]{2,0,1:T(8,128)(2,1)} %all-gather.13.cloned.1.call-done) | data formatting | bytes 16777216 | tf_op jit(solution)/shard_map/all_gather | solution.py:643
  328.8 13.5 %fusion.27 = f32[1024,2048]{1,0:T(8,128)} fusion(bf16[1024,2048]{1,0:T(8,128)(2,1)S(1)} %copy-done.13, bf16[2048,2048]{1,0:T(8,128)(2,1)} %bitcast.104), kind=kOutput, calls=%fused_computation.81 | convolution fusion | flops 8589934592 | bytes 20971520 | tf_op jit(solution)/shard_map/dot_general | solution.py:57
  342.2 13.1 %multiply_convert_fusion.1 = (bf16[1024,1024]{1,0:T(8,128)(2,1)S(1)}, bf16[1024,1024]{1,0:T(8,128)(2,1)S(1)}, bf16[1024,1024]{1,0:T(8,128)(2,1)}) fusion(f32[1024,2048]{1,0:T(8,128)} %fusion.27, bf16[1024,2048]{1,0:T(8,128)(2,1)} %gather_ctx.6, bf16[1024,2048]{1,0:T(8,128)(2,1)} %all-gather.9.cloned.1.call-done), kind=kOutput, calls=%fused_computation.3 | convolution fusion | flops 4310695936 | bytes 23068672 | tf_op jit(solution)/shard_map/dot_general | solution.py:61
  355.3 1.3 copy-done.25
  356.6 11.4 %convolution_convert_fusion.2.x_ref = bf16[1024,2048]{1,0:T(8,128)(2,1)S(1)} fusion(bf16[2048,2048]{1,0:T(8,128)(2,1)} %bitcast.105, bf16[1024,1024]{1,0:T(8,128)(2,1)S(1)} %get-tuple-element.28, bf16[1024,1024]{1,0:T(8,128)(2,1)S(1)} %get-tuple-element.27), kind=kOutput, calls=%fused_computation.8 | convolution fusion | flops 8600420352 | bytes 16777216 | tf_op jit(solution)/shard_map/dot_general | solution.py:61
  368.0 44.7 %scatter_ctx.6 = f32[128,2048]{1,0:T(8,128)S(1)} custom-call(bf16[1024,2048]{1,0:T(8,128)(2,1)S(1)} %convolution_convert_fusion.2.x_ref), custom_call_target="tpu_custom_call" | custom-call | tf_op jit(solution)/shard_map/scatter_ctx/pallas_call | solution.py:546
  412.8 0.9 multiply_reduce_fusion
  413.7 1.2 multiply_convert_fusion.3.x_ref
  414.8 44.3 %gather_ctx.7 = bf16[1024,2048]{1,0:T(8,128)(2,1)} custom-call(bf16[128,2048]{1,0:T(8,128)(2,1)} %multiply_convert_fusion.3.x_ref), custom_call_target="tpu_custom_call" | custom-call | tf_op jit(solution)/shard_map/gather_ctx/pallas_call | solution.py:431
  459.2 3.9 convolution_convert_fusion.8.do_ref
  463.1 13.4 %attend_back.1 = bf16[1024,384]{1,0:T(8,128)(2,1)S(1)} custom-call(bf16[1024,256]{1,0:T(8,128)(2,1)S(1)} %copy-done.3, bf16[1024,128]{1,0:T(8,128)(2,1)S(1)} %get-tuple-element.17.kv_ref, bf16[1024,256]{1,0:T(8,128)(2,1)S(1)} %convolution_convert_fusion.8.do_ref, f32[1024,4]{1,0:T(8,128)S(1)} %copy-done.5, f32[1024,128]{1,0:T(8,128)S(1)} %get-tuple-element.41.cos_ref, ...), custom_call_target="tpu_custom_call" | custom-call | tf_op jit(solution)/shard_map/attend_back/pallas_call | solution.py:763
  476.5 2.4 convolution_convert_fusion.6
  478.9 1.4 copy.89
  480.4 14.0 %convolution_convert_fusion = bf16[2048,2048]{1,0:T(8,128)(2,1)} fusion(bf16[1024,2048]{1,0:T(8,128)(2,1)} %gather_ctx.5, bf16[1024,1024]{1,0:T(8,128)(2,1)} %copy-done.26, bf16[1024,1024]{1,0:T(8,128)(2,1)} %copy-done.25), kind=kOutput, calls=%fused_computation | convolution fusion | flops 8602517504 | bytes 16777216 | tf_op jit(solution)/shard_map/dot_general | solution.py:67
  494.4 8.6 %copy.93 = bf16[8,4,64,2048]{3,2,0,1:T(8,128)(2,1)} copy(bf16[8,4,64,2048]{3,2,1,0:T(8,128)(2,1)} %bitcast.106) | data formatting | bytes 16777216 | tf_op jit(solution)/shard_map/reshape | solution.py:648
  503.0 4.5 convolution_convert_fusion.7
  507.8 9.4 %convolution_convert_fusion.4 = bf16[1024,2048]{1,0:T(8,128)(2,1)} fusion(bf16[1024,1024]{1,0:T(8,128)(2,1)} %get-tuple-element.29, bf16[1024,2048]{1,0:T(8,128)(2,1)} %gather_ctx.6), kind=kOutput, calls=%fused_computation.10 | convolution fusion | flops 4297064448 | bytes 10485760 | tf_op jit(solution)/shard_map/dot_general | solution.py:67
  517.2 13.1 %all_to_all.20 = bf16[8,64,384]{2,1,0:T(8,128)(2,1)S(1)} all-to-all(bf16[8,64,384]{2,1,0:T(8,128)(2,1)} %bitcast.120), channel_id=1, replica_groups=mesh['ctx'=8,'fsdp'=4] {'ctx'}, dimensions={0} | all-to-all | bytes 786432 | tf_op jit(solution)/shard_map/all_to_all | solution.py:638
  530.3 51.3 %reduce-scatter.9.cloned.1.call-done = bf16[512,2048]{1,0:T(8,128)(2,1)} async-done(((bf16[2048,2048]{1,0:T(8,128)(2,1)}), bf16[512,2048]{1,0:T(8,128)(2,1)}) %reduce-scatter.9.cloned.1.call-update) | async-done | bytes 2097168 | tf_op jit(solution)/shard_map/reduce_scatter | solution.py:649
  581.7 5.5 all-to-all-start.3
  587.2 6.9 convolution_convert_fusion.5.x_ref
  594.1 64.4 %scatter_ctx.5 = f32[128,2048]{1,0:T(8,128)S(1)} custom-call(bf16[1024,2048]{1,0:T(8,128)(2,1)S(1)} %convolution_convert_fusion.5.x_ref), custom_call_target="tpu_custom_call" | custom-call | tf_op jit(solution)/shard_map/scatter_ctx/pallas_call | solution.py:546
  659.3 3.8 convolution_convert_fusion.1.x_ref
  663.1 46.8 %scatter_ctx.7 = f32[128,2048]{1,0:T(8,128)S(1)} custom-call(bf16[1024,2048]{1,0:T(8,128)(2,1)S(1)} %convolution_convert_fusion.1.x_ref), custom_call_target="tpu_custom_call" | custom-call | tf_op jit(solution)/shard_map/scatter_ctx/pallas_call | solution.py:546
  709.9 0.9 fusion.12
  710.8 1.4 stack.21
  713.6 9.9 %exchange.3 = f32[32,8,128]{2,1,0:T(8,128)} custom-call(f32[32,8,128]{2,1,0:T(8,128)} %pad.10.x_ref), custom_call_target="tpu_custom_call" | custom-call | tf_op jit(solution)/shard_map/exchange/pallas_call | solution.py:610
  723.6 1.5 reduce_sum.79
  725.8 1.3 slice_bitcast_fusion.1
  727.0 3.2 fusion.11
  730.2 1.8 convert_element_type.180
  732.0 0.8 copy.97
  734.8 2.8 convert_element_type.189
  737.6 2.0 convert_bitcast_fusion
  739.6 1.5 copy.99
  741.1 1.5 copy.98
  (106 shorter events, 11.2 us)
Async XLA Ops:
  7.2 13.2 %copy-start.15 = (bf16[64,8192]{1,0:T(8,128)(2,1)S(1)}, bf16[64,8192]{1,0:T(8,128)(2,1)}, u32[]{:S(2)}) copy-start(bf16[64,8192]{1,0:T(8,128)(2,1)} %param.22) | copy-start | bytes 3145732
  11.2 19.0 %all-to-all-start = ((bf16[8,64,384]{2,1,0:T(8,128)(2,1)}), bf16[8,64,384]{2,1,0:T(8,128)(2,1)S(1)}, u32[]{:S(2)}, u32[]{:S(2)}) async-start(bf16[8,64,384]{2,1,0:T(8,128)(2,1)} %copy.78), calls=%async_computation | async-start | bytes 786432 | tf_op jit(solution)/shard_map/all_to_all | solution.py:638
  18.5 184.5 %all-gather.11.cloned.1.call-start = ((), (), s32[]{:S(2)}) async-start(), calls=%async_computation.14 | async-start | bytes 1966080 | tf_op jit(solution)/shard_map/all_gather | solution.py:643
  33.8 51.8 %all-to-all-start.1 = ((bf16[8,64,2048]{2,1,0:T(8,128)(2,1)}), bf16[8,64,2048]{2,1,0:T(8,128)(2,1)S(1)}, u32[]{:S(2)}, u32[]{:S(2)}) async-start(bf16[8,64,2048]{2,1,0:T(8,128)(2,1)} %copy.83), calls=%async_computation.1 | async-start | bytes 4194304 | tf_op jit(solution)/shard_map/all_to_all | solution.py:638
  37.5 51.3 %copy-start.21 = (bf16[64]{0:T(256)(128)(2,1)S(1)}, bf16[64]{0:T(256)(128)(2,1)}, u32[]{:S(2)}) copy-start(bf16[64]{0:T(256)(128)(2,1)} %param.20) | copy-start | bytes 388
  37.5 51.3 %copy-start.22 = (bf16[64]{0:T(256)(128)(2,1)S(1)}, bf16[64]{0:T(256)(128)(2,1)}, u32[]{:S(2)}) copy-start(bf16[64]{0:T(256)(128)(2,1)} %param.15) | copy-start | bytes 388
  37.5 63.1 %copy-start.23 = (s32[1,8]{1,0:T(1,128)S(1)}, s32[1,8]{1,0:T(1,128)}, u32[]{:S(2)}) copy-start(s32[1,8]{1,0:T(1,128)} %param.13) | copy-start | bytes 100
  37.5 182.1 %all-gather.7.cloned.1.call-start = ((), (), s32[]{:S(2)}) async-start(), calls=%async_computation.8 | async-start | bytes 1310720 | tf_op jit(solution)/shard_map/all_gather | solution.py:816
  38.2 62.8 %copy-start.10 = (bf16[1,128,2048]{2,1,0:T(8,128)(2,1)S(1)}, bf16[1,128,2048]{2,1,0:T(8,128)(2,1)}, u32[]{:S(2)}) copy-start(bf16[1,128,2048]{2,1,0:T(8,128)(2,1)} %param.14) | copy-start | bytes 1572868
  38.2 279.1 %all-gather.13.cloned.1.call-start = ((), (), s32[]{:S(2)}) async-start(), calls=%async_computation.15 | async-start | bytes 10485760 | tf_op jit(solution)/shard_map/all_gather | solution.py:643
  88.1 63.1 %copy-start.8 = (bf16[1,128,2048]{2,1,0:T(8,128)(2,1)S(1)}, bf16[1,128,2048]{2,1,0:T(8,128)(2,1)}, u32[]{:S(2)}) copy-start(bf16[1,128,2048]{2,1,0:T(8,128)(2,1)} %param.12) | copy-start | bytes 1572868
  88.1 254.1 %all-gather.9.cloned.1.call-start = ((), (), s32[]{:S(2)}) async-start(), calls=%async_computation.9 | async-start | bytes 5242880 | tf_op jit(solution)/shard_map/all_gather | solution.py:819
  88.7 428.5 %reduce-scatter.5.cloned.1.call-start = ((), (), s32[]{:S(2)}) async-start(), calls=%async_computation.10 | async-start | bytes 1966080 | tf_op jit(solution)/shard_map/reduce_scatter | solution.py:649
  151.4 48.8 %copy-start.18 = (f32[128]{0:T(128)}, f32[128]{0:T(128)S(1)}, u32[]{:S(2)}) copy-start(f32[128]{0:T(128)S(1)} %add_rsqrt_fusion.1) | copy-start | bytes 1540
  204.6 5.1 copy-start.14
  218.0 0.8 copy-start.2
  218.8 0.8 copy-start.4
  269.4 1.0 copy-start.6
  269.4 144.3 %copy-start.17 = (f32[128]{0:T(128)}, f32[128]{0:T(128)S(1)}, u32[]{:S(2)}) copy-start(f32[128]{0:T(128)S(1)} %add_rsqrt_fusion) | copy-start | bytes 1540
  317.4 11.4 %copy-start.13 = (bf16[1024,2048]{1,0:T(8,128)(2,1)S(1)}, bf16[1024,2048]{1,0:T(8,128)(2,1)}, u32[]{:S(2)}) copy-start(bf16[1024,2048]{1,0:T(8,128)(2,1)} %gather_ctx.5) | copy-start | bytes 12582916
  355.3 1.3 copy-start.25
  355.3 12.7 %copy-start.26 = (bf16[1024,1024]{1,0:T(8,128)(2,1)}, bf16[1024,1024]{1,0:T(8,128)(2,1)S(1)}, u32[]{:S(2)}) copy-start(bf16[1024,1024]{1,0:T(8,128)(2,1)S(1)} %get-tuple-element.28) | copy-start | bytes 6291460
  368.0 44.8 %copy-start.7 = (f32[128,2048]{1,0:T(8,128)S(1)}, f32[128,2048]{1,0:T(8,128)}, u32[]{:S(2)}) copy-start(f32[128,2048]{1,0:T(8,128)} %copy-done.6) | copy-start | bytes 3145732
  368.0 45.6 %copy-start.11 = (bf16[1,128,2048]{2,1,0:T(8,128)(2,1)S(1)}, bf16[1,128,2048]{2,1,0:T(8,128)(2,1)}, u32[]{:S(2)}) copy-start(bf16[1,128,2048]{2,1,0:T(8,128)(2,1)} %param.14) | copy-start | bytes 1572868
  413.7 49.4 %copy-start.20 = (f32[128]{0:T(128)}, f32[128]{0:T(128)S(1)}, u32[]{:S(2)}) copy-start(f32[128]{0:T(128)S(1)} %broadcast_multiply_fusion.1) | copy-start | bytes 1540
  459.2 3.9 copy-start.3
  459.2 3.9 copy-start.5
  463.1 13.4 %copy-start.12 = (bf16[1024,2048]{1,0:T(8,128)(2,1)S(1)}, bf16[1024,2048]{1,0:T(8,128)(2,1)}, u32[]{:S(2)}) copy-start(bf16[1024,2048]{1,0:T(8,128)(2,1)} %gather_ctx.4) | copy-start | bytes 12582916
  476.5 2.4 copy-start
  480.3 101.3 %reduce-scatter.9.cloned.1.call-start = ((), (), s32[]{:S(2)}) async-start(), calls=%async_computation.12 | async-start | bytes 10485760 | tf_op jit(solution)/shard_map/reduce_scatter | solution.py:649
  503.0 227.3 %reduce-scatter.7.cloned.1.call-start = ((), (), s32[]{:S(2)}) async-start(), calls=%async_computation.11 | async-start | bytes 1310720 | tf_op jit(solution)/shard_map/reduce_scatter | solution.py:859
  507.5 227.3 %reduce-scatter.11.cloned.1.call-start = ((), (), s32[]{:S(2)}) async-start(), calls=%async_computation.13 | async-start | bytes 5242880 | tf_op jit(solution)/shard_map/reduce_scatter | solution.py:851
  517.2 70.0 %copy-start.24 = (bf16[1024,1024]{1,0:T(8,128)(2,1)S(1)}, bf16[1024,1024]{1,0:T(8,128)(2,1)}, u32[]{:S(2)}) copy-start(bf16[1024,1024]{1,0:T(8,128)(2,1)} %get-tuple-element.29) | copy-start | bytes 6291460
  581.7 156.0 %all-to-all-start.3 = ((bf16[8,64,2048]{2,1,0:T(8,128)(2,1)}), bf16[8,64,2048]{2,1,0:T(8,128)(2,1)}, u32[]{:S(2)}, u32[]{:S(2)}) async-start(bf16[8,64,2048]{2,1,0:T(8,128)(2,1)} %bitcast.110), calls=%async_computation.6 | async-start | bytes 4194304 | tf_op jit(solution)/shard_map/all_to_all | solution.py:638
  594.1 64.5 %copy-start.16 = (f32[2048]{0:T(1024)S(1)}, f32[2048]{0:T(1024)}, u32[]{:S(2)}) copy-start(f32[2048]{0:T(1024)} %get-tuple-element.19) | copy-start | bytes 24580
  594.1 65.2 %copy-start.1 = (bf16[1024,384]{1,0:T(8,128)(2,1)S(1)}, bf16[1024,384]{1,0:T(8,128)(2,1)}, u32[]{:S(2)}) copy-start(bf16[1024,384]{1,0:T(8,128)(2,1)} %copy-done) | copy-start | bytes 2359300
  663.0 46.8 %copy-start.9 = (bf16[1,128,2048]{2,1,0:T(8,128)(2,1)S(1)}, bf16[1,128,2048]{2,1,0:T(8,128)(2,1)}, u32[]{:S(2)}) copy-start(bf16[1,128,2048]{2,1,0:T(8,128)(2,1)} %param.12) | copy-start | bytes 1572868
  663.1 46.8 %copy-start.19 = (f32[128]{0:T(128)S(1)}, f32[128]{0:T(128)}, u32[]{:S(2)}) copy-start(f32[128]{0:T(128)} %copy-done.18) | copy-start | bytes 1540
Sparse Core Ops, SparseCore 0:
  31.3 18.6 all-gather.10
  51.5 16.6 all-gather.6
  88.2 57.2 all-gather.12
  147.0 34.4 all-gather.8
  480.4 27.3 reduce-scatter.4
  510.2 71.3 reduce-scatter.8
  584.8 24.8 reduce-scatter.6
  612.1 44.5 reduce-scatter.10

commit v3 on v2

--- a/solution.py
+++ b/solution.py
@@ -22,6 +22,7 @@
 MESH = pl.DeviceIdType.MESH
 PAIR = 2
 CHUNKS = 2
+LINK_COST = pl.CostEstimate(flops=0, bytes_accessed=150_000_000, transcendentals=0)
 
 
 def doc_index(positions, starts):
@@ -439,6 +440,7 @@
             pltpu.SemaphoreType.DMA,
         ],
         compiler_params=pltpu.CompilerParams(collective_id=0, has_side_effects=True),
+        cost_estimate=LINK_COST,
         name="gather_ctx",
     )(local)
 
@@ -558,6 +560,7 @@
         compiler_params=pltpu.CompilerParams(
             collective_id=1, has_side_effects=True, vmem_limit_bytes=32 * 2**20
         ),
+        cost_estimate=LINK_COST,
         name="scatter_ctx",
     )(partial)
 
@@ -614,6 +617,7 @@
         out_specs=pl.BlockSpec(memory_space=pltpu.VMEM),
         scratch_shapes=[pltpu.SemaphoreType.DMA((count,)), pltpu.SemaphoreType.DMA((count,))],
         compiler_params=pltpu.CompilerParams(collective_id=2, has_side_effects=True),
+        cost_estimate=pl.CostEstimate(flops=0, bytes_accessed=25_000_000, transcendentals=0),
         name="exchange",
     )(tiles)
 
@@ -638,16 +642,18 @@
     return lax.all_to_all(blocks, "ctx", split_axis=0, concat_axis=0, tiled=True)
 
 
-def spread_columns(blocks):
-    mine = swap_ctx(blocks)
+def spread_columns(mine):
     full = lax.all_gather(mine[:, None], "fsdp", axis=1, tiled=True)
-    return full.reshape(-1, blocks.shape[-1])
-
-
-def return_columns(grad, ctx_size, fsdp_size):
-    by_owner = grad.reshape(ctx_size, fsdp_size, -1, grad.shape[-1]).transpose(1, 0, 2, 3)
-    mine = lax.psum_scatter(rows_of(rows_of(by_owner)), "fsdp", scatter_dimension=0, tiled=True)
-    return swap_ctx(mine.reshape(ctx_size, -1, grad.shape[-1]))
+    return full.reshape(-1, mine.shape[-1])
+
+
+def by_fsdp(grad, ctx_size, fsdp_size):
+    parts = grad.reshape(ctx_size, fsdp_size, -1, grad.shape[-1]).transpose(1, 0, 2, 3)
+    return rows_of(rows_of(parts))
+
+
+def return_columns(terms, ctx_size):
+    return swap_ctx(terms.reshape(ctx_size, -1, terms.shape[-1]))
 
 
 def half_turn(values, sign_table):
@@ -788,7 +794,7 @@
     w_up,
     w_down,
 ):
-    local_rows, model = tokens.shape[1:]
+    local_rows, _ = tokens.shape[1:]
     ctx_size = lax.axis_size("ctx")
     fsdp_size = lax.axis_size("fsdp")
     length = local_rows * ctx_size
@@ -812,21 +818,25 @@
         return weight.reshape(held_rows, ctx_size, -1)
 
     qkv_parts = jnp.concatenate([by_slice(w_query), by_slice(w_key), by_slice(w_value)], axis=2)
-    w_qkv = spread_columns(qkv_parts.transpose(1, 0, 2))
+    w_qkv = spread_columns(swap_ctx(qkv_parts.transpose(1, 0, 2)))
     wo_mine = lax.all_gather(w_output, "fsdp", axis=0, tiled=True)
     gu_parts = jnp.concatenate([by_slice(w_gate), by_slice(w_up)], axis=2)
-    w_gu = spread_columns(gu_parts.transpose(1, 0, 2))
-    wd_mine = lax.all_gather(w_down, "fsdp", axis=0, tiled=True)
+    gu_mine = swap_ctx(gu_parts.transpose(1, 0, 2))
 
     inputs = tokens[0].astype(jnp.float32)
     inv_one = lax.rsqrt(jnp.mean(inputs * inputs, axis=-1, keepdims=True) + EPSILON)
     unit_one = inputs * inv_one
     normed1 = gather_ctx((unit_one * gain1).astype(bf16))
+    normed1, gu_mine = lax.optimization_barrier((normed1, gu_mine))
+    w_gu = spread_columns(gu_mine)
+    wd_mine = lax.all_gather(w_down, "fsdp", axis=0, tiled=True)
     grad_out = cotangent[0].astype(jnp.float32)
-    grad_mlp = gather_ctx((RESIDUAL_MULT * grad_out).astype(bf16))
+    grad_mlp = (RESIDUAL_MULT * grad_out).astype(bf16)
 
     block_rows = math.gcd(length, 256)
     qkv = dot_plain(normed1, w_qkv)
+    qkv, grad_mlp = lax.optimization_barrier((qkv, grad_mlp))
+    grad_mlp = lax.all_gather(grad_mlp, "ctx", axis=0, tiled=True)
     q, kv, mixed_heads, log_sum = attention_forward(qkv, tables, block_rows)
     hidden = inputs + RESIDUAL_MULT * scatter_ctx(dot_plain(mixed_heads, wo_mine).astype(bf16))
     inv_two = lax.rsqrt(jnp.mean(hidden * hidden, axis=-1, keepdims=True) + EPSILON)
@@ -838,30 +848,50 @@
     sig_gate = jax.nn.sigmoid(gate_pre)
     silu_gate = gate_pre * sig_gate
     activ = (silu_gate * up_pre).astype(bf16)
-    branch = scatter_ctx(dot_plain(activ, wd_mine).astype(bf16))
-    output = (hidden + RESIDUAL_MULT * branch).astype(bf16)[None]
+    out_terms = dot_plain(activ, wd_mine).astype(bf16)
 
     silu_slope = sig_gate * (1.0 + gate_pre * (1.0 - sig_gate))
     grad_act = dot_back(grad_mlp, wd_mine)
     grad_gu = jnp.concatenate(
         [(grad_act * up_pre * silu_slope).astype(bf16), (grad_act * silu_gate).astype(bf16)], axis=1
     )
-    grad_norm2 = scatter_ctx(dot_back(grad_gu, w_gu).astype(bf16))
-    gu_back = return_columns(dot_outer(normed2, grad_gu).astype(bf16), ctx_size, fsdp_size)
-    wd_back = lax.psum_scatter(
-        dot_outer(activ, grad_mlp).astype(bf16), "fsdp", scatter_dimension=0, tiled=True
-    )
+    out_terms, partial2, gu_terms, wd_terms = lax.optimization_barrier(
+        (
+            out_terms,
+            dot_back(grad_gu, w_gu).astype(bf16),
+            by_fsdp(dot_outer(normed2, grad_gu).astype(bf16), ctx_size, fsdp_size),
+            dot_outer(activ, grad_mlp).astype(bf16),
+        )
+    )
+    branch = lax.psum_scatter(out_terms, "ctx", scatter_dimension=0, tiled=True)
+    output = (hidden + RESIDUAL_MULT * branch.astype(jnp.float32)).astype(bf16)[None]
+    grad_norm2 = scatter_ctx(partial2)
+    gu_back = lax.psum_scatter(gu_terms, "fsdp", scatter_dimension=0, tiled=True)
+    wd_back = lax.psum_scatter(wd_terms, "fsdp", scatter_dimension=0, tiled=True)
 
     grad_g2 = jnp.sum(grad_norm2 * unit_two, axis=0)
     grad_hidden = grad_out + norm_back(grad_norm2, unit_two, inv_two, gain2)
     grad_attn = gather_ctx((RESIDUAL_MULT * grad_hidden).astype(bf16))
-    grad_mixed = dot_back(grad_attn, wo_mine).astype(bf16)
-    wo_back = lax.psum_scatter(
-        dot_outer(mixed_heads, grad_attn).astype(bf16), "fsdp", scatter_dimension=0, tiled=True
-    )
+    grad_mixed, wo_terms = lax.optimization_barrier(
+        (
+            dot_back(grad_attn, wo_mine).astype(bf16),
+            dot_outer(mixed_heads, grad_attn).astype(bf16),
+        )
+    )
+    wo_back = lax.psum_scatter(wo_terms, "fsdp", scatter_dimension=0, tiled=True)
     grad_qkv = attention_backward(q, kv, grad_mixed, log_sum, tables, block_rows)
-    grad_norm1 = scatter_ctx(dot_back(grad_qkv, w_qkv).astype(bf16))
-    qkv_back = return_columns(dot_outer(normed1, grad_qkv).astype(bf16), ctx_size, fsdp_size)
+    grad_qkv, gu_back = lax.optimization_barrier((grad_qkv, gu_back))
+    gu_back = return_columns(gu_back, ctx_size)
+    partial1, qkv_terms = lax.optimization_barrier(
+        (
+            dot_back(grad_qkv, w_qkv).astype(bf16),
+            by_fsdp(dot_outer(normed1, grad_qkv).astype(bf16), ctx_size, fsdp_size),
+        )
+    )
+    grad_norm1 = scatter_ctx(partial1)
+    qkv_back = lax.psum_scatter(qkv_terms, "fsdp", scatter_dimension=0, tiled=True)
+    grad_norm1, qkv_back = lax.optimization_barrier((grad_norm1, qkv_back))
+    qkv_back = return_columns(qkv_back, ctx_size)
     grad_g1 = jnp.sum(grad_norm1 * unit_one, axis=0)
     grad_inputs = grad_hidden + norm_back(grad_norm1, unit_one, inv_one, gain1)
     gain_back = scatter_rows(jnp.stack([grad_g1, grad_g2]))
@@ -913,7 +943,11 @@
         P(("ctx", "fsdp"), None),
         P(("ctx", "fsdp"), None),
     )
-    split_heads = mesh.shape["ctx"] == KVH == 4 * PAIR
+    if mesh.shape["ctx"] != KVH or KVH != 4 * PAIR:
+        return jax.shard_map(
+            general_device, mesh=mesh, in_specs=in_specs, out_specs=out_specs, check_vma=False
+        )
+
     return jax.shard_map(
-        on_device if split_heads else general_device, mesh=mesh, in_specs=in_specs, out_specs=out_specs, check_vma=False
-    )
+        on_device, mesh=mesh, in_specs=in_specs, out_specs=out_specs, check_vma=False
+    )

time: 756 us -> 734 us (0.971)
  Pallas kernels: 431 us -> 390 us
  waiting for transfers between devices: 109 us -> 129 us
  blocking collectives: 13.1 us -> 0 us
    pallas_call x4 -> x3, Pallas kernels: 203 us -> 150 us  [scatter_ctx(): pl.pallas_call(functools.partial(scatter_kernel, line_size), out_shape=ja...]
    reduce_scatter x4 -> x5, waiting for transfers between devices: 51.3 us -> 101 us  [the longest x1 64.9 us: on_device(): branch = lax.psum_scatter(out_terms, 'ctx', scatter_dimension=0, tiled=True)]
    pallas_call x2, Pallas kernels: 19.9 us -> 68.5 us  [exchange(): pl.pallas_call(functools.partial(exchange_kernel, ctx_size, fsdp_size), o...]
    all_to_all x3 -> x4, waiting for transfers between devices: 56.5 us -> 9.2 us  [swap_ctx(): lax.all_to_all(blocks, 'ctx', split_axis=0, concat_axis=0, tiled=True)]
    pallas_call x4 -> x3, Pallas kernels: 187 us -> 149 us  [gather_ctx(): pl.pallas_call(functools.partial(gather_kernel, ctx_size // PAIR), out_sh...]
    all_gather x0 -> x1, waiting for transfers between devices: none -> 16.1 us  [on_device(): grad_mlp = lax.all_gather(grad_mlp, 'ctx', axis=0, tiled=True)]
    all_to_all x1 -> x0, blocking collectives: 13.1 us -> none  [swap_ctx(): lax.all_to_all(blocks, 'ctx', split_axis=0, concat_axis=0, tiled=True)]
    unnamed x57 -> x53, local copies, waits for them, and re-layouts: 7.4 us -> 16.3 us
  transfers between devices with their start and end apart: 11 -> 14, of which waited for: 3 -> 4; matrix products, arithmetic and copies ran while one was open for 15% -> 12% of each run, Pallas kernels for 44% -> 54%
where the time goes in v3:
time: 734 us; the launch traced here: 726 us
  Pallas kernels  390 us (53%)
  waiting for transfers between devices  129 us (18%)
  matrix products  94.7 us (13%)
  local copies, waits for them, and re-layouts  57.4 us (8%)
  starting transfers between devices  20.7 us (3%)
  other arithmetic  20.4 us (3%)
  between operations  14.8 us (2%)
    pallas_call x3, Pallas kernels, scatter_ctx(): pl.pallas_call(functools.partial(scatter_kernel, line_size), out_shape=ja...  150 us
    pallas_call x3, Pallas kernels, gather_ctx(): pl.pallas_call(functools.partial(gather_kernel, ctx_size // PAIR), out_sh...  149 us
    pallas_call x2, Pallas kernels, exchange(): pl.pallas_call(functools.partial(exchange_kernel, ctx_size, fsdp_size), o...  68.5 us
    reduce_scatter x1, waiting for transfers between devices, on_device(): branch = lax.psum_scatter(out_terms, 'ctx', scatter_dimension=0, tiled=True)  64.9 us
    reduce_scatter x1, waiting for transfers between devices, on_device(): lax.psum_scatter(wd_terms, 'fsdp', scatter_dimension=0, tiled=True)  35.9 us
    dot_general x4, matrix products, dot_back(): lax.dot_general(left, right, (((1,), (1,)), ((), ())), preferred_element_...  34.8 us
    dot_general x4, matrix products, dot_plain(): return jnp.dot(left, right, preferred_element_type=jnp.float32)  31.6 us
    dot_general x4, matrix products, dot_outer(): lax.dot_general(left, right, (((0,), (0,)), ((), ())), preferred_element_...  28.4 us
  transfers between devices with their start and end apart: 14, of which 4 were waited for; matrix products, arithmetic and copies ran while one was open for 12% of the time, Pallas kernels for 54%

profile of v3, /device:TPU:0, one launch (start us, length us, event | category | flops | bytes accessed | tf_op | source)
XLA Modules:
  0.0 726.5 jit_solution(13382591752167408127)
XLA Ops:
  7.2 1.1 reshape.177
  8.3 1.0 reshape.178
  9.2 1.0 copy.102
  11.2 7.3 %all-to-all-start.1 = ((bf16[8,64,384]{2,1,0:T(8,128)(2,1)}), bf16[8,64,384]{2,1,0:T(8,128)(2,1)S(1)}, u32[]{:S(2)}, u32[]{:S(2)}) async-start(bf16[8,64,384]{2,1,0:T(8,128)(2,1)} %copy.79), calls=%async_computation.1 | async-start | bytes 786432 | tf_op jit(solution)/shard_map/all_to_all | solution.py:642
  18.5 1.8 copy.100
  21.0 9.2 %all-to-all-done.1 = bf16[8,64,384]{2,1,0:T(8,128)(2,1)S(1)} async-done(((bf16[8,64,384]{2,1,0:T(8,128)(2,1)}), bf16[8,64,384]{2,1,0:T(8,128)(2,1)S(1)}, u32[]{:S(2)}, u32[]{:S(2)}) %all-to-all-start.1) | async-done | bytes 393248 | tf_op jit(solution)/shard_map/all_to_all | solution.py:642
  30.1 1.0 copy.80
  31.4 2.5 copy.78
  33.8 3.6 all-to-all-start
  39.0 52.0 %exchange.2 = f32[32,8,128]{2,1,0:T(8,128)} custom-call(f32[32,8,128]{2,1,0:T(8,128)} %broadcast_in_dim.17.x_ref), custom_call_target="tpu_custom_call" | custom-call | bytes 25000000 | tf_op jit(solution)/shard_map/exchange/pallas_call | solution.py:613
  91.0 0.9 slice_bitcast_fusion
  92.3 1.0 fusion.6.x_ref
  93.3 48.6 %gather_ctx.3 = bf16[1024,2048]{1,0:T(8,128)(2,1)} custom-call(bf16[128,2048]{1,0:T(8,128)(2,1)} %fusion.6.x_ref), custom_call_target="tpu_custom_call" | custom-call | bytes 150000000 | tf_op jit(solution)/shard_map/gather_ctx/pallas_call | solution.py:432
  141.9 2.5 copy.84
  145.0 0.9 fusion.5
  145.9 1.6 copy.81
  147.5 1.1 copy-done.18
  148.7 6.2 fusion.26.qkv_ref
  155.8 1.9 fusion.15
  157.7 0.9 pad_maximum_fusion.3
  158.6 8.2 %attend.1 = (bf16[1024,256]{1,0:T(8,128)(2,1)S(1)}, bf16[1024,128]{1,0:T(8,128)(2,1)S(1)}, bf16[1024,256]{1,0:T(8,128)(2,1)S(1)}, f32[1024,4]{1,0:T(8,128)S(1)}) custom-call(f32[1024,384]{1,0:T(8,128)S(1)} %copy-done.2, f32[1024,128]{1,0:T(8,128)S(1)} %get-tuple-element.73.cos_ref, f32[1024,128]{1,0:T(8,128)S(1)} %get-tuple-element.74.sin_ref, ...), custom_call_target="tpu_custom_call" | custom-call | tf_op jit(solution)/shard_map/attend/pallas_call | solution.py:752
  169.0 2.5 convolution_convert_fusion.3.x_ref
  171.5 47.1 %scatter_ctx.3 = f32[128,2048]{1,0:T(8,128)S(1)} custom-call(bf16[1024,2048]{1,0:T(8,128)(2,1)S(1)} %convolution_convert_fusion.3.x_ref), custom_call_target="tpu_custom_call" | custom-call | bytes 150000000 | tf_op jit(solution)/shard_map/scatter_ctx/pallas_call | solution.py:548
  218.9 1.0 copy-done.10
  219.9 0.9 multiply_convert_fusion.4.x_ref
  220.8 53.4 %gather_ctx.4 = bf16[1024,2048]{1,0:T(8,128)(2,1)} custom-call(bf16[128,2048]{1,0:T(8,128)(2,1)} %multiply_convert_fusion.4.x_ref), custom_call_target="tpu_custom_call" | custom-call | bytes 150000000 | tf_op jit(solution)/shard_map/gather_ctx/pallas_call | solution.py:432
  274.3 11.9 %copy.85 = bf16[8,256,2048]{2,1,0:T(8,128)(2,1)} copy(bf16[8,256,2048]{2,0,1:T(8,128)(2,1)} %all-gather.16.cloned.1.call-done) | data formatting | bytes 16777216 | tf_op jit(solution)/shard_map/all_gather | solution.py:646
  286.2 13.6 %fusion.27 = f32[1024,2048]{1,0:T(8,128)} fusion(bf16[1024,2048]{1,0:T(8,128)(2,1)S(1)} %copy-done.16, bf16[2048,2048]{1,0:T(8,128)(2,1)} %bitcast.104), kind=kOutput, calls=%fused_computation.81 | convolution fusion | flops 8589934592 | bytes 20971520 | tf_op jit(solution)/shard_map/dot_general | solution.py:58
  299.8 16.1 %all-gather.12.cloned.1.call-done = bf16[1024,2048]{1,0:T(8,128)(2,1)} async-done(((bf16[128,2048]{1,0:T(8,128)(2,1)}), bf16[1024,2048]{1,0:T(8,128)(2,1)}) %all-gather.12.cloned.1.call-update) | async-done | bytes 4194320 | tf_op jit(solution)/shard_map/all_gather | solution.py:839
  315.9 13.1 %multiply_convert_fusion.1 = (bf16[1024,1024]{1,0:T(8,128)(2,1)S(1)}, bf16[1024,1024]{1,0:T(8,128)(2,1)S(1)}, bf16[1024,1024]{1,0:T(8,128)(2,1)}) fusion(f32[1024,2048]{1,0:T(8,128)} %fusion.27, bf16[1024,2048]{1,0:T(8,128)(2,1)} %all-gather.12.cloned.1.call-done, bf16[1024,2048]{1,0:T(8,128)(2,1)} %all-gather.10.cloned.1.call-done), kind=kOutput, calls=%fused_computation.3 | convolution fusion | flops 4310695936 | bytes 23068672 | tf_op jit(solution)/shard_map/dot_general | solution.py:62
  329.0 12.8 %convolution_convert_fusion.2.x_ref = bf16[1024,2048]{1,0:T(8,128)(2,1)} fusion(bf16[2048,2048]{1,0:T(8,128)(2,1)} %bitcast.105, bf16[1024,1024]{1,0:T(8,128)(2,1)S(1)} %get-tuple-element.60, bf16[1024,1024]{1,0:T(8,128)(2,1)S(1)} %get-tuple-element.59), kind=kOutput, calls=%fused_computation.8 | convolution fusion | flops 8600420352 | bytes 16777216 | tf_op jit(solution)/shard_map/dot_general | solution.py:62
  341.8 11.5 %convolution_convert_fusion = bf16[2048,2048]{1,0:T(8,128)(2,1)} fusion(bf16[1024,2048]{1,0:T(8,128)(2,1)S(1)} %copy-done.17, bf16[1024,1024]{1,0:T(8,128)(2,1)S(1)} %get-tuple-element.60, bf16[1024,1024]{1,0:T(8,128)(2,1)S(1)} %get-tuple-element.59), kind=kOutput, calls=%fused_computation | convolution fusion | flops 8602517504 | bytes 16777216 | tf_op jit(solution)/shard_map/dot_general | solution.py:68
  353.3 8.5 %copy.88 = bf16[8,4,64,2048]{3,2,0,1:T(8,128)(2,1)} copy(bf16[8,4,64,2048]{3,2,1,0:T(8,128)(2,1)} %bitcast.106) | data formatting | bytes 16777216 | tf_op jit(solution)/shard_map/reshape | solution.py:651
  361.8 7.8 %convolution_convert_fusion.4 = bf16[1024,2048]{1,0:T(8,128)(2,1)} fusion(bf16[1024,1024]{1,0:T(8,128)(2,1)} %get-tuple-element.61, bf16[1024,2048]{1,0:T(8,128)(2,1)S(1)} %copy-done.23), kind=kOutput, calls=%fused_computation.10 | convolution fusion | flops 4297064448 | bytes 10485760 | tf_op jit(solution)/shard_map/dot_general | solution.py:68
  369.5 9.3 %convolution_convert_fusion.5 = bf16[1024,2048]{1,0:T(8,128)(2,1)} fusion(bf16[1024,1024]{1,0:T(8,128)(2,1)} %get-tuple-element.61, bf16[1024,2048]{1,0:T(8,128)(2,1)} %all-gather.10.cloned.1.call-done), kind=kOutput, calls=%fused_computation.11 | convolution fusion | flops 4297064448 | bytes 10485760 | tf_op jit(solution)/shard_map/dot_general | solution.py:58
  378.9 2.2 copy-done.1
  381.1 46.6 %scatter_ctx.4 = f32[128,2048]{1,0:T(8,128)S(1)} custom-call(bf16[1024,2048]{1,0:T(8,128)(2,1)S(1)} %copy-done.1), custom_call_target="tpu_custom_call" | custom-call | bytes 150000000 | tf_op jit(solution)/shard_map/scatter_ctx/pallas_call | solution.py:548
  428.1 1.2 multiply_convert_fusion.3.x_ref
  429.3 47.2 %gather_ctx.5 = bf16[1024,2048]{1,0:T(8,128)(2,1)} custom-call(bf16[128,2048]{1,0:T(8,128)(2,1)} %multiply_convert_fusion.3.x_ref), custom_call_target="tpu_custom_call" | custom-call | bytes 150000000 | tf_op jit(solution)/shard_map/gather_ctx/pallas_call | solution.py:432
  476.5 4.4 convolution_convert_fusion.7
  480.9 4.6 convolution_convert_fusion.8.do_ref
  486.7 1.0 copy-done.4
  487.7 1.0 copy-done.6
  488.8 1.0 copy-done.7
  489.8 0.9 copy-done.9
  490.8 13.3 %attend_back.1 = bf16[1024,384]{1,0:T(8,128)(2,1)S(1)} custom-call(bf16[1024,256]{1,0:T(8,128)(2,1)S(1)} %copy-done.4, bf16[1024,128]{1,0:T(8,128)(2,1)S(1)} %copy-done.9, bf16[1024,256]{1,0:T(8,128)(2,1)S(1)} %copy-done.7, f32[1024,4]{1,0:T(8,128)S(1)} %copy-done.6, f32[1024,128]{1,0:T(8,128)S(1)} %get-tuple-element.73.cos_ref, ...), custom_call_target="tpu_custom_call" | custom-call | tf_op jit(solution)/shard_map/attend_back/pallas_call | solution.py:769
  504.2 4.7 convolution_convert_fusion.6
  508.8 1.3 copy.90
  510.2 4.3 convolution_convert_fusion.1.x_ref
  515.1 4.6 all-to-all-start.3
  519.8 1.8 convert_element_type.186
  521.6 35.9 %reduce-scatter.14.cloned.1.call-done = bf16[256,2048]{1,0:T(8,128)(2,1)} async-done(((bf16[1024,2048]{1,0:T(8,128)(2,1)}), bf16[256,2048]{1,0:T(8,128)(2,1)}) %reduce-scatter.14.cloned.1.call-update) | async-done | bytes 1048592 | tf_op jit(solution)/shard_map/reduce_scatter | solution.py:870
  557.5 2.8 convert_element_type.193
  560.3 2.2 copy-done
  562.5 56.8 %scatter_ctx.5 = f32[128,2048]{1,0:T(8,128)S(1)} custom-call(bf16[1024,2048]{1,0:T(8,128)(2,1)S(1)} %copy-done), custom_call_target="tpu_custom_call" | custom-call | bytes 150000000 | tf_op jit(solution)/shard_map/scatter_ctx/pallas_call | solution.py:548
  619.3 1.4 fusion.12
  620.9 64.9 %reduce-scatter.6.cloned.1.call-done = bf16[128,2048]{1,0:T(8,128)(2,1)} async-done(((bf16[1024,2048]{1,0:T(8,128)(2,1)}), bf16[128,2048]{1,0:T(8,128)(2,1)}) %reduce-scatter.6.cloned.1.call-update) | async-done | bytes 524304 | tf_op jit(solution)/shard_map/reduce_scatter | solution.py:866
  685.7 3.0 fusion.11
  688.8 4.2 all-to-all-start.2
  693.7 16.5 %exchange.3 = f32[32,8,128]{2,1,0:T(8,128)} custom-call(f32[32,8,128]{2,1,0:T(8,128)} %pad.10.x_ref), custom_call_target="tpu_custom_call" | custom-call | bytes 25000000 | tf_op jit(solution)/shard_map/exchange/pallas_call | solution.py:613
  710.2 0.9 reduce_sum.79
  711.7 2.0 convert_bitcast_fusion
  713.7 1.5 copy.99
  715.2 1.5 copy.98
  (107 shorter events, 14.1 us)
Async XLA Ops:
  7.2 13.2 %copy-start.20 = (bf16[64,8192]{1,0:T(8,128)(2,1)S(1)}, bf16[64,8192]{1,0:T(8,128)(2,1)}, u32[]{:S(2)}) copy-start(bf16[64,8192]{1,0:T(8,128)(2,1)} %param.22) | copy-start | bytes 3145732
  11.2 19.0 %all-to-all-start.1 = ((bf16[8,64,384]{2,1,0:T(8,128)(2,1)}), bf16[8,64,384]{2,1,0:T(8,128)(2,1)S(1)}, u32[]{:S(2)}, u32[]{:S(2)}) async-start(bf16[8,64,384]{2,1,0:T(8,128)(2,1)} %copy.79), calls=%async_computation.1 | async-start | bytes 786432 | tf_op jit(solution)/shard_map/all_to_all | solution.py:642
  18.5 127.4 %all-gather.14.cloned.1.call-start = ((), (), s32[]{:S(2)}) async-start(), calls=%async_computation.17 | async-start | bytes 1966080 | tf_op jit(solution)/shard_map/all_gather | solution.py:646
  31.3 6.9 copy-start.21
  31.4 6.9 copy-start.22
  31.4 60.7 %copy-start.13 = (bf16[1,128,2048]{2,1,0:T(8,128)(2,1)S(1)}, bf16[1,128,2048]{2,1,0:T(8,128)(2,1)}, u32[]{:S(2)}) copy-start(bf16[1,128,2048]{2,1,0:T(8,128)(2,1)} %param.12) | copy-start | bytes 1572868
  33.8 108.0 %all-to-all-start = ((bf16[8,64,2048]{2,1,0:T(8,128)(2,1)}), bf16[8,64,2048]{2,1,0:T(8,128)(2,1)S(1)}, u32[]{:S(2)}, u32[]{:S(2)}) async-start(bf16[8,64,2048]{2,1,0:T(8,128)(2,1)} %copy.78), calls=%async_computation | async-start | bytes 4194304 | tf_op jit(solution)/shard_map/all_to_all | solution.py:642
  37.5 131.6 %all-gather.8.cloned.1.call-start = ((), (), s32[]{:S(2)}) async-start(), calls=%async_computation.9 | async-start | bytes 1310720 | tf_op jit(solution)/shard_map/all_gather | solution.py:822
  38.2 236.0 %all-gather.16.cloned.1.call-start = ((), (), s32[]{:S(2)}) async-start(), calls=%async_computation.18 | async-start | bytes 10485760 | tf_op jit(solution)/shard_map/all_gather | solution.py:646
  141.9 3.1 copy-start.14
  144.4 155.4 %all-gather.10.cloned.1.call-start = ((), (), s32[]{:S(2)}) async-start(), calls=%async_computation.10 | async-start | bytes 5242880 | tf_op jit(solution)/shard_map/all_gather | solution.py:832
  145.0 171.0 %all-gather.12.cloned.1.call-start = ((), (), s32[]{:S(2)}) async-start(), calls=%async_computation.11 | async-start | bytes 4718592 | tf_op jit(solution)/shard_map/all_gather | solution.py:839
  147.5 1.1 copy-start.18
  148.7 6.5 copy-start.24
  154.9 349.2 %reduce-scatter.8.cloned.1.call-start = ((), (), s32[]{:S(2)}) async-start(), calls=%async_computation.13 | async-start | bytes 10485760 | tf_op jit(solution)/shard_map/reduce_scatter | solution.py:869
  155.7 2.8 copy-start.2
  166.7 0.8 copy-start.3
  167.5 0.8 copy-start.5
  168.3 0.7 copy-start.8
  218.9 1.0 copy-start.10
  274.3 11.9 %copy-start.16 = (bf16[1024,2048]{1,0:T(8,128)(2,1)S(1)}, bf16[1024,2048]{1,0:T(8,128)(2,1)}, u32[]{:S(2)}) copy-start(bf16[1024,2048]{1,0:T(8,128)(2,1)} %gather_ctx.4) | copy-start | bytes 12582916
  329.0 12.8 %copy-start.17 = (bf16[1024,2048]{1,0:T(8,128)(2,1)S(1)}, bf16[1024,2048]{1,0:T(8,128)(2,1)}, u32[]{:S(2)}) copy-start(bf16[1024,2048]{1,0:T(8,128)(2,1)} %gather_ctx.4) | copy-start | bytes 12582916
  353.3 8.5 %copy-start.23 = (bf16[1024,2048]{1,0:T(8,128)(2,1)S(1)}, bf16[1024,2048]{1,0:T(8,128)(2,1)}, u32[]{:S(2)}) copy-start(bf16[1024,2048]{1,0:T(8,128)(2,1)} %all-gather.12.cloned.1.call-done) | copy-start | bytes 12582916
  378.8 141.0 %reduce-scatter.12.cloned.1.call-start = ((), (), s32[]{:S(2)}) async-start(), calls=%async_computation.15 | async-start | bytes 1310720 | tf_op jit(solution)/shard_map/reduce_scatter | solution.py:881
  378.9 2.2 copy-start.1
  381.1 46.7 %copy-start.11 = (f32[128,2048]{1,0:T(8,128)S(1)}, f32[128,2048]{1,0:T(8,128)}, u32[]{:S(2)}) copy-start(f32[128,2048]{1,0:T(8,128)} %copy-done.10) | copy-start | bytes 3145732
  381.1 47.0 %copy-start.15 = (bf16[1,128,2048]{2,1,0:T(8,128)(2,1)S(1)}, bf16[1,128,2048]{2,1,0:T(8,128)(2,1)}, u32[]{:S(2)}) copy-start(bf16[1,128,2048]{2,1,0:T(8,128)(2,1)} %param.14) | copy-start | bytes 1572868
  485.5 72.0 %reduce-scatter.14.cloned.1.call-start = ((), (), s32[]{:S(2)}) async-start(), calls=%async_computation.16 | async-start | bytes 5242880 | tf_op jit(solution)/shard_map/reduce_scatter | solution.py:870
  486.2 133.1 %reduce-scatter.10.cloned.1.call-start = ((), (), s32[]{:S(2)}) async-start(), calls=%async_computation.14 | async-start | bytes 1966080 | tf_op jit(solution)/shard_map/reduce_scatter | solution.py:892
  486.7 1.0 copy-start.4
  487.7 1.0 copy-start.6
  488.8 1.0 copy-start.7
  489.8 1.0 copy-start.9
  504.1 6.0 copy-start.19
  514.5 171.2 %reduce-scatter.6.cloned.1.call-start = ((), (), s32[]{:S(2)}) async-start(), calls=%async_computation.12 | async-start | bytes 4718592 | tf_op jit(solution)/shard_map/reduce_scatter | solution.py:866
  515.1 173.7 %all-to-all-start.3 = ((bf16[8,64,2048]{2,1,0:T(8,128)(2,1)}), bf16[8,64,2048]{2,1,0:T(8,128)(2,1)}, u32[]{:S(2)}, u32[]{:S(2)}) async-start(bf16[8,64,2048]{2,1,0:T(8,128)(2,1)} %bitcast.30), calls=%async_computation.7 | async-start | bytes 4194304 | tf_op jit(solution)/shard_map/all_to_all | solution.py:642
  560.3 2.2 copy-start
  562.5 123.2 %copy-start.12 = (f32[128,2048]{1,0:T(8,128)S(1)}, f32[128,2048]{1,0:T(8,128)}, u32[]{:S(2)}) copy-start(f32[128,2048]{1,0:T(8,128)} %copy-done.10) | copy-start | bytes 3145732
  688.8 27.8 %all-to-all-start.2 = ((bf16[8,64,384]{2,1,0:T(8,128)(2,1)}), bf16[8,64,384]{2,1,0:T(8,128)(2,1)S(1)}, u32[]{:S(2)}, u32[]{:S(2)}) async-start(bf16[8,64,384]{2,1,0:T(8,128)(2,1)} %bitcast.25), calls=%async_computation.5 | async-start | bytes 786432 | tf_op jit(solution)/shard_map/all_to_all | solution.py:642
Sparse Core Ops, SparseCore 0:
  31.3 19.0 all-gather.13
  51.9 16.6 all-gather.7
  144.5 57.0 all-gather.15
  203.0 34.4 all-gather.9
  240.1 75.8 all-gather.11
  378.9 69.9 reduce-scatter.7
  485.6 24.7 reduce-scatter.11
  512.9 44.5 reduce-scatter.13
  560.6 28.0 reduce-scatter.9
  592.2 93.4 reduce-scatter.5

commit v4 on v3

--- a/solution.py
+++ b/solution.py
@@ -656,6 +656,11 @@
     return swap_ctx(terms.reshape(ctx_size, -1, terms.shape[-1]))
 
 
+def swap_groups(values, outer, inner):
+    parts = values.reshape(values.shape[0], outer, inner, -1)
+    return parts.transpose(0, 2, 1, 3).reshape(values.shape)
+
+
 def half_turn(values, sign_table):
     lane = lax.broadcasted_iota(jnp.int32, values.shape, 1)
     width = values.shape[1]
@@ -828,7 +833,7 @@
     unit_one = inputs * inv_one
     normed1 = gather_ctx((unit_one * gain1).astype(bf16))
     normed1, gu_mine = lax.optimization_barrier((normed1, gu_mine))
-    w_gu = spread_columns(gu_mine)
+    w_gu = lax.all_gather(rows_of(gu_mine), "fsdp", axis=0, tiled=True)
     wd_mine = lax.all_gather(w_down, "fsdp", axis=0, tiled=True)
     grad_out = cotangent[0].astype(jnp.float32)
     grad_mlp = (RESIDUAL_MULT * grad_out).astype(bf16)
@@ -841,31 +846,36 @@
     hidden = inputs + RESIDUAL_MULT * scatter_ctx(dot_plain(mixed_heads, wo_mine).astype(bf16))
     inv_two = lax.rsqrt(jnp.mean(hidden * hidden, axis=-1, keepdims=True) + EPSILON)
     unit_two = hidden * inv_two
-    normed2 = gather_ctx((unit_two * gain2).astype(bf16))
+    normed2 = gather_ctx(swap_groups((unit_two * gain2).astype(bf16), ctx_size, fsdp_size))
 
     gate_up = dot_plain(normed2, w_gu)
     gate_pre, up_pre = gate_up[:, :ff_slice], gate_up[:, ff_slice:]
     sig_gate = jax.nn.sigmoid(gate_pre)
     silu_gate = gate_pre * sig_gate
     activ = (silu_gate * up_pre).astype(bf16)
-    out_terms = dot_plain(activ, wd_mine).astype(bf16)
+    activ, gate_up = lax.optimization_barrier((activ, gate_up))
+    gate_pre, up_pre = gate_up[:, :ff_slice], gate_up[:, ff_slice:]
+    sig_gate = jax.nn.sigmoid(gate_pre)
+    silu_gate = gate_pre * sig_gate
+    out_terms, grad_mlp = lax.optimization_barrier(
+        (dot_plain(activ, wd_mine).astype(bf16), grad_mlp)
+    )
+    branch = lax.psum_scatter(out_terms, "ctx", scatter_dimension=0, tiled=True)
+    output = (hidden + RESIDUAL_MULT * branch.astype(jnp.float32)).astype(bf16)[None]
 
     silu_slope = sig_gate * (1.0 + gate_pre * (1.0 - sig_gate))
     grad_act = dot_back(grad_mlp, wd_mine)
     grad_gu = jnp.concatenate(
         [(grad_act * up_pre * silu_slope).astype(bf16), (grad_act * silu_gate).astype(bf16)], axis=1
     )
-    out_terms, partial2, gu_terms, wd_terms = lax.optimization_barrier(
+    partial2, gu_terms, wd_terms = lax.optimization_barrier(
         (
-            out_terms,
             dot_back(grad_gu, w_gu).astype(bf16),
-            by_fsdp(dot_outer(normed2, grad_gu).astype(bf16), ctx_size, fsdp_size),
+            dot_outer(normed2, grad_gu).astype(bf16),
             dot_outer(activ, grad_mlp).astype(bf16),
         )
     )
-    branch = lax.psum_scatter(out_terms, "ctx", scatter_dimension=0, tiled=True)
-    output = (hidden + RESIDUAL_MULT * branch.astype(jnp.float32)).astype(bf16)[None]
-    grad_norm2 = scatter_ctx(partial2)
+    grad_norm2 = swap_groups(scatter_ctx(partial2), fsdp_size, ctx_size)
     gu_back = lax.psum_scatter(gu_terms, "fsdp", scatter_dimension=0, tiled=True)
     wd_back = lax.psum_scatter(wd_terms, "fsdp", scatter_dimension=0, tiled=True)
 

time: 734 us -> 730 us (level)
  local copies, waits for them, and re-layouts: 57.4 us -> 49.3 us
    all_gather x2 -> x1, local copies, waits for them, and re-layouts: 13.5 us -> 1.61 us  [spread_columns(): full = lax.all_gather(mine[:, None], 'fsdp', axis=1, tiled=True)]
    reshape x2 -> x1, local copies, waits for them, and re-layouts: 9.78 us -> 1.32 us  [by_fsdp(): grad.reshape(ctx_size, fsdp_size, -1, grad.shape[-1]).transpose(1, 0, 2, 3)]
    unnamed x53 -> x63, local copies, waits for them, and re-layouts: 16.3 us -> 20.6 us
  transfers between devices with their start and end apart: 14 -> 14, of which waited for: 4 -> 4; matrix products, arithmetic and copies ran while one was open for 12% -> 14% of each run, Pallas kernels for 54% -> 54%
where the time goes in v4:
time: 730 us; the launch traced here: 724 us
  Pallas kernels  394 us (54%)
  waiting for transfers between devices  124 us (17%)
  matrix products  95.3 us (13%)
  local copies, waits for them, and re-layouts  49.3 us (7%)
  other arithmetic  26 us (4%)
  starting transfers between devices  20.7 us (3%)
  between operations  14.9 us (2%)
    pallas_call x3, Pallas kernels, gather_ctx(): pl.pallas_call(functools.partial(gather_kernel, ctx_size // PAIR), out_sh...  153 us
    pallas_call x3, Pallas kernels, scatter_ctx(): pl.pallas_call(functools.partial(scatter_kernel, line_size), out_shape=ja...  151 us
    pallas_call x2, Pallas kernels, exchange(): pl.pallas_call(functools.partial(exchange_kernel, ctx_size, fsdp_size), o...  68.5 us
    reduce_scatter x1, waiting for transfers between devices, on_device(): branch = lax.psum_scatter(out_terms, 'ctx', scatter_dimension=0, tiled=True)  64.9 us
    reduce_scatter x1, waiting for transfers between devices, on_device(): lax.psum_scatter(wd_terms, 'fsdp', scatter_dimension=0, tiled=True)  37.9 us
    dot_general x4, matrix products, dot_back(): lax.dot_general(left, right, (((1,), (1,)), ((), ())), preferred_element_...  35.1 us
    dot_general x4, matrix products, dot_outer(): lax.dot_general(left, right, (((0,), (0,)), ((), ())), preferred_element_...  30.3 us
    dot_general x4, matrix products, dot_plain(): return jnp.dot(left, right, preferred_element_type=jnp.float32)  29.9 us
  transfers between devices with their start and end apart: 14, of which 4 were waited for; matrix products, arithmetic and copies ran while one was open for 14% of the time, Pallas kernels for 54%

profile of v4, /device:TPU:0, one launch (start us, length us, event | category | flops | bytes accessed | tf_op | source)
XLA Modules:
  0.0 724.0 jit_solution(4259489038045298439)
XLA Ops:
  7.2 1.1 reshape.186
  8.3 1.0 reshape.187
  9.2 1.0 copy.132
  11.2 7.3 %all-to-all-start.1 = ((bf16[8,64,384]{2,1,0:T(8,128)(2,1)}), bf16[8,64,384]{2,1,0:T(8,128)(2,1)S(1)}, u32[]{:S(2)}, u32[]{:S(2)}) async-start(bf16[8,64,384]{2,1,0:T(8,128)(2,1)} %copy.105), calls=%async_computation.1 | async-start | bytes 786432 | tf_op jit(solution)/shard_map/all_to_all | solution.py:642
  18.5 1.8 copy.130
  21.0 9.2 %all-to-all-done.1 = bf16[8,64,384]{2,1,0:T(8,128)(2,1)S(1)} async-done(((bf16[8,64,384]{2,1,0:T(8,128)(2,1)}), bf16[8,64,384]{2,1,0:T(8,128)(2,1)S(1)}, u32[]{:S(2)}, u32[]{:S(2)}) %all-to-all-start.1) | async-done | bytes 393248 | tf_op jit(solution)/shard_map/all_to_all | solution.py:642
  30.1 1.0 copy.106
  31.4 2.5 copy.104
  33.8 3.6 all-to-all-start
  39.0 52.0 %exchange.2 = f32[32,8,128]{2,1,0:T(8,128)} custom-call(f32[32,8,128]{2,1,0:T(8,128)} %broadcast_in_dim.15.x_ref), custom_call_target="tpu_custom_call" | custom-call | bytes 25000000 | tf_op jit(solution)/shard_map/exchange/pallas_call | solution.py:613
  92.3 1.0 fusion.6.x_ref
  93.3 48.6 %gather_ctx.3 = bf16[1024,2048]{1,0:T(8,128)(2,1)} custom-call(bf16[128,2048]{1,0:T(8,128)(2,1)} %fusion.6.x_ref), custom_call_target="tpu_custom_call" | custom-call | bytes 150000000 | tf_op jit(solution)/shard_map/gather_ctx/pallas_call | solution.py:432
  141.9 1.3 copy-done.18
  144.8 1.6 copy.107
  146.4 1.1 copy-done.21
  147.5 5.1 fusion.26.qkv_ref
  153.5 1.9 fusion.15
  156.3 8.2 %attend.1 = (bf16[1024,256]{1,0:T(8,128)(2,1)S(1)}, bf16[1024,128]{1,0:T(8,128)(2,1)S(1)}, bf16[1024,256]{1,0:T(8,128)(2,1)S(1)}, f32[1024,4]{1,0:T(8,128)S(1)}) custom-call(f32[1024,384]{1,0:T(8,128)S(1)} %fusion.26.qkv_ref, f32[1024,128]{1,0:T(8,128)S(1)} %get-tuple-element.78.cos_ref, f32[1024,128]{1,0:T(8,128)S(1)} %get-tuple-element.79.sin_ref, ...), custom_call_target="tpu_custom_call" | custom-call | tf_op jit(solution)/shard_map/attend/pallas_call | solution.py:757
  167.5 2.6 convolution_convert_fusion.3.x_ref
  170.2 47.0 %scatter_ctx.3 = f32[128,2048]{1,0:T(8,128)S(1)} custom-call(bf16[1024,2048]{1,0:T(8,128)(2,1)S(1)} %convolution_convert_fusion.3.x_ref), custom_call_target="tpu_custom_call" | custom-call | bytes 150000000 | tf_op jit(solution)/shard_map/scatter_ctx/pallas_call | solution.py:548
  217.6 1.1 multiply_convert_fusion.3
  218.7 1.3 copy.110
  220.9 2.0 copy.112.x_ref
  222.9 57.7 %gather_ctx.4 = bf16[1024,2048]{1,0:T(8,128)(2,1)} custom-call(bf16[128,2048]{1,0:T(8,128)(2,1)} %copy.112.x_ref), custom_call_target="tpu_custom_call" | custom-call | bytes 150000000 | tf_op jit(solution)/shard_map/gather_ctx/pallas_call | solution.py:432
  280.7 12.9 %fusion.27 = f32[1024,2048]{1,0:T(8,128)S(1)} fusion(bf16[1024,2048]{1,0:T(8,128)(2,1)} %gather_ctx.4, bf16[2048,2048]{1,0:T(8,128)(2,1)} %all-gather.9.cloned.1.call-done), kind=kOutput, calls=%fused_computation.81 | convolution fusion | flops 8589934592 | bytes 20971520 | tf_op jit(solution)/shard_map/dot_general | solution.py:58
  293.6 3.2 copy-done.17
  296.8 2.7 fusion
  299.5 9.3 %convolution_convert_fusion.5 = bf16[1024,2048]{1,0:T(8,128)(2,1)} fusion(bf16[1024,1024]{1,0:T(8,128)(2,1)} %fusion, bf16[1024,2048]{1,0:T(8,128)(2,1)} %all-gather.11.cloned.1.call-done), kind=kOutput, calls=%fused_computation.11 | convolution fusion | flops 4297064448 | bytes 10485760 | tf_op jit(solution)/shard_map/dot_general | solution.py:58
  308.9 9.0 %all-gather.13.cloned.1.call-done = bf16[1024,2048]{1,0:T(8,128)(2,1)} async-done(((bf16[128,2048]{1,0:T(8,128)(2,1)}), bf16[1024,2048]{1,0:T(8,128)(2,1)}) %all-gather.13.cloned.1.call-update) | async-done | bytes 4194320 | tf_op jit(solution)/shard_map/all_gather | solution.py:844
  317.8 9.4 %convolution_convert_fusion.4 = bf16[1024,2048]{1,0:T(8,128)(2,1)} fusion(bf16[1024,1024]{1,0:T(8,128)(2,1)} %fusion, bf16[1024,2048]{1,0:T(8,128)(2,1)} %all-gather.13.cloned.1.call-done), kind=kOutput, calls=%fused_computation.10 | convolution fusion | flops 4297064448 | bytes 10485760 | tf_op jit(solution)/shard_map/dot_general | solution.py:68
  327.2 12.1 %multiply_convert_fusion.1 = (bf16[1024,1024]{1,0:T(8,128)(2,1)S(1)}, bf16[1024,1024]{1,0:T(8,128)(2,1)S(1)}) fusion(f32[1024,2048]{1,0:T(8,128)} %copy-done.17, bf16[1024,2048]{1,0:T(8,128)(2,1)} %all-gather.13.cloned.1.call-done, bf16[1024,2048]{1,0:T(8,128)(2,1)} %all-gather.11.cloned.1.call-done), kind=kOutput, calls=%fused_computation.5 | convolution fusion | flops 4308598784 | bytes 20971520 | tf_op jit(solution)/shard_map/dot_general | solution.py:62
  339.4 1.3 copy-done.28
  341.3 11.6 %convolution_convert_fusion = bf16[2048,2048]{1,0:T(8,128)(2,1)} fusion(bf16[1024,2048]{1,0:T(8,128)(2,1)S(1)} %copy-done.20, bf16[1024,1024]{1,0:T(8,128)(2,1)S(1)} %get-tuple-element.66, bf16[1024,1024]{1,0:T(8,128)(2,1)S(1)} %get-tuple-element.65), kind=kOutput, calls=%fused_computation | convolution fusion | flops 8602517504 | bytes 16777216 | tf_op jit(solution)/shard_map/dot_general | solution.py:68
  353.0 14.4 %convolution_convert_fusion.2.x_ref = bf16[1024,2048]{1,0:T(8,128)(2,1)} fusion(bf16[2048,2048]{1,0:T(8,128)(2,1)} %all-gather.9.cloned.1.call-done, bf16[1024,1024]{1,0:T(8,128)(2,1)} %copy-done.29, bf16[1024,1024]{1,0:T(8,128)(2,1)} %copy-done.28), kind=kOutput, calls=%fused_computation.8 | convolution fusion | flops 8600420352 | bytes 16777216 | tf_op jit(solution)/shard_map/dot_general | solution.py:62
  367.5 2.2 copy-done.1
  369.7 46.7 %scatter_ctx.4 = f32[128,2048]{1,0:T(8,128)S(1)} custom-call(bf16[1024,2048]{1,0:T(8,128)(2,1)S(1)} %copy-done.1), custom_call_target="tpu_custom_call" | custom-call | bytes 150000000 | tf_op jit(solution)/shard_map/scatter_ctx/pallas_call | solution.py:548
  416.3 1.3 copy.115
  417.6 2.4 copy.116
  420.0 2.6 copy.117
  422.6 1.6 multiply_reduce_fusion
  424.2 2.6 multiply_convert_fusion.2.x_ref
  426.8 47.2 %gather_ctx.5 = bf16[1024,2048]{1,0:T(8,128)(2,1)} custom-call(bf16[128,2048]{1,0:T(8,128)(2,1)} %multiply_convert_fusion.2.x_ref), custom_call_target="tpu_custom_call" | custom-call | bytes 150000000 | tf_op jit(solution)/shard_map/gather_ctx/pallas_call | solution.py:432
  474.0 4.5 convolution_convert_fusion.7
  478.5 4.3 convolution_convert_fusion.8.do_ref
  484.1 1.0 copy-done.8
  485.1 0.9 copy-done.10
  486.1 13.3 %attend_back.1 = bf16[1024,384]{1,0:T(8,128)(2,1)S(1)} custom-call(bf16[1024,256]{1,0:T(8,128)(2,1)S(1)} %copy-done.5, bf16[1024,128]{1,0:T(8,128)(2,1)S(1)} %copy-done.10, bf16[1024,256]{1,0:T(8,128)(2,1)S(1)} %copy-done.8, f32[1024,4]{1,0:T(8,128)S(1)} %copy-done.7, f32[1024,128]{1,0:T(8,128)S(1)} %get-tuple-element.78.cos_ref, ...), custom_call_target="tpu_custom_call" | custom-call | tf_op jit(solution)/shard_map/attend_back/pallas_call | solution.py:774
  499.4 4.7 convolution_convert_fusion.6
  504.1 1.3 copy.119
  505.5 4.3 convolution_convert_fusion.1.x_ref
  510.4 4.6 all-to-all-start.3
  515.1 1.9 convert_element_type.186
  517.0 37.9 %reduce-scatter.14.cloned.1.call-done = bf16[256,2048]{1,0:T(8,128)(2,1)} async-done(((bf16[1024,2048]{1,0:T(8,128)(2,1)}), bf16[256,2048]{1,0:T(8,128)(2,1)}) %reduce-scatter.14.cloned.1.call-update) | async-done | bytes 1048592 | tf_op jit(solution)/shard_map/reduce_scatter | solution.py:880
  554.9 2.8 convert_element_type.193
  557.7 2.2 copy-done
  559.9 56.8 %scatter_ctx.5 = f32[128,2048]{1,0:T(8,128)S(1)} custom-call(bf16[1024,2048]{1,0:T(8,128)(2,1)S(1)} %copy-done), custom_call_target="tpu_custom_call" | custom-call | bytes 150000000 | tf_op jit(solution)/shard_map/scatter_ctx/pallas_call | solution.py:548
  616.8 1.4 fusion.12
  618.3 64.9 %reduce-scatter.6.cloned.1.call-done = bf16[128,2048]{1,0:T(8,128)(2,1)} async-done(((bf16[1024,2048]{1,0:T(8,128)(2,1)}), bf16[128,2048]{1,0:T(8,128)(2,1)}) %reduce-scatter.6.cloned.1.call-update) | async-done | bytes 524304 | tf_op jit(solution)/shard_map/reduce_scatter | solution.py:863
  683.2 3.0 fusion.11
  686.3 4.2 all-to-all-start.2
  691.2 16.5 %exchange.3 = f32[32,8,128]{2,1,0:T(8,128)} custom-call(f32[32,8,128]{2,1,0:T(8,128)} %pad.10.x_ref), custom_call_target="tpu_custom_call" | custom-call | bytes 25000000 | tf_op jit(solution)/shard_map/exchange/pallas_call | solution.py:613
  709.2 2.0 convert_bitcast_fusion
  711.2 1.5 copy.129
  712.6 1.5 copy.128
  (121 shorter events, 19.8 us)
Async XLA Ops:
  7.2 13.2 %copy-start.23 = (bf16[64,8192]{1,0:T(8,128)(2,1)S(1)}, bf16[64,8192]{1,0:T(8,128)(2,1)}, u32[]{:S(2)}) copy-start(bf16[64,8192]{1,0:T(8,128)(2,1)} %param.22) | copy-start | bytes 3145732
  11.2 19.0 %all-to-all-start.1 = ((bf16[8,64,384]{2,1,0:T(8,128)(2,1)}), bf16[8,64,384]{2,1,0:T(8,128)(2,1)S(1)}, u32[]{:S(2)}, u32[]{:S(2)}) async-start(bf16[8,64,384]{2,1,0:T(8,128)(2,1)} %copy.105), calls=%async_computation.1 | async-start | bytes 786432 | tf_op jit(solution)/shard_map/all_to_all | solution.py:642
  18.5 126.3 %all-gather.15.cloned.1.call-start = ((), (), s32[]{:S(2)}) async-start(), calls=%async_computation.18 | async-start | bytes 1966080 | tf_op jit(solution)/shard_map/all_gather | solution.py:646
  31.3 6.9 copy-start.25
  31.4 6.9 copy-start.26
  31.4 60.7 %copy-start.15 = (bf16[1,128,2048]{2,1,0:T(8,128)(2,1)S(1)}, bf16[1,128,2048]{2,1,0:T(8,128)(2,1)}, u32[]{:S(2)}) copy-start(bf16[1,128,2048]{2,1,0:T(8,128)(2,1)} %param.12) | copy-start | bytes 1572868
  33.8 108.0 %all-to-all-start = ((bf16[8,64,2048]{2,1,0:T(8,128)(2,1)}), bf16[8,64,2048]{2,1,0:T(8,128)(2,1)S(1)}, u32[]{:S(2)}, u32[]{:S(2)}) async-start(bf16[8,64,2048]{2,1,0:T(8,128)(2,1)} %copy.104), calls=%async_computation | async-start | bytes 4194304 | tf_op jit(solution)/shard_map/all_to_all | solution.py:642
  37.5 130.1 %all-gather.7.cloned.1.call-start = ((), (), s32[]{:S(2)}) async-start(), calls=%async_computation.9 | async-start | bytes 1310720 | tf_op jit(solution)/shard_map/all_gather | solution.py:827
  38.2 242.4 %all-gather.9.cloned.1.call-start = ((), (), s32[]{:S(2)}) async-start(), calls=%async_computation.10 | async-start | bytes 10485760 | tf_op jit(solution)/shard_map/all_gather | solution.py:836
  93.3 50.6 %copy-start.19 = (bf16[1,128,2048]{2,1,0:T(8,128)(2,1)S(1)}, bf16[1,128,2048]{2,1,0:T(8,128)(2,1)}, u32[]{:S(2)}) copy-start(bf16[1,128,2048]{2,1,0:T(8,128)(2,1)} %param.14) | copy-start | bytes 1572868
  141.9 1.3 copy-start.18
  143.2 156.3 %all-gather.11.cloned.1.call-start = ((), (), s32[]{:S(2)}) async-start(), calls=%async_computation.11 | async-start | bytes 5242880 | tf_op jit(solution)/shard_map/all_gather | solution.py:837
  143.8 174.0 %all-gather.13.cloned.1.call-start = ((), (), s32[]{:S(2)}) async-start(), calls=%async_computation.12 | async-start | bytes 4718592 | tf_op jit(solution)/shard_map/all_gather | solution.py:844
  146.4 1.1 copy-start.21
  147.5 5.4 copy-start.27
  152.6 346.8 %reduce-scatter.8.cloned.1.call-start = ((), (), s32[]{:S(2)}) async-start(), calls=%async_computation.14 | async-start | bytes 10485760 | tf_op jit(solution)/shard_map/reduce_scatter | solution.py:879
  164.5 0.8 copy-start.2
  165.2 0.8 copy-start.4
  166.0 0.8 copy-start.6
  166.8 0.7 copy-start.9
  170.2 47.1 %copy-start.16 = (bf16[1,128,2048]{2,1,0:T(8,128)(2,1)S(1)}, bf16[1,128,2048]{2,1,0:T(8,128)(2,1)}, u32[]{:S(2)}) copy-start(bf16[1,128,2048]{2,1,0:T(8,128)(2,1)} %param.12) | copy-start | bytes 1572868
  217.5 63.1 %copy-start.11 = (f32[128,2048]{1,0:T(8,128)}, f32[128,2048]{1,0:T(8,128)S(1)}, u32[]{:S(2)}) copy-start(f32[128,2048]{1,0:T(8,128)S(1)} %get-tuple-element.64) | copy-start | bytes 3145732
  293.6 3.2 copy-start.17
  327.2 14.1 %copy-start.20 = (bf16[1024,2048]{1,0:T(8,128)(2,1)S(1)}, bf16[1024,2048]{1,0:T(8,128)(2,1)}, u32[]{:S(2)}) copy-start(bf16[1024,2048]{1,0:T(8,128)(2,1)} %gather_ctx.4) | copy-start | bytes 12582916
  339.3 1.3 copy-start.28
  339.3 2.0 copy-start.29
  367.4 147.7 %reduce-scatter.12.cloned.1.call-start = ((), (), s32[]{:S(2)}) async-start(), calls=%async_computation.16 | async-start | bytes 1310720 | tf_op jit(solution)/shard_map/reduce_scatter | solution.py:891
  367.5 2.2 copy-start.1
  417.6 5.0 copy-start.12
  424.2 49.8 %copy-start.3 = (bf16[1024,256]{1,0:T(8,128)(2,1)S(1)}, bf16[1024,256]{1,0:T(8,128)(2,1)}, u32[]{:S(2)}) copy-start(bf16[1024,256]{1,0:T(8,128)(2,1)} %copy-done.2) | copy-start | bytes 1572868
  474.0 4.5 copy-start.24
  482.8 1.2 copy-start.5
  482.8 1.2 copy-start.7
  482.8 72.1 %reduce-scatter.14.cloned.1.call-start = ((), (), s32[]{:S(2)}) async-start(), calls=%async_computation.17 | async-start | bytes 5242880 | tf_op jit(solution)/shard_map/reduce_scatter | solution.py:880
  483.6 133.2 %reduce-scatter.10.cloned.1.call-start = ((), (), s32[]{:S(2)}) async-start(), calls=%async_computation.15 | async-start | bytes 1966080 | tf_op jit(solution)/shard_map/reduce_scatter | solution.py:902
  484.1 1.0 copy-start.8
  485.1 0.9 copy-start.10
  499.4 6.1 copy-start.22
  509.8 173.4 %reduce-scatter.6.cloned.1.call-start = ((), (), s32[]{:S(2)}) async-start(), calls=%async_computation.13 | async-start | bytes 4718592 | tf_op jit(solution)/shard_map/reduce_scatter | solution.py:863
  510.4 175.8 %all-to-all-start.3 = ((bf16[8,64,2048]{2,1,0:T(8,128)(2,1)}), bf16[8,64,2048]{2,1,0:T(8,128)(2,1)}, u32[]{:S(2)}, u32[]{:S(2)}) async-start(bf16[8,64,2048]{2,1,0:T(8,128)(2,1)} %bitcast.33), calls=%async_computation.7 | async-start | bytes 4194304 | tf_op jit(solution)/shard_map/all_to_all | solution.py:642
  557.7 2.2 copy-start
  559.9 123.3 %copy-start.13 = (f32[128,2048]{1,0:T(8,128)S(1)}, f32[128,2048]{1,0:T(8,128)}, u32[]{:S(2)}) copy-start(f32[128,2048]{1,0:T(8,128)} %copy-done.11) | copy-start | bytes 3145732
  559.9 123.3 %copy-start.14 = (f32[128,2048]{1,0:T(8,128)S(1)}, f32[128,2048]{1,0:T(8,128)}, u32[]{:S(2)}) copy-start(f32[128,2048]{1,0:T(8,128)} %copy.117) | copy-start | bytes 3145732
  686.3 27.8 %all-to-all-start.2 = ((bf16[8,64,384]{2,1,0:T(8,128)(2,1)}), bf16[8,64,384]{2,1,0:T(8,128)(2,1)S(1)}, u32[]{:S(2)}, u32[]{:S(2)}) async-start(bf16[8,64,384]{2,1,0:T(8,128)(2,1)} %bitcast.28), calls=%async_computation.5 | async-start | bytes 786432 | tf_op jit(solution)/shard_map/all_to_all | solution.py:642
Sparse Core Ops, SparseCore 0:
  31.3 19.0 all-gather.14
  51.9 16.6 all-gather.6
  143.3 57.0 all-gather.8
  201.8 34.4 all-gather.10
  238.9 78.9 all-gather.12
  367.6 69.9 reduce-scatter.7
  483.0 24.7 reduce-scatter.11
  510.3 44.5 reduce-scatter.13
  558.0 28.0 reduce-scatter.9
  589.6 93.5 reduce-scatter.5

commit v5 on v4

--- a/solution.py
+++ b/solution.py
@@ -22,6 +22,7 @@
 MESH = pl.DeviceIdType.MESH
 PAIR = 2
 CHUNKS = 2
+ANYWHERE = pl.BlockSpec(memory_space=pl.ANY)
 LINK_COST = pl.CostEstimate(flops=0, bytes_accessed=150_000_000, transcendentals=0)
 
 
@@ -350,6 +351,10 @@
     return blocks.reshape((-1,) + blocks.shape[2:])
 
 
+def in_vmem(count):
+    return [pl.BlockSpec(memory_space=pltpu.VMEM)] * count
+
+
 def greet_line(barrier, ctx_at, line_at, line_size):
     other = ctx_at + 1 - 2 * (ctx_at % PAIR)
     pl.semaphore_signal(barrier, inc=1, device_id={"ctx": other}, device_id_type=MESH)
@@ -367,25 +372,35 @@
     pl.semaphore_wait(barrier, neighbours)
 
 
-def gather_kernel(line_size, x_ref, out_ref, send_sem, recv_sem, own_sem):
+def greet_all(barrier, me, count, fsdp_size):
+    def greet(k, unused):
+        target = (me + k) % count
+        pl.semaphore_signal(
+            barrier, inc=1, device_id=(target // fsdp_size, target % fsdp_size), device_id_type=MESH
+        )
+        return unused
+
+    lax.fori_loop(1, count, greet, 0)
+    pl.semaphore_wait(barrier, count - 1)
+
+
+def gather_phase(line_size, x_ref, out_ref, send_sem, recv_sem, own_sem):
     me = lax.axis_index("ctx")
     line_at, pair_at = me // PAIR, me % PAIR
     rows = x_ref.shape[0]
     step = rows // CHUNKS
-    greet_line(pltpu.get_barrier_semaphore(), me, line_at, line_size)
 
     def piece(block, part):
         return out_ref.at[pl.ds(pl.multiple_of(block * rows + part * step, step), step), :]
 
     def copy(block, part, way, own):
-        target = (me + 1 - 2 * pair_at, me + PAIR, me - PAIR)[way]
         slot = block * CHUNKS + part
         return pltpu.make_async_remote_copy(
             src_ref=x_ref.at[pl.ds(part * step, step), :] if own else piece(block, part),
             dst_ref=piece(block, part),
             send_sem=send_sem.at[way, slot],
             recv_sem=recv_sem.at[slot],
-            device_id={"ctx": target},
+            device_id={"ctx": (me + 1 - 2 * pair_at, me + PAIR, me - PAIR)[way]},
             device_id_type=MESH,
         )
 
@@ -396,9 +411,10 @@
             pl.when(downward)(lambda: act(copy(block, part, 2, own)))
         act(copy(block, part, 0, own))
 
-    def visit(act, arrive):
-        for part in range(CHUNKS):
-            pass_on(me, part, line_at < line_size - 1, line_at > 0, True, act)
+    def own_part(part, act):
+        pass_on(me, part, line_at < line_size - 1, line_at > 0, True, act)
+
+    def others(act, arrive):
         for distance in range(1, line_size):
             for part in range(CHUNKS):
 
@@ -414,56 +430,50 @@
                     arrive(block, part)
                     pass_on(block, part, None, line_at > 0, False, act)
 
-    keep = pltpu.make_async_copy(
-        x_ref, out_ref.at[pl.ds(pl.multiple_of(me * rows, rows), rows), :], own_sem
-    )
-    keep.start()
-    visit(lambda c: c.start(), lambda block, part: copy(block, part, 0, False).wait_recv())
-    for place in range(line_size):
+    def start_own(part):
+        own_part(part, lambda c: c.start())
+
+    def finish():
+        keep = pltpu.make_async_copy(
+            x_ref, out_ref.at[pl.ds(pl.multiple_of(me * rows, rows), rows), :], own_sem
+        )
+        keep.start()
+        others(lambda c: c.start(), lambda block, part: copy(block, part, 0, False).wait_recv())
+        for place in range(line_size):
+            for part in range(CHUNKS):
+                copy(place * PAIR + 1 - pair_at, part, 0, False).wait_recv()
         for part in range(CHUNKS):
-            copy(place * PAIR + 1 - pair_at, part, 0, False).wait_recv()
-    visit(lambda c: c.wait_send(), lambda block, part: None)
-    keep.wait()
-
-
-def gather_ctx(local):
-    ctx_size = lax.axis_size("ctx")
-    rows, width = local.shape
-    return pl.pallas_call(
-        functools.partial(gather_kernel, ctx_size // PAIR),
-        out_shape=jax.ShapeDtypeStruct((ctx_size * rows, width), local.dtype),
-        in_specs=[pl.BlockSpec(memory_space=pl.ANY)],
-        out_specs=pl.BlockSpec(memory_space=pl.ANY),
-        scratch_shapes=[
-            pltpu.SemaphoreType.DMA((3, ctx_size * CHUNKS)),
-            pltpu.SemaphoreType.DMA((ctx_size * CHUNKS,)),
-            pltpu.SemaphoreType.DMA,
-        ],
-        compiler_params=pltpu.CompilerParams(collective_id=0, has_side_effects=True),
-        cost_estimate=LINK_COST,
-        name="gather_ctx",
-    )(local)
-
-
-def scatter_kernel(line_size, x_ref, out_ref, near, below, above, send_sem, near_sem, line_sem, line_send):
+            own_part(part, lambda c: c.wait_send())
+        others(lambda c: c.wait_send(), lambda block, part: None)
+        keep.wait()
+
+    return start_own, finish
+
+
+def gather_scratch(ctx_size):
+    return [
+        pltpu.SemaphoreType.DMA((3, ctx_size * CHUNKS)),
+        pltpu.SemaphoreType.DMA((ctx_size * CHUNKS,)),
+        pltpu.SemaphoreType.DMA,
+    ]
+
+
+def scatter_phase(line_size, x_ref, sum_ref, near, below, above, near_send, near_sem, line_send, line_sem, emit):
     me = lax.axis_index("ctx")
     line_at, pair_at = me // PAIR, me % PAIR
-    rows = out_ref.shape[0]
+    rows = sum_ref.shape[0]
     step = rows // CHUNKS
-    greet_line(pltpu.get_barrier_semaphore(), me, line_at, line_size)
-    half = line_size // 2
-    low = line_at // half
     last = line_size - 1
-    order = [k + (last - 2 * k) * (1 - low) for k in range(half)]
-    if line_size == 4:
-        order += [line_at + 1 - 2 * (line_at % 2), line_at]
+    low = line_at // (line_size // 2)
+    order = [k + (last - 2 * k) * (1 - low) for k in range(line_size // 2)]
+    order += [line_at + 1 - 2 * (line_at % 2), line_at]
 
     def near_copy(place, part):
         start = (place * PAIR + 1 - pair_at) * rows + part * step
         return pltpu.make_async_remote_copy(
             src_ref=x_ref.at[pl.ds(pl.multiple_of(start, step), step), :],
             dst_ref=near.at[place, pl.ds(part * step, step), :],
-            send_sem=send_sem.at[place, part],
+            send_sem=near_send.at[place, part],
             recv_sem=near_sem.at[place, part],
             device_id={"ctx": me + 1 - 2 * pair_at},
             device_id_type=MESH,
@@ -480,6 +490,10 @@
             device_id_type=MESH,
         )
 
+    def mine(place, part):
+        start = (place * PAIR + pair_at) * rows + part * step
+        return x_ref[pl.ds(pl.multiple_of(start, step), step), :].astype(jnp.float32)
+
     for place in order:
         for part in range(CHUNKS):
             near_copy(place, part).start()
@@ -487,7 +501,6 @@
     for place in order[:-1]:
         for part in range(CHUNKS):
             part_rows = pl.ds(part * step, step)
-            mine = x_ref.at[pl.ds(pl.multiple_of((place * PAIR + pair_at) * rows + part * step, step), step), :]
             near_copy(place, part).wait_recv()
 
             def send(up, waits, arrived):
@@ -495,7 +508,7 @@
                 def _():
                     line_copy(place, part, up).wait_recv()
                     near[place, part_rows, :] = (
-                        mine[...].astype(jnp.float32)
+                        mine(place, part)
                         + near[place, part_rows, :].astype(jnp.float32)
                         + arrived[place, part_rows, :].astype(jnp.float32)
                     ).astype(near.dtype)
@@ -503,62 +516,299 @@
                 @pl.when(jnp.logical_not(waits))
                 def _():
                     near[place, part_rows, :] = (
-                        mine[...].astype(jnp.float32) + near[place, part_rows, :].astype(jnp.float32)
+                        mine(place, part) + near[place, part_rows, :].astype(jnp.float32)
                     ).astype(near.dtype)
 
                 line_copy(place, part, up).start()
 
-            @pl.when(place > line_at)
-            def _():
-                send(True, line_at > 0, below)
-
-            @pl.when(place < line_at)
-            def _():
-                send(False, line_at < last, above)
+            pl.when(place > line_at)(lambda: send(True, line_at > 0, below))
+            pl.when(place < line_at)(lambda: send(False, line_at < last, above))
 
     for part in range(CHUNKS):
         part_rows = pl.ds(part * step, step)
-        mine = x_ref.at[pl.ds(pl.multiple_of(me * rows + part * step, step), step), :]
         near_copy(line_at, part).wait_recv()
-        out_ref[part_rows, :] = mine[...].astype(jnp.float32) + near[line_at, part_rows, :].astype(jnp.float32)
+        sum_ref[part_rows, :] = mine(line_at, part) + near[line_at, part_rows, :].astype(jnp.float32)
 
         @pl.when(line_at > 0)
         def _():
             line_copy(line_at, part, True).wait_recv()
-            out_ref[part_rows, :] += below[line_at, part_rows, :].astype(jnp.float32)
+            sum_ref[part_rows, :] += below[line_at, part_rows, :].astype(jnp.float32)
 
         @pl.when(line_at < last)
         def _():
             line_copy(line_at, part, False).wait_recv()
-            out_ref[part_rows, :] += above[line_at, part_rows, :].astype(jnp.float32)
-
-    for place in order:
-        for part in range(CHUNKS):
-            near_copy(place, part).wait_send()
-    for place in order[:-1]:
-        for part in range(CHUNKS):
-            line_copy(place, part, True).wait_send()
+            sum_ref[part_rows, :] += above[line_at, part_rows, :].astype(jnp.float32)
+
+        emit(part, slice(part * step, (part + 1) * step))
+
+    def finish():
+        for place in order:
+            for part in range(CHUNKS):
+                near_copy(place, part).wait_send()
+        for place in order[:-1]:
+            for part in range(CHUNKS):
+                line_copy(place, part, True).wait_send()
+
+    return finish
+
+
+def scatter_scratch(ctx_size, rows, width):
+    line_size = ctx_size // PAIR
+    held = pltpu.VMEM((line_size, rows, width), jnp.bfloat16)
+    return [
+        held,
+        held,
+        held,
+        pltpu.SemaphoreType.DMA((line_size, CHUNKS)),
+        pltpu.SemaphoreType.DMA((line_size, CHUNKS)),
+        pltpu.SemaphoreType.DMA((line_size, CHUNKS)),
+        pltpu.SemaphoreType.DMA((2, line_size, CHUNKS)),
+    ]
+
+
+def swap_lanes(values, outer, inner):
+    tile = 128
+    half = tile // 2
+    low = lax.broadcasted_iota(jnp.int32, (values.shape[0], tile), 1) < half
+    placed = [None] * (outer * inner // 2)
+    for first in range(0, outer, 2):
+        for second in range(0, inner, 2):
+            at = (first * inner + second) // 2
+            one = values[:, at * tile : (at + 1) * tile]
+            at += inner // 2
+            two = values[:, at * tile : (at + 1) * tile]
+            at = (second * outer + first) // 2
+            placed[at] = jnp.where(low, one, pltpu.roll(two, half, 1))
+            placed[at + outer // 2] = jnp.where(low, pltpu.roll(one, half, 1), two)
+    return jnp.concatenate(placed, axis=1)
+
+
+def start_kernel(
+    ctx_size, fsdp_size, tokens_ref, tile_ref, parts_ref, out_ref, gains_ref, weight_ref,
+    tiles, normed, tile_send, tile_recv, far_send, far_recv, near_send, near_recv, kept, *sems
+):
+    me_ctx, me_fsdp = lax.axis_index("ctx"), lax.axis_index("fsdp")
+    count = ctx_size * fsdp_size
+    me = me_ctx * fsdp_size + me_fsdp
+    greet_all(pltpu.get_barrier_semaphore(), me, count, fsdp_size)
+
+    def tile_copy(k, source):
+        target = (me + k) % count
+        return pltpu.make_async_remote_copy(
+            src_ref=tile_ref,
+            dst_ref=tiles.at[source],
+            send_sem=tile_send.at[k],
+            recv_sem=tile_recv.at[k],
+            device_id=(target // fsdp_size, target % fsdp_size),
+            device_id_type=MESH,
+        )
+
+    def start_tile(k, unused):
+        tile_copy(k, me).start()
+        return unused
+
+    def finish_tile(k, unused):
+        tile_copy(k, (me + count - k) % count).wait_recv()
+        return unused
+
+    lax.fori_loop(1, count, start_tile, 0)
+    tiles[pl.ds(me, 1)] = tile_ref[...][None]
+
+    def far_copy(k, source):
+        target = (me_ctx + k) % ctx_size
+        return pltpu.make_async_remote_copy(
+            src_ref=parts_ref.at[target],
+            dst_ref=weight_ref.at[source * fsdp_size + me_fsdp],
+            send_sem=far_send.at[k],
+            recv_sem=far_recv.at[k],
+            device_id={"ctx": target},
+            device_id_type=MESH,
+        )
+
+    def near_copy(k, j, fsdp_source):
+        block = (me_ctx + ctx_size - k) % ctx_size * fsdp_size + fsdp_source
+        return pltpu.make_async_remote_copy(
+            src_ref=parts_ref.at[me_ctx] if k == 0 else weight_ref.at[block],
+            dst_ref=weight_ref.at[block],
+            send_sem=near_send.at[k, j],
+            recv_sem=near_recv.at[k, j],
+            device_id={"fsdp": (me_fsdp + j) % fsdp_size},
+            device_id_type=MESH,
+        )
+
+    for k in range(1, ctx_size):
+        far_copy(k, me_ctx).start()
+    for j in range(1, fsdp_size):
+        near_copy(0, j, me_fsdp).start()
+    keep = pltpu.make_async_copy(parts_ref.at[me_ctx], weight_ref.at[me], kept)
+    keep.start()
+
+    rows, model = tokens_ref.shape
+    lax.fori_loop(1, count, finish_tile, 0)
+    held = model // count
+    for pair in range(count // 2):
+        cols = slice(pair * 2 * held, (pair + 1) * 2 * held)
+        gains_ref[:, cols] = tiles[2 * pair] + tiles[2 * pair + 1]
+    start_own, finish_gather = gather_phase(ctx_size // PAIR, normed, out_ref, *sems)
+    step = rows // CHUNKS
+    for part in range(CHUNKS):
+        part_rows = slice(part * step, (part + 1) * step)
+        values = tokens_ref[part_rows, :].astype(jnp.float32)
+        scale = lax.rsqrt(jnp.mean(values * values, axis=-1, keepdims=True) + EPSILON)
+        normed[part_rows, :] = (values * scale * gains_ref[0:1, :]).astype(normed.dtype)
+        start_own(part)
+    for k in range(1, ctx_size):
+        far_copy(k, (me_ctx + ctx_size - k) % ctx_size).wait_recv()
+        for j in range(1, fsdp_size):
+            near_copy(k, j, me_fsdp).start()
+    finish_gather()
+    for k in range(ctx_size):
+        for j in range(1, fsdp_size):
+            near_copy(k, j, (me_fsdp + fsdp_size - j) % fsdp_size).wait_recv()
+    for k in range(ctx_size):
+        for j in range(1, fsdp_size):
+            near_copy(k, j, me_fsdp).wait_send()
+    for k in range(1, ctx_size):
+        far_copy(k, me_ctx).wait_send()
+
+    def sent_tile(k, unused):
+        tile_copy(k, me).wait_send()
+        return unused
+
+    lax.fori_loop(1, count, sent_tile, 0)
+    keep.wait()
+
+
+def start_layer(tokens, tile, parts):
+    ctx_size, fsdp_size = lax.axis_size("ctx"), lax.axis_size("fsdp")
+    count = ctx_size * fsdp_size
+    rows, model = tokens.shape
+    dma = pltpu.SemaphoreType.DMA
+    normed1, gains, weight = pl.pallas_call(
+        functools.partial(start_kernel, ctx_size, fsdp_size),
+        out_shape=(
+            jax.ShapeDtypeStruct((ctx_size * rows, model), jnp.bfloat16),
+            jax.ShapeDtypeStruct((8, model), jnp.float32),
+            jax.ShapeDtypeStruct((count,) + parts.shape[1:], parts.dtype),
+        ),
+        in_specs=in_vmem(3),
+        out_specs=(ANYWHERE, in_vmem(1)[0], ANYWHERE),
+        scratch_shapes=[
+            pltpu.VMEM((count, 8, 128), jnp.float32),
+            pltpu.VMEM((rows, model), jnp.bfloat16),
+            dma((count,)),
+            dma((count,)),
+            dma((ctx_size,)),
+            dma((ctx_size,)),
+            dma((ctx_size, fsdp_size)),
+            dma((ctx_size, fsdp_size)),
+            dma,
+        ]
+        + gather_scratch(ctx_size),
+        compiler_params=pltpu.CompilerParams(
+            collective_id=0, has_side_effects=True, vmem_limit_bytes=32 * 2**20
+        ),
+        cost_estimate=LINK_COST,
+        name="start_layer",
+    )(tokens, tile, parts)
+    return normed1, gains, rows_of(weight)
+
+
+def mlp_forward_kernel(
+    ctx_size, fsdp_size, x_ref, tokens_ref, gains_ref, hidden_ref, out_ref, sums, normed, *sems
+):
+    line_size = ctx_size // PAIR
+    me = lax.axis_index("ctx")
+    greet_line(pltpu.get_barrier_semaphore(), me, me // PAIR, line_size)
+    start_own, finish_gather = gather_phase(line_size, normed, out_ref, *sems[7:])
+
+    def emit(part, rows):
+        hidden = tokens_ref[rows, :].astype(jnp.float32) + RESIDUAL_MULT * sums[rows, :]
+        hidden_ref[rows, :] = hidden
+        scale = lax.rsqrt(jnp.mean(hidden * hidden, axis=-1, keepdims=True) + EPSILON)
+        scaled = hidden * scale * gains_ref[1:2, :]
+        normed[rows, :] = swap_lanes(scaled, ctx_size, fsdp_size).astype(normed.dtype)
+        start_own(part)
+
+    finish_scatter = scatter_phase(line_size, x_ref, sums, *sems[:7], emit)
+    finish_gather()
+    finish_scatter()
+
+
+def mlp_backward_kernel(
+    ctx_size, fsdp_size, x_ref, hidden_ref, grad_ref, gains_ref, grad_hidden_ref, grad_gain_ref, out_ref,
+    sums, normed, *sems
+):
+    line_size = ctx_size // PAIR
+    me = lax.axis_index("ctx")
+    greet_line(pltpu.get_barrier_semaphore(), me, me // PAIR, line_size)
+    start_own, finish_gather = gather_phase(line_size, normed, out_ref, *sems[7:])
+
+    def emit(part, rows):
+        grad_norm = swap_lanes(sums[rows, :], fsdp_size, ctx_size)
+        hidden = hidden_ref[rows, :]
+        scale = lax.rsqrt(jnp.mean(hidden * hidden, axis=-1, keepdims=True) + EPSILON)
+        unit = hidden * scale
+        grad_gain_ref[part : part + 1, :] = jnp.sum(grad_norm * unit, axis=0, keepdims=True)
+        grad_hidden = grad_ref[rows, :].astype(jnp.float32) + norm_back(
+            grad_norm, unit, scale, gains_ref[1:2, :]
+        )
+        grad_hidden_ref[rows, :] = grad_hidden
+        normed[rows, :] = (RESIDUAL_MULT * grad_hidden).astype(normed.dtype)
+        start_own(part)
+
+    finish_scatter = scatter_phase(line_size, x_ref, sums, *sems[:7], emit)
+    finish_gather()
+    finish_scatter()
+
+
+def scatter_gather(kernel, collective_id, extra_shapes, partial, *others):
+    ctx_size, fsdp_size = lax.axis_size("ctx"), lax.axis_size("fsdp")
+    rows, model = partial.shape[0] // ctx_size, partial.shape[1]
+    return pl.pallas_call(
+        functools.partial(kernel, ctx_size, fsdp_size),
+        out_shape=extra_shapes + (jax.ShapeDtypeStruct(partial.shape, jnp.bfloat16),),
+        in_specs=in_vmem(1 + len(others)),
+        out_specs=tuple(in_vmem(len(extra_shapes))) + (ANYWHERE,),
+        scratch_shapes=[pltpu.VMEM((rows, model), jnp.float32), pltpu.VMEM((rows, model), jnp.bfloat16)]
+        + scatter_scratch(ctx_size, rows, model)
+        + gather_scratch(ctx_size),
+        compiler_params=pltpu.CompilerParams(
+            collective_id=collective_id, has_side_effects=True, vmem_limit_bytes=40 * 2**20
+        ),
+        cost_estimate=LINK_COST,
+    )(partial, *others)
+
+
+def mlp_forward(partial, tokens, gains):
+    hidden = jax.ShapeDtypeStruct(tokens.shape, jnp.float32)
+    return scatter_gather(mlp_forward_kernel, 1, (hidden,), partial, tokens, gains)
+
+
+def mlp_backward(partial, hidden, grad_out, gains):
+    like = jax.ShapeDtypeStruct(hidden.shape, jnp.float32)
+    gain = jax.ShapeDtypeStruct((CHUNKS, hidden.shape[1]), jnp.float32)
+    return scatter_gather(mlp_backward_kernel, 2, (like, gain), partial, hidden, grad_out, gains)
+
+
+def scatter_kernel(ctx_size, x_ref, out_ref, *sems):
+    line_size = ctx_size // PAIR
+    me = lax.axis_index("ctx")
+    greet_line(pltpu.get_barrier_semaphore(), me, me // PAIR, line_size)
+    scatter_phase(line_size, x_ref, out_ref, *sems, lambda part, rows: None)()
 
 
 def scatter_ctx(partial):
     ctx_size = lax.axis_size("ctx")
-    line_size = ctx_size // PAIR
-    rows, width = partial.shape[0] // ctx_size, partial.shape[1]
-    held = pltpu.VMEM((line_size, rows, width), partial.dtype)
+    rows, model = partial.shape[0] // ctx_size, partial.shape[1]
     return pl.pallas_call(
-        functools.partial(scatter_kernel, line_size),
-        out_shape=jax.ShapeDtypeStruct((rows, width), jnp.float32),
-        in_specs=[pl.BlockSpec(memory_space=pltpu.VMEM)],
-        out_specs=pl.BlockSpec(memory_space=pltpu.VMEM),
-        scratch_shapes=[
-            held, held, held,
-            pltpu.SemaphoreType.DMA((line_size, CHUNKS)),
-            pltpu.SemaphoreType.DMA((line_size, CHUNKS)),
-            pltpu.SemaphoreType.DMA((2, line_size, CHUNKS)),
-            pltpu.SemaphoreType.DMA((line_size, CHUNKS)),
-        ],
+        functools.partial(scatter_kernel, ctx_size),
+        out_shape=jax.ShapeDtypeStruct((rows, model), jnp.float32),
+        in_specs=in_vmem(1),
+        out_specs=in_vmem(1)[0],
+        scratch_shapes=scatter_scratch(ctx_size, rows, model),
         compiler_params=pltpu.CompilerParams(
-            collective_id=1, has_side_effects=True, vmem_limit_bytes=32 * 2**20
+            collective_id=3, has_side_effects=True, vmem_limit_bytes=32 * 2**20
         ),
         cost_estimate=LINK_COST,
         name="scatter_ctx",
@@ -616,7 +866,7 @@
         in_specs=[pl.BlockSpec(memory_space=pltpu.VMEM)],
         out_specs=pl.BlockSpec(memory_space=pltpu.VMEM),
         scratch_shapes=[pltpu.SemaphoreType.DMA((count,)), pltpu.SemaphoreType.DMA((count,))],
-        compiler_params=pltpu.CompilerParams(collective_id=2, has_side_effects=True),
+        compiler_params=pltpu.CompilerParams(collective_id=4, has_side_effects=True),
         cost_estimate=pl.CostEstimate(flops=0, bytes_accessed=25_000_000, transcendentals=0),
         name="exchange",
     )(tiles)
@@ -624,12 +874,6 @@
 
 def padded(rows):
     return jnp.pad(rows, ((0, 0), (0, 8 - rows.shape[1]), (0, 128 - rows.shape[2])))
-
-
-def gather_rows(rows):
-    count = lax.axis_size("ctx") * lax.axis_size("fsdp")
-    tiles = jnp.broadcast_to(padded(rows[None]), (count, 8, 128))
-    return exchange(tiles)[:, : rows.shape[0], : rows.shape[1]].transpose(1, 0, 2).reshape(rows.shape[0], -1)
 
 
 def scatter_rows(rows):
@@ -642,11 +886,6 @@
     return lax.all_to_all(blocks, "ctx", split_axis=0, concat_axis=0, tiled=True)
 
 
-def spread_columns(mine):
-    full = lax.all_gather(mine[:, None], "fsdp", axis=1, tiled=True)
-    return full.reshape(-1, mine.shape[-1])
-
-
 def by_fsdp(grad, ctx_size, fsdp_size):
     parts = grad.reshape(ctx_size, fsdp_size, -1, grad.shape[-1]).transpose(1, 0, 2, 3)
     return rows_of(rows_of(parts))
@@ -654,11 +893,6 @@
 
 def return_columns(terms, ctx_size):
     return swap_ctx(terms.reshape(ctx_size, -1, terms.shape[-1]))
-
-
-def swap_groups(values, outer, inner):
-    parts = values.reshape(values.shape[0], outer, inner, -1)
-    return parts.transpose(0, 2, 1, 3).reshape(values.shape)
 
 
 def half_turn(values, sign_table):
@@ -747,10 +981,6 @@
     grad_ref[:, width:] = jnp.where(lane < HD, turned, pair).astype(jnp.bfloat16)
 
 
-def in_vmem(count):
-    return [pl.BlockSpec(memory_space=pltpu.VMEM)] * count
-
-
 def attention_forward(qkv, tables, block_rows):
     length = qkv.shape[0]
     width = (H // KVH) * HD
@@ -817,24 +1047,24 @@
     sin_table = jnp.concatenate([-sin_half, sin_half] * 2, axis=1)
     tables = (cos_table, sin_table, doc_ids[:, None], doc_ids[None, :])
 
-    gain1, gain2 = gather_rows(jnp.stack([gain_attn, gain_mlp]).astype(jnp.float32))
 
     def by_slice(weight):
         return weight.reshape(held_rows, ctx_size, -1)
 
     qkv_parts = jnp.concatenate([by_slice(w_query), by_slice(w_key), by_slice(w_value)], axis=2)
-    w_qkv = spread_columns(swap_ctx(qkv_parts.transpose(1, 0, 2)))
     wo_mine = lax.all_gather(w_output, "fsdp", axis=0, tiled=True)
-    gu_parts = jnp.concatenate([by_slice(w_gate), by_slice(w_up)], axis=2)
-    gu_mine = swap_ctx(gu_parts.transpose(1, 0, 2))
-
+    gain_rows = jnp.stack([gain_attn, gain_mlp]).astype(jnp.float32)
+    odd = lax.axis_index("fsdp") % 2
+    gain_tile = jnp.concatenate([gain_rows * (1 - odd), gain_rows * odd], axis=1)
+    gain_tile = jnp.pad(gain_tile, ((0, 8 - gain_tile.shape[0]), (0, 128 - gain_tile.shape[1])))
+    normed1, gains, w_qkv = start_layer(tokens[0], gain_tile, qkv_parts.transpose(1, 0, 2))
+    gu_parts = jnp.concatenate([by_slice(w_gate), by_slice(w_up)], axis=2).transpose(1, 0, 2)
+    normed1, gu_parts = lax.optimization_barrier((normed1, gu_parts))
+    w_gu = lax.all_gather(rows_of(swap_ctx(gu_parts)), "fsdp", axis=0, tiled=True)
+    wd_mine = lax.all_gather(w_down, "fsdp", axis=0, tiled=True)
     inputs = tokens[0].astype(jnp.float32)
     inv_one = lax.rsqrt(jnp.mean(inputs * inputs, axis=-1, keepdims=True) + EPSILON)
     unit_one = inputs * inv_one
-    normed1 = gather_ctx((unit_one * gain1).astype(bf16))
-    normed1, gu_mine = lax.optimization_barrier((normed1, gu_mine))
-    w_gu = lax.all_gather(rows_of(gu_mine), "fsdp", axis=0, tiled=True)
-    wd_mine = lax.all_gather(w_down, "fsdp", axis=0, tiled=True)
     grad_out = cotangent[0].astype(jnp.float32)
     grad_mlp = (RESIDUAL_MULT * grad_out).astype(bf16)
 
@@ -843,10 +1073,7 @@
     qkv, grad_mlp = lax.optimization_barrier((qkv, grad_mlp))
     grad_mlp = lax.all_gather(grad_mlp, "ctx", axis=0, tiled=True)
     q, kv, mixed_heads, log_sum = attention_forward(qkv, tables, block_rows)
-    hidden = inputs + RESIDUAL_MULT * scatter_ctx(dot_plain(mixed_heads, wo_mine).astype(bf16))
-    inv_two = lax.rsqrt(jnp.mean(hidden * hidden, axis=-1, keepdims=True) + EPSILON)
-    unit_two = hidden * inv_two
-    normed2 = gather_ctx(swap_groups((unit_two * gain2).astype(bf16), ctx_size, fsdp_size))
+    hidden, normed2 = mlp_forward(dot_plain(mixed_heads, wo_mine).astype(bf16), tokens[0], gains)
 
     gate_up = dot_plain(normed2, w_gu)
     gate_pre, up_pre = gate_up[:, :ff_slice], gate_up[:, ff_slice:]
@@ -875,13 +1102,10 @@
             dot_outer(activ, grad_mlp).astype(bf16),
         )
     )
-    grad_norm2 = swap_groups(scatter_ctx(partial2), fsdp_size, ctx_size)
+    grad_hidden, grad_g2, grad_attn = mlp_backward(partial2, hidden, cotangent[0], gains)
     gu_back = lax.psum_scatter(gu_terms, "fsdp", scatter_dimension=0, tiled=True)
     wd_back = lax.psum_scatter(wd_terms, "fsdp", scatter_dimension=0, tiled=True)
 
-    grad_g2 = jnp.sum(grad_norm2 * unit_two, axis=0)
-    grad_hidden = grad_out + norm_back(grad_norm2, unit_two, inv_two, gain2)
-    grad_attn = gather_ctx((RESIDUAL_MULT * grad_hidden).astype(bf16))
     grad_mixed, wo_terms = lax.optimization_barrier(
         (
             dot_back(grad_attn, wo_mine).astype(bf16),
@@ -903,8 +1127,8 @@
     grad_norm1, qkv_back = lax.optimization_barrier((grad_norm1, qkv_back))
     qkv_back = return_columns(qkv_back, ctx_size)
     grad_g1 = jnp.sum(grad_norm1 * unit_one, axis=0)
-    grad_inputs = grad_hidden + norm_back(grad_norm1, unit_one, inv_one, gain1)
-    gain_back = scatter_rows(jnp.stack([grad_g1, grad_g2]))
+    grad_inputs = grad_hidden + norm_back(grad_norm1, unit_one, inv_one, gains[0])
+    gain_back = scatter_rows(jnp.stack([grad_g1, jnp.sum(grad_g2, axis=0)]))
 
     def joined(parts):
         return parts.transpose(1, 0, 2).reshape(held_rows, -1).astype(jnp.float32)

time: 730 us -> 722 us (0.989)
  waiting for transfers between devices: 124 us -> 196 us
  Pallas kernels: 394 us -> 338 us
  local copies, waits for them, and re-layouts: 49.3 us -> 38.9 us
    pallas_call x2 -> x1, Pallas kernels: 68.5 us -> 15.6 us  [exchange(): pl.pallas_call(functools.partial(exchange_kernel, ctx_size, fsdp_size), o...]
    all_to_all x4 -> x3, waiting for transfers between devices: 9.2 us -> 47.8 us  [swap_ctx(): lax.all_to_all(blocks, 'ctx', split_axis=0, concat_axis=0, tiled=True)]
    reduce_scatter x1, waiting for transfers between devices: 64.9 us -> 89.2 us  [on_device(): branch = lax.psum_scatter(out_terms, 'ctx', scatter_dimension=0, tiled=True)]
    all_gather x1, waiting for transfers between devices: 8.96 us -> 21.1 us  [on_device(): grad_mlp = lax.all_gather(grad_mlp, 'ctx', axis=0, tiled=True)]
    transpose x5 -> x0, local copies, waits for them, and re-layouts: 7.42 us -> none  [the longest x2 3.23 us: swap_groups(): return parts.transpose(0, 2, 1, 3).reshape(values.shape)]
    all_to_all x4 -> x3, starting transfers between devices: 19.8 us -> 14.1 us  [swap_ctx(): lax.all_to_all(blocks, 'ctx', split_axis=0, concat_axis=0, tiled=True)]
    unnamed x63 -> x62, local copies, waits for them, and re-layouts: 20.6 us -> 24.9 us
    pallas_call x6 -> x4, Pallas kernels: 304 us -> 301 us  [the longest x2 190 us: scatter_gather(): pl.pallas_call(functools.partial(kernel, ctx_size, fsdp_size), out_shape=...]
  transfers between devices with their start and end apart: 14 -> 12, of which waited for: 4 -> 4; matrix products, arithmetic and copies ran while one was open for 14% -> 10% of each run, Pallas kernels for 54% -> 39%
where the time goes in v5:
time: 722 us; the launch traced here: 716 us
  Pallas kernels  338 us (47%)
  waiting for transfers between devices  196 us (27%)
  matrix products  94.5 us (13%)
  local copies, waits for them, and re-layouts  38.9 us (5%)
  other arithmetic  18.8 us (3%)
  starting transfers between devices  15 us (2%)
  between operations  14.5 us (2%)
    pallas_call x2, Pallas kernels, scatter_gather(): pl.pallas_call(functools.partial(kernel, ctx_size, fsdp_size), out_shape=...  190 us
    reduce_scatter x1, waiting for transfers between devices, on_device(): branch = lax.psum_scatter(out_terms, 'ctx', scatter_dimension=0, tiled=True)  89.2 us
    pallas_call x1, Pallas kernels, start_layer(): pl.pallas_call(functools.partial(start_kernel, ctx_size, fsdp_size), out_...  62.3 us
    pallas_call x1, Pallas kernels, scatter_ctx(): pl.pallas_call(functools.partial(scatter_kernel, ctx_size), out_shape=jax...  48.6 us
    all_to_all x3, waiting for transfers between devices, swap_ctx(): lax.all_to_all(blocks, 'ctx', split_axis=0, concat_axis=0, tiled=True)  47.8 us
    dot_general x4, matrix products, dot_back(): lax.dot_general(left, right, (((1,), (1,)), ((), ())), preferred_element_...  35.4 us
    reduce_scatter x1, waiting for transfers between devices, on_device(): lax.psum_scatter(wd_terms, 'fsdp', scatter_dimension=0, tiled=True)  35.1 us
    dot_general x4, matrix products, dot_plain(): return jnp.dot(left, right, preferred_element_type=jnp.float32)  30.8 us
  transfers between devices with their start and end apart: 12, of which 4 were waited for; matrix products, arithmetic and copies ran while one was open for 10% of the time, Pallas kernels for 39%

profile of v5, /device:TPU:0, one launch (start us, length us, event | category | flops | bytes accessed | tf_op | source)
XLA Modules:
  0.0 715.8 jit_solution(15617324494248079740)
XLA Ops:
  7.2 1.1 reshape.121
  8.3 1.0 reshape.120
  9.3 1.0 copy.102
  10.3 1.9 copy.100
  13.2 62.3 %start_layer.1 = (bf16[1024,2048]{1,0:T(8,128)(2,1)S(1)}, f32[8,2048]{1,0:T(8,128)S(1)}, bf16[32,64,384]{2,1,0:T(8,128)(2,1)S(1)}) custom-call(bf16[128,2048]{1,0:T(8,128)(2,1)S(1)} %bitcast.82, f32[8,128]{1,0:T(8,128)S(1)} %select_maximum_fusion.tile_ref, bf16[8,64,384]{2,1,0:T(8,128)(2,1)S(1)} %maximum_bitcast_fusion.1.parts_ref), custom_call_target="tpu_custom_call" | custom-call | bytes 150000000 | tf_op jit(solution)/shard_map/start_layer/pallas_call | solution.py:687
  75.6 2.0 copy-done.17
  77.6 2.5 copy.84
  80.0 5.9 all-to-all-start
  86.8 47.8 %all-to-all-done = bf16[8,64,2048]{2,1,0:T(8,128)(2,1)} async-done(((bf16[8,64,2048]{2,1,0:T(8,128)(2,1)}), bf16[8,64,2048]{2,1,0:T(8,128)(2,1)}, u32[]{:S(2)}, u32[]{:S(2)}) %all-to-all-start) | async-done | bytes 2097184 | tf_op jit(solution)/shard_map/all_to_all | solution.py:886
  135.3 0.9 multiply_convert_fusion.2
  136.2 5.7 fusion.15.qkv_ref
  142.7 1.9 fusion.12
  144.6 0.9 pad_maximum_fusion.3
  145.5 8.2 %attend.1 = (bf16[1024,256]{1,0:T(8,128)(2,1)S(1)}, bf16[1024,128]{1,0:T(8,128)(2,1)S(1)}, bf16[1024,256]{1,0:T(8,128)(2,1)S(1)}, f32[1024,4]{1,0:T(8,128)S(1)}) custom-call(f32[1024,384]{1,0:T(8,128)S(1)} %copy-done.5, f32[1024,128]{1,0:T(8,128)S(1)} %get-tuple-element.88.cos_ref, f32[1024,128]{1,0:T(8,128)S(1)} %get-tuple-element.89.sin_ref, ...), custom_call_target="tpu_custom_call" | custom-call | tf_op jit(solution)/shard_map/attend/pallas_call | solution.py:987
  153.7 0.8 copy-done.14
  154.5 2.9 convolution_convert_fusion.3.x_ref
  157.4 98.0 %shard_map.203 = (f32[128,2048]{1,0:T(8,128)S(1)}, bf16[1024,2048]{1,0:T(8,128)(2,1)S(1)}) custom-call(bf16[1024,2048]{1,0:T(8,128)(2,1)S(1)} %convolution_convert_fusion.3.x_ref, bf16[128,2048]{1,0:T(8,128)(2,1)S(1)} %bitcast.83, f32[8,2048]{1,0:T(8,128)S(1)} %get-tuple-element.47.gains_ref), custom_call_target="tpu_custom_call" | custom-call | bytes 150000000 | tf_op jit(solution)/shard_map/pallas_call | solution.py:768
  255.4 2.0 copy-done.18
  257.4 12.9 %fusion.16 = f32[1024,2048]{1,0:T(8,128)S(1)} fusion(bf16[1024,2048]{1,0:T(8,128)(2,1)} %copy-done.18, bf16[2048,2048]{1,0:T(8,128)(2,1)} %all-gather.7.cloned.1.call-done), kind=kOutput, calls=%fused_computation.62 | convolution fusion | flops 8589934592 | bytes 20971520 | tf_op jit(solution)/shard_map/dot_general | solution.py:59
  270.3 3.2 copy-done.23
  273.6 2.7 fusion
  276.3 9.4 %convolution_convert_fusion.5 = bf16[1024,2048]{1,0:T(8,128)(2,1)} fusion(bf16[1024,1024]{1,0:T(8,128)(2,1)} %fusion, bf16[1024,2048]{1,0:T(8,128)(2,1)} %all-gather.9.cloned.1.call-done), kind=kOutput, calls=%fused_computation.11 | convolution fusion | flops 4297064448 | bytes 10485760 | tf_op jit(solution)/shard_map/dot_general | solution.py:59
  285.7 21.1 %all-gather.11.cloned.1.call-done = bf16[1024,2048]{1,0:T(8,128)(2,1)} async-done(((bf16[128,2048]{1,0:T(8,128)(2,1)}), bf16[1024,2048]{1,0:T(8,128)(2,1)}) %all-gather.11.cloned.1.call-update) | async-done | bytes 4194320 | tf_op jit(solution)/shard_map/all_gather | solution.py:1074
  306.8 9.4 %convolution_convert_fusion.4 = bf16[1024,2048]{1,0:T(8,128)(2,1)} fusion(bf16[1024,1024]{1,0:T(8,128)(2,1)} %fusion, bf16[1024,2048]{1,0:T(8,128)(2,1)} %all-gather.11.cloned.1.call-done), kind=kOutput, calls=%fused_computation.10 | convolution fusion | flops 4297064448 | bytes 10485760 | tf_op jit(solution)/shard_map/dot_general | solution.py:69
  316.2 12.1 %multiply_convert_fusion.1 = (bf16[1024,1024]{1,0:T(8,128)(2,1)S(1)}, bf16[1024,1024]{1,0:T(8,128)(2,1)S(1)}) fusion(f32[1024,2048]{1,0:T(8,128)} %copy-done.23, bf16[1024,2048]{1,0:T(8,128)(2,1)} %all-gather.11.cloned.1.call-done, bf16[1024,2048]{1,0:T(8,128)(2,1)} %all-gather.9.cloned.1.call-done), kind=kOutput, calls=%fused_computation.5 | convolution fusion | flops 4308598784 | bytes 20971520 | tf_op jit(solution)/shard_map/dot_general | solution.py:63
  328.3 1.3 copy-done.28
  329.6 0.7 copy-done.29
  330.3 11.6 %convolution_convert_fusion = bf16[2048,2048]{1,0:T(8,128)(2,1)} fusion(bf16[1024,2048]{1,0:T(8,128)(2,1)S(1)} %copy-done.19, bf16[1024,1024]{1,0:T(8,128)(2,1)S(1)} %get-tuple-element.76, bf16[1024,1024]{1,0:T(8,128)(2,1)S(1)} %get-tuple-element.75), kind=kOutput, calls=%fused_computation | convolution fusion | flops 8602517504 | bytes 16777216 | tf_op jit(solution)/shard_map/dot_general | solution.py:69
  341.9 14.4 %convolution_convert_fusion.2.x_ref = bf16[1024,2048]{1,0:T(8,128)(2,1)} fusion(bf16[2048,2048]{1,0:T(8,128)(2,1)} %all-gather.7.cloned.1.call-done, bf16[1024,1024]{1,0:T(8,128)(2,1)} %copy-done.29, bf16[1024,1024]{1,0:T(8,128)(2,1)} %copy-done.28), kind=kOutput, calls=%fused_computation.8 | convolution fusion | flops 8600420352 | bytes 16777216 | tf_op jit(solution)/shard_map/dot_general | solution.py:63
  356.4 2.2 copy-done.2
  358.6 1.0 copy-done.4
  359.6 92.1 %shard_map.204 = (f32[128,2048]{1,0:T(8,128)S(1)}, f32[2,2048]{1,0:T(2,128)S(1)}, bf16[1024,2048]{1,0:T(8,128)(2,1)S(1)}) custom-call(bf16[1024,2048]{1,0:T(8,128)(2,1)S(1)} %copy-done.2, f32[128,2048]{1,0:T(8,128)S(1)} %get-tuple-element.48.hidden_ref, bf16[128,2048]{1,0:T(8,128)(2,1)S(1)} %bitcast.84, f32[8,2048]{1,0:T(8,128)S(1)} %get-tuple-element.47.gains_ref), custom_call_target="tpu_custom_call" | custom-call | bytes 150000000 | tf_op jit(solution)/shard_map/pallas_call | solution.py:768
  451.7 1.0 copy-done.8
  452.7 2.0 copy-done.20
  454.7 2.2 convolution_convert_fusion.7
  456.9 4.6 convolution_convert_fusion.8.do_ref
  461.5 0.7 reduce-scatter.14.cloned.1.call-update
  462.3 0.7 reduce-scatter.6.cloned.1.call-update
  463.5 1.0 copy-done.13
  464.5 1.0 copy-done.15
  465.5 1.1 copy-done.16
  466.6 13.4 %attend_back.1 = bf16[1024,384]{1,0:T(8,128)(2,1)S(1)} custom-call(bf16[1024,256]{1,0:T(8,128)(2,1)S(1)} %copy-done.13, bf16[1024,128]{1,0:T(8,128)(2,1)S(1)} %get-tuple-element.59.kv_ref, bf16[1024,256]{1,0:T(8,128)(2,1)S(1)} %copy-done.16, f32[1024,4]{1,0:T(8,128)S(1)} %copy-done.15, f32[1024,128]{1,0:T(8,128)S(1)} %get-tuple-element.88.cos_ref, ...), custom_call_target="tpu_custom_call" | custom-call | tf_op jit(solution)/shard_map/attend_back/pallas_call | solution.py:1004
  480.0 0.9 copy-done.10
  480.8 5.0 convolution_convert_fusion.6
  485.8 1.3 copy.88
  487.1 4.4 convolution_convert_fusion.1.x_ref
  491.5 4.4 all-to-all-start.2
  496.3 1.9 convert_element_type.170
  498.2 35.1 %reduce-scatter.14.cloned.1.call-done = bf16[256,2048]{1,0:T(8,128)(2,1)} async-done(((bf16[1024,2048]{1,0:T(8,128)(2,1)}), bf16[256,2048]{1,0:T(8,128)(2,1)}) %reduce-scatter.14.cloned.1.call-update) | async-done | bytes 1048592 | tf_op jit(solution)/shard_map/reduce_scatter | solution.py:1107
  533.2 2.8 convert_element_type.177
  536.0 89.2 %reduce-scatter.6.cloned.1.call-done = bf16[128,2048]{1,0:T(8,128)(2,1)} async-done(((bf16[1024,2048]{1,0:T(8,128)(2,1)}), bf16[128,2048]{1,0:T(8,128)(2,1)}) %reduce-scatter.6.cloned.1.call-update) | async-done | bytes 524304 | tf_op jit(solution)/shard_map/reduce_scatter | solution.py:1090
  625.2 2.0 fusion.11
  627.2 2.2 copy-done.1
  629.4 48.6 %scatter_ctx.1 = f32[128,2048]{1,0:T(8,128)S(1)} custom-call(bf16[1024,2048]{1,0:T(8,128)(2,1)S(1)} %copy-done.1), custom_call_target="tpu_custom_call" | custom-call | bytes 150000000 | tf_op jit(solution)/shard_map/scatter_ctx/pallas_call | solution.py:804
  678.5 1.3 fusion.8
  679.8 3.7 all-to-all-start.1
  684.3 15.6 %exchange.1 = f32[32,8,128]{2,1,0:T(8,128)} custom-call(f32[32,8,128]{2,1,0:T(8,128)} %pad.9.x_ref), custom_call_target="tpu_custom_call" | custom-call | bytes 25000000 | tf_op jit(solution)/shard_map/exchange/pallas_call | solution.py:863
  699.9 0.9 reduce_sum.59
  701.3 2.0 convert_bitcast_fusion
  703.3 1.5 copy.97
  704.8 1.5 copy.98
  706.3 0.8 copy.96
  707.4 0.8 reshape.130
  708.3 0.8 reshape.131
  (98 shorter events, 6.5 us)
Async XLA Ops:
  7.2 5.0 copy-start.24
  7.2 5.6 copy-start.25
  7.2 5.6 copy-start.26
  10.3 2.9 copy-start
  75.6 2.0 copy-start.17
  77.6 58.7 %copy-start.21 = (bf16[32,64,384]{2,1,0:T(8,128)(2,1)}, bf16[32,64,384]{2,1,0:T(8,128)(2,1)S(1)}, u32[]{:S(2)}) copy-start(bf16[32,64,384]{2,1,0:T(8,128)(2,1)S(1)} %get-tuple-element.44) | copy-start | bytes 4718596
  80.0 55.3 %copy-start.3 = (bf16[1,128,2048]{2,1,0:T(8,128)(2,1)S(1)}, bf16[1,128,2048]{2,1,0:T(8,128)(2,1)}, u32[]{:S(2)}) copy-start(bf16[1,128,2048]{2,1,0:T(8,128)(2,1)} %param.14) | copy-start | bytes 1572868
  80.0 54.5 %all-to-all-start = ((bf16[8,64,2048]{2,1,0:T(8,128)(2,1)}), bf16[8,64,2048]{2,1,0:T(8,128)(2,1)}, u32[]{:S(2)}, u32[]{:S(2)}) async-start(bf16[8,64,2048]{2,1,0:T(8,128)(2,1)} %copy.84), calls=%async_computation | async-start | bytes 4194304 | tf_op jit(solution)/shard_map/all_to_all | solution.py:886
  86.0 68.6 %all-gather.5.cloned.1.call-start = ((), (), s32[]{:S(2)}) async-start(), calls=%async_computation.8 | async-start | bytes 1310720 | tf_op jit(solution)/shard_map/all_gather | solution.py:1055
  86.7 170.7 %all-gather.7.cloned.1.call-start = ((), (), s32[]{:S(2)}) async-start(), calls=%async_computation.9 | async-start | bytes 10485760 | tf_op jit(solution)/shard_map/all_gather | solution.py:1063
  134.5 141.8 %all-gather.9.cloned.1.call-start = ((), (), s32[]{:S(2)}) async-start(), calls=%async_computation.10 | async-start | bytes 5242880 | tf_op jit(solution)/shard_map/all_gather | solution.py:1064
  135.3 171.5 %all-gather.11.cloned.1.call-start = ((), (), s32[]{:S(2)}) async-start(), calls=%async_computation.11 | async-start | bytes 4718592 | tf_op jit(solution)/shard_map/all_gather | solution.py:1074
  136.2 5.9 copy-start.27
  141.9 338.9 %reduce-scatter.8.cloned.1.call-start = ((), (), s32[]{:S(2)}) async-start(), calls=%async_computation.13 | async-start | bytes 10485760 | tf_op jit(solution)/shard_map/reduce_scatter | solution.py:1106
  142.7 2.8 copy-start.5
  153.7 0.8 copy-start.14
  154.5 2.9 copy-start.6
  154.5 2.9 copy-start.12
  255.4 2.0 copy-start.18
  270.3 3.2 copy-start.23
  316.2 14.1 %copy-start.19 = (bf16[1024,2048]{1,0:T(8,128)(2,1)S(1)}, bf16[1024,2048]{1,0:T(8,128)(2,1)}, u32[]{:S(2)}) copy-start(bf16[1024,2048]{1,0:T(8,128)(2,1)} %copy-done.18) | copy-start | bytes 12582916
  328.2 1.3 copy-start.28
  328.3 2.0 copy-start.29
  356.3 140.0 %reduce-scatter.12.cloned.1.call-start = ((), (), s32[]{:S(2)}) async-start(), calls=%async_computation.15 | async-start | bytes 1310720 | tf_op jit(solution)/shard_map/reduce_scatter | solution.py:1115
  356.4 2.2 copy-start.2
  358.6 1.0 copy-start.4
  359.6 95.0 %copy-start.7 = (bf16[1024,256]{1,0:T(8,128)(2,1)S(1)}, bf16[1024,256]{1,0:T(8,128)(2,1)}, u32[]{:S(2)}) copy-start(bf16[1024,256]{1,0:T(8,128)(2,1)} %copy-done.6) | copy-start | bytes 1572868
  451.7 1.0 copy-start.8
  452.7 2.0 copy-start.20
  461.5 71.7 %reduce-scatter.14.cloned.1.call-start = ((), (), s32[]{:S(2)}) async-start(), calls=%async_computation.16 | async-start | bytes 5242880 | tf_op jit(solution)/shard_map/reduce_scatter | solution.py:1107
  462.2 163.0 %reduce-scatter.6.cloned.1.call-start = ((), (), s32[]{:S(2)}) async-start(), calls=%async_computation.12 | async-start | bytes 4718592 | tf_op jit(solution)/shard_map/reduce_scatter | solution.py:1090
  463.0 215.0 %reduce-scatter.10.cloned.1.call-start = ((), (), s32[]{:S(2)}) async-start(), calls=%async_computation.14 | async-start | bytes 1966080 | tf_op jit(solution)/shard_map/reduce_scatter | solution.py:1126
  463.4 1.0 copy-start.13
  464.5 1.0 copy-start.15
  465.5 1.1 copy-start.16
  480.0 0.9 copy-start.10
  480.8 6.3 copy-start.11
  480.8 6.3 copy-start.22
  491.5 188.3 %all-to-all-start.2 = ((bf16[8,64,2048]{2,1,0:T(8,128)(2,1)}), bf16[8,64,2048]{2,1,0:T(8,128)(2,1)}, u32[]{:S(2)}, u32[]{:S(2)}) async-start(bf16[8,64,2048]{2,1,0:T(8,128)(2,1)} %bitcast.93), calls=%async_computation.6 | async-start | bytes 4194304 | tf_op jit(solution)/shard_map/all_to_all | solution.py:886
  536.0 142.5 %copy-start.9 = (f32[128,2048]{1,0:T(8,128)S(1)}, f32[128,2048]{1,0:T(8,128)}, u32[]{:S(2)}) copy-start(f32[128,2048]{1,0:T(8,128)} %copy-done.8) | copy-start | bytes 3145732
  627.2 2.2 copy-start.1
  679.8 26.4 %all-to-all-start.1 = ((bf16[8,64,384]{2,1,0:T(8,128)(2,1)}), bf16[8,64,384]{2,1,0:T(8,128)(2,1)S(1)}, u32[]{:S(2)}, u32[]{:S(2)}) async-start(bf16[8,64,384]{2,1,0:T(8,128)(2,1)} %bitcast.19), calls=%async_computation.4 | async-start | bytes 786432 | tf_op jit(solution)/shard_map/all_to_all | solution.py:886
Sparse Core Ops, SparseCore 0:
  88.3 18.7 all-gather.4
  134.7 57.6 all-gather.6
  194.0 34.4 all-gather.8
  231.0 75.6 all-gather.10
  356.5 69.9 reduce-scatter.7
  461.6 24.4 reduce-scatter.11
  488.6 44.5 reduce-scatter.13
  536.9 88.3 reduce-scatter.5
  628.3 27.7 reduce-scatter.9

commit v6 on v5

--- a/solution.py
+++ b/solution.py
@@ -414,8 +414,9 @@
     def own_part(part, act):
         pass_on(me, part, line_at < line_size - 1, line_at > 0, True, act)
 
-    def others(act, arrive):
+    def others(act, arrive, between):
         for distance in range(1, line_size):
+            between(distance)
             for part in range(CHUNKS):
 
                 @pl.when(line_at >= distance)
@@ -433,18 +434,22 @@
     def start_own(part):
         own_part(part, lambda c: c.start())
 
-    def finish():
+    def finish(between=lambda distance: None):
         keep = pltpu.make_async_copy(
             x_ref, out_ref.at[pl.ds(pl.multiple_of(me * rows, rows), rows), :], own_sem
         )
         keep.start()
-        others(lambda c: c.start(), lambda block, part: copy(block, part, 0, False).wait_recv())
+        others(
+            lambda c: c.start(),
+            lambda block, part: copy(block, part, 0, False).wait_recv(),
+            between,
+        )
         for place in range(line_size):
             for part in range(CHUNKS):
                 copy(place * PAIR + 1 - pair_at, part, 0, False).wait_recv()
         for part in range(CHUNKS):
             own_part(part, lambda c: c.wait_send())
-        others(lambda c: c.wait_send(), lambda block, part: None)
+        others(lambda c: c.wait_send(), lambda block, part: None, lambda distance: None)
         keep.wait()
 
     return start_own, finish
@@ -458,7 +463,7 @@
     ]
 
 
-def scatter_phase(line_size, x_ref, sum_ref, near, below, above, near_send, near_sem, line_send, line_sem, emit):
+def scatter_phase(line_size, x_ref, sum_ref, near, below, above, near_send, near_sem, line_send, line_sem, emit, midway=lambda: None):
     me = lax.axis_index("ctx")
     line_at, pair_at = me // PAIR, me % PAIR
     rows = sum_ref.shape[0]
@@ -524,6 +529,7 @@
             pl.when(place > line_at)(lambda: send(True, line_at > 0, below))
             pl.when(place < line_at)(lambda: send(False, line_at < last, above))
 
+    midway()
     for part in range(CHUNKS):
         part_rows = pl.ds(part * step, step)
         near_copy(line_at, part).wait_recv()
@@ -584,8 +590,9 @@
 
 
 def start_kernel(
-    ctx_size, fsdp_size, tokens_ref, tile_ref, parts_ref, out_ref, gains_ref, weight_ref,
-    tiles, normed, tile_send, tile_recv, far_send, far_recv, near_send, near_recv, kept, *sems
+    ctx_size, fsdp_size, tokens_ref, tile_ref, parts_ref, gate_ref, up_ref, out_ref, gains_ref, weight_ref,
+    wide_ref, tiles, normed, tile_send, tile_recv, far_send, far_recv, near_send, near_recv, wide_send,
+    wide_recv, kept, wide_kept, *sems
 ):
     me_ctx, me_fsdp = lax.axis_index("ctx"), lax.axis_index("fsdp")
     count = ctx_size * fsdp_size
@@ -636,10 +643,44 @@
             device_id_type=MESH,
         )
 
+    wide = gate_ref.shape[1] // ctx_size
+
+    def wide_part(which, target, source):
+        cols = pl.ds(pl.multiple_of(target * wide, wide), wide)
+        return (
+            (gate_ref, up_ref)[which].at[:, cols],
+            wide_ref.at[source, :, which * wide : (which + 1) * wide],
+        )
+
+    def wide_copy(which, k, source):
+        target = (me_ctx + k) % ctx_size
+        src, dst = wide_part(which, target, source)
+        return pltpu.make_async_remote_copy(
+            src_ref=src,
+            dst_ref=dst,
+            send_sem=wide_send.at[which, k],
+            recv_sem=wide_recv.at[which, k],
+            device_id={"ctx": target},
+            device_id_type=MESH,
+        )
+
+    def wide_keep(which):
+        return pltpu.make_async_copy(*wide_part(which, me_ctx, me_ctx), wide_kept.at[which])
+
+    def wide_start(distance):
+        for k in range(2 * distance - 1, min(2 * distance + 1, ctx_size)):
+            for which in range(2):
+                wide_copy(which, k, me_ctx).start()
+        if distance == ctx_size // PAIR - 1:
+            for which in range(2):
+                wide_copy(which, ctx_size - 1, me_ctx).start()
+
     for k in range(1, ctx_size):
         far_copy(k, me_ctx).start()
     for j in range(1, fsdp_size):
         near_copy(0, j, me_fsdp).start()
+    for which in range(2):
+        wide_keep(which).start()
     keep = pltpu.make_async_copy(parts_ref.at[me_ctx], weight_ref.at[me], kept)
     keep.start()
 
@@ -661,7 +702,13 @@
         far_copy(k, (me_ctx + ctx_size - k) % ctx_size).wait_recv()
         for j in range(1, fsdp_size):
             near_copy(k, j, me_fsdp).start()
-    finish_gather()
+    finish_gather(wide_start)
+    for which in range(2):
+        for k in range(1, ctx_size):
+            wide_copy(which, k, (me_ctx + ctx_size - k) % ctx_size).wait_recv()
+        for k in range(1, ctx_size):
+            wide_copy(which, k, me_ctx).wait_send()
+        wide_keep(which).wait()
     for k in range(ctx_size):
         for j in range(1, fsdp_size):
             near_copy(k, j, (me_fsdp + fsdp_size - j) % fsdp_size).wait_recv()
@@ -679,20 +726,22 @@
     keep.wait()
 
 
-def start_layer(tokens, tile, parts):
+def start_layer(tokens, tile, parts, w_gate, w_up):
     ctx_size, fsdp_size = lax.axis_size("ctx"), lax.axis_size("fsdp")
     count = ctx_size * fsdp_size
     rows, model = tokens.shape
     dma = pltpu.SemaphoreType.DMA
-    normed1, gains, weight = pl.pallas_call(
+    held = w_gate.shape[0]
+    normed1, gains, weight, wide = pl.pallas_call(
         functools.partial(start_kernel, ctx_size, fsdp_size),
         out_shape=(
             jax.ShapeDtypeStruct((ctx_size * rows, model), jnp.bfloat16),
             jax.ShapeDtypeStruct((8, model), jnp.float32),
             jax.ShapeDtypeStruct((count,) + parts.shape[1:], parts.dtype),
+            jax.ShapeDtypeStruct((ctx_size, held, 2 * w_gate.shape[1] // ctx_size), w_gate.dtype),
         ),
-        in_specs=in_vmem(3),
-        out_specs=(ANYWHERE, in_vmem(1)[0], ANYWHERE),
+        in_specs=in_vmem(5),
+        out_specs=(ANYWHERE, in_vmem(1)[0], ANYWHERE, ANYWHERE),
         scratch_shapes=[
             pltpu.VMEM((count, 8, 128), jnp.float32),
             pltpu.VMEM((rows, model), jnp.bfloat16),
@@ -702,7 +751,10 @@
             dma((ctx_size,)),
             dma((ctx_size, fsdp_size)),
             dma((ctx_size, fsdp_size)),
+            dma((2, ctx_size)),
+            dma((2, ctx_size)),
             dma,
+            dma((2,)),
         ]
         + gather_scratch(ctx_size),
         compiler_params=pltpu.CompilerParams(
@@ -710,8 +762,8 @@
         ),
         cost_estimate=LINK_COST,
         name="start_layer",
-    )(tokens, tile, parts)
-    return normed1, gains, rows_of(weight)
+    )(tokens, tile, parts, w_gate, w_up)
+    return normed1, gains, rows_of(weight), rows_of(wide)
 
 
 def mlp_forward_kernel(
@@ -791,95 +843,154 @@
     return scatter_gather(mlp_backward_kernel, 2, (like, gain), partial, hidden, grad_out, gains)
 
 
-def scatter_kernel(ctx_size, x_ref, out_ref, *sems):
+def finish_kernel(
+    ctx_size, fsdp_size, x_ref, tokens_ref, grad_ref, gains_ref, gain2_ref, wo_ref, qkv_ref,
+    grad_tokens_ref, gain_out_ref, wo_out_ref, qkv_out_ref,
+    sums, gain1, tiles, arrived, wo_in, qkv_in, qkv_sum, tile_send, tile_recv, near_send, near_recv,
+    far_send, far_recv, *sems
+):
     line_size = ctx_size // PAIR
-    me = lax.axis_index("ctx")
-    greet_line(pltpu.get_barrier_semaphore(), me, me // PAIR, line_size)
-    scatter_phase(line_size, x_ref, out_ref, *sems, lambda part, rows: None)()
-
-
-def scatter_ctx(partial):
-    ctx_size = lax.axis_size("ctx")
-    rows, model = partial.shape[0] // ctx_size, partial.shape[1]
+    me_ctx, me_fsdp = lax.axis_index("ctx"), lax.axis_index("fsdp")
+    count = ctx_size * fsdp_size
+    me = me_ctx * fsdp_size + me_fsdp
+    greet_all(pltpu.get_barrier_semaphore(), me, count, fsdp_size)
+
+    def near_copy(which, j):
+        target = (me_fsdp + j) % fsdp_size
+        terms, landing = ((wo_ref, wo_in), (qkv_ref, qkv_in))[which]
+        return pltpu.make_async_remote_copy(
+            src_ref=terms.at[target],
+            dst_ref=landing.at[j],
+            send_sem=near_send.at[which, j],
+            recv_sem=near_recv.at[which, j],
+            device_id={"fsdp": target},
+            device_id_type=MESH,
+        )
+
+    def far_copy(k, source):
+        target = (me_ctx + k) % ctx_size
+        return pltpu.make_async_remote_copy(
+            src_ref=qkv_sum.at[target],
+            dst_ref=qkv_out_ref.at[source],
+            send_sem=far_send.at[k],
+            recv_sem=far_recv.at[k],
+            device_id={"ctx": target},
+            device_id_type=MESH,
+        )
+
+    def tile_copy(k, source):
+        target = (me + k) % count
+        return pltpu.make_async_remote_copy(
+            src_ref=tiles.at[target // 2],
+            dst_ref=arrived.at[source],
+            send_sem=tile_send.at[k],
+            recv_sem=tile_recv.at[k],
+            device_id=(target // fsdp_size, target % fsdp_size),
+            device_id_type=MESH,
+        )
+
+    def midway():
+        for which, own, landing in ((1, qkv_ref, qkv_in), (0, wo_ref, wo_in)):
+            for j in range(1, fsdp_size):
+                near_copy(which, j).wait_recv()
+            total = own[pl.ds(me_fsdp, 1)][0].astype(jnp.float32)
+            for j in range(1, fsdp_size):
+                total += landing[j].astype(jnp.float32)
+            if which:
+                qkv_sum[...] = total.astype(qkv_sum.dtype)
+                for k in range(1, ctx_size):
+                    far_copy(k, me_ctx).start()
+                qkv_out_ref[pl.ds(me_ctx, 1)] = qkv_sum[pl.ds(me_ctx, 1)]
+            else:
+                wo_out_ref[...] = total
+
+    def emit(part, rows):
+        grad_norm = sums[rows, :]
+        values = tokens_ref[rows, :].astype(jnp.float32)
+        scale = lax.rsqrt(jnp.mean(values * values, axis=-1, keepdims=True) + EPSILON)
+        unit = values * scale
+        gain1[part : part + 1, :] = jnp.sum(grad_norm * unit, axis=0, keepdims=True)
+        grad_tokens_ref[rows, :] = grad_ref[rows, :] + norm_back(
+            grad_norm, unit, scale, gains_ref[0:1, :]
+        )
+
+    for which in (1, 0):
+        for j in range(1, fsdp_size):
+            near_copy(which, j).start()
+    finish_scatter = scatter_phase(line_size, x_ref, sums, *sems, emit, midway)
+    row = lax.broadcasted_iota(jnp.int32, (8, 128), 0)
+    for pair in range(count // 2):
+        cols = slice(pair * 128, (pair + 1) * 128)
+        first = jnp.sum(gain1[:, cols], axis=0, keepdims=True)
+        second = jnp.sum(gain2_ref[:, cols], axis=0, keepdims=True)
+        tiles[pair] = jnp.where(row == 0, first, jnp.where(row == 1, second, 0.0))
+
+    def start_tile(k, unused):
+        tile_copy(k, me).start()
+        return unused
+
+    def finish_tile(k, unused):
+        tile_copy(k, (me + count - k) % count).wait_recv()
+        return unused
+
+    def sent_tile(k, unused):
+        tile_copy(k, me).wait_send()
+        return unused
+
+    lax.fori_loop(1, count, start_tile, 0)
+    arrived[pl.ds(me, 1)] = tiles[pl.ds(me // 2, 1)]
+    for k in range(1, ctx_size):
+        far_copy(k, (me_ctx + ctx_size - k) % ctx_size).wait_recv()
+    lax.fori_loop(1, count, finish_tile, 0)
+    gain_out_ref[...] = jnp.sum(arrived[...], axis=0)
+    finish_scatter()
+    for which in range(2):
+        for j in range(1, fsdp_size):
+            near_copy(which, j).wait_send()
+    for k in range(1, ctx_size):
+        far_copy(k, me_ctx).wait_send()
+    lax.fori_loop(1, count, sent_tile, 0)
+
+
+def finish_layer(partial, tokens, grad_hidden, gains, grad_gain2, wo_terms, qkv_terms):
+    ctx_size, fsdp_size = lax.axis_size("ctx"), lax.axis_size("fsdp")
+    count = ctx_size * fsdp_size
+    rows, model = tokens.shape
+    dma = pltpu.SemaphoreType.DMA
+    f32, bf16 = jnp.float32, jnp.bfloat16
+    held, width = qkv_terms.shape[2:]
     return pl.pallas_call(
-        functools.partial(scatter_kernel, ctx_size),
-        out_shape=jax.ShapeDtypeStruct((rows, model), jnp.float32),
-        in_specs=in_vmem(1),
-        out_specs=in_vmem(1)[0],
-        scratch_shapes=scatter_scratch(ctx_size, rows, model),
+        functools.partial(finish_kernel, ctx_size, fsdp_size),
+        out_shape=(
+            jax.ShapeDtypeStruct((rows, model), f32),
+            jax.ShapeDtypeStruct((8, 128), f32),
+            jax.ShapeDtypeStruct(wo_terms.shape[1:], f32),
+            jax.ShapeDtypeStruct((ctx_size, held, width), bf16),
+        ),
+        in_specs=in_vmem(7),
+        out_specs=tuple(in_vmem(4)),
+        scratch_shapes=[
+            pltpu.VMEM((rows, model), f32),
+            pltpu.VMEM((CHUNKS, model), f32),
+            pltpu.VMEM((count // 2, 8, 128), f32),
+            pltpu.VMEM((count, 8, 128), f32),
+            pltpu.VMEM(wo_terms.shape, bf16),
+            pltpu.VMEM(qkv_terms.shape, bf16),
+            pltpu.VMEM((ctx_size, held, width), bf16),
+            dma((count,)),
+            dma((count,)),
+            dma((2, fsdp_size)),
+            dma((2, fsdp_size)),
+            dma((ctx_size,)),
+            dma((ctx_size,)),
+        ]
+        + scatter_scratch(ctx_size, rows, model),
         compiler_params=pltpu.CompilerParams(
-            collective_id=3, has_side_effects=True, vmem_limit_bytes=32 * 2**20
+            collective_id=3, has_side_effects=True, vmem_limit_bytes=40 * 2**20
         ),
         cost_estimate=LINK_COST,
-        name="scatter_ctx",
-    )(partial)
-
-
-def exchange_kernel(ctx_size, fsdp_size, x_ref, out_ref, send_sem, recv_sem):
-    count = ctx_size * fsdp_size
-    me = lax.axis_index("ctx") * fsdp_size + lax.axis_index("fsdp")
-    barrier = pltpu.get_barrier_semaphore()
-
-    def device(index):
-        return (index // fsdp_size, index % fsdp_size)
-
-    def greet(k, unused):
-        pl.semaphore_signal(barrier, inc=1, device_id=device((me + k) % count), device_id_type=MESH)
-        return unused
-
-    lax.fori_loop(1, count, greet, 0)
-    pl.semaphore_wait(barrier, count - 1)
-
-    def copy(k):
-        target = (me + k) % count
-        return pltpu.make_async_remote_copy(
-            src_ref=x_ref.at[target], dst_ref=out_ref.at[me],
-            send_sem=send_sem.at[k], recv_sem=recv_sem.at[k],
-            device_id=device(target), device_id_type=MESH,
-        )
-
-    def start(k, unused):
-        copy(k).start()
-        return unused
-
-    def finish(k, unused):
-        source = (me + count - k) % count
-        pltpu.make_async_remote_copy(
-            src_ref=x_ref.at[source], dst_ref=out_ref.at[source],
-            send_sem=send_sem.at[k], recv_sem=recv_sem.at[k],
-            device_id=device(source), device_id_type=MESH,
-        ).wait_recv()
-        copy(k).wait_send()
-        return unused
-
-    lax.fori_loop(1, count, start, 0)
-    out_ref[pl.ds(me, 1)] = x_ref[pl.ds(me, 1)]
-    lax.fori_loop(1, count, finish, 0)
-
-
-def exchange(tiles):
-    ctx_size, fsdp_size = lax.axis_size("ctx"), lax.axis_size("fsdp")
-    count = ctx_size * fsdp_size
-    return pl.pallas_call(
-        functools.partial(exchange_kernel, ctx_size, fsdp_size),
-        out_shape=jax.ShapeDtypeStruct(tiles.shape, tiles.dtype),
-        in_specs=[pl.BlockSpec(memory_space=pltpu.VMEM)],
-        out_specs=pl.BlockSpec(memory_space=pltpu.VMEM),
-        scratch_shapes=[pltpu.SemaphoreType.DMA((count,)), pltpu.SemaphoreType.DMA((count,))],
-        compiler_params=pltpu.CompilerParams(collective_id=4, has_side_effects=True),
-        cost_estimate=pl.CostEstimate(flops=0, bytes_accessed=25_000_000, transcendentals=0),
-        name="exchange",
-    )(tiles)
-
-
-def padded(rows):
-    return jnp.pad(rows, ((0, 0), (0, 8 - rows.shape[1]), (0, 128 - rows.shape[2])))
-
-
-def scatter_rows(rows):
-    count = lax.axis_size("ctx") * lax.axis_size("fsdp")
-    by_owner = rows.reshape(rows.shape[0], count, -1).transpose(1, 0, 2)
-    return jnp.sum(exchange(padded(by_owner)), axis=0)[: rows.shape[0], : by_owner.shape[2]]
+        name="finish_layer",
+    )(partial, tokens, grad_hidden, gains, grad_gain2, wo_terms, qkv_terms)
 
 
 def swap_ctx(blocks):
@@ -1029,7 +1140,7 @@
     w_up,
     w_down,
 ):
-    local_rows, _ = tokens.shape[1:]
+    local_rows, model = tokens.shape[1:]
     ctx_size = lax.axis_size("ctx")
     fsdp_size = lax.axis_size("fsdp")
     length = local_rows * ctx_size
@@ -1053,18 +1164,15 @@
 
     qkv_parts = jnp.concatenate([by_slice(w_query), by_slice(w_key), by_slice(w_value)], axis=2)
     wo_mine = lax.all_gather(w_output, "fsdp", axis=0, tiled=True)
+    wd_mine = lax.all_gather(w_down, "fsdp", axis=0, tiled=True)
     gain_rows = jnp.stack([gain_attn, gain_mlp]).astype(jnp.float32)
     odd = lax.axis_index("fsdp") % 2
     gain_tile = jnp.concatenate([gain_rows * (1 - odd), gain_rows * odd], axis=1)
     gain_tile = jnp.pad(gain_tile, ((0, 8 - gain_tile.shape[0]), (0, 128 - gain_tile.shape[1])))
-    normed1, gains, w_qkv = start_layer(tokens[0], gain_tile, qkv_parts.transpose(1, 0, 2))
-    gu_parts = jnp.concatenate([by_slice(w_gate), by_slice(w_up)], axis=2).transpose(1, 0, 2)
-    normed1, gu_parts = lax.optimization_barrier((normed1, gu_parts))
-    w_gu = lax.all_gather(rows_of(swap_ctx(gu_parts)), "fsdp", axis=0, tiled=True)
-    wd_mine = lax.all_gather(w_down, "fsdp", axis=0, tiled=True)
-    inputs = tokens[0].astype(jnp.float32)
-    inv_one = lax.rsqrt(jnp.mean(inputs * inputs, axis=-1, keepdims=True) + EPSILON)
-    unit_one = inputs * inv_one
+    normed1, gains, w_qkv, gu_mine = start_layer(
+        tokens[0], gain_tile, qkv_parts.transpose(1, 0, 2), w_gate, w_up
+    )
+    w_gu = lax.all_gather(gu_mine, "fsdp", axis=0, tiled=True)
     grad_out = cotangent[0].astype(jnp.float32)
     grad_mlp = (RESIDUAL_MULT * grad_out).astype(bf16)
 
@@ -1106,29 +1214,24 @@
     gu_back = lax.psum_scatter(gu_terms, "fsdp", scatter_dimension=0, tiled=True)
     wd_back = lax.psum_scatter(wd_terms, "fsdp", scatter_dimension=0, tiled=True)
 
-    grad_mixed, wo_terms = lax.optimization_barrier(
-        (
-            dot_back(grad_attn, wo_mine).astype(bf16),
-            dot_outer(mixed_heads, grad_attn).astype(bf16),
-        )
-    )
-    wo_back = lax.psum_scatter(wo_terms, "fsdp", scatter_dimension=0, tiled=True)
+    grad_mixed = dot_back(grad_attn, wo_mine).astype(bf16)
+    wo_terms = dot_outer(mixed_heads, grad_attn).astype(bf16)
     grad_qkv = attention_backward(q, kv, grad_mixed, log_sum, tables, block_rows)
     grad_qkv, gu_back = lax.optimization_barrier((grad_qkv, gu_back))
     gu_back = return_columns(gu_back, ctx_size)
-    partial1, qkv_terms = lax.optimization_barrier(
-        (
-            dot_back(grad_qkv, w_qkv).astype(bf16),
-            by_fsdp(dot_outer(normed1, grad_qkv).astype(bf16), ctx_size, fsdp_size),
-        )
-    )
-    grad_norm1 = scatter_ctx(partial1)
-    qkv_back = lax.psum_scatter(qkv_terms, "fsdp", scatter_dimension=0, tiled=True)
-    grad_norm1, qkv_back = lax.optimization_barrier((grad_norm1, qkv_back))
-    qkv_back = return_columns(qkv_back, ctx_size)
-    grad_g1 = jnp.sum(grad_norm1 * unit_one, axis=0)
-    grad_inputs = grad_hidden + norm_back(grad_norm1, unit_one, inv_one, gains[0])
-    gain_back = scatter_rows(jnp.stack([grad_g1, jnp.sum(grad_g2, axis=0)]))
+    partial1 = dot_back(grad_qkv, w_qkv).astype(bf16)
+    qkv_terms = by_fsdp(dot_outer(normed1, grad_qkv).astype(bf16), ctx_size, fsdp_size)
+    grad_inputs, gain_back, wo_back, qkv_back = finish_layer(
+        partial1,
+        tokens[0],
+        grad_hidden,
+        gains,
+        grad_g2,
+        wo_terms.reshape(fsdp_size, held_rows, model),
+        qkv_terms.reshape(fsdp_size, ctx_size, held_rows, -1),
+    )
+    grad_inputs, wd_back = lax.optimization_barrier((grad_inputs, wd_back))
+    gain_back = jnp.where(odd == 0, gain_back[:2, :held_rows], gain_back[:2, held_rows:])
 
     def joined(parts):
         return parts.transpose(1, 0, 2).reshape(held_rows, -1).astype(jnp.float32)
@@ -1141,7 +1244,7 @@
         joined(qkv_back[:, :, :group_width]),
         joined(qkv_back[:, :, group_width:key_end]),
         joined(qkv_back[:, :, key_end:]),
-        wo_back.astype(jnp.float32),
+        wo_back,
         gain_back[1],
         joined(gu_back[:, :, :ff_slice]),
         joined(gu_back[:, :, ff_slice:]),

time: 722 us -> 624 us (0.86)
  waiting for transfers between devices: 196 us -> 86.8 us
  Pallas kernels: 338 us -> 376 us
  starting transfers between devices: 15 us -> 5.68 us
  local copies, waits for them, and re-layouts: 38.9 us -> 31.2 us
    all_to_all x3 -> x1, waiting for transfers between devices: 47.8 us -> 0.01 us  [swap_ctx(): lax.all_to_all(blocks, 'ctx', split_axis=0, concat_axis=0, tiled=True)]
    pallas_call x1, Pallas kernels: 62.3 us -> 97.6 us  [start_layer(): pl.pallas_call(functools.partial(start_kernel, ctx_size, fsdp_size), out_...]
    reduce_scatter x1, waiting for transfers between devices: 35.1 us -> 0.02 us  [on_device(): lax.psum_scatter(wd_terms, 'fsdp', scatter_dimension=0, tiled=True)]
    reduce_scatter x1, waiting for transfers between devices: 89.2 us -> 60.2 us  [on_device(): branch = lax.psum_scatter(out_terms, 'ctx', scatter_dimension=0, tiled=True)]
    all_to_all x3 -> x1, starting transfers between devices: 14.1 us -> 5.11 us  [swap_ctx(): lax.all_to_all(blocks, 'ctx', split_axis=0, concat_axis=0, tiled=True)]
    unnamed x62 -> x64, local copies, waits for them, and re-layouts: 24.9 us -> 21.7 us
    pallas_call x2 -> x1, Pallas kernels: 64.2 us -> 61.2 us  [finish_layer(): pl.pallas_call(functools.partial(finish_kernel, ctx_size, fsdp_size), out...]
  transfers between devices with their start and end apart: 12 -> 8, of which waited for: 4 -> 2; matrix products, arithmetic and copies ran while one was open for 10% -> 10% of each run, Pallas kernels for 39% -> 61%
where the time goes in v6:
time: 624 us; the launch traced here: 620 us
  Pallas kernels  376 us (60%)
  matrix products  91 us (15%)
  waiting for transfers between devices  86.8 us (14%)
  local copies, waits for them, and re-layouts  31.2 us (5%)
  between operations  14.8 us (2%)
  other arithmetic  14.6 us (2%)
    pallas_call x2, Pallas kernels, scatter_gather(): pl.pallas_call(functools.partial(kernel, ctx_size, fsdp_size), out_shape=...  196 us
    pallas_call x1, Pallas kernels, start_layer(): pl.pallas_call(functools.partial(start_kernel, ctx_size, fsdp_size), out_...  97.6 us
    pallas_call x1, Pallas kernels, finish_layer(): pl.pallas_call(functools.partial(finish_kernel, ctx_size, fsdp_size), out...  61.2 us
    reduce_scatter x1, waiting for transfers between devices, on_device(): branch = lax.psum_scatter(out_terms, 'ctx', scatter_dimension=0, tiled=True)  60.2 us
    dot_general x4, matrix products, dot_plain(): return jnp.dot(left, right, preferred_element_type=jnp.float32)  30.6 us
    dot_general x4, matrix products, dot_back(): lax.dot_general(left, right, (((1,), (1,)), ((), ())), preferred_element_...  30.4 us
    dot_general x4, matrix products, dot_outer(): lax.dot_general(left, right, (((0,), (0,)), ((), ())), preferred_element_...  29.9 us
    all_gather x1, waiting for transfers between devices, on_device(): grad_mlp = lax.all_gather(grad_mlp, 'ctx', axis=0, tiled=True)  24 us
  transfers between devices with their start and end apart: 8, of which 2 were waited for; matrix products, arithmetic and copies ran while one was open for 10% of the time, Pallas kernels for 61%

profile of v6, /device:TPU:0, one launch (start us, length us, event | category | flops | bytes accessed | tf_op | source)
XLA Modules:
  0.0 620.2 jit_solution(515668211879065919)
XLA Ops:
  7.2 0.7 all-gather.5.cloned.1.call-update
  8.0 1.0 reshape.98
  9.0 1.0 reshape.97
  10.1 1.0 copy.75
  11.0 0.7 convert_multiply_fusion.1
  11.9 1.0 copy-done
  13.0 1.2 copy-done.8
  14.2 1.2 copy-done.9
  15.4 97.6 %start_layer.1 = (bf16[1024,2048]{1,0:T(8,128)(2,1)S(1)}, f32[8,2048]{1,0:T(8,128)S(1)}, bf16[32,64,384]{2,1,0:T(8,128)(2,1)S(1)}, bf16[8,64,2048]{2,1,0:T(8,128)(2,1)}) custom-call(bf16[128,2048]{1,0:T(8,128)(2,1)S(1)} %bitcast.69, f32[8,128]{1,0:T(8,128)S(1)} %select_maximum_fusion.tile_ref, bf16[8,64,384]{2,1,0:T(8,128)(2,1)S(1)} %maximum_bitcast_fusion.parts_ref, ...), custom_call_target="tpu_custom_call" | custom-call | bytes 150000000 | tf_op jit(solution)/shard_map/start_layer/pallas_call | solution.py:735
  113.0 2.0 copy-done.19
  114.9 1.1 copy-done.23
  116.2 0.7 all-gather.9.cloned.1.call-update
  116.9 0.9 multiply_convert_fusion.2
  117.8 5.7 fusion.5.qkv_ref
  123.5 0.3 reduce-scatter.6.cloned.1.call-start
  123.9 0.2 reduce-window_clone.1
  124.1 0.2 copy.57.doc_col_ref
  124.4 1.9 fusion.2
  126.3 0.9 pad_maximum_fusion.3
  127.2 8.2 %attend.1 = (bf16[1024,256]{1,0:T(8,128)(2,1)S(1)}, bf16[1024,128]{1,0:T(8,128)(2,1)S(1)}, bf16[1024,256]{1,0:T(8,128)(2,1)S(1)}, f32[1024,4]{1,0:T(8,128)S(1)}) custom-call(f32[1024,384]{1,0:T(8,128)S(1)} %copy-done.5, f32[1024,128]{1,0:T(8,128)S(1)} %get-tuple-element.84.cos_ref, f32[1024,128]{1,0:T(8,128)S(1)} %get-tuple-element.85.sin_ref, ...), custom_call_target="tpu_custom_call" | custom-call | tf_op jit(solution)/shard_map/attend/pallas_call | solution.py:1098
  135.4 0.8 copy-done.15
  136.2 2.9 convolution_convert_fusion.3.x_ref
  139.1 98.1 %shard_map.203 = (f32[128,2048]{1,0:T(8,128)S(1)}, bf16[1024,2048]{1,0:T(8,128)(2,1)S(1)}) custom-call(bf16[1024,2048]{1,0:T(8,128)(2,1)S(1)} %convolution_convert_fusion.3.x_ref, bf16[128,2048]{1,0:T(8,128)(2,1)S(1)} %bitcast.70, f32[8,2048]{1,0:T(8,128)S(1)} %get-tuple-element.45.gains_ref), custom_call_target="tpu_custom_call" | custom-call | bytes 150000000 | tf_op jit(solution)/shard_map/pallas_call | solution.py:820
  237.2 2.0 copy-done.20
  239.2 12.7 %fusion.6 = f32[1024,2048]{1,0:T(8,128)S(1)} fusion(bf16[1024,2048]{1,0:T(8,128)(2,1)} %copy-done.20, bf16[2048,2048]{1,0:T(8,128)(2,1)} %all-gather.7.cloned.1.call-done), kind=kOutput, calls=%fused_computation.48 | convolution fusion | flops 8589934592 | bytes 20971520 | tf_op jit(solution)/shard_map/dot_general | solution.py:59
  251.9 3.2 copy-done.26
  255.1 2.7 fusion
  257.9 9.4 %convolution_convert_fusion.5 = bf16[1024,2048]{1,0:T(8,128)(2,1)} fusion(bf16[1024,1024]{1,0:T(8,128)(2,1)} %fusion, bf16[1024,2048]{1,0:T(8,128)(2,1)} %all-gather.9.cloned.1.call-done), kind=kOutput, calls=%fused_computation.11 | convolution fusion | flops 4297064448 | bytes 10485760 | tf_op jit(solution)/shard_map/dot_general | solution.py:59
  267.3 24.0 %all-gather.11.cloned.1.call-done = bf16[1024,2048]{1,0:T(8,128)(2,1)} async-done(((bf16[128,2048]{1,0:T(8,128)(2,1)}), bf16[1024,2048]{1,0:T(8,128)(2,1)}) %all-gather.11.cloned.1.call-update) | async-done | bytes 4194320 | tf_op jit(solution)/shard_map/all_gather | solution.py:1182
  291.3 9.4 %convolution_convert_fusion.4 = bf16[1024,2048]{1,0:T(8,128)(2,1)} fusion(bf16[1024,1024]{1,0:T(8,128)(2,1)} %fusion, bf16[1024,2048]{1,0:T(8,128)(2,1)} %all-gather.11.cloned.1.call-done), kind=kOutput, calls=%fused_computation.10 | convolution fusion | flops 4297064448 | bytes 10485760 | tf_op jit(solution)/shard_map/dot_general | solution.py:69
  300.7 12.3 %multiply_convert_fusion.1 = (bf16[1024,1024]{1,0:T(8,128)(2,1)S(1)}, bf16[1024,1024]{1,0:T(8,128)(2,1)S(1)}) fusion(f32[1024,2048]{1,0:T(8,128)} %copy-done.26, bf16[1024,2048]{1,0:T(8,128)(2,1)} %all-gather.11.cloned.1.call-done, bf16[1024,2048]{1,0:T(8,128)(2,1)} %all-gather.9.cloned.1.call-done), kind=kOutput, calls=%fused_computation.5 | convolution fusion | flops 4308598784 | bytes 20971520 | tf_op jit(solution)/shard_map/dot_general | solution.py:63
  313.0 1.3 copy-done.29
  314.3 0.7 copy-done.30
  315.0 11.3 %convolution_convert_fusion = bf16[2048,2048]{1,0:T(8,128)(2,1)} fusion(bf16[1024,2048]{1,0:T(8,128)(2,1)S(1)} %copy-done.21, bf16[1024,1024]{1,0:T(8,128)(2,1)S(1)} %get-tuple-element.72, bf16[1024,1024]{1,0:T(8,128)(2,1)S(1)} %get-tuple-element.71), kind=kOutput, calls=%fused_computation | convolution fusion | flops 8602517504 | bytes 16777216 | tf_op jit(solution)/shard_map/dot_general | solution.py:69
  326.3 14.4 %convolution_convert_fusion.2.x_ref = bf16[1024,2048]{1,0:T(8,128)(2,1)} fusion(bf16[2048,2048]{1,0:T(8,128)(2,1)} %all-gather.7.cloned.1.call-done, bf16[1024,1024]{1,0:T(8,128)(2,1)} %copy-done.30, bf16[1024,1024]{1,0:T(8,128)(2,1)} %copy-done.29), kind=kOutput, calls=%fused_computation.8 | convolution fusion | flops 8600420352 | bytes 16777216 | tf_op jit(solution)/shard_map/dot_general | solution.py:63
  340.8 0.5 reduce-scatter.4.cloned.1.call-update
  341.4 0.7 reduce-scatter.8.cloned.1.call-update
  342.1 2.2 copy-done.2
  344.3 1.2 copy-done.4
  345.5 97.5 %shard_map.204 = (f32[128,2048]{1,0:T(8,128)S(1)}, f32[2,2048]{1,0:T(2,128)S(1)}, bf16[1024,2048]{1,0:T(8,128)(2,1)S(1)}) custom-call(bf16[1024,2048]{1,0:T(8,128)(2,1)S(1)} %copy-done.2, f32[128,2048]{1,0:T(8,128)S(1)} %get-tuple-element.46.hidden_ref, bf16[128,2048]{1,0:T(8,128)(2,1)S(1)} %bitcast.72, f32[8,2048]{1,0:T(8,128)S(1)} %get-tuple-element.45.gains_ref), custom_call_target="tpu_custom_call" | custom-call | bytes 150000000 | tf_op jit(solution)/shard_map/pallas_call | solution.py:820
  443.1 1.3 convolution_convert_fusion.8.do_ref
  444.4 0.9 copy-done.22
  445.4 13.5 %attend_back.1 = bf16[1024,384]{1,0:T(8,128)(2,1)S(1)} custom-call(bf16[1024,256]{1,0:T(8,128)(2,1)S(1)} %copy-done.16, bf16[1024,128]{1,0:T(8,128)(2,1)S(1)} %get-tuple-element.53.kv_ref, bf16[1024,256]{1,0:T(8,128)(2,1)S(1)} %convolution_convert_fusion.8.do_ref, f32[1024,4]{1,0:T(8,128)S(1)} %copy-done.18, f32[1024,128]{1,0:T(8,128)S(1)} %get-tuple-element.84.cos_ref, ...), custom_call_target="tpu_custom_call" | custom-call | tf_op jit(solution)/shard_map/attend_back/pallas_call | solution.py:1115
  458.9 0.9 copy-done.13
  459.7 5.1 all-to-all-start
  464.9 4.5 convolution_convert_fusion.7
  469.4 60.2 %reduce-scatter.4.cloned.1.call-done = bf16[128,2048]{1,0:T(8,128)(2,1)} async-done(((bf16[1024,2048]{1,0:T(8,128)(2,1)}), bf16[128,2048]{1,0:T(8,128)(2,1)}) %reduce-scatter.4.cloned.1.call-update) | async-done | bytes 524304 | tf_op jit(solution)/shard_map/reduce_scatter | solution.py:1198
  529.6 2.0 fusion.1
  531.6 4.7 convolution_convert_fusion.6
  536.3 0.2 copy.74
  536.5 2.4 convolution_convert_fusion.1.x_ref
  538.9 61.2 %finish_layer.1 = (f32[128,2048]{1,0:T(8,128)S(1)}, f32[8,128]{1,0:T(8,128)S(1)}, f32[64,2048]{1,0:T(8,128)S(1)}, bf16[8,64,384]{2,1,0:T(8,128)(2,1)S(1)}) custom-call(bf16[1024,2048]{1,0:T(8,128)(2,1)S(1)} %convolution_convert_fusion.1.x_ref, bf16[128,2048]{1,0:T(8,128)(2,1)S(1)} %bitcast.71, f32[128,2048]{1,0:T(8,128)S(1)} %copy-done.11, ...), custom_call_target="tpu_custom_call" | custom-call | bytes 150000000 | tf_op jit(solution)/shard_map/finish_layer/pallas_call | solution.py:962
  600.2 0.8 copy.69
  601.2 0.2 copy.63
  601.3 0.8 reshape.105
  602.1 0.2 copy.64
  602.3 0.8 reshape.106
  603.0 2.8 convert_element_type.167
  605.9 0.5 slice_bitcast_fusion
  606.4 2.0 convert_bitcast_fusion
  608.4 1.5 copy.70
  609.9 1.5 copy.71
  611.3 1.0 copy.78
  612.3 0.8 copy.79
  (75 shorter events, 1.0 us)
Async XLA Ops:
  7.2 129.0 %all-gather.5.cloned.1.call-start = ((), (), s32[]{:S(2)}) async-start(), calls=%async_computation.4 | async-start | bytes 1310720 | tf_op jit(solution)/shard_map/all_gather | solution.py:1166
  7.9 231.3 %all-gather.7.cloned.1.call-start = ((), (), s32[]{:S(2)}) async-start(), calls=%async_computation.5 | async-start | bytes 10485760 | tf_op jit(solution)/shard_map/all_gather | solution.py:1175
  9.0 107.9 %copy-start.3 = (bf16[1,128,2048]{2,1,0:T(8,128)(2,1)S(1)}, bf16[1,128,2048]{2,1,0:T(8,128)(2,1)}, u32[]{:S(2)}) copy-start(bf16[1,128,2048]{2,1,0:T(8,128)(2,1)} %param.14) | copy-start | bytes 1572868
  11.9 1.0 copy-start
  13.0 1.2 copy-start.8
  14.2 1.2 copy-start.9
  113.0 2.0 copy-start.19
  114.9 1.1 copy-start.23
  116.1 1.7 copy-start.24
  116.1 141.8 %all-gather.9.cloned.1.call-start = ((), (), s32[]{:S(2)}) async-start(), calls=%async_computation.6 | async-start | bytes 5242880 | tf_op jit(solution)/shard_map/all_gather | solution.py:1167
  116.8 174.4 %all-gather.11.cloned.1.call-start = ((), (), s32[]{:S(2)}) async-start(), calls=%async_computation.7 | async-start | bytes 4718592 | tf_op jit(solution)/shard_map/all_gather | solution.py:1182
  117.8 6.0 copy-start.28
  123.5 336.2 %reduce-scatter.6.cloned.1.call-start = ((), (), s32[]{:S(2)}) async-start(), calls=%async_computation.9 | async-start | bytes 10485760 | tf_op jit(solution)/shard_map/reduce_scatter | solution.py:1214
  124.4 2.8 copy-start.5
  135.4 0.8 copy-start.15
  136.2 2.9 copy-start.6
  136.2 2.9 copy-start.17
  136.2 2.9 copy-start.1
  237.2 2.0 copy-start.20
  251.9 3.3 copy-start.26
  300.7 14.3 %copy-start.21 = (bf16[1024,2048]{1,0:T(8,128)(2,1)S(1)}, bf16[1024,2048]{1,0:T(8,128)(2,1)}, u32[]{:S(2)}) copy-start(bf16[1024,2048]{1,0:T(8,128)(2,1)} %copy-done.20) | copy-start | bytes 12582916
  313.0 1.3 copy-start.29
  313.0 2.0 copy-start.30
  340.8 188.8 %reduce-scatter.4.cloned.1.call-start = ((), (), s32[]{:S(2)}) async-start(), calls=%async_computation.8 | async-start | bytes 4718592 | tf_op jit(solution)/shard_map/reduce_scatter | solution.py:1198
  341.4 258.8 %reduce-scatter.8.cloned.1.call-start = ((), (), s32[]{:S(2)}) async-start(), calls=%async_computation.10 | async-start | bytes 5242880 | tf_op jit(solution)/shard_map/reduce_scatter | solution.py:1215
  342.1 2.2 copy-start.2
  344.3 1.2 copy-start.4
  345.5 97.6 %copy-start.27 = (bf16[256,2048]{1,0:T(8,128)(2,1)S(1)}, bf16[256,2048]{1,0:T(8,128)(2,1)}, u32[]{:S(2)}) copy-start(bf16[256,2048]{1,0:T(8,128)(2,1)} %all-gather.5.cloned.1.call-done) | copy-start | bytes 3145732
  443.0 1.4 copy-start.10
  443.0 2.3 copy-start.22
  443.1 2.3 copy-start.16
  443.1 2.3 copy-start.18
  458.9 0.9 copy-start.13
  459.7 5.1 copy-start.7
  459.7 146.7 %all-to-all-start = ((bf16[8,64,2048]{2,1,0:T(8,128)(2,1)}), bf16[8,64,2048]{2,1,0:T(8,128)(2,1)}, u32[]{:S(2)}, u32[]{:S(2)}) async-start(bf16[8,64,2048]{2,1,0:T(8,128)(2,1)} %bitcast.80), calls=%async_computation.3 | async-start | bytes 4194304 | tf_op jit(solution)/shard_map/all_to_all | solution.py:997
  464.9 66.7 %copy-start.14 = (bf16[1024,384]{1,0:T(8,128)(2,1)S(1)}, bf16[1024,384]{1,0:T(8,128)(2,1)}, u32[]{:S(2)}) copy-start(bf16[1024,384]{1,0:T(8,128)(2,1)} %copy-done.13) | copy-start | bytes 2359300
  531.6 4.9 copy-start.25
  536.5 2.4 copy-start.11
  536.5 2.4 copy-start.12
Sparse Core Ops, SparseCore 0:
  9.5 24.2 all-gather.4
  116.2 61.5 all-gather.6
  179.4 34.4 all-gather.8
  216.4 74.8 all-gather.10
  340.9 69.8 reduce-scatter.5
  414.3 115.1 reduce-scatter.3
  532.1 63.6 reduce-scatter.7

commit v7 on v6

--- a/solution.py
+++ b/solution.py
@@ -22,6 +22,8 @@
 MESH = pl.DeviceIdType.MESH
 PAIR = 2
 CHUNKS = 2
+EVEN = 384
+EVEN_LAST = 0
 ANYWHERE = pl.BlockSpec(memory_space=pl.ANY)
 LINK_COST = pl.CostEstimate(flops=0, bytes_accessed=150_000_000, transcendentals=0)
 
@@ -384,52 +386,61 @@
     pl.semaphore_wait(barrier, count - 1)
 
 
-def gather_phase(line_size, x_ref, out_ref, send_sem, recv_sem, own_sem):
+def gather_phase(line_size, across_first, x_ref, out_ref, send_sem, recv_sem, own_sem):
     me = lax.axis_index("ctx")
     line_at, pair_at = me // PAIR, me % PAIR
-    rows = x_ref.shape[0]
+    other = me + 1 - 2 * pair_at
+    rows, width = x_ref.shape
     step = rows // CHUNKS
-
-    def piece(block, part):
-        return out_ref.at[pl.ds(pl.multiple_of(block * rows + part * step, step), step), :]
-
-    def copy(block, part, way, own):
-        slot = block * CHUNKS + part
+    split = width - across_first
+    columns = (slice(0, split), slice(split, width))
+    sides = (0, 1) if across_first else (0,)
+
+    def piece(block, part, side):
+        start = pl.multiple_of(block * rows + part * step, step)
+        return out_ref.at[pl.ds(start, step), columns[side]]
+
+    def copy(block, part, side, way, own=False):
+        slot = (block * CHUNKS + part) * 2 + side
         return pltpu.make_async_remote_copy(
-            src_ref=x_ref.at[pl.ds(part * step, step), :] if own else piece(block, part),
-            dst_ref=piece(block, part),
+            src_ref=x_ref.at[pl.ds(part * step, step), columns[side]] if own else piece(block, part, side),
+            dst_ref=piece(block, part, side),
             send_sem=send_sem.at[way, slot],
             recv_sem=recv_sem.at[slot],
-            device_id={"ctx": (me + 1 - 2 * pair_at, me + PAIR, me - PAIR)[way]},
+            device_id={"ctx": (other, me + PAIR, me - PAIR)[way]},
             device_id_type=MESH,
         )
 
-    def pass_on(block, part, upward, downward, own, act):
-        if upward is not None:
-            pl.when(upward)(lambda: act(copy(block, part, 1, own)))
-        if downward is not None:
-            pl.when(downward)(lambda: act(copy(block, part, 2, own)))
-        act(copy(block, part, 0, own))
+    up, down = line_at < line_size - 1, line_at > 0
 
     def own_part(part, act):
-        pass_on(me, part, line_at < line_size - 1, line_at > 0, True, act)
+        for side in reversed(sides):
+            pl.when(up)(lambda: act(copy(me, part, side, 1, True)))
+            pl.when(down)(lambda: act(copy(me, part, side, 2, True)))
+            act(copy(me, part, side, 0, True))
 
     def others(act, arrive, between):
+        if across_first:
+            for part in range(CHUNKS):
+                arrive(other, part, 1)
+                pl.when(up)(lambda: act(copy(other, part, 1, 1)))
+                pl.when(down)(lambda: act(copy(other, part, 1, 2)))
         for distance in range(1, line_size):
             between(distance)
             for part in range(CHUNKS):
 
-                @pl.when(line_at >= distance)
-                def _():
-                    block = me - PAIR * distance
-                    arrive(block, part)
-                    pass_on(block, part, line_at < line_size - 1, None, False, act)
-
-                @pl.when(line_at + distance < line_size)
-                def _():
-                    block = me + PAIR * distance
-                    arrive(block, part)
-                    pass_on(block, part, None, line_at > 0, False, act)
+                def relay(sign, way, more):
+                    block = me + sign * PAIR * distance
+                    arrive(block, part, 0)
+                    pl.when(more)(lambda: act(copy(block, part, 0, way)))
+                    act(copy(block, part, 0, 0))
+                    if across_first:
+                        for passing in (block, other + sign * PAIR * distance):
+                            arrive(passing, part, 1)
+                            pl.when(more)(lambda: act(copy(passing, part, 1, way)))
+
+                pl.when(line_at >= distance)(lambda: relay(-1, 1, up))
+                pl.when(line_at + distance < line_size)(lambda: relay(1, 2, down))
 
     def start_own(part):
         own_part(part, lambda c: c.start())
@@ -441,15 +452,15 @@
         keep.start()
         others(
             lambda c: c.start(),
-            lambda block, part: copy(block, part, 0, False).wait_recv(),
+            lambda block, part, side: copy(block, part, side, 0).wait_recv(),
             between,
         )
         for place in range(line_size):
             for part in range(CHUNKS):
-                copy(place * PAIR + 1 - pair_at, part, 0, False).wait_recv()
+                copy(place * PAIR + 1 - pair_at, part, 0, 0).wait_recv()
         for part in range(CHUNKS):
             own_part(part, lambda c: c.wait_send())
-        others(lambda c: c.wait_send(), lambda block, part: None, lambda distance: None)
+        others(lambda c: c.wait_send(), lambda block, part, side: None, lambda distance: None)
         keep.wait()
 
     return start_own, finish
@@ -457,94 +468,154 @@
 
 def gather_scratch(ctx_size):
     return [
-        pltpu.SemaphoreType.DMA((3, ctx_size * CHUNKS)),
-        pltpu.SemaphoreType.DMA((ctx_size * CHUNKS,)),
+        pltpu.SemaphoreType.DMA((3, ctx_size * CHUNKS * 2)),
+        pltpu.SemaphoreType.DMA((ctx_size * CHUNKS * 2,)),
         pltpu.SemaphoreType.DMA,
     ]
 
 
-def scatter_phase(line_size, x_ref, sum_ref, near, below, above, near_send, near_sem, line_send, line_sem, emit, midway=lambda: None):
+def scatter_phase(
+    line_size, along_first, x_ref, sum_ref, near, below, above, pass_far, below_far, above_far, across,
+    near_send, near_sem, line_send, line_sem, far_send, far_sem, across_send, across_sem, emit,
+    midway=lambda: None,
+):
     me = lax.axis_index("ctx")
     line_at, pair_at = me // PAIR, me % PAIR
-    rows = sum_ref.shape[0]
+    other = me + 1 - 2 * pair_at
+    rows, width = sum_ref.shape
     step = rows // CHUNKS
+    split = width - along_first
+    head, tail = slice(0, split), slice(split, width)
     last = line_size - 1
+    up, down = line_at < last, line_at > 0
     low = line_at // (line_size // 2)
     order = [k + (last - 2 * k) * (1 - low) for k in range(line_size // 2)]
     order += [line_at + 1 - 2 * (line_at % 2), line_at]
+    wide = lambda ref: ref.astype(jnp.float32)
 
     def near_copy(place, part):
         start = (place * PAIR + 1 - pair_at) * rows + part * step
         return pltpu.make_async_remote_copy(
-            src_ref=x_ref.at[pl.ds(pl.multiple_of(start, step), step), :],
+            src_ref=x_ref.at[pl.ds(pl.multiple_of(start, step), step), head],
             dst_ref=near.at[place, pl.ds(part * step, step), :],
             send_sem=near_send.at[place, part],
             recv_sem=near_sem.at[place, part],
-            device_id={"ctx": me + 1 - 2 * pair_at},
+            device_id={"ctx": other},
             device_id_type=MESH,
         )
 
-    def line_copy(place, part, up):
+    def line_copy(place, part, upward):
         part_rows = pl.ds(part * step, step)
         return pltpu.make_async_remote_copy(
             src_ref=near.at[place, part_rows, :],
-            dst_ref=(below if up else above).at[place, part_rows, :],
+            dst_ref=(below if upward else above).at[place, part_rows, :],
             send_sem=line_send.at[place, part],
-            recv_sem=line_sem.at[0 if up else 1, place, part],
-            device_id={"ctx": me + PAIR if up else me - PAIR},
+            recv_sem=line_sem.at[0 if upward else 1, place, part],
+            device_id={"ctx": me + PAIR if upward else me - PAIR},
             device_id_type=MESH,
         )
 
-    def mine(place, part):
-        start = (place * PAIR + pair_at) * rows + part * step
-        return x_ref[pl.ds(pl.multiple_of(start, step), step), :].astype(jnp.float32)
+    def far_copy(block, part, upward):
+        part_rows = pl.ds(part * step, step)
+        return pltpu.make_async_remote_copy(
+            src_ref=pass_far.at[block, part_rows, :],
+            dst_ref=(below_far if upward else above_far).at[block, part_rows, :],
+            send_sem=far_send.at[block, part],
+            recv_sem=far_sem.at[0 if upward else 1, block, part],
+            device_id={"ctx": me + PAIR if upward else me - PAIR},
+            device_id_type=MESH,
+        )
+
+    def across_copy(part):
+        part_rows = pl.ds(part * step, step)
+        return pltpu.make_async_remote_copy(
+            src_ref=pass_far.at[other, part_rows, :],
+            dst_ref=across.at[part_rows, :],
+            send_sem=across_send.at[part],
+            recv_sem=across_sem.at[part],
+            device_id={"ctx": other},
+            device_id_type=MESH,
+        )
+
+    def mine(block, part, columns):
+        start = block * rows + part * step
+        return wide(x_ref[pl.ds(pl.multiple_of(start, step), step), columns])
 
     for place in order:
         for part in range(CHUNKS):
             near_copy(place, part).start()
 
+    def send(place, part, upward):
+        part_rows = pl.ds(part * step, step)
+        waits = down if upward else up
+        if along_first:
+            arrived = below_far if upward else above_far
+            for pair in range(PAIR):
+                block = place * PAIR + pair
+                pass_far[block, part_rows, :] = mine(block, part, tail).astype(pass_far.dtype)
+
+                @pl.when(waits)
+                def _():
+                    far_copy(block, part, upward).wait_recv()
+                    pass_far[block, part_rows, :] = (
+                        mine(block, part, tail) + wide(arrived[block, part_rows, :])
+                    ).astype(pass_far.dtype)
+
+                far_copy(block, part, upward).start()
+        near_copy(place, part).wait_recv()
+        total = mine(place * PAIR + pair_at, part, head) + wide(near[place, part_rows, :])
+        arrived_near = below if upward else above
+
+        @pl.when(waits)
+        def _():
+            line_copy(place, part, upward).wait_recv()
+            near[place, part_rows, :] = (total + wide(arrived_near[place, part_rows, :])).astype(near.dtype)
+
+        @pl.when(jnp.logical_not(waits))
+        def _():
+            near[place, part_rows, :] = total.astype(near.dtype)
+
+        line_copy(place, part, upward).start()
+
     for place in order[:-1]:
         for part in range(CHUNKS):
+            pl.when(place > line_at)(lambda: send(place, part, True))
+            pl.when(place < line_at)(lambda: send(place, part, False))
+
+    def add_far(block, part, total_ref, total_rows, total_columns):
+        part_rows = pl.ds(part * step, step)
+        for there, arrived, upward in ((down, below_far, True), (up, above_far, False)):
+
+            @pl.when(there)
+            def _():
+                far_copy(block, part, upward).wait_recv()
+                total_ref[total_rows, total_columns] += wide(arrived[block, part_rows, :])
+
+    if along_first:
+        for part in range(CHUNKS):
             part_rows = pl.ds(part * step, step)
-            near_copy(place, part).wait_recv()
-
-            def send(up, waits, arrived):
-                @pl.when(waits)
-                def _():
-                    line_copy(place, part, up).wait_recv()
-                    near[place, part_rows, :] = (
-                        mine(place, part)
-                        + near[place, part_rows, :].astype(jnp.float32)
-                        + arrived[place, part_rows, :].astype(jnp.float32)
-                    ).astype(near.dtype)
-
-                @pl.when(jnp.logical_not(waits))
-                def _():
-                    near[place, part_rows, :] = (
-                        mine(place, part) + near[place, part_rows, :].astype(jnp.float32)
-                    ).astype(near.dtype)
-
-                line_copy(place, part, up).start()
-
-            pl.when(place > line_at)(lambda: send(True, line_at > 0, below))
-            pl.when(place < line_at)(lambda: send(False, line_at < last, above))
-
+            sum_ref[part_rows, tail] = mine(other, part, tail)
+            add_far(other, part, sum_ref, part_rows, tail)
+            pass_far[pl.ds(other, 1), part_rows, :] = sum_ref[part_rows, tail].astype(pass_far.dtype)[None]
+            across_copy(part).start()
     midway()
     for part in range(CHUNKS):
         part_rows = pl.ds(part * step, step)
+        if along_first:
+            sum_ref[part_rows, tail] = mine(me, part, tail)
+            add_far(me, part, sum_ref, part_rows, tail)
         near_copy(line_at, part).wait_recv()
-        sum_ref[part_rows, :] = mine(line_at, part) + near[line_at, part_rows, :].astype(jnp.float32)
-
-        @pl.when(line_at > 0)
-        def _():
-            line_copy(line_at, part, True).wait_recv()
-            sum_ref[part_rows, :] += below[line_at, part_rows, :].astype(jnp.float32)
-
-        @pl.when(line_at < last)
-        def _():
-            line_copy(line_at, part, False).wait_recv()
-            sum_ref[part_rows, :] += above[line_at, part_rows, :].astype(jnp.float32)
-
+        sum_ref[part_rows, head] = mine(me, part, head) + wide(near[line_at, part_rows, :])
+        for there, arrived, upward in ((down, below, True), (up, above, False)):
+
+            @pl.when(there)
+            def _():
+                line_copy(line_at, part, upward).wait_recv()
+                sum_ref[part_rows, head] += wide(arrived[line_at, part_rows, :])
+
+        if along_first:
+            across_copy(part).wait_recv()
+            sum_ref[part_rows, tail] += wide(across[part_rows, :])
         emit(part, slice(part * step, (part + 1) * step))
 
     def finish():
@@ -554,21 +625,38 @@
         for place in order[:-1]:
             for part in range(CHUNKS):
                 line_copy(place, part, True).wait_send()
+                if along_first:
+                    for pair in range(PAIR):
+                        far_copy(place * PAIR + pair, part, True).wait_send()
+        if along_first:
+            for part in range(CHUNKS):
+                across_copy(part).wait_send()
 
     return finish
 
 
-def scatter_scratch(ctx_size, rows, width):
+def scatter_scratch(ctx_size, rows, width, along_first):
     line_size = ctx_size // PAIR
-    held = pltpu.VMEM((line_size, rows, width), jnp.bfloat16)
+    dma = pltpu.SemaphoreType.DMA
+    held = pltpu.VMEM((line_size, rows, width - along_first), jnp.bfloat16)
+    far_blocks, far_width = (ctx_size, along_first) if along_first else (1, 128)
+    far = pltpu.VMEM((far_blocks, rows, far_width), jnp.bfloat16)
     return [
         held,
         held,
         held,
-        pltpu.SemaphoreType.DMA((line_size, CHUNKS)),
-        pltpu.SemaphoreType.DMA((line_size, CHUNKS)),
-        pltpu.SemaphoreType.DMA((line_size, CHUNKS)),
-        pltpu.SemaphoreType.DMA((2, line_size, CHUNKS)),
+        far,
+        far,
+        far,
+        pltpu.VMEM((rows, far_width), jnp.bfloat16),
+        dma((line_size, CHUNKS)),
+        dma((line_size, CHUNKS)),
+        dma((line_size, CHUNKS)),
+        dma((2, line_size, CHUNKS)),
+        dma((ctx_size, CHUNKS)),
+        dma((2, ctx_size, CHUNKS)),
+        dma((CHUNKS,)),
+        dma((CHUNKS,)),
     ]
 
 
@@ -690,7 +778,7 @@
     for pair in range(count // 2):
         cols = slice(pair * 2 * held, (pair + 1) * 2 * held)
         gains_ref[:, cols] = tiles[2 * pair] + tiles[2 * pair + 1]
-    start_own, finish_gather = gather_phase(ctx_size // PAIR, normed, out_ref, *sems)
+    start_own, finish_gather = gather_phase(ctx_size // PAIR, 0, normed, out_ref, *sems)
     step = rows // CHUNKS
     for part in range(CHUNKS):
         part_rows = slice(part * step, (part + 1) * step)
@@ -772,7 +860,7 @@
     line_size = ctx_size // PAIR
     me = lax.axis_index("ctx")
     greet_line(pltpu.get_barrier_semaphore(), me, me // PAIR, line_size)
-    start_own, finish_gather = gather_phase(line_size, normed, out_ref, *sems[7:])
+    start_own, finish_gather = gather_phase(line_size, EVEN, normed, out_ref, *sems[15:])
 
     def emit(part, rows):
         hidden = tokens_ref[rows, :].astype(jnp.float32) + RESIDUAL_MULT * sums[rows, :]
@@ -782,7 +870,7 @@
         normed[rows, :] = swap_lanes(scaled, ctx_size, fsdp_size).astype(normed.dtype)
         start_own(part)
 
-    finish_scatter = scatter_phase(line_size, x_ref, sums, *sems[:7], emit)
+    finish_scatter = scatter_phase(line_size, EVEN, x_ref, sums, *sems[:15], emit)
     finish_gather()
     finish_scatter()
 
@@ -794,7 +882,7 @@
     line_size = ctx_size // PAIR
     me = lax.axis_index("ctx")
     greet_line(pltpu.get_barrier_semaphore(), me, me // PAIR, line_size)
-    start_own, finish_gather = gather_phase(line_size, normed, out_ref, *sems[7:])
+    start_own, finish_gather = gather_phase(line_size, EVEN, normed, out_ref, *sems[15:])
 
     def emit(part, rows):
         grad_norm = swap_lanes(sums[rows, :], fsdp_size, ctx_size)
@@ -809,7 +897,7 @@
         normed[rows, :] = (RESIDUAL_MULT * grad_hidden).astype(normed.dtype)
         start_own(part)
 
-    finish_scatter = scatter_phase(line_size, x_ref, sums, *sems[:7], emit)
+    finish_scatter = scatter_phase(line_size, EVEN, x_ref, sums, *sems[:15], emit)
     finish_gather()
     finish_scatter()
 
@@ -823,7 +911,7 @@
         in_specs=in_vmem(1 + len(others)),
         out_specs=tuple(in_vmem(len(extra_shapes))) + (ANYWHERE,),
         scratch_shapes=[pltpu.VMEM((rows, model), jnp.float32), pltpu.VMEM((rows, model), jnp.bfloat16)]
-        + scatter_scratch(ctx_size, rows, model)
+        + scatter_scratch(ctx_size, rows, model, EVEN)
         + gather_scratch(ctx_size),
         compiler_params=pltpu.CompilerParams(
             collective_id=collective_id, has_side_effects=True, vmem_limit_bytes=40 * 2**20
@@ -917,7 +1005,7 @@
     for which in (1, 0):
         for j in range(1, fsdp_size):
             near_copy(which, j).start()
-    finish_scatter = scatter_phase(line_size, x_ref, sums, *sems, emit, midway)
+    finish_scatter = scatter_phase(line_size, EVEN_LAST, x_ref, sums, *sems, emit, midway)
     row = lax.broadcasted_iota(jnp.int32, (8, 128), 0)
     for pair in range(count // 2):
         cols = slice(pair * 128, (pair + 1) * 128)
@@ -984,7 +1072,7 @@
             dma((ctx_size,)),
             dma((ctx_size,)),
         ]
-        + scatter_scratch(ctx_size, rows, model),
+        + scatter_scratch(ctx_size, rows, model, EVEN_LAST),
         compiler_params=pltpu.CompilerParams(
             collective_id=3, has_side_effects=True, vmem_limit_bytes=40 * 2**20
         ),
@@ -1172,13 +1260,13 @@
     normed1, gains, w_qkv, gu_mine = start_layer(
         tokens[0], gain_tile, qkv_parts.transpose(1, 0, 2), w_gate, w_up
     )
+    normed1, grad_mlp = lax.optimization_barrier(
+        (normed1, (RESIDUAL_MULT * cotangent[0].astype(jnp.float32)).astype(bf16))
+    )
     w_gu = lax.all_gather(gu_mine, "fsdp", axis=0, tiled=True)
-    grad_out = cotangent[0].astype(jnp.float32)
-    grad_mlp = (RESIDUAL_MULT * grad_out).astype(bf16)
 
     block_rows = math.gcd(length, 256)
     qkv = dot_plain(normed1, w_qkv)
-    qkv, grad_mlp = lax.optimization_barrier((qkv, grad_mlp))
     grad_mlp = lax.all_gather(grad_mlp, "ctx", axis=0, tiled=True)
     q, kv, mixed_heads, log_sum = attention_forward(qkv, tables, block_rows)
     hidden, normed2 = mlp_forward(dot_plain(mixed_heads, wo_mine).astype(bf16), tokens[0], gains)

time: 624 us -> 621 us (level)
  waiting for transfers between devices: 86.8 us -> 79 us
    reduce_scatter x1, waiting for transfers between devices: 60.2 us -> 45.9 us  [on_device(): branch = lax.psum_scatter(out_terms, 'ctx', scatter_dimension=0, tiled=True)]
    all_gather x1, waiting for transfers between devices: 24 us -> 30.4 us  [on_device(): grad_mlp = lax.all_gather(grad_mlp, 'ctx', axis=0, tiled=True)]
    unnamed x64 -> x62, local copies, waits for them, and re-layouts: 21.7 us -> 21.6 us
  transfers between devices with their start and end apart: 8 -> 8, of which waited for: 2 -> 2; matrix products, arithmetic and copies ran while one was open for 10% -> 10% of each run, Pallas kernels for 61% -> 62%
where the time goes in v7:
time: 621 us; the launch traced here: 618 us
  Pallas kernels  382 us (62%)
  matrix products  89.9 us (14%)
  waiting for transfers between devices  79 us (13%)
  local copies, waits for them, and re-layouts  31.2 us (5%)
  between operations  14.9 us (2%)
  other arithmetic  14.6 us (2%)
  starting transfers between devices  6.83 us (1%)
    pallas_call x2, Pallas kernels, scatter_gather(): pl.pallas_call(functools.partial(kernel, ctx_size, fsdp_size), out_shape=...  200 us
    pallas_call x1, Pallas kernels, start_layer(): pl.pallas_call(functools.partial(start_kernel, ctx_size, fsdp_size), out_...  98.1 us
    pallas_call x1, Pallas kernels, finish_layer(): pl.pallas_call(functools.partial(finish_kernel, ctx_size, fsdp_size), out...  61.8 us
    reduce_scatter x1, waiting for transfers between devices, on_device(): branch = lax.psum_scatter(out_terms, 'ctx', scatter_dimension=0, tiled=True)  45.9 us
    dot_general x4, matrix products, dot_back(): lax.dot_general(left, right, (((1,), (1,)), ((), ())), preferred_element_...  30.5 us
    all_gather x1, waiting for transfers between devices, on_device(): grad_mlp = lax.all_gather(grad_mlp, 'ctx', axis=0, tiled=True)  30.4 us
    dot_general x4, matrix products, dot_outer(): lax.dot_general(left, right, (((0,), (0,)), ((), ())), preferred_element_...  30 us
    dot_general x4, matrix products, dot_plain(): return jnp.dot(left, right, preferred_element_type=jnp.float32)  29.5 us
  transfers between devices with their start and end apart: 8, of which 2 were waited for; matrix products, arithmetic and copies ran while one was open for 10% of the time, Pallas kernels for 62%

profile of v7, /device:TPU:0, one launch (start us, length us, event | category | flops | bytes accessed | tf_op | source)
XLA Modules:
  0.0 618.3 jit_solution(13085374958468093199)
XLA Ops:
  7.2 0.7 all-gather.5.cloned.1.call-update
  8.0 1.0 reshape.98
  9.0 1.0 reshape.97
  10.1 1.0 copy.75
  11.0 0.7 convert_multiply_fusion.1
  11.9 1.0 copy-done
  13.0 1.2 copy-done.7
  14.2 1.2 copy-done.8
  15.4 98.1 %start_layer.1 = (bf16[1024,2048]{1,0:T(8,128)(2,1)S(1)}, f32[8,2048]{1,0:T(8,128)S(1)}, bf16[32,64,384]{2,1,0:T(8,128)(2,1)S(1)}, bf16[8,64,2048]{2,1,0:T(8,128)(2,1)}) custom-call(bf16[128,2048]{1,0:T(8,128)(2,1)S(1)} %bitcast.69, f32[8,128]{1,0:T(8,128)S(1)} %select_maximum_fusion.tile_ref, bf16[8,64,384]{2,1,0:T(8,128)(2,1)S(1)} %maximum_bitcast_fusion.parts_ref, ...), custom_call_target="tpu_custom_call" | custom-call | bytes 150000000 | tf_op jit(solution)/shard_map/start_layer/pallas_call | solution.py:823
  113.6 1.9 copy-done.18
  115.5 1.1 copy-done.23
  116.7 0.7 all-gather.9.cloned.1.call-update
  117.5 0.9 multiply_convert_fusion.2
  118.4 0.6 reduce-scatter.6.cloned.1.call-start
  119.0 0.2 reduce-window_clone.1
  119.3 0.2 copy.57.doc_col_ref
  119.5 1.9 fusion.2
  121.4 0.9 pad_maximum_fusion.3
  122.3 3.7 fusion.5.qkv_ref
  126.1 8.2 %attend.1 = (bf16[1024,256]{1,0:T(8,128)(2,1)S(1)}, bf16[1024,128]{1,0:T(8,128)(2,1)S(1)}, bf16[1024,256]{1,0:T(8,128)(2,1)S(1)}, f32[1024,4]{1,0:T(8,128)S(1)}) custom-call(f32[1024,384]{1,0:T(8,128)S(1)} %fusion.5.qkv_ref, f32[1024,128]{1,0:T(8,128)S(1)} %get-tuple-element.84.cos_ref, f32[1024,128]{1,0:T(8,128)S(1)} %get-tuple-element.85.sin_ref, ...), custom_call_target="tpu_custom_call" | custom-call | tf_op jit(solution)/shard_map/attend/pallas_call | solution.py:1186
  134.3 0.8 copy-done.14
  135.1 3.1 convolution_convert_fusion.3.x_ref
  138.2 90.5 %shard_map.203 = (f32[128,2048]{1,0:T(8,128)S(1)}, bf16[1024,2048]{1,0:T(8,128)(2,1)S(1)}) custom-call(bf16[1024,2048]{1,0:T(8,128)(2,1)S(1)} %convolution_convert_fusion.3.x_ref, bf16[128,2048]{1,0:T(8,128)(2,1)S(1)} %bitcast.70, f32[8,2048]{1,0:T(8,128)S(1)} %get-tuple-element.45.gains_ref), custom_call_target="tpu_custom_call" | custom-call | bytes 150000000 | tf_op jit(solution)/shard_map/pallas_call | solution.py:908
  228.7 2.0 copy-done.20
  230.7 12.7 %fusion.6 = f32[1024,2048]{1,0:T(8,128)S(1)} fusion(bf16[1024,2048]{1,0:T(8,128)(2,1)} %copy-done.20, bf16[2048,2048]{1,0:T(8,128)(2,1)} %all-gather.7.cloned.1.call-done), kind=kOutput, calls=%fused_computation.48 | convolution fusion | flops 8589934592 | bytes 20971520 | tf_op jit(solution)/shard_map/dot_general | solution.py:61
  243.5 3.2 copy-done.25
  246.7 2.7 fusion
  249.5 9.9 %convolution_convert_fusion.5 = bf16[1024,2048]{1,0:T(8,128)(2,1)} fusion(bf16[1024,1024]{1,0:T(8,128)(2,1)} %fusion, bf16[1024,2048]{1,0:T(8,128)(2,1)} %all-gather.9.cloned.1.call-done), kind=kOutput, calls=%fused_computation.11 | convolution fusion | flops 4297064448 | bytes 10485760 | tf_op jit(solution)/shard_map/dot_general | solution.py:61
  259.4 30.4 %all-gather.11.cloned.1.call-done = bf16[1024,2048]{1,0:T(8,128)(2,1)} async-done(((bf16[128,2048]{1,0:T(8,128)(2,1)}), bf16[1024,2048]{1,0:T(8,128)(2,1)}) %all-gather.11.cloned.1.call-update) | async-done | bytes 4194320 | tf_op jit(solution)/shard_map/all_gather | solution.py:1270
  289.8 9.4 %convolution_convert_fusion.4 = bf16[1024,2048]{1,0:T(8,128)(2,1)} fusion(bf16[1024,1024]{1,0:T(8,128)(2,1)} %fusion, bf16[1024,2048]{1,0:T(8,128)(2,1)} %all-gather.11.cloned.1.call-done), kind=kOutput, calls=%fused_computation.10 | convolution fusion | flops 4297064448 | bytes 10485760 | tf_op jit(solution)/shard_map/dot_general | solution.py:71
  299.2 12.4 %multiply_convert_fusion.1 = (bf16[1024,1024]{1,0:T(8,128)(2,1)S(1)}, bf16[1024,1024]{1,0:T(8,128)(2,1)S(1)}) fusion(f32[1024,2048]{1,0:T(8,128)} %copy-done.25, bf16[1024,2048]{1,0:T(8,128)(2,1)} %all-gather.11.cloned.1.call-done, bf16[1024,2048]{1,0:T(8,128)(2,1)} %all-gather.9.cloned.1.call-done), kind=kOutput, calls=%fused_computation.5 | convolution fusion | flops 4308598784 | bytes 20971520 | tf_op jit(solution)/shard_map/dot_general | solution.py:65
  311.6 1.3 copy-done.28
  312.9 0.7 copy-done.29
  313.6 11.3 %convolution_convert_fusion = bf16[2048,2048]{1,0:T(8,128)(2,1)} fusion(bf16[1024,2048]{1,0:T(8,128)(2,1)S(1)} %copy-done.21, bf16[1024,1024]{1,0:T(8,128)(2,1)S(1)} %get-tuple-element.72, bf16[1024,1024]{1,0:T(8,128)(2,1)S(1)} %get-tuple-element.71), kind=kOutput, calls=%fused_computation | convolution fusion | flops 8602517504 | bytes 16777216 | tf_op jit(solution)/shard_map/dot_general | solution.py:71
  324.9 14.4 %convolution_convert_fusion.2.x_ref = bf16[1024,2048]{1,0:T(8,128)(2,1)} fusion(bf16[2048,2048]{1,0:T(8,128)(2,1)} %all-gather.7.cloned.1.call-done, bf16[1024,1024]{1,0:T(8,128)(2,1)} %copy-done.29, bf16[1024,1024]{1,0:T(8,128)(2,1)} %copy-done.28), kind=kOutput, calls=%fused_computation.8 | convolution fusion | flops 8600420352 | bytes 16777216 | tf_op jit(solution)/shard_map/dot_general | solution.py:65
  339.4 0.5 reduce-scatter.4.cloned.1.call-update
  340.0 0.7 reduce-scatter.8.cloned.1.call-update
  340.7 2.2 copy-done.2
  342.9 1.2 copy-done.4
  344.1 109.7 %shard_map.204 = (f32[128,2048]{1,0:T(8,128)S(1)}, f32[2,2048]{1,0:T(2,128)S(1)}, bf16[1024,2048]{1,0:T(8,128)(2,1)S(1)}) custom-call(bf16[1024,2048]{1,0:T(8,128)(2,1)S(1)} %copy-done.2, f32[128,2048]{1,0:T(8,128)S(1)} %get-tuple-element.46.hidden_ref, bf16[128,2048]{1,0:T(8,128)(2,1)S(1)} %bitcast.72, f32[8,2048]{1,0:T(8,128)S(1)} %get-tuple-element.45.gains_ref), custom_call_target="tpu_custom_call" | custom-call | bytes 150000000 | tf_op jit(solution)/shard_map/pallas_call | solution.py:908
  453.9 1.3 convolution_convert_fusion.8.do_ref
  455.2 0.9 copy-done.22
  456.2 13.5 %attend_back.1 = bf16[1024,384]{1,0:T(8,128)(2,1)S(1)} custom-call(bf16[1024,256]{1,0:T(8,128)(2,1)S(1)} %copy-done.15, bf16[1024,128]{1,0:T(8,128)(2,1)S(1)} %get-tuple-element.53.kv_ref, bf16[1024,256]{1,0:T(8,128)(2,1)S(1)} %convolution_convert_fusion.8.do_ref, f32[1024,4]{1,0:T(8,128)S(1)} %copy-done.17, f32[1024,128]{1,0:T(8,128)S(1)} %get-tuple-element.84.cos_ref, ...), custom_call_target="tpu_custom_call" | custom-call | tf_op jit(solution)/shard_map/attend_back/pallas_call | solution.py:1203
  469.7 0.9 copy-done.12
  470.5 6.0 all-to-all-start
  476.6 4.6 convolution_convert_fusion.7
  481.2 45.9 %reduce-scatter.4.cloned.1.call-done = bf16[128,2048]{1,0:T(8,128)(2,1)} async-done(((bf16[1024,2048]{1,0:T(8,128)(2,1)}), bf16[128,2048]{1,0:T(8,128)(2,1)}) %reduce-scatter.4.cloned.1.call-update) | async-done | bytes 524304 | tf_op jit(solution)/shard_map/reduce_scatter | solution.py:1286
  527.1 2.0 fusion.1
  529.1 4.7 convolution_convert_fusion.6
  533.8 0.2 copy.74
  534.0 2.4 convolution_convert_fusion.1.x_ref
  536.4 61.8 %finish_layer.1 = (f32[128,2048]{1,0:T(8,128)S(1)}, f32[8,128]{1,0:T(8,128)S(1)}, f32[64,2048]{1,0:T(8,128)S(1)}, bf16[8,64,384]{2,1,0:T(8,128)(2,1)S(1)}) custom-call(bf16[1024,2048]{1,0:T(8,128)(2,1)S(1)} %convolution_convert_fusion.1.x_ref, bf16[128,2048]{1,0:T(8,128)(2,1)S(1)} %bitcast.71, f32[128,2048]{1,0:T(8,128)S(1)} %copy-done.10, ...), custom_call_target="tpu_custom_call" | custom-call | bytes 150000000 | tf_op jit(solution)/shard_map/finish_layer/pallas_call | solution.py:1050
  598.3 0.8 copy.69
  599.3 0.2 copy.63
  599.4 0.8 reshape.105
  600.2 0.2 copy.64
  600.4 0.8 reshape.106
  601.1 2.8 convert_element_type.167
  604.0 0.5 slice_bitcast_fusion
  604.5 2.0 convert_bitcast_fusion
  606.5 1.5 copy.70
  608.0 1.5 copy.71
  609.4 1.0 copy.78
  610.4 0.8 copy.79
  (73 shorter events, 1.0 us)
Async XLA Ops:
  7.2 127.9 %all-gather.5.cloned.1.call-start = ((), (), s32[]{:S(2)}) async-start(), calls=%async_computation.4 | async-start | bytes 1310720 | tf_op jit(solution)/shard_map/all_gather | solution.py:1254
  7.9 222.8 %all-gather.7.cloned.1.call-start = ((), (), s32[]{:S(2)}) async-start(), calls=%async_computation.5 | async-start | bytes 10485760 | tf_op jit(solution)/shard_map/all_gather | solution.py:1266
  9.0 108.5 %copy-start.3 = (bf16[1,128,2048]{2,1,0:T(8,128)(2,1)S(1)}, bf16[1,128,2048]{2,1,0:T(8,128)(2,1)}, u32[]{:S(2)}) copy-start(bf16[1,128,2048]{2,1,0:T(8,128)(2,1)} %param.14) | copy-start | bytes 1572868
  11.8 107.2 %copy-start.27 = (s32[1,8]{1,0:T(1,128)S(1)}, s32[1,8]{1,0:T(1,128)}, u32[]{:S(2)}) copy-start(s32[1,8]{1,0:T(1,128)} %param.13) | copy-start | bytes 100
  11.9 1.0 copy-start
  13.0 1.2 copy-start.7
  14.2 1.2 copy-start.8
  113.5 2.0 copy-start.18
  115.5 1.1 copy-start.23
  116.7 132.8 %all-gather.9.cloned.1.call-start = ((), (), s32[]{:S(2)}) async-start(), calls=%async_computation.6 | async-start | bytes 5242880 | tf_op jit(solution)/shard_map/all_gather | solution.py:1255
  117.4 172.4 %all-gather.11.cloned.1.call-start = ((), (), s32[]{:S(2)}) async-start(), calls=%async_computation.7 | async-start | bytes 4718592 | tf_op jit(solution)/shard_map/all_gather | solution.py:1270
  118.4 352.1 %reduce-scatter.6.cloned.1.call-start = ((), (), s32[]{:S(2)}) async-start(), calls=%async_computation.9 | async-start | bytes 10485760 | tf_op jit(solution)/shard_map/reduce_scatter | solution.py:1302
  119.5 2.8 copy-start.19
  134.3 0.8 copy-start.14
  135.1 3.1 copy-start.5
  135.1 3.1 copy-start.16
  135.1 3.1 copy-start.1
  228.7 2.0 copy-start.20
  243.5 3.2 copy-start.25
  299.2 14.4 %copy-start.21 = (bf16[1024,2048]{1,0:T(8,128)(2,1)S(1)}, bf16[1024,2048]{1,0:T(8,128)(2,1)}, u32[]{:S(2)}) copy-start(bf16[1024,2048]{1,0:T(8,128)(2,1)} %copy-done.20) | copy-start | bytes 12582916
  311.6 1.3 copy-start.28
  311.6 2.0 copy-start.29
  339.4 187.7 %reduce-scatter.4.cloned.1.call-start = ((), (), s32[]{:S(2)}) async-start(), calls=%async_computation.8 | async-start | bytes 4718592 | tf_op jit(solution)/shard_map/reduce_scatter | solution.py:1286
  340.0 258.3 %reduce-scatter.8.cloned.1.call-start = ((), (), s32[]{:S(2)}) async-start(), calls=%async_computation.10 | async-start | bytes 5242880 | tf_op jit(solution)/shard_map/reduce_scatter | solution.py:1303
  340.7 2.2 copy-start.2
  342.9 1.2 copy-start.4
  344.1 109.8 %copy-start.26 = (bf16[256,2048]{1,0:T(8,128)(2,1)S(1)}, bf16[256,2048]{1,0:T(8,128)(2,1)}, u32[]{:S(2)}) copy-start(bf16[256,2048]{1,0:T(8,128)(2,1)} %all-gather.5.cloned.1.call-done) | copy-start | bytes 3145732
  453.9 1.4 copy-start.9
  453.9 2.3 copy-start.22
  453.9 2.3 copy-start.15
  453.9 2.3 copy-start.17
  469.6 0.9 copy-start.12
  470.5 6.0 copy-start.6
  470.5 134.0 %all-to-all-start = ((bf16[8,64,2048]{2,1,0:T(8,128)(2,1)}), bf16[8,64,2048]{2,1,0:T(8,128)(2,1)}, u32[]{:S(2)}, u32[]{:S(2)}) async-start(bf16[8,64,2048]{2,1,0:T(8,128)(2,1)} %bitcast.80), calls=%async_computation.3 | async-start | bytes 4194304 | tf_op jit(solution)/shard_map/all_to_all | solution.py:1085
  476.6 52.5 %copy-start.13 = (bf16[1024,384]{1,0:T(8,128)(2,1)S(1)}, bf16[1024,384]{1,0:T(8,128)(2,1)}, u32[]{:S(2)}) copy-start(bf16[1024,384]{1,0:T(8,128)(2,1)} %copy-done.12) | copy-start | bytes 2359300
  529.1 4.9 copy-start.24
  534.0 2.4 copy-start.10
  534.0 2.4 copy-start.11
Sparse Core Ops, SparseCore 0:
  9.5 24.2 all-gather.4
  116.8 61.5 all-gather.6
  179.9 34.4 all-gather.8
  217.0 72.7 all-gather.10
  339.5 69.9 reduce-scatter.5
  413.0 114.0 reduce-scatter.3
  529.6 64.5 reduce-scatter.7

commit v8 on v6

--- a/solution.py
+++ b/solution.py
@@ -355,7 +355,10 @@
     return [pl.BlockSpec(memory_space=pltpu.VMEM)] * count
 
 
-def greet_line(barrier, ctx_at, line_at, line_size):
+def greet_line(barrier, ctx_at, line_at, line_size, fsdp_size=1):
+    for j in range(1, fsdp_size):
+        peer = (lax.axis_index("fsdp") + j) % fsdp_size
+        pl.semaphore_signal(barrier, inc=1, device_id={"fsdp": peer}, device_id_type=MESH)
     other = ctx_at + 1 - 2 * (ctx_at % PAIR)
     pl.semaphore_signal(barrier, inc=1, device_id={"ctx": other}, device_id_type=MESH)
 
@@ -368,7 +371,7 @@
         pl.semaphore_signal(barrier, inc=1, device_id={"ctx": ctx_at + PAIR}, device_id_type=MESH)
 
     last = line_size - 1
-    neighbours = 1 + (line_at + last - 1) // last + (2 * last - 1 - line_at) // last
+    neighbours = fsdp_size + (line_at + last - 1) // last + (2 * last - 1 - line_at) // last
     pl.semaphore_wait(barrier, neighbours)
 
 
@@ -788,12 +791,28 @@
 
 
 def mlp_backward_kernel(
-    ctx_size, fsdp_size, x_ref, hidden_ref, grad_ref, gains_ref, grad_hidden_ref, grad_gain_ref, out_ref,
-    sums, normed, *sems
+    ctx_size, fsdp_size, x_ref, hidden_ref, grad_ref, gains_ref, terms_ref, grad_hidden_ref, grad_gain_ref,
+    total_ref, out_ref, sums, normed, landing, side_send, side_recv, own_sem, *sems
 ):
     line_size = ctx_size // PAIR
-    me = lax.axis_index("ctx")
-    greet_line(pltpu.get_barrier_semaphore(), me, me // PAIR, line_size)
+    me, me_fsdp = lax.axis_index("ctx"), lax.axis_index("fsdp")
+    greet_line(pltpu.get_barrier_semaphore(), me, me // PAIR, line_size, fsdp_size)
+
+    def side_copy(j):
+        target = (me_fsdp + j) % fsdp_size
+        return pltpu.make_async_remote_copy(
+            src_ref=terms_ref.at[target],
+            dst_ref=landing.at[j],
+            send_sem=side_send.at[j],
+            recv_sem=side_recv.at[j],
+            device_id={"fsdp": target},
+            device_id_type=MESH,
+        )
+
+    own_copy = pltpu.make_async_copy(terms_ref.at[me_fsdp], landing.at[0], own_sem)
+    for j in range(1, fsdp_size):
+        side_copy(j).start()
+    own_copy.start()
     start_own, finish_gather = gather_phase(line_size, normed, out_ref, *sems[7:])
 
     def emit(part, rows):
@@ -811,22 +830,39 @@
 
     finish_scatter = scatter_phase(line_size, x_ref, sums, *sems[:7], emit)
     finish_gather()
+    own_copy.wait()
+    for j in range(1, fsdp_size):
+        side_copy(j).wait_recv()
+    step = 64
+
+    def add(at, unused):
+        rows = pl.ds(pl.multiple_of(at * step, step), step)
+        total = landing[0, rows, :].astype(jnp.float32)
+        for j in range(1, fsdp_size):
+            total += landing[j, rows, :].astype(jnp.float32)
+        total_ref[rows, :] = total.astype(total_ref.dtype)
+        return unused
+
+    lax.fori_loop(0, total_ref.shape[0] // step, add, 0)
+    for j in range(1, fsdp_size):
+        side_copy(j).wait_send()
     finish_scatter()
 
 
-def scatter_gather(kernel, collective_id, extra_shapes, partial, *others):
+def scatter_gather(kernel, collective_id, extra_shapes, partial, *others, specs=(), scratch=()):
     ctx_size, fsdp_size = lax.axis_size("ctx"), lax.axis_size("fsdp")
     rows, model = partial.shape[0] // ctx_size, partial.shape[1]
     return pl.pallas_call(
         functools.partial(kernel, ctx_size, fsdp_size),
         out_shape=extra_shapes + (jax.ShapeDtypeStruct(partial.shape, jnp.bfloat16),),
-        in_specs=in_vmem(1 + len(others)),
+        in_specs=in_vmem(1 + len(others) - len(specs)) + list(specs),
         out_specs=tuple(in_vmem(len(extra_shapes))) + (ANYWHERE,),
         scratch_shapes=[pltpu.VMEM((rows, model), jnp.float32), pltpu.VMEM((rows, model), jnp.bfloat16)]
+        + list(scratch)
         + scatter_scratch(ctx_size, rows, model)
         + gather_scratch(ctx_size),
         compiler_params=pltpu.CompilerParams(
-            collective_id=collective_id, has_side_effects=True, vmem_limit_bytes=40 * 2**20
+            collective_id=collective_id, has_side_effects=True, vmem_limit_bytes=48 * 2**20
         ),
         cost_estimate=LINK_COST,
     )(partial, *others)
@@ -837,10 +873,26 @@
     return scatter_gather(mlp_forward_kernel, 1, (hidden,), partial, tokens, gains)
 
 
-def mlp_backward(partial, hidden, grad_out, gains):
+def mlp_backward(partial, hidden, grad_out, gains, terms):
     like = jax.ShapeDtypeStruct(hidden.shape, jnp.float32)
     gain = jax.ShapeDtypeStruct((CHUNKS, hidden.shape[1]), jnp.float32)
-    return scatter_gather(mlp_backward_kernel, 2, (like, gain), partial, hidden, grad_out, gains)
+    return scatter_gather(
+        mlp_backward_kernel,
+        2,
+        (like, gain, jax.ShapeDtypeStruct(terms.shape[1:], terms.dtype)),
+        partial,
+        hidden,
+        grad_out,
+        gains,
+        terms,
+        specs=(ANYWHERE,),
+        scratch=(
+            pltpu.VMEM(terms.shape, terms.dtype),
+            pltpu.SemaphoreType.DMA((terms.shape[0],)),
+            pltpu.SemaphoreType.DMA((terms.shape[0],)),
+            pltpu.SemaphoreType.DMA,
+        ),
+    )
 
 
 def finish_kernel(
@@ -1196,7 +1248,6 @@
         (dot_plain(activ, wd_mine).astype(bf16), grad_mlp)
     )
     branch = lax.psum_scatter(out_terms, "ctx", scatter_dimension=0, tiled=True)
-    output = (hidden + RESIDUAL_MULT * branch.astype(jnp.float32)).astype(bf16)[None]
 
     silu_slope = sig_gate * (1.0 + gate_pre * (1.0 - sig_gate))
     grad_act = dot_back(grad_mlp, wd_mine)
@@ -1210,15 +1261,15 @@
             dot_outer(activ, grad_mlp).astype(bf16),
         )
     )
-    grad_hidden, grad_g2, grad_attn = mlp_backward(partial2, hidden, cotangent[0], gains)
-    gu_back = lax.psum_scatter(gu_terms, "fsdp", scatter_dimension=0, tiled=True)
+    grad_hidden, grad_g2, gu_back, grad_attn = mlp_backward(
+        partial2, hidden, cotangent[0], gains, gu_terms.reshape(fsdp_size, -1, gu_terms.shape[1])
+    )
+    gu_back = return_columns(gu_back, ctx_size)
     wd_back = lax.psum_scatter(wd_terms, "fsdp", scatter_dimension=0, tiled=True)
 
     grad_mixed = dot_back(grad_attn, wo_mine).astype(bf16)
     wo_terms = dot_outer(mixed_heads, grad_attn).astype(bf16)
     grad_qkv = attention_backward(q, kv, grad_mixed, log_sum, tables, block_rows)
-    grad_qkv, gu_back = lax.optimization_barrier((grad_qkv, gu_back))
-    gu_back = return_columns(gu_back, ctx_size)
     partial1 = dot_back(grad_qkv, w_qkv).astype(bf16)
     qkv_terms = by_fsdp(dot_outer(normed1, grad_qkv).astype(bf16), ctx_size, fsdp_size)
     grad_inputs, gain_back, wo_back, qkv_back = finish_layer(
@@ -1230,7 +1281,10 @@
         wo_terms.reshape(fsdp_size, held_rows, model),
         qkv_terms.reshape(fsdp_size, ctx_size, held_rows, -1),
     )
-    grad_inputs, wd_back = lax.optimization_barrier((grad_inputs, wd_back))
+    grad_inputs, wd_back, gu_back, branch = lax.optimization_barrier(
+        (grad_inputs, wd_back, gu_back, branch)
+    )
+    output = (hidden + RESIDUAL_MULT * branch.astype(jnp.float32)).astype(bf16)[None]
     gain_back = jnp.where(odd == 0, gain_back[:2, :held_rows], gain_back[:2, held_rows:])
 
     def joined(parts):

time: 624 us -> 573 us (0.918)
  waiting for transfers between devices: 86.8 us -> 21.2 us
  Pallas kernels: 376 us -> 397 us
    reduce_scatter x1, waiting for transfers between devices: 60.2 us -> 0.01 us  [on_device(): branch = lax.psum_scatter(out_terms, 'ctx', scatter_dimension=0, tiled=True)]
    pallas_call x2, Pallas kernels: 196 us -> 211 us  [scatter_gather(): pl.pallas_call(functools.partial(kernel, ctx_size, fsdp_size), out_shape=...]
    unnamed x64 -> x52, local copies, waits for them, and re-layouts: 21.7 us -> 17.4 us
  transfers between devices with their start and end apart: 8 -> 7, of which waited for: 2 -> 1; matrix products, arithmetic and copies ran while one was open for 10% -> 18% of each run, Pallas kernels for 61% -> 70%
where the time goes in v8:
time: 573 us; the launch traced here: 569 us
  Pallas kernels  397 us (69%)
  matrix products  88.3 us (15%)
  local copies, waits for them, and re-layouts  27 us (5%)
  waiting for transfers between devices  21.2 us (4%)
  between operations  14.8 us (3%)
  other arithmetic  14.5 us (3%)
  starting transfers between devices  5.94 us (1%)
    pallas_call x2, Pallas kernels, scatter_gather(): pl.pallas_call(functools.partial(kernel, ctx_size, fsdp_size), out_shape=...  211 us
    pallas_call x1, Pallas kernels, start_layer(): pl.pallas_call(functools.partial(start_kernel, ctx_size, fsdp_size), out_...  97.6 us
    pallas_call x1, Pallas kernels, finish_layer(): pl.pallas_call(functools.partial(finish_kernel, ctx_size, fsdp_size), out...  67.1 us
    dot_general x4, matrix products, dot_plain(): return jnp.dot(left, right, preferred_element_type=jnp.float32)  32.3 us
    dot_general x4, matrix products, dot_back(): lax.dot_general(left, right, (((1,), (1,)), ((), ())), preferred_element_...  30.9 us
    dot_general x4, matrix products, dot_outer(): lax.dot_general(left, right, (((0,), (0,)), ((), ())), preferred_element_...  25.1 us
    all_gather x1, waiting for transfers between devices, on_device(): grad_mlp = lax.all_gather(grad_mlp, 'ctx', axis=0, tiled=True)  19.8 us
    unnamed x52, local copies, waits for them, and re-layouts  17.4 us
  transfers between devices with their start and end apart: 7, of which 1 were waited for; matrix products, arithmetic and copies ran while one was open for 18% of the time, Pallas kernels for 70%

profile of v8, /device:TPU:0, one launch (start us, length us, event | category | flops | bytes accessed | tf_op | source)
XLA Modules:
  0.0 568.7 jit_solution(8519713424855063046)
XLA Ops:
  7.2 0.7 all-gather.5.cloned.1.call-update
  8.0 1.0 reshape.100
  9.0 1.0 reshape.101
  10.1 1.0 copy.75
  11.0 0.7 convert_multiply_fusion.1
  11.7 0.1 select_maximum_fusion.tile_ref
  11.8 0.1 maximum_bitcast_fusion.parts_ref
  11.9 1.0 copy-done
  13.0 1.2 copy-done.8
  14.2 1.2 copy-done.9
  15.4 97.6 %start_layer.1 = (bf16[1024,2048]{1,0:T(8,128)(2,1)S(1)}, f32[8,2048]{1,0:T(8,128)S(1)}, bf16[32,64,384]{2,1,0:T(8,128)(2,1)S(1)}, bf16[8,64,2048]{2,1,0:T(8,128)(2,1)}) custom-call(bf16[128,2048]{1,0:T(8,128)(2,1)S(1)} %bitcast.70, f32[8,128]{1,0:T(8,128)S(1)} %select_maximum_fusion.tile_ref, bf16[8,64,384]{2,1,0:T(8,128)(2,1)S(1)} %maximum_bitcast_fusion.parts_ref, ...), custom_call_target="tpu_custom_call" | custom-call | bytes 150000000 | tf_op jit(solution)/shard_map/start_layer/pallas_call | solution.py:738
  113.0 2.0 copy-done.16
  115.0 0.7 all-gather.9.cloned.1.call-update
  115.8 0.9 multiply_convert_fusion.2
  116.7 5.7 fusion.5.qkv_ref
  122.4 0.5 reduce-scatter.5.cloned.1.call-start
  122.9 0.2 reduce-window_clone.1
  123.1 0.1 convert_reduce_fusion
  123.2 0.2 copy.57.doc_col_ref
  123.4 1.9 fusion.2
  125.3 0.9 pad_maximum_fusion.3
  126.2 8.2 %attend.1 = (bf16[1024,256]{1,0:T(8,128)(2,1)S(1)}, bf16[1024,128]{1,0:T(8,128)(2,1)S(1)}, bf16[1024,256]{1,0:T(8,128)(2,1)S(1)}, f32[1024,4]{1,0:T(8,128)S(1)}) custom-call(f32[1024,384]{1,0:T(8,128)S(1)} %copy-done.5, f32[1024,128]{1,0:T(8,128)S(1)} %get-tuple-element.86.cos_ref, f32[1024,128]{1,0:T(8,128)S(1)} %get-tuple-element.87.sin_ref, ...), custom_call_target="tpu_custom_call" | custom-call | tf_op jit(solution)/shard_map/attend/pallas_call | solution.py:1150
  134.5 0.8 copy-done.12
  135.3 0.8 copy-done.14
  136.1 4.8 convolution_convert_fusion.3.x_ref
  140.9 100.5 %shard_map.203 = (f32[128,2048]{1,0:T(8,128)S(1)}, bf16[1024,2048]{1,0:T(8,128)(2,1)S(1)}) custom-call(bf16[1024,2048]{1,0:T(8,128)(2,1)} %convolution_convert_fusion.3.x_ref, bf16[128,2048]{1,0:T(8,128)(2,1)S(1)} %bitcast.71, f32[8,2048]{1,0:T(8,128)S(1)} %get-tuple-element.46.gains_ref), custom_call_target="tpu_custom_call" | custom-call | bytes 150000000 | tf_op jit(solution)/shard_map/pallas_call | solution.py:855
  241.4 2.0 copy-done.18
  243.4 12.5 %fusion.6 = f32[1024,2048]{1,0:T(8,128)S(1)} fusion(bf16[1024,2048]{1,0:T(8,128)(2,1)} %copy-done.18, bf16[2048,2048]{1,0:T(8,128)(2,1)} %all-gather.7.cloned.1.call-done), kind=kOutput, calls=%fused_computation.48 | convolution fusion | flops 8589934592 | bytes 20971520 | tf_op jit(solution)/shard_map/dot_general | solution.py:59
  255.9 3.2 copy-done.22
  259.2 2.7 fusion
  261.9 9.3 %convolution_convert_fusion.5 = bf16[1024,2048]{1,0:T(8,128)(2,1)} fusion(bf16[1024,1024]{1,0:T(8,128)(2,1)} %fusion, bf16[1024,2048]{1,0:T(8,128)(2,1)} %all-gather.9.cloned.1.call-done), kind=kOutput, calls=%fused_computation.11 | convolution fusion | flops 4297064448 | bytes 10485760 | tf_op jit(solution)/shard_map/dot_general | solution.py:59
  271.2 19.8 %all-gather.11.cloned.1.call-done = bf16[1024,2048]{1,0:T(8,128)(2,1)} async-done(((bf16[128,2048]{1,0:T(8,128)(2,1)}), bf16[1024,2048]{1,0:T(8,128)(2,1)}) %all-gather.11.cloned.1.call-update) | async-done | bytes 4194320 | tf_op jit(solution)/shard_map/all_gather | solution.py:1234
  291.0 0.2 reduce-scatter.3.cloned.1.call-start
  291.3 9.4 %convolution_convert_fusion.4 = bf16[1024,2048]{1,0:T(8,128)(2,1)} fusion(bf16[1024,1024]{1,0:T(8,128)(2,1)} %fusion, bf16[1024,2048]{1,0:T(8,128)(2,1)} %all-gather.11.cloned.1.call-done), kind=kOutput, calls=%fused_computation.10 | convolution fusion | flops 4297064448 | bytes 10485760 | tf_op jit(solution)/shard_map/dot_general | solution.py:69
  300.7 11.9 %multiply_convert_fusion.1 = (bf16[1024,1024]{1,0:T(8,128)(2,1)S(1)}, bf16[1024,1024]{1,0:T(8,128)(2,1)S(1)}) fusion(f32[1024,2048]{1,0:T(8,128)} %copy-done.22, bf16[1024,2048]{1,0:T(8,128)(2,1)} %all-gather.11.cloned.1.call-done, bf16[1024,2048]{1,0:T(8,128)(2,1)} %all-gather.9.cloned.1.call-done), kind=kOutput, calls=%fused_computation.5 | convolution fusion | flops 4308598784 | bytes 20971520 | tf_op jit(solution)/shard_map/dot_general | solution.py:63
  312.7 12.0 %convolution_convert_fusion = bf16[2048,2048]{1,0:T(8,128)(2,1)} fusion(bf16[1024,2048]{1,0:T(8,128)(2,1)S(1)} %copy-done.19, bf16[1024,1024]{1,0:T(8,128)(2,1)S(1)} %get-tuple-element.74, bf16[1024,1024]{1,0:T(8,128)(2,1)S(1)} %get-tuple-element.73), kind=kOutput, calls=%fused_computation | convolution fusion | flops 8602517504 | bytes 16777216 | tf_op jit(solution)/shard_map/dot_general | solution.py:69
  324.6 12.7 %convolution_convert_fusion.2.x_ref = bf16[1024,2048]{1,0:T(8,128)(2,1)} fusion(bf16[2048,2048]{1,0:T(8,128)(2,1)} %all-gather.7.cloned.1.call-done, bf16[1024,1024]{1,0:T(8,128)(2,1)S(1)} %get-tuple-element.74, bf16[1024,1024]{1,0:T(8,128)(2,1)S(1)} %get-tuple-element.73), kind=kOutput, calls=%fused_computation.8 | convolution fusion | flops 8600420352 | bytes 16777216 | tf_op jit(solution)/shard_map/dot_general | solution.py:63
  337.4 1.0 copy-done.3
  338.4 110.1 %shard_map.204 = (f32[128,2048]{1,0:T(8,128)S(1)}, f32[2,2048]{1,0:T(2,128)S(1)}, bf16[512,2048]{1,0:T(8,128)(2,1)S(1)}, bf16[1024,2048]{1,0:T(8,128)(2,1)}) custom-call(bf16[1024,2048]{1,0:T(8,128)(2,1)} %convolution_convert_fusion.2.x_ref, f32[128,2048]{1,0:T(8,128)S(1)} %get-tuple-element.47.hidden_ref, bf16[128,2048]{1,0:T(8,128)(2,1)S(1)} %bitcast.73, ...), custom_call_target="tpu_custom_call" | custom-call | bytes 150000000 | tf_op jit(solution)/shard_map/pallas_call | solution.py:855
  448.5 1.3 copy-done.4
  449.8 1.0 copy-done.10
  450.8 5.0 all-to-all-start
  455.9 4.0 convolution_convert_fusion.8.do_ref
  459.9 13.4 %attend_back.1 = bf16[1024,384]{1,0:T(8,128)(2,1)S(1)} custom-call(bf16[1024,256]{1,0:T(8,128)(2,1)S(1)} %copy-done.13, bf16[1024,128]{1,0:T(8,128)(2,1)S(1)} %get-tuple-element.49.kv_ref, bf16[1024,256]{1,0:T(8,128)(2,1)S(1)} %convolution_convert_fusion.8.do_ref, f32[1024,4]{1,0:T(8,128)S(1)} %copy-done.15, f32[1024,128]{1,0:T(8,128)S(1)} %get-tuple-element.86.cos_ref, ...), custom_call_target="tpu_custom_call" | custom-call | tf_op jit(solution)/shard_map/attend_back/pallas_call | solution.py:1167
  473.3 2.4 convolution_convert_fusion.6
  475.7 0.2 copy.74
  475.9 2.4 convolution_convert_fusion.1.x_ref
  478.3 1.3 convolution_convert_fusion.7
  479.6 67.1 %finish_layer.1 = (f32[128,2048]{1,0:T(8,128)S(1)}, f32[8,128]{1,0:T(8,128)S(1)}, f32[64,2048]{1,0:T(8,128)S(1)}, bf16[8,64,384]{2,1,0:T(8,128)(2,1)S(1)}) custom-call(bf16[1024,2048]{1,0:T(8,128)(2,1)S(1)} %convolution_convert_fusion.1.x_ref, bf16[128,2048]{1,0:T(8,128)(2,1)S(1)} %bitcast.72, f32[128,2048]{1,0:T(8,128)S(1)} %copy-done.11, ...), custom_call_target="tpu_custom_call" | custom-call | bytes 150000000 | tf_op jit(solution)/shard_map/finish_layer/pallas_call | solution.py:1014
  546.8 0.8 copy.69
  547.6 0.1 convert_bitcast_fusion.3
  547.7 0.2 copy.64
  547.9 0.8 reshape.110
  548.7 0.2 copy.63
  548.8 0.8 reshape.109
  549.6 0.1 slice_select_fusion
  549.7 0.5 slice_bitcast_fusion
  550.2 2.0 fusion.1
  552.2 2.8 convert_element_type.167
  555.0 2.0 convert_bitcast_fusion
  557.0 1.5 copy.71
  558.4 1.5 copy.70
  559.9 1.0 copy.78
  560.9 0.8 copy.79
  (60 shorter events, 0.4 us)
Async XLA Ops:
  7.2 128.9 %all-gather.5.cloned.1.call-start = ((), (), s32[]{:S(2)}) async-start(), calls=%async_computation.3 | async-start | bytes 1310720 | tf_op jit(solution)/shard_map/all_gather | solution.py:1218
  7.9 235.5 %all-gather.7.cloned.1.call-start = ((), (), s32[]{:S(2)}) async-start(), calls=%async_computation.4 | async-start | bytes 10485760 | tf_op jit(solution)/shard_map/all_gather | solution.py:1227
  9.0 106.8 %copy-start.2 = (bf16[1,128,2048]{2,1,0:T(8,128)(2,1)S(1)}, bf16[1,128,2048]{2,1,0:T(8,128)(2,1)}, u32[]{:S(2)}) copy-start(bf16[1,128,2048]{2,1,0:T(8,128)(2,1)} %param.14) | copy-start | bytes 1572868
  11.9 1.0 copy-start
  13.0 1.2 copy-start.8
  14.2 1.2 copy-start.9
  113.0 2.0 copy-start.16
  114.9 7.4 %copy-start.20 = (bf16[32,64,384]{2,1,0:T(8,128)(2,1)}, bf16[32,64,384]{2,1,0:T(8,128)(2,1)S(1)}, u32[]{:S(2)}) copy-start(bf16[32,64,384]{2,1,0:T(8,128)(2,1)S(1)} %get-tuple-element.43) | copy-start | bytes 4718596
  115.0 146.9 %all-gather.9.cloned.1.call-start = ((), (), s32[]{:S(2)}) async-start(), calls=%async_computation.5 | async-start | bytes 5242880 | tf_op jit(solution)/shard_map/all_gather | solution.py:1219
  115.7 175.3 %all-gather.11.cloned.1.call-start = ((), (), s32[]{:S(2)}) async-start(), calls=%async_computation.6 | async-start | bytes 4718592 | tf_op jit(solution)/shard_map/all_gather | solution.py:1234
  116.7 6.2 %copy-start.24 = (s32[1,8]{1,0:T(1,128)S(1)}, s32[1,8]{1,0:T(1,128)}, u32[]{:S(2)}) copy-start(s32[1,8]{1,0:T(1,128)} %param.13) | copy-start | bytes 100
  122.4 427.8 %reduce-scatter.5.cloned.1.call-start = ((), (), s32[]{:S(2)}) async-start(), calls=%async_computation.8 | async-start | bytes 4718592 | tf_op jit(solution)/shard_map/reduce_scatter | solution.py:1250
  123.4 2.8 copy-start.5
  134.5 0.8 copy-start.12
  135.3 0.8 copy-start.14
  136.0 4.8 copy-start.6
  136.1 4.8 copy-start.1
  241.4 2.0 copy-start.18
  255.9 3.3 copy-start.22
  291.0 259.2 %reduce-scatter.3.cloned.1.call-start = ((), (), s32[]{:S(2)}) async-start(), calls=%async_computation.7 | async-start | bytes 5242880 | tf_op jit(solution)/shard_map/reduce_scatter | solution.py:1268
  300.7 11.9 %copy-start.19 = (bf16[1024,2048]{1,0:T(8,128)(2,1)S(1)}, bf16[1024,2048]{1,0:T(8,128)(2,1)}, u32[]{:S(2)}) copy-start(bf16[1024,2048]{1,0:T(8,128)(2,1)} %copy-done.18) | copy-start | bytes 12582916
  337.3 1.0 copy-start.3
  448.5 1.3 copy-start.4
  449.8 1.0 copy-start.10
  450.8 99.4 %all-to-all-start = ((bf16[8,64,2048]{2,1,0:T(8,128)(2,1)}), bf16[8,64,2048]{2,1,0:T(8,128)(2,1)}, u32[]{:S(2)}, u32[]{:S(2)}) async-start(bf16[8,64,2048]{2,1,0:T(8,128)(2,1)} %bitcast.74), calls=%async_computation.1 | async-start | bytes 4194304 | tf_op jit(solution)/shard_map/all_to_all | solution.py:1049
  455.8 4.0 copy-start.13
  455.9 4.0 copy-start.15
  459.8 13.4 %copy-start.17 = (bf16[1024,2048]{1,0:T(8,128)(2,1)S(1)}, bf16[1024,2048]{1,0:T(8,128)(2,1)}, u32[]{:S(2)}) copy-start(bf16[1024,2048]{1,0:T(8,128)(2,1)} %copy-done.16) | copy-start | bytes 12582916
  473.3 2.6 copy-start.21
  475.9 2.4 copy-start.7
  475.9 2.4 copy-start.23
  478.3 1.3 copy-start.11
Sparse Core Ops, SparseCore 0:
  9.5 24.2 all-gather.4
  115.1 61.5 all-gather.6
  178.2 34.4 all-gather.8
  215.3 75.7 all-gather.10
  294.5 107.3 reduce-scatter.4
  404.2 53.3 reduce-scatter.2

commit v9 on v8

--- a/solution.py
+++ b/solution.py
@@ -447,6 +447,7 @@
             lambda block, part: copy(block, part, 0, False).wait_recv(),
             between,
         )
+        between(line_size)
         for place in range(line_size):
             for part in range(CHUNKS):
                 copy(place * PAIR + 1 - pair_at, part, 0, False).wait_recv()
@@ -466,7 +467,7 @@
     ]
 
 
-def scatter_phase(line_size, x_ref, sum_ref, near, below, above, near_send, near_sem, line_send, line_sem, emit, midway=lambda: None):
+def scatter_phase(line_size, x_ref, sum_ref, near, below, above, near_send, near_sem, line_send, line_sem, emit, midway=lambda: None, between=lambda turn: None):
     me = lax.axis_index("ctx")
     line_at, pair_at = me // PAIR, me % PAIR
     rows = sum_ref.shape[0]
@@ -506,7 +507,8 @@
         for part in range(CHUNKS):
             near_copy(place, part).start()
 
-    for place in order[:-1]:
+    for turn, place in enumerate(order[:-1]):
+        between(turn)
         for part in range(CHUNKS):
             part_rows = pl.ds(part * step, step)
             near_copy(place, part).wait_recv()
@@ -593,9 +595,8 @@
 
 
 def start_kernel(
-    ctx_size, fsdp_size, tokens_ref, tile_ref, parts_ref, gate_ref, up_ref, out_ref, gains_ref, weight_ref,
-    wide_ref, tiles, normed, tile_send, tile_recv, far_send, far_recv, near_send, near_recv, wide_send,
-    wide_recv, kept, wide_kept, *sems
+    ctx_size, fsdp_size, tokens_ref, tile_ref, parts_ref, out_ref, gains_ref, weight_ref,
+    tiles, normed, tile_send, tile_recv, far_send, far_recv, near_send, near_recv, kept, *sems
 ):
     me_ctx, me_fsdp = lax.axis_index("ctx"), lax.axis_index("fsdp")
     count = ctx_size * fsdp_size
@@ -646,44 +647,10 @@
             device_id_type=MESH,
         )
 
-    wide = gate_ref.shape[1] // ctx_size
-
-    def wide_part(which, target, source):
-        cols = pl.ds(pl.multiple_of(target * wide, wide), wide)
-        return (
-            (gate_ref, up_ref)[which].at[:, cols],
-            wide_ref.at[source, :, which * wide : (which + 1) * wide],
-        )
-
-    def wide_copy(which, k, source):
-        target = (me_ctx + k) % ctx_size
-        src, dst = wide_part(which, target, source)
-        return pltpu.make_async_remote_copy(
-            src_ref=src,
-            dst_ref=dst,
-            send_sem=wide_send.at[which, k],
-            recv_sem=wide_recv.at[which, k],
-            device_id={"ctx": target},
-            device_id_type=MESH,
-        )
-
-    def wide_keep(which):
-        return pltpu.make_async_copy(*wide_part(which, me_ctx, me_ctx), wide_kept.at[which])
-
-    def wide_start(distance):
-        for k in range(2 * distance - 1, min(2 * distance + 1, ctx_size)):
-            for which in range(2):
-                wide_copy(which, k, me_ctx).start()
-        if distance == ctx_size // PAIR - 1:
-            for which in range(2):
-                wide_copy(which, ctx_size - 1, me_ctx).start()
-
     for k in range(1, ctx_size):
         far_copy(k, me_ctx).start()
     for j in range(1, fsdp_size):
         near_copy(0, j, me_fsdp).start()
-    for which in range(2):
-        wide_keep(which).start()
     keep = pltpu.make_async_copy(parts_ref.at[me_ctx], weight_ref.at[me], kept)
     keep.start()
 
@@ -705,13 +672,7 @@
         far_copy(k, (me_ctx + ctx_size - k) % ctx_size).wait_recv()
         for j in range(1, fsdp_size):
             near_copy(k, j, me_fsdp).start()
-    finish_gather(wide_start)
-    for which in range(2):
-        for k in range(1, ctx_size):
-            wide_copy(which, k, (me_ctx + ctx_size - k) % ctx_size).wait_recv()
-        for k in range(1, ctx_size):
-            wide_copy(which, k, me_ctx).wait_send()
-        wide_keep(which).wait()
+    finish_gather()
     for k in range(ctx_size):
         for j in range(1, fsdp_size):
             near_copy(k, j, (me_fsdp + fsdp_size - j) % fsdp_size).wait_recv()
@@ -729,22 +690,20 @@
     keep.wait()
 
 
-def start_layer(tokens, tile, parts, w_gate, w_up):
+def start_layer(tokens, tile, parts):
     ctx_size, fsdp_size = lax.axis_size("ctx"), lax.axis_size("fsdp")
     count = ctx_size * fsdp_size
     rows, model = tokens.shape
     dma = pltpu.SemaphoreType.DMA
-    held = w_gate.shape[0]
-    normed1, gains, weight, wide = pl.pallas_call(
+    normed1, gains, weight = pl.pallas_call(
         functools.partial(start_kernel, ctx_size, fsdp_size),
         out_shape=(
             jax.ShapeDtypeStruct((ctx_size * rows, model), jnp.bfloat16),
             jax.ShapeDtypeStruct((8, model), jnp.float32),
             jax.ShapeDtypeStruct((count,) + parts.shape[1:], parts.dtype),
-            jax.ShapeDtypeStruct((ctx_size, held, 2 * w_gate.shape[1] // ctx_size), w_gate.dtype),
         ),
-        in_specs=in_vmem(5),
-        out_specs=(ANYWHERE, in_vmem(1)[0], ANYWHERE, ANYWHERE),
+        in_specs=in_vmem(3),
+        out_specs=(ANYWHERE, in_vmem(1)[0], ANYWHERE),
         scratch_shapes=[
             pltpu.VMEM((count, 8, 128), jnp.float32),
             pltpu.VMEM((rows, model), jnp.bfloat16),
@@ -754,10 +713,7 @@
             dma((ctx_size,)),
             dma((ctx_size, fsdp_size)),
             dma((ctx_size, fsdp_size)),
-            dma((2, ctx_size)),
-            dma((2, ctx_size)),
             dma,
-            dma((2,)),
         ]
         + gather_scratch(ctx_size),
         compiler_params=pltpu.CompilerParams(
@@ -765,17 +721,131 @@
         ),
         cost_estimate=LINK_COST,
         name="start_layer",
-    )(tokens, tile, parts, w_gate, w_up)
-    return normed1, gains, rows_of(weight), rows_of(wide)
+    )(tokens, tile, parts)
+    return normed1, gains, rows_of(weight)
+
+
+def spread_phase(ctx_size, fsdp_size, gate_ref, up_ref, wide_ref, send, recv, side_send, side_recv, kept):
+    me, me_fsdp = lax.axis_index("ctx"), lax.axis_index("fsdp")
+    along = (me_fsdp + fsdp_size // 2) % fsdp_size
+    beside = me_fsdp + 1 - 2 * (me_fsdp % 2)
+    diagonal = (beside + fsdp_size // 2) % fsdp_size
+    wide = gate_ref.shape[1] // ctx_size
+
+    def part(which, target, source):
+        cols = pl.ds(pl.multiple_of(target * wide, wide), wide)
+        return (
+            (gate_ref, up_ref)[which].at[:, cols],
+            wide_ref.at[me_fsdp, source, :, which * wide : (which + 1) * wide],
+        )
+
+    def copy(which, k, source):
+        target = (me + k) % ctx_size
+        src, dst = part(which, target, source)
+        return pltpu.make_async_remote_copy(
+            src_ref=src,
+            dst_ref=dst,
+            send_sem=send.at[which, k],
+            recv_sem=recv.at[which, k],
+            device_id={"ctx": target},
+            device_id_type=MESH,
+        )
+
+    def keep(which):
+        return pltpu.make_async_copy(*part(which, me, me), kept.at[which])
+
+    def side(way, k, rows_of_device):
+        block = (rows_of_device, (me + ctx_size - k) % ctx_size)
+        return pltpu.make_async_remote_copy(
+            src_ref=wide_ref.at[block],
+            dst_ref=wide_ref.at[block],
+            send_sem=side_send.at[way, k],
+            recv_sem=side_recv.at[way, k],
+            device_id={"fsdp": along if way == 0 else beside},
+            device_id_type=MESH,
+        )
+
+    def begin():
+        for which in range(2):
+            keep(which).start()
+        for k in list(range(2, ctx_size, 2)) + list(range(1, ctx_size, 2)):
+            for which in range(2):
+                copy(which, k, me).start()
+
+    def pass_on(k):
+        for which in range(2):
+            if k:
+                copy(which, k, (me + ctx_size - k) % ctx_size).wait_recv()
+            else:
+                keep(which).wait()
+        side(0, k, me_fsdp).start()
+        side(1, k, me_fsdp).start()
+
+    def relay(k):
+        side(0, k, along).wait_recv()
+        side(2, k, along).start()
+
+    def finish():
+        for k in range(ctx_size):
+            side(1, k, beside).wait_recv()
+            side(2, k, diagonal).wait_recv()
+        for k in range(ctx_size):
+            for way in range(3):
+                side(way, k, me_fsdp).wait_send()
+            if k:
+                for which in range(2):
+                    copy(which, k, me).wait_send()
+
+    return begin, pass_on, relay, finish
 
 
 def mlp_forward_kernel(
-    ctx_size, fsdp_size, x_ref, tokens_ref, gains_ref, hidden_ref, out_ref, sums, normed, *sems
+    ctx_size, fsdp_size, x_ref, tokens_ref, gains_ref, gate_ref, up_ref, hidden_ref, wide_ref, out_ref,
+    sums, normed, wide_send, wide_recv, side_send, side_recv, kept, *sems
 ):
     line_size = ctx_size // PAIR
-    me = lax.axis_index("ctx")
-    greet_line(pltpu.get_barrier_semaphore(), me, me // PAIR, line_size)
+    me, me_fsdp = lax.axis_index("ctx"), lax.axis_index("fsdp")
+    barrier = pltpu.get_barrier_semaphore()
+    for k in range(1, ctx_size):
+        pl.semaphore_signal(barrier, inc=1, device_id={"ctx": (me + k) % ctx_size}, device_id_type=MESH)
+    for j in range(1, fsdp_size):
+        pl.semaphore_signal(
+            barrier, inc=1, device_id={"fsdp": (me_fsdp + j) % fsdp_size}, device_id_type=MESH
+        )
+    pl.semaphore_wait(barrier, ctx_size + fsdp_size - 2)
     start_own, finish_gather = gather_phase(line_size, normed, out_ref, *sems[7:])
+    begin, pass_on, relay, finish_spread = spread_phase(
+        ctx_size, fsdp_size, gate_ref, up_ref, wide_ref, wide_send, wide_recv, side_send, side_recv, kept
+    )
+    even = list(range(0, ctx_size, 2))
+    odd = list(range(1, ctx_size, 2))
+
+    def during_scatter(turn):
+        if turn == 0:
+            begin()
+        if turn == 1:
+            pass_on(0)
+        if turn == 2:
+            pass_on(2)
+
+    def midway():
+        for k in even[2:]:
+            pass_on(k)
+        for k in even[:2]:
+            relay(k)
+
+    def during_gather(distance):
+        if distance == line_size - 2:
+            for k in even[2:]:
+                relay(k)
+            for k in odd[:2]:
+                pass_on(k)
+        if distance == line_size - 1:
+            for k in odd[2:]:
+                pass_on(k)
+        if distance == line_size:
+            for k in odd:
+                relay(k)
 
     def emit(part, rows):
         hidden = tokens_ref[rows, :].astype(jnp.float32) + RESIDUAL_MULT * sums[rows, :]
@@ -785,8 +855,11 @@
         normed[rows, :] = swap_lanes(scaled, ctx_size, fsdp_size).astype(normed.dtype)
         start_own(part)
 
-    finish_scatter = scatter_phase(line_size, x_ref, sums, *sems[:7], emit)
-    finish_gather()
+    finish_scatter = scatter_phase(
+        line_size, x_ref, sums, *sems[:7], emit, midway, during_scatter
+    )
+    finish_gather(during_gather)
+    finish_spread()
     finish_scatter()
 
 
@@ -849,14 +922,14 @@
     finish_scatter()
 
 
-def scatter_gather(kernel, collective_id, extra_shapes, partial, *others, specs=(), scratch=()):
+def scatter_gather(kernel, collective_id, extra_shapes, partial, *others, specs=(), out_specs=(), scratch=()):
     ctx_size, fsdp_size = lax.axis_size("ctx"), lax.axis_size("fsdp")
     rows, model = partial.shape[0] // ctx_size, partial.shape[1]
     return pl.pallas_call(
         functools.partial(kernel, ctx_size, fsdp_size),
         out_shape=extra_shapes + (jax.ShapeDtypeStruct(partial.shape, jnp.bfloat16),),
         in_specs=in_vmem(1 + len(others) - len(specs)) + list(specs),
-        out_specs=tuple(in_vmem(len(extra_shapes))) + (ANYWHERE,),
+        out_specs=tuple(in_vmem(len(extra_shapes) - len(out_specs))) + tuple(out_specs) + (ANYWHERE,),
         scratch_shapes=[pltpu.VMEM((rows, model), jnp.float32), pltpu.VMEM((rows, model), jnp.bfloat16)]
         + list(scratch)
         + scatter_scratch(ctx_size, rows, model)
@@ -868,9 +941,29 @@
     )(partial, *others)
 
 
-def mlp_forward(partial, tokens, gains):
+def mlp_forward(partial, tokens, gains, w_gate, w_up):
+    ctx_size, fsdp_size = lax.axis_size("ctx"), lax.axis_size("fsdp")
     hidden = jax.ShapeDtypeStruct(tokens.shape, jnp.float32)
-    return scatter_gather(mlp_forward_kernel, 1, (hidden,), partial, tokens, gains)
+    slices = (fsdp_size, ctx_size, w_gate.shape[0], 2 * w_gate.shape[1] // ctx_size)
+    dma = pltpu.SemaphoreType.DMA
+    return scatter_gather(
+        mlp_forward_kernel,
+        1,
+        (hidden, jax.ShapeDtypeStruct(slices, w_gate.dtype)),
+        partial,
+        tokens,
+        gains,
+        w_gate,
+        w_up,
+        out_specs=(ANYWHERE,),
+        scratch=(
+            dma((2, ctx_size)),
+            dma((2, ctx_size)),
+            dma((3, ctx_size)),
+            dma((3, ctx_size)),
+            dma((2,)),
+        ),
+    )
 
 
 def mlp_backward(partial, hidden, grad_out, gains, terms):
@@ -1221,19 +1314,19 @@
     odd = lax.axis_index("fsdp") % 2
     gain_tile = jnp.concatenate([gain_rows * (1 - odd), gain_rows * odd], axis=1)
     gain_tile = jnp.pad(gain_tile, ((0, 8 - gain_tile.shape[0]), (0, 128 - gain_tile.shape[1])))
-    normed1, gains, w_qkv, gu_mine = start_layer(
-        tokens[0], gain_tile, qkv_parts.transpose(1, 0, 2), w_gate, w_up
-    )
-    w_gu = lax.all_gather(gu_mine, "fsdp", axis=0, tiled=True)
+    normed1, gains, w_qkv = start_layer(tokens[0], gain_tile, qkv_parts.transpose(1, 0, 2))
     grad_out = cotangent[0].astype(jnp.float32)
     grad_mlp = (RESIDUAL_MULT * grad_out).astype(bf16)
 
     block_rows = math.gcd(length, 256)
+    normed1, grad_mlp = lax.optimization_barrier((normed1, grad_mlp))
+    grad_mlp = lax.all_gather(grad_mlp, "ctx", axis=0, tiled=True)
     qkv = dot_plain(normed1, w_qkv)
-    qkv, grad_mlp = lax.optimization_barrier((qkv, grad_mlp))
-    grad_mlp = lax.all_gather(grad_mlp, "ctx", axis=0, tiled=True)
     q, kv, mixed_heads, log_sum = attention_forward(qkv, tables, block_rows)
-    hidden, normed2 = mlp_forward(dot_plain(mixed_heads, wo_mine).astype(bf16), tokens[0], gains)
+    hidden, w_gu, normed2 = mlp_forward(
+        dot_plain(mixed_heads, wo_mine).astype(bf16), tokens[0], gains, w_gate, w_up
+    )
+    w_gu = rows_of(rows_of(w_gu))
 
     gate_up = dot_plain(normed2, w_gu)
     gate_pre, up_pre = gate_up[:, :ff_slice], gate_up[:, ff_slice:]

time: 573 us -> 572 us (level); the launches traced: 569 us -> 562 us
  waiting for transfers between devices: 21.2 us -> 1.45 us
  Pallas kernels: 397 us -> 412 us
    pallas_call x2, Pallas kernels: 211 us -> 260 us  [scatter_gather(): pl.pallas_call(functools.partial(kernel, ctx_size, fsdp_size), out_shape=...]
    pallas_call x1, Pallas kernels: 97.6 us -> 62 us  [start_layer(): pl.pallas_call(functools.partial(start_kernel, ctx_size, fsdp_size), out_...]
    all_gather x1, waiting for transfers between devices: 19.8 us -> 0.01 us  [on_device(): grad_mlp = lax.all_gather(grad_mlp, 'ctx', axis=0, tiled=True)]
    unnamed x52 -> x50, local copies, waits for them, and re-layouts: 17.4 us -> 14.1 us
  transfers between devices with their start and end apart: 7 -> 6, of which waited for: 1 -> 0; matrix products, arithmetic and copies ran while one was open for 18% -> 18% of each run, Pallas kernels for 70% -> 73%
where the time goes in v9:
time: 572 us; the launch traced here: 562 us
  Pallas kernels  412 us (72%)
  matrix products  86.4 us (15%)
  local copies, waits for them, and re-layouts  23.6 us (4%)
  other arithmetic  14.6 us (3%)
  between operations  14.6 us (3%)
  starting transfers between devices  9.48 us (2%)
    pallas_call x2, Pallas kernels, scatter_gather(): pl.pallas_call(functools.partial(kernel, ctx_size, fsdp_size), out_shape=...  260 us
    pallas_call x1, Pallas kernels, finish_layer(): pl.pallas_call(functools.partial(finish_kernel, ctx_size, fsdp_size), out...  67.4 us
    pallas_call x1, Pallas kernels, start_layer(): pl.pallas_call(functools.partial(start_kernel, ctx_size, fsdp_size), out_...  62 us
    dot_general x4, matrix products, dot_back(): lax.dot_general(left, right, (((1,), (1,)), ((), ())), preferred_element_...  30.8 us
    dot_general x4, matrix products, dot_plain(): return jnp.dot(left, right, preferred_element_type=jnp.float32)  30.5 us
    dot_general x4, matrix products, dot_outer(): lax.dot_general(left, right, (((0,), (0,)), ((), ())), preferred_element_...  25 us
    unnamed x50, local copies, waits for them, and re-layouts  14.1 us
    pallas_call x1, Pallas kernels, attention_backward(): pl.pallas_call(functools.partial(attention_backward_kernel, block_rows),...  13.4 us
  transfers between devices with their start and end apart: 6, of which 0 were waited for; matrix products, arithmetic and copies ran while one was open for 18% of the time, Pallas kernels for 73%

profile of v9, /device:TPU:0, one launch (start us, length us, event | category | flops | bytes accessed | tf_op | source)
XLA Modules:
  0.0 561.6 jit_solution(8220202107944416870)
XLA Ops:
  7.2 0.0 all-gather.4.cloned.1.call-start
  7.2 0.7 all-gather.4.cloned.1.call-update
  7.9 0.0 all-gather.6.cloned.1.call-start
  8.0 0.7 all-gather.6.cloned.1.call-update
  8.7 0.0 all-gather.8.cloned.1.call-start
  8.7 1.0 reshape.97
  9.8 1.0 reshape.98
  10.8 1.0 copy.75
  11.7 0.7 convert_multiply_fusion.1
  12.4 0.1 select_maximum_fusion.tile_ref
  12.5 0.1 maximum_bitcast_fusion.parts_ref
  12.6 1.0 copy-done
  13.7 62.0 %start_layer.1 = (bf16[1024,2048]{1,0:T(8,128)(2,1)S(1)}, f32[8,2048]{1,0:T(8,128)S(1)}, bf16[32,64,384]{2,1,0:T(8,128)(2,1)S(1)}) custom-call(bf16[128,2048]{1,0:T(8,128)(2,1)S(1)} %bitcast.70, f32[8,128]{1,0:T(8,128)S(1)} %select_maximum_fusion.tile_ref, bf16[8,64,384]{2,1,0:T(8,128)(2,1)S(1)} %maximum_bitcast_fusion.parts_ref), custom_call_target="tpu_custom_call" | custom-call | bytes 150000000 | tf_op jit(solution)/shard_map/start_layer/pallas_call | solution.py:698
  75.7 2.0 copy-done.15
  77.7 1.1 copy-done.18
  78.8 0.9 multiply_convert_fusion.2
  79.7 0.0 reduce-scatter.5.cloned.1.call-start
  79.8 0.2 reduce-window_clone.1
  80.0 0.1 convert_reduce_fusion
  80.1 0.2 copy.57.doc_col_ref
  80.3 1.9 fusion.2
  82.3 0.9 pad_maximum_fusion.3
  83.1 3.7 fusion.5.qkv_ref
  86.9 8.2 %attend.1 = (bf16[1024,256]{1,0:T(8,128)(2,1)S(1)}, bf16[1024,128]{1,0:T(8,128)(2,1)S(1)}, bf16[1024,256]{1,0:T(8,128)(2,1)S(1)}, f32[1024,4]{1,0:T(8,128)S(1)}) custom-call(f32[1024,384]{1,0:T(8,128)S(1)} %fusion.5.qkv_ref, f32[1024,128]{1,0:T(8,128)S(1)} %get-tuple-element.86.cos_ref, f32[1024,128]{1,0:T(8,128)S(1)} %get-tuple-element.87.sin_ref, ...), custom_call_target="tpu_custom_call" | custom-call | tf_op jit(solution)/shard_map/attend/pallas_call | solution.py:1243
  95.1 0.8 copy-done.11
  95.9 0.8 copy-done.13
  96.7 4.9 convolution_convert_fusion.3.x_ref
  101.7 152.3 %shard_map.203 = (f32[128,2048]{1,0:T(8,128)S(1)}, bf16[4,8,64,2048]{3,2,1,0:T(8,128)(2,1)}, bf16[1024,2048]{1,0:T(8,128)(2,1)}) custom-call(bf16[1024,2048]{1,0:T(8,128)(2,1)} %convolution_convert_fusion.3.x_ref, bf16[128,2048]{1,0:T(8,128)(2,1)S(1)} %bitcast.71, f32[8,2048]{1,0:T(8,128)S(1)} %get-tuple-element.46.gains_ref, ...), custom_call_target="tpu_custom_call" | custom-call | bytes 150000000 | tf_op jit(solution)/shard_map/pallas_call | solution.py:928
  254.0 12.5 %fusion.6 = f32[1024,2048]{1,0:T(8,128)S(1)} fusion(bf16[1024,2048]{1,0:T(8,128)(2,1)} %get-tuple-element.50, bf16[2048,2048]{1,0:T(8,128)(2,1)} %bitcast.91), kind=kOutput, calls=%fused_computation.48 | convolution fusion | flops 8589934592 | bytes 20971520 | tf_op jit(solution)/shard_map/dot_general | solution.py:59
  266.5 3.2 copy-done.20
  269.7 2.7 fusion
  272.5 9.4 %convolution_convert_fusion.5 = bf16[1024,2048]{1,0:T(8,128)(2,1)} fusion(bf16[1024,1024]{1,0:T(8,128)(2,1)} %fusion, bf16[1024,2048]{1,0:T(8,128)(2,1)} %all-gather.6.cloned.1.call-done), kind=kOutput, calls=%fused_computation.11 | convolution fusion | flops 4297064448 | bytes 10485760 | tf_op jit(solution)/shard_map/dot_general | solution.py:59
  281.9 0.2 reduce-scatter.3.cloned.1.call-start
  282.1 9.4 %convolution_convert_fusion.4 = bf16[1024,2048]{1,0:T(8,128)(2,1)} fusion(bf16[1024,1024]{1,0:T(8,128)(2,1)} %fusion, bf16[1024,2048]{1,0:T(8,128)(2,1)} %all-gather.8.cloned.1.call-done), kind=kOutput, calls=%fused_computation.10 | convolution fusion | flops 4297064448 | bytes 10485760 | tf_op jit(solution)/shard_map/dot_general | solution.py:69
  291.5 11.9 %multiply_convert_fusion.1 = (bf16[1024,1024]{1,0:T(8,128)(2,1)S(1)}, bf16[1024,1024]{1,0:T(8,128)(2,1)S(1)}) fusion(f32[1024,2048]{1,0:T(8,128)} %copy-done.20, bf16[1024,2048]{1,0:T(8,128)(2,1)} %all-gather.8.cloned.1.call-done, bf16[1024,2048]{1,0:T(8,128)(2,1)} %all-gather.6.cloned.1.call-done), kind=kOutput, calls=%fused_computation.5 | convolution fusion | flops 4308598784 | bytes 20971520 | tf_op jit(solution)/shard_map/dot_general | solution.py:63
  303.5 12.0 %convolution_convert_fusion = bf16[2048,2048]{1,0:T(8,128)(2,1)} fusion(bf16[1024,2048]{1,0:T(8,128)(2,1)S(1)} %copy-done.21, bf16[1024,1024]{1,0:T(8,128)(2,1)S(1)} %get-tuple-element.74, bf16[1024,1024]{1,0:T(8,128)(2,1)S(1)} %get-tuple-element.73), kind=kOutput, calls=%fused_computation | convolution fusion | flops 8602517504 | bytes 16777216 | tf_op jit(solution)/shard_map/dot_general | solution.py:69
  315.4 12.7 %convolution_convert_fusion.2.x_ref = bf16[1024,2048]{1,0:T(8,128)(2,1)} fusion(bf16[2048,2048]{1,0:T(8,128)(2,1)} %bitcast.92, bf16[1024,1024]{1,0:T(8,128)(2,1)S(1)} %get-tuple-element.74, bf16[1024,1024]{1,0:T(8,128)(2,1)S(1)} %get-tuple-element.73), kind=kOutput, calls=%fused_computation.8 | convolution fusion | flops 8600420352 | bytes 16777216 | tf_op jit(solution)/shard_map/dot_general | solution.py:63
  328.2 1.0 copy-done.3
  329.2 108.2 %shard_map.204 = (f32[128,2048]{1,0:T(8,128)S(1)}, f32[2,2048]{1,0:T(2,128)S(1)}, bf16[512,2048]{1,0:T(8,128)(2,1)S(1)}, bf16[1024,2048]{1,0:T(8,128)(2,1)}) custom-call(bf16[1024,2048]{1,0:T(8,128)(2,1)} %convolution_convert_fusion.2.x_ref, f32[128,2048]{1,0:T(8,128)S(1)} %get-tuple-element.47.hidden_ref, bf16[128,2048]{1,0:T(8,128)(2,1)S(1)} %bitcast.73, ...), custom_call_target="tpu_custom_call" | custom-call | bytes 150000000 | tf_op jit(solution)/shard_map/pallas_call | solution.py:928
  437.4 1.3 copy-done.4
  438.7 1.0 copy-done.9
  439.7 9.1 %all-to-all-start = ((bf16[8,64,2048]{2,1,0:T(8,128)(2,1)}), bf16[8,64,2048]{2,1,0:T(8,128)(2,1)}, u32[]{:S(2)}, u32[]{:S(2)}) async-start(bf16[8,64,2048]{2,1,0:T(8,128)(2,1)} %bitcast.74), calls=%async_computation.1 | async-start | bytes 4194304 | tf_op jit(solution)/shard_map/all_to_all | solution.py:1142
  448.8 3.9 convolution_convert_fusion.8.do_ref
  452.7 13.4 %attend_back.1 = bf16[1024,384]{1,0:T(8,128)(2,1)S(1)} custom-call(bf16[1024,256]{1,0:T(8,128)(2,1)S(1)} %copy-done.12, bf16[1024,128]{1,0:T(8,128)(2,1)S(1)} %get-tuple-element.49.kv_ref, bf16[1024,256]{1,0:T(8,128)(2,1)S(1)} %convolution_convert_fusion.8.do_ref, f32[1024,4]{1,0:T(8,128)S(1)} %copy-done.14, f32[1024,128]{1,0:T(8,128)S(1)} %get-tuple-element.86.cos_ref, ...), custom_call_target="tpu_custom_call" | custom-call | tf_op jit(solution)/shard_map/attend_back/pallas_call | solution.py:1260
  466.1 2.4 convolution_convert_fusion.6
  468.5 0.2 copy.74
  468.7 2.4 convolution_convert_fusion.1.x_ref
  471.1 1.3 convolution_convert_fusion.7
  472.4 67.4 %finish_layer.1 = (f32[128,2048]{1,0:T(8,128)S(1)}, f32[8,128]{1,0:T(8,128)S(1)}, f32[64,2048]{1,0:T(8,128)S(1)}, bf16[8,64,384]{2,1,0:T(8,128)(2,1)S(1)}) custom-call(bf16[1024,2048]{1,0:T(8,128)(2,1)S(1)} %convolution_convert_fusion.1.x_ref, bf16[128,2048]{1,0:T(8,128)(2,1)S(1)} %bitcast.72, f32[128,2048]{1,0:T(8,128)S(1)} %copy-done.10, ...), custom_call_target="tpu_custom_call" | custom-call | bytes 150000000 | tf_op jit(solution)/shard_map/finish_layer/pallas_call | solution.py:1107
  539.9 0.8 copy.69
  540.7 0.1 convert_bitcast_fusion.3
  540.8 0.2 copy.64
  541.0 0.8 reshape.106
  541.7 0.2 copy.63
  541.9 0.8 reshape.105
  542.7 0.1 slice_select_fusion
  542.7 0.5 slice_bitcast_fusion
  543.3 2.0 fusion.1
  545.3 2.8 convert_element_type.167
  548.1 2.0 convert_bitcast_fusion
  550.1 1.5 copy.71
  551.5 1.5 copy.70
  553.0 1.0 copy.78
  553.9 0.8 copy.79
  (55 shorter events, 0.3 us)
Async XLA Ops:
  7.2 71.6 %copy-start.2 = (bf16[1,128,2048]{2,1,0:T(8,128)(2,1)S(1)}, bf16[1,128,2048]{2,1,0:T(8,128)(2,1)}, u32[]{:S(2)}) copy-start(bf16[1,128,2048]{2,1,0:T(8,128)(2,1)} %param.14) | copy-start | bytes 1572868
  7.2 72.6 %copy-start.23 = (s32[1,8]{1,0:T(1,128)S(1)}, s32[1,8]{1,0:T(1,128)}, u32[]{:S(2)}) copy-start(s32[1,8]{1,0:T(1,128)} %param.13) | copy-start | bytes 100
  7.2 89.5 %all-gather.4.cloned.1.call-start = ((), (), s32[]{:S(2)}) async-start(), calls=%async_computation.3 | async-start | bytes 1310720 | tf_op jit(solution)/shard_map/all_gather | solution.py:1311
  7.9 264.5 %all-gather.6.cloned.1.call-start = ((), (), s32[]{:S(2)}) async-start(), calls=%async_computation.4 | async-start | bytes 5242880 | tf_op jit(solution)/shard_map/all_gather | solution.py:1312
  8.7 273.1 %all-gather.8.cloned.1.call-start = ((), (), s32[]{:S(2)}) async-start(), calls=%async_computation.5 | async-start | bytes 4718592 | tf_op jit(solution)/shard_map/all_gather | solution.py:1323
  12.6 1.0 copy-start
  75.7 2.0 copy-start.15
  77.7 1.1 copy-start.18
  79.7 463.5 %reduce-scatter.5.cloned.1.call-start = ((), (), s32[]{:S(2)}) async-start(), calls=%async_computation.7 | async-start | bytes 4718592 | tf_op jit(solution)/shard_map/reduce_scatter | solution.py:1343
  80.3 2.8 copy-start.16
  95.1 0.8 copy-start.11
  95.9 0.8 copy-start.13
  96.7 5.0 copy-start.5
  96.7 5.0 copy-start.1
  96.7 5.0 copy-start.7
  96.7 5.0 copy-start.8
  266.5 3.3 copy-start.20
  281.9 261.4 %reduce-scatter.3.cloned.1.call-start = ((), (), s32[]{:S(2)}) async-start(), calls=%async_computation.6 | async-start | bytes 5242880 | tf_op jit(solution)/shard_map/reduce_scatter | solution.py:1361
  291.5 11.9 %copy-start.21 = (bf16[1024,2048]{1,0:T(8,128)(2,1)S(1)}, bf16[1024,2048]{1,0:T(8,128)(2,1)}, u32[]{:S(2)}) copy-start(bf16[1024,2048]{1,0:T(8,128)(2,1)} %get-tuple-element.50) | copy-start | bytes 12582916
  328.2 1.0 copy-start.3
  437.4 1.3 copy-start.4
  438.7 1.0 copy-start.9
  439.7 103.6 %all-to-all-start = ((bf16[8,64,2048]{2,1,0:T(8,128)(2,1)}), bf16[8,64,2048]{2,1,0:T(8,128)(2,1)}, u32[]{:S(2)}, u32[]{:S(2)}) async-start(bf16[8,64,2048]{2,1,0:T(8,128)(2,1)} %bitcast.74), calls=%async_computation.1 | async-start | bytes 4194304 | tf_op jit(solution)/shard_map/all_to_all | solution.py:1142
  448.8 3.9 copy-start.12
  448.8 3.9 copy-start.14
  452.6 13.4 %copy-start.17 = (bf16[1024,2048]{1,0:T(8,128)(2,1)S(1)}, bf16[1024,2048]{1,0:T(8,128)(2,1)}, u32[]{:S(2)}) copy-start(bf16[1024,2048]{1,0:T(8,128)(2,1)} %copy-done.15) | copy-start | bytes 12582916
  466.1 2.6 copy-start.19
  468.7 2.4 copy-start.6
  468.7 2.4 copy-start.22
  471.1 1.3 copy-start.10
Sparse Core Ops, SparseCore 0:
  9.6 26.1 all-gather.3
  37.3 32.5 all-gather.5
  79.9 122.8 all-gather.7
  282.0 109.3 reduce-scatter.4
  393.8 54.6 reduce-scatter.2

commit v10 on v9

--- a/solution.py
+++ b/solution.py
@@ -717,7 +717,7 @@
         ]
         + gather_scratch(ctx_size),
         compiler_params=pltpu.CompilerParams(
-            collective_id=0, has_side_effects=True, vmem_limit_bytes=32 * 2**20
+            collective_id=0, has_side_effects=True, vmem_limit_bytes=10 * 2**20
         ),
         cost_estimate=LINK_COST,
         name="start_layer",
@@ -922,7 +922,7 @@
     finish_scatter()
 
 
-def scatter_gather(kernel, collective_id, extra_shapes, partial, *others, specs=(), out_specs=(), scratch=()):
+def scatter_gather(kernel, collective_id, extra_shapes, partial, *others, specs=(), out_specs=(), scratch=(), grant=24):
     ctx_size, fsdp_size = lax.axis_size("ctx"), lax.axis_size("fsdp")
     rows, model = partial.shape[0] // ctx_size, partial.shape[1]
     return pl.pallas_call(
@@ -935,7 +935,7 @@
         + scatter_scratch(ctx_size, rows, model)
         + gather_scratch(ctx_size),
         compiler_params=pltpu.CompilerParams(
-            collective_id=collective_id, has_side_effects=True, vmem_limit_bytes=48 * 2**20
+            collective_id=collective_id, has_side_effects=True, vmem_limit_bytes=grant * 2**20
         ),
         cost_estimate=LINK_COST,
     )(partial, *others)
@@ -978,6 +978,7 @@
         grad_out,
         gains,
         terms,
+        grant=36,
         specs=(ANYWHERE,),
         scratch=(
             pltpu.VMEM(terms.shape, terms.dtype),
@@ -1131,7 +1132,7 @@
         ]
         + scatter_scratch(ctx_size, rows, model),
         compiler_params=pltpu.CompilerParams(
-            collective_id=3, has_side_effects=True, vmem_limit_bytes=40 * 2**20
+            collective_id=3, has_side_effects=True, vmem_limit_bytes=32 * 2**20
         ),
         cost_estimate=LINK_COST,
         name="finish_layer",
@@ -1250,7 +1251,7 @@
         ),
         in_specs=in_vmem(5),
         out_specs=tuple(in_vmem(4)),
-        compiler_params=pltpu.CompilerParams(vmem_limit_bytes=48 * 2**20),
+        compiler_params=pltpu.CompilerParams(vmem_limit_bytes=24 * 2**20),
         name="attend",
     )(qkv, *tables)
 
@@ -1266,7 +1267,7 @@
             pltpu.VMEM((length, width), jnp.float32),
             pltpu.VMEM((length, 2 * HD), jnp.float32),
         ],
-        compiler_params=pltpu.CompilerParams(vmem_limit_bytes=48 * 2**20),
+        compiler_params=pltpu.CompilerParams(vmem_limit_bytes=24 * 2**20),
         name="attend_back",
     )(q, kv, grad_out, lse, *tables)
 

time: 572 us -> 577 us (level)
    unnamed x50 -> x58, local copies, waits for them, and re-layouts: 14.1 us -> 18.3 us
  transfers between devices with their start and end apart: 6 -> 6, of which waited for: 0 -> 0; matrix products, arithmetic and copies ran while one was open for 18% -> 19% of each run, Pallas kernels for 73% -> 72%
where the time goes in v10:
time: 577 us; the launch traced here: 567 us
  Pallas kernels  410 us (71%)
  matrix products  91.4 us (16%)
  local copies, waits for them, and re-layouts  27.8 us (5%)
  other arithmetic  14.6 us (3%)
  between operations  14.5 us (3%)
  starting transfers between devices  6.91 us (1%)
    pallas_call x2, Pallas kernels, scatter_gather(): pl.pallas_call(functools.partial(kernel, ctx_size, fsdp_size), out_shape=...  259 us
    pallas_call x1, Pallas kernels, finish_layer(): pl.pallas_call(functools.partial(finish_kernel, ctx_size, fsdp_size), out...  67.8 us
    pallas_call x1, Pallas kernels, start_layer(): pl.pallas_call(functools.partial(start_kernel, ctx_size, fsdp_size), out_...  62 us
    dot_general x4, matrix products, dot_plain(): return jnp.dot(left, right, preferred_element_type=jnp.float32)  35.7 us
    dot_general x4, matrix products, dot_back(): lax.dot_general(left, right, (((1,), (1,)), ((), ())), preferred_element_...  30.9 us
    dot_general x4, matrix products, dot_outer(): lax.dot_general(left, right, (((0,), (0,)), ((), ())), preferred_element_...  24.8 us
    unnamed x58, local copies, waits for them, and re-layouts  18.3 us
    pallas_call x1, Pallas kernels, attention_backward(): pl.pallas_call(functools.partial(attention_backward_kernel, block_rows),...  13.4 us
  transfers between devices with their start and end apart: 6, of which 0 were waited for; matrix products, arithmetic and copies ran while one was open for 19% of the time, Pallas kernels for 72%

profile of v10, /device:TPU:0, one launch (start us, length us, event | category | flops | bytes accessed | tf_op | source)
XLA Modules:
  0.0 566.6 jit_solution(295250425463624784)
XLA Ops:
  7.2 0.7 all-gather.4.cloned.1.call-update
  8.0 0.7 all-gather.6.cloned.1.call-update
  8.7 0.0 all-gather.8.cloned.1.call-start
  8.7 1.0 reshape.97
  9.8 1.0 reshape.98
  10.8 1.0 copy.75
  11.7 0.7 convert_multiply_fusion.1
  12.4 0.1 select_maximum_fusion.tile_ref
  12.5 0.1 maximum_bitcast_fusion.parts_ref
  12.6 1.0 copy-done
  13.7 62.0 %start_layer.1 = (bf16[1024,2048]{1,0:T(8,128)(2,1)S(1)}, f32[8,2048]{1,0:T(8,128)S(1)}, bf16[32,64,384]{2,1,0:T(8,128)(2,1)S(1)}) custom-call(bf16[128,2048]{1,0:T(8,128)(2,1)S(1)} %bitcast.70, f32[8,128]{1,0:T(8,128)S(1)} %select_maximum_fusion.tile_ref, bf16[8,64,384]{2,1,0:T(8,128)(2,1)S(1)} %maximum_bitcast_fusion.parts_ref), custom_call_target="tpu_custom_call" | custom-call | bytes 150000000 | tf_op jit(solution)/shard_map/start_layer/pallas_call | solution.py:698
  75.7 2.0 copy-done.17
  77.7 1.1 copy-done.24
  78.8 0.9 multiply_convert_fusion.2
  79.7 0.0 reduce-scatter.5.cloned.1.call-start
  79.8 0.2 reduce-window_clone.1
  80.0 0.1 convert_reduce_fusion
  80.1 0.2 copy.57.doc_col_ref
  80.3 1.9 fusion.2
  82.3 0.9 pad_maximum_fusion.3
  83.1 3.7 fusion.5.qkv_ref
  86.9 8.2 %attend.1 = (bf16[1024,256]{1,0:T(8,128)(2,1)S(1)}, bf16[1024,128]{1,0:T(8,128)(2,1)S(1)}, bf16[1024,256]{1,0:T(8,128)(2,1)S(1)}, f32[1024,4]{1,0:T(8,128)S(1)}) custom-call(f32[1024,384]{1,0:T(8,128)S(1)} %fusion.5.qkv_ref, f32[1024,128]{1,0:T(8,128)S(1)} %get-tuple-element.86.cos_ref, f32[1024,128]{1,0:T(8,128)S(1)} %get-tuple-element.87.sin_ref, ...), custom_call_target="tpu_custom_call" | custom-call | tf_op jit(solution)/shard_map/attend/pallas_call | solution.py:1244
  95.1 0.8 copy-done.12
  95.9 0.8 copy-done.14
  96.7 13.7 %convolution_convert_fusion.3.x_ref = bf16[1024,2048]{1,0:T(8,128)(2,1)S(1)} fusion(bf16[1024,256]{1,0:T(8,128)(2,1)S(1)} %get-tuple-element.45, bf16[256,2048]{1,0:T(8,128)(2,1)} %all-gather.4.cloned.1.call-done), kind=kOutput, calls=%fused_computation.9 | convolution fusion | flops 1075838976 | bytes 5767168 | tf_op jit(solution)/shard_map/dot_general | solution.py:59
  110.5 151.9 %shard_map.203 = (f32[128,2048]{1,0:T(8,128)S(1)}, bf16[4,8,64,2048]{3,2,1,0:T(8,128)(2,1)S(1)}, bf16[1024,2048]{1,0:T(8,128)(2,1)S(1)}) custom-call(bf16[1024,2048]{1,0:T(8,128)(2,1)S(1)} %convolution_convert_fusion.3.x_ref, bf16[128,2048]{1,0:T(8,128)(2,1)S(1)} %bitcast.71, f32[8,2048]{1,0:T(8,128)S(1)} %get-tuple-element.46.gains_ref, ...), custom_call_target="tpu_custom_call" | custom-call | bytes 150000000 | tf_op jit(solution)/shard_map/pallas_call | solution.py:928
  262.4 8.9 %fusion.6 = f32[1024,2048]{1,0:T(8,128)S(1)} fusion(bf16[1024,2048]{1,0:T(8,128)(2,1)S(1)} %get-tuple-element.50, bf16[2048,2048]{1,0:T(8,128)(2,1)S(1)} %bitcast.80), kind=kOutput, calls=%fused_computation.48 | convolution fusion | flops 8589934592 | bytes 20971520 | tf_op jit(solution)/shard_map/dot_general | solution.py:59
  271.3 3.2 copy-done.26
  274.6 2.7 fusion
  277.3 9.3 %convolution_convert_fusion.5 = bf16[1024,2048]{1,0:T(8,128)(2,1)} fusion(bf16[1024,1024]{1,0:T(8,128)(2,1)} %fusion, bf16[1024,2048]{1,0:T(8,128)(2,1)} %all-gather.6.cloned.1.call-done), kind=kOutput, calls=%fused_computation.11 | convolution fusion | flops 4297064448 | bytes 10485760 | tf_op jit(solution)/shard_map/dot_general | solution.py:59
  286.7 0.4 reduce-scatter.3.cloned.1.call-start
  287.1 9.4 %convolution_convert_fusion.4 = bf16[1024,2048]{1,0:T(8,128)(2,1)} fusion(bf16[1024,1024]{1,0:T(8,128)(2,1)} %fusion, bf16[1024,2048]{1,0:T(8,128)(2,1)} %all-gather.8.cloned.1.call-done), kind=kOutput, calls=%fused_computation.10 | convolution fusion | flops 4297064448 | bytes 10485760 | tf_op jit(solution)/shard_map/dot_general | solution.py:69
  296.6 12.0 %multiply_convert_fusion.1 = (bf16[1024,1024]{1,0:T(8,128)(2,1)S(1)}, bf16[1024,1024]{1,0:T(8,128)(2,1)S(1)}) fusion(f32[1024,2048]{1,0:T(8,128)} %copy-done.26, bf16[1024,2048]{1,0:T(8,128)(2,1)} %all-gather.8.cloned.1.call-done, bf16[1024,2048]{1,0:T(8,128)(2,1)} %all-gather.6.cloned.1.call-done), kind=kOutput, calls=%fused_computation.5 | convolution fusion | flops 4308598784 | bytes 20971520 | tf_op jit(solution)/shard_map/dot_general | solution.py:63
  308.6 11.7 %convolution_convert_fusion = bf16[2048,2048]{1,0:T(8,128)(2,1)} fusion(bf16[1024,2048]{1,0:T(8,128)(2,1)S(1)} %copy-done.21, bf16[1024,1024]{1,0:T(8,128)(2,1)S(1)} %get-tuple-element.74, bf16[1024,1024]{1,0:T(8,128)(2,1)S(1)} %get-tuple-element.73), kind=kOutput, calls=%fused_computation | convolution fusion | flops 8602517504 | bytes 16777216 | tf_op jit(solution)/shard_map/dot_general | solution.py:69
  320.3 12.7 %convolution_convert_fusion.2.x_ref = bf16[1024,2048]{1,0:T(8,128)(2,1)} fusion(bf16[2048,2048]{1,0:T(8,128)(2,1)} %bitcast.81, bf16[1024,1024]{1,0:T(8,128)(2,1)S(1)} %get-tuple-element.74, bf16[1024,1024]{1,0:T(8,128)(2,1)S(1)} %get-tuple-element.73), kind=kOutput, calls=%fused_computation.8 | convolution fusion | flops 8600420352 | bytes 16777216 | tf_op jit(solution)/shard_map/dot_general | solution.py:63
  333.1 2.2 copy-done.2
  335.2 1.1 copy-done.4
  336.3 106.6 %shard_map.204 = (f32[128,2048]{1,0:T(8,128)S(1)}, f32[2,2048]{1,0:T(2,128)S(1)}, bf16[512,2048]{1,0:T(8,128)(2,1)S(1)}, bf16[1024,2048]{1,0:T(8,128)(2,1)S(1)}) custom-call(bf16[1024,2048]{1,0:T(8,128)(2,1)S(1)} %copy-done.2, f32[128,2048]{1,0:T(8,128)S(1)} %get-tuple-element.47.hidden_ref, bf16[128,2048]{1,0:T(8,128)(2,1)S(1)} %bitcast.73, ...), custom_call_target="tpu_custom_call" | custom-call | bytes 150000000 | tf_op jit(solution)/shard_map/pallas_call | solution.py:928
  442.9 1.3 copy-done.5
  444.3 1.0 copy-done.10
  445.2 2.0 copy-done.22
  447.2 6.3 %all-to-all-start = ((bf16[8,64,2048]{2,1,0:T(8,128)(2,1)}), bf16[8,64,2048]{2,1,0:T(8,128)(2,1)}, u32[]{:S(2)}, u32[]{:S(2)}) async-start(bf16[8,64,2048]{2,1,0:T(8,128)(2,1)} %bitcast.74), calls=%async_computation.1 | async-start | bytes 4194304 | tf_op jit(solution)/shard_map/all_to_all | solution.py:1143
  453.5 3.9 convolution_convert_fusion.8.do_ref
  457.4 13.4 %attend_back.1 = bf16[1024,384]{1,0:T(8,128)(2,1)S(1)} custom-call(bf16[1024,256]{1,0:T(8,128)(2,1)S(1)} %copy-done.13, bf16[1024,128]{1,0:T(8,128)(2,1)S(1)} %get-tuple-element.49.kv_ref, bf16[1024,256]{1,0:T(8,128)(2,1)S(1)} %convolution_convert_fusion.8.do_ref, f32[1024,4]{1,0:T(8,128)S(1)} %copy-done.15, f32[1024,128]{1,0:T(8,128)S(1)} %get-tuple-element.86.cos_ref, ...), custom_call_target="tpu_custom_call" | custom-call | tf_op jit(solution)/shard_map/attend_back/pallas_call | solution.py:1261
  470.8 2.4 convolution_convert_fusion.6
  473.2 0.2 copy.74
  473.5 2.4 convolution_convert_fusion.1.x_ref
  475.9 1.3 convolution_convert_fusion.7
  477.2 67.8 %finish_layer.1 = (f32[128,2048]{1,0:T(8,128)S(1)}, f32[8,128]{1,0:T(8,128)S(1)}, f32[64,2048]{1,0:T(8,128)S(1)}, bf16[8,64,384]{2,1,0:T(8,128)(2,1)S(1)}) custom-call(bf16[1024,2048]{1,0:T(8,128)(2,1)S(1)} %convolution_convert_fusion.1.x_ref, bf16[128,2048]{1,0:T(8,128)(2,1)S(1)} %bitcast.72, f32[128,2048]{1,0:T(8,128)S(1)} %copy-done.11, ...), custom_call_target="tpu_custom_call" | custom-call | bytes 150000000 | tf_op jit(solution)/shard_map/finish_layer/pallas_call | solution.py:1108
  545.0 0.8 copy.69
  545.8 0.1 convert_bitcast_fusion.3
  545.9 0.2 copy.64
  546.1 0.8 reshape.106
  546.9 0.2 copy.63
  547.0 0.8 reshape.105
  547.8 0.1 slice_select_fusion
  547.9 0.5 slice_bitcast_fusion
  548.4 2.0 fusion.1
  550.4 2.8 convert_element_type.167
  553.2 2.0 convert_bitcast_fusion
  555.2 1.5 copy.71
  556.6 1.5 copy.70
  558.1 1.0 copy.78
  559.1 0.8 copy.79
  (63 shorter events, 0.4 us)
Async XLA Ops:
  7.2 71.6 %copy-start.3 = (bf16[1,128,2048]{2,1,0:T(8,128)(2,1)S(1)}, bf16[1,128,2048]{2,1,0:T(8,128)(2,1)}, u32[]{:S(2)}) copy-start(bf16[1,128,2048]{2,1,0:T(8,128)(2,1)} %param.14) | copy-start | bytes 1572868
  7.2 72.6 %copy-start.27 = (s32[1,8]{1,0:T(1,128)S(1)}, s32[1,8]{1,0:T(1,128)}, u32[]{:S(2)}) copy-start(s32[1,8]{1,0:T(1,128)} %param.13) | copy-start | bytes 100
  7.2 89.5 %all-gather.4.cloned.1.call-start = ((), (), s32[]{:S(2)}) async-start(), calls=%async_computation.3 | async-start | bytes 1310720 | tf_op jit(solution)/shard_map/all_gather | solution.py:1312
  7.9 269.4 %all-gather.6.cloned.1.call-start = ((), (), s32[]{:S(2)}) async-start(), calls=%async_computation.4 | async-start | bytes 5242880 | tf_op jit(solution)/shard_map/all_gather | solution.py:1313
  8.7 278.0 %all-gather.8.cloned.1.call-start = ((), (), s32[]{:S(2)}) async-start(), calls=%async_computation.5 | async-start | bytes 4718592 | tf_op jit(solution)/shard_map/all_gather | solution.py:1324
  12.6 1.0 copy-start
  75.7 2.0 copy-start.17
  77.7 1.1 copy-start.24
  79.7 468.6 %reduce-scatter.5.cloned.1.call-start = ((), (), s32[]{:S(2)}) async-start(), calls=%async_computation.7 | async-start | bytes 4718592 | tf_op jit(solution)/shard_map/reduce_scatter | solution.py:1344
  80.3 2.8 copy-start.18
  95.1 0.8 copy-start.12
  95.9 0.8 copy-start.14
  96.7 13.7 %copy-start.6 = (bf16[1024,256]{1,0:T(8,128)(2,1)}, bf16[1024,256]{1,0:T(8,128)(2,1)S(1)}, u32[]{:S(2)}) copy-start(bf16[1024,256]{1,0:T(8,128)(2,1)S(1)} %get-tuple-element.45) | copy-start | bytes 1572868
  96.7 13.7 %copy-start.1 = (bf16[1,128,2048]{2,1,0:T(8,128)(2,1)S(1)}, bf16[1,128,2048]{2,1,0:T(8,128)(2,1)}, u32[]{:S(2)}) copy-start(bf16[1,128,2048]{2,1,0:T(8,128)(2,1)} %param.12) | copy-start | bytes 1572868
  96.7 13.7 %copy-start.8 = (bf16[64,8192]{1,0:T(8,128)(2,1)S(1)}, bf16[64,8192]{1,0:T(8,128)(2,1)}, u32[]{:S(2)}) copy-start(bf16[64,8192]{1,0:T(8,128)(2,1)} %gate_ref.1) | copy-start | bytes 3145732
  96.7 13.7 %copy-start.9 = (bf16[64,8192]{1,0:T(8,128)(2,1)S(1)}, bf16[64,8192]{1,0:T(8,128)(2,1)}, u32[]{:S(2)}) copy-start(bf16[64,8192]{1,0:T(8,128)(2,1)} %up_ref.1) | copy-start | bytes 3145732
  262.4 8.9 %copy-start.16 = (bf16[4,8,64,2048]{3,2,1,0:T(8,128)(2,1)}, bf16[4,8,64,2048]{3,2,1,0:T(8,128)(2,1)S(1)}, u32[]{:S(2)}) copy-start(bf16[4,8,64,2048]{3,2,1,0:T(8,128)(2,1)S(1)} %get-tuple-element.51) | copy-start | bytes 25165828
  262.4 8.9 %copy-start.20 = (bf16[1024,2048]{1,0:T(8,128)(2,1)}, bf16[1024,2048]{1,0:T(8,128)(2,1)S(1)}, u32[]{:S(2)}) copy-start(bf16[1024,2048]{1,0:T(8,128)(2,1)S(1)} %get-tuple-element.50) | copy-start | bytes 12582916
  271.3 3.3 copy-start.26
  286.7 261.7 %reduce-scatter.3.cloned.1.call-start = ((), (), s32[]{:S(2)}) async-start(), calls=%async_computation.6 | async-start | bytes 5242880 | tf_op jit(solution)/shard_map/reduce_scatter | solution.py:1362
  296.6 12.0 %copy-start.21 = (bf16[1024,2048]{1,0:T(8,128)(2,1)S(1)}, bf16[1024,2048]{1,0:T(8,128)(2,1)}, u32[]{:S(2)}) copy-start(bf16[1024,2048]{1,0:T(8,128)(2,1)} %copy-done.20) | copy-start | bytes 12582916
  333.0 2.2 copy-start.2
  335.2 1.1 copy-start.4
  442.9 1.3 copy-start.5
  444.3 1.0 copy-start.10
  445.2 2.0 copy-start.22
  447.2 101.2 %all-to-all-start = ((bf16[8,64,2048]{2,1,0:T(8,128)(2,1)}), bf16[8,64,2048]{2,1,0:T(8,128)(2,1)}, u32[]{:S(2)}, u32[]{:S(2)}) async-start(bf16[8,64,2048]{2,1,0:T(8,128)(2,1)} %bitcast.74), calls=%async_computation.1 | async-start | bytes 4194304 | tf_op jit(solution)/shard_map/all_to_all | solution.py:1143
  453.5 3.9 copy-start.13
  453.5 3.9 copy-start.15
  457.4 13.4 %copy-start.19 = (bf16[1024,2048]{1,0:T(8,128)(2,1)S(1)}, bf16[1024,2048]{1,0:T(8,128)(2,1)}, u32[]{:S(2)}) copy-start(bf16[1024,2048]{1,0:T(8,128)(2,1)} %copy-done.17) | copy-start | bytes 12582916
  470.8 2.6 copy-start.25
  473.4 2.4 copy-start.7
  473.5 2.4 copy-start.23
  475.9 1.3 copy-start.11
Sparse Core Ops, SparseCore 0:
  9.6 26.1 all-gather.3
  37.3 32.5 all-gather.5
  79.9 116.4 all-gather.7
  286.8 107.4 reduce-scatter.4
  396.7 56.5 reduce-scatter.2

commit v11 on v10

--- a/solution.py
+++ b/solution.py
@@ -1170,7 +1170,8 @@
 
 
 def attention_forward_kernel(
-    block_rows, qkv_ref, cos_ref, sin_ref, doc_col_ref, doc_row_ref, q_ref, kv_ref, out_ref, lse_ref
+    block_rows, qkv_ref, wo_ref, cos_ref, sin_ref, doc_col_ref, doc_row_ref, q_ref, kv_ref, out_ref, lse_ref,
+    branch_ref,
 ):
     length = qkv_ref.shape[0]
     group = H // KVH
@@ -1198,6 +1199,7 @@
             mixed = dot_plain(weights.astype(jnp.bfloat16), values)
             out_ref[rows, cols] = (mixed / total).astype(jnp.bfloat16)
             lse_ref[rows, head : head + 1] = top + jnp.log(total)
+        branch_ref[rows, :] = dot_plain(out_ref[rows, :], wo_ref[...]).astype(jnp.bfloat16)
 
 
 def attention_backward_kernel(
@@ -1238,7 +1240,7 @@
     grad_ref[:, width:] = jnp.where(lane < HD, turned, pair).astype(jnp.bfloat16)
 
 
-def attention_forward(qkv, tables, block_rows):
+def attention_forward(qkv, w_output, tables, block_rows):
     length = qkv.shape[0]
     width = (H // KVH) * HD
     return pl.pallas_call(
@@ -1248,12 +1250,13 @@
             jax.ShapeDtypeStruct((length, 2 * HD), jnp.bfloat16),
             jax.ShapeDtypeStruct((length, width), jnp.bfloat16),
             jax.ShapeDtypeStruct((length, H // KVH), jnp.float32),
+            jax.ShapeDtypeStruct((length, w_output.shape[1]), jnp.bfloat16),
         ),
-        in_specs=in_vmem(5),
-        out_specs=tuple(in_vmem(4)),
+        in_specs=in_vmem(6),
+        out_specs=tuple(in_vmem(5)),
         compiler_params=pltpu.CompilerParams(vmem_limit_bytes=24 * 2**20),
         name="attend",
-    )(qkv, *tables)
+    )(qkv, w_output, *tables)
 
 
 def attention_backward(q, kv, grad_out, lse, tables, block_rows):
@@ -1323,10 +1326,8 @@
     normed1, grad_mlp = lax.optimization_barrier((normed1, grad_mlp))
     grad_mlp = lax.all_gather(grad_mlp, "ctx", axis=0, tiled=True)
     qkv = dot_plain(normed1, w_qkv)
-    q, kv, mixed_heads, log_sum = attention_forward(qkv, tables, block_rows)
-    hidden, w_gu, normed2 = mlp_forward(
-        dot_plain(mixed_heads, wo_mine).astype(bf16), tokens[0], gains, w_gate, w_up
-    )
+    q, kv, mixed_heads, log_sum, branch1 = attention_forward(qkv, wo_mine, tables, block_rows)
+    hidden, w_gu, normed2 = mlp_forward(branch1, tokens[0], gains, w_gate, w_up)
     w_gu = rows_of(rows_of(w_gu))
 
     gate_up = dot_plain(normed2, w_gu)

time: 577 us -> 579 us (level)
  matrix products: 91.4 us -> 78.8 us
  local copies, waits for them, and re-layouts: 27.8 us -> 36.3 us
  Pallas kernels: 410 us -> 416 us
    dot_general x4 -> x3, matrix products: 35.7 us -> 23.1 us  [dot_plain(): return jnp.dot(left, right, preferred_element_type=jnp.float32)]
    pallas_call x1, Pallas kernels: 8.22 us -> 20.7 us  [attention_forward(): pl.pallas_call(functools.partial(attention_forward_kernel, block_rows), o...]
    unnamed x58 -> x62, local copies, waits for them, and re-layouts: 18.3 us -> 26.8 us
    pallas_call x2, Pallas kernels: 259 us -> 253 us  [scatter_gather(): pl.pallas_call(functools.partial(kernel, ctx_size, fsdp_size), out_shape=...]
  transfers between devices with their start and end apart: 6 -> 6, of which waited for: 0 -> 0; matrix products, arithmetic and copies ran while one was open for 19% -> 16% of each run, Pallas kernels for 72% -> 73%
where the time goes in v11:
time: 579 us; the launch traced here: 569 us
  Pallas kernels  416 us (72%)
  matrix products  78.8 us (14%)
  local copies, waits for them, and re-layouts  36.3 us (6%)
  other arithmetic  14.6 us (3%)
  between operations  14.5 us (3%)
  starting transfers between devices  7.44 us (1%)
    pallas_call x2, Pallas kernels, scatter_gather(): pl.pallas_call(functools.partial(kernel, ctx_size, fsdp_size), out_shape=...  253 us
    pallas_call x1, Pallas kernels, finish_layer(): pl.pallas_call(functools.partial(finish_kernel, ctx_size, fsdp_size), out...  67.2 us
    pallas_call x1, Pallas kernels, start_layer(): pl.pallas_call(functools.partial(start_kernel, ctx_size, fsdp_size), out_...  62 us
    dot_general x4, matrix products, dot_back(): lax.dot_general(left, right, (((1,), (1,)), ((), ())), preferred_element_...  30.9 us
    unnamed x62, local copies, waits for them, and re-layouts  26.8 us
    dot_general x4, matrix products, dot_outer(): lax.dot_general(left, right, (((0,), (0,)), ((), ())), preferred_element_...  24.8 us
    dot_general x3, matrix products, dot_plain(): return jnp.dot(left, right, preferred_element_type=jnp.float32)  23.1 us
    pallas_call x1, Pallas kernels, attention_forward(): pl.pallas_call(functools.partial(attention_forward_kernel, block_rows), o...  20.7 us
  transfers between devices with their start and end apart: 6, of which 0 were waited for; matrix products, arithmetic and copies ran while one was open for 16% of the time, Pallas kernels for 73%

profile of v11, /device:TPU:0, one launch (start us, length us, event | category | flops | bytes accessed | tf_op | source)
XLA Modules:
  0.0 569.0 jit_solution(1808831149044715579)
XLA Ops:
  7.2 0.7 all-gather.4.cloned.1.call-update
  8.0 0.7 all-gather.6.cloned.1.call-update
  8.7 1.0 reshape.97
  9.8 1.0 reshape.98
  10.8 1.0 copy.75
  11.7 0.7 convert_multiply_fusion.1
  12.5 0.1 maximum_bitcast_fusion.parts_ref
  12.6 1.0 copy-done
  13.7 62.0 %start_layer.1 = (bf16[1024,2048]{1,0:T(8,128)(2,1)S(1)}, f32[8,2048]{1,0:T(8,128)S(1)}, bf16[32,64,384]{2,1,0:T(8,128)(2,1)S(1)}) custom-call(bf16[128,2048]{1,0:T(8,128)(2,1)S(1)} %bitcast.68, f32[8,128]{1,0:T(8,128)S(1)} %select_maximum_fusion.tile_ref, bf16[8,64,384]{2,1,0:T(8,128)(2,1)S(1)} %maximum_bitcast_fusion.parts_ref), custom_call_target="tpu_custom_call" | custom-call | bytes 150000000 | tf_op jit(solution)/shard_map/start_layer/pallas_call | solution.py:698
  75.7 2.0 copy-done.17
  77.7 1.1 copy-done.24
  78.8 0.9 multiply_convert_fusion.2
  79.8 0.2 reduce-window_clone.1
  80.1 0.2 copy.57.doc_col_ref
  80.3 1.9 fusion.2
  82.2 0.9 pad_maximum_fusion.3
  83.1 4.9 fusion.5.qkv_ref
  88.0 1.6 copy-done.6
  89.6 1.3 copy-done.7
  91.0 20.7 %attend.1 = (bf16[1024,256]{1,0:T(8,128)(2,1)S(1)}, bf16[1024,128]{1,0:T(8,128)(2,1)S(1)}, bf16[1024,256]{1,0:T(8,128)(2,1)S(1)}, f32[1024,4]{1,0:T(8,128)S(1)}, bf16[1024,2048]{1,0:T(8,128)(2,1)S(1)}) custom-call(f32[1024,384]{1,0:T(8,128)S(1)} %copy-done.6, bf16[256,2048]{1,0:T(8,128)(2,1)S(1)} %copy-done.7, f32[1024,128]{1,0:T(8,128)S(1)} %get-tuple-element.88.cos_ref, ...), custom_call_target="tpu_custom_call" | custom-call | tf_op jit(solution)/shard_map/attend/pallas_call | solution.py:1246
  111.7 0.8 copy-done.12
  112.5 0.8 copy-done.14
  113.2 0.8 copy-done.26
  114.0 1.5 copy-done.8
  115.6 1.2 copy-done.9
  116.8 145.5 %shard_map.203 = (f32[128,2048]{1,0:T(8,128)S(1)}, bf16[4,8,64,2048]{3,2,1,0:T(8,128)(2,1)S(1)}, bf16[1024,2048]{1,0:T(8,128)(2,1)S(1)}) custom-call(bf16[1024,2048]{1,0:T(8,128)(2,1)S(1)} %get-tuple-element.46.x_ref, bf16[128,2048]{1,0:T(8,128)(2,1)S(1)} %bitcast.69, f32[8,2048]{1,0:T(8,128)S(1)} %get-tuple-element.47.gains_ref, ...), custom_call_target="tpu_custom_call" | custom-call | bytes 150000000 | tf_op jit(solution)/shard_map/pallas_call | solution.py:928
  262.3 2.0 copy-done.20
  264.3 8.9 %fusion.6 = f32[1024,2048]{1,0:T(8,128)S(1)} fusion(bf16[1024,2048]{1,0:T(8,128)(2,1)S(1)} %get-tuple-element.51, bf16[2048,2048]{1,0:T(8,128)(2,1)S(1)} %bitcast.78), kind=kOutput, calls=%fused_computation.47 | convolution fusion | flops 8589934592 | bytes 20971520 | tf_op jit(solution)/shard_map/dot_general | solution.py:59
  273.2 3.3 copy-done.28
  276.5 2.7 fusion
  279.2 9.3 %convolution_convert_fusion.4 = bf16[1024,2048]{1,0:T(8,128)(2,1)} fusion(bf16[1024,1024]{1,0:T(8,128)(2,1)} %fusion, bf16[1024,2048]{1,0:T(8,128)(2,1)} %all-gather.6.cloned.1.call-done), kind=kOutput, calls=%fused_computation.10 | convolution fusion | flops 4297064448 | bytes 10485760 | tf_op jit(solution)/shard_map/dot_general | solution.py:59
  288.6 0.4 reduce-scatter.3.cloned.1.call-start
  289.1 9.4 %convolution_convert_fusion.3 = bf16[1024,2048]{1,0:T(8,128)(2,1)} fusion(bf16[1024,1024]{1,0:T(8,128)(2,1)} %fusion, bf16[1024,2048]{1,0:T(8,128)(2,1)} %all-gather.8.cloned.1.call-done), kind=kOutput, calls=%fused_computation.9 | convolution fusion | flops 4297064448 | bytes 10485760 | tf_op jit(solution)/shard_map/dot_general | solution.py:69
  298.5 12.0 %multiply_convert_fusion.1 = (bf16[1024,1024]{1,0:T(8,128)(2,1)S(1)}, bf16[1024,1024]{1,0:T(8,128)(2,1)S(1)}) fusion(f32[1024,2048]{1,0:T(8,128)} %copy-done.28, bf16[1024,2048]{1,0:T(8,128)(2,1)} %all-gather.8.cloned.1.call-done, bf16[1024,2048]{1,0:T(8,128)(2,1)} %all-gather.6.cloned.1.call-done), kind=kOutput, calls=%fused_computation.5 | convolution fusion | flops 4308598784 | bytes 20971520 | tf_op jit(solution)/shard_map/dot_general | solution.py:63
  310.5 11.8 %convolution_convert_fusion = bf16[2048,2048]{1,0:T(8,128)(2,1)} fusion(bf16[1024,2048]{1,0:T(8,128)(2,1)S(1)} %copy-done.21, bf16[1024,1024]{1,0:T(8,128)(2,1)S(1)} %get-tuple-element.76, bf16[1024,1024]{1,0:T(8,128)(2,1)S(1)} %get-tuple-element.75), kind=kOutput, calls=%fused_computation | convolution fusion | flops 8602517504 | bytes 16777216 | tf_op jit(solution)/shard_map/dot_general | solution.py:69
  322.2 12.7 %convolution_convert_fusion.2.x_ref = bf16[1024,2048]{1,0:T(8,128)(2,1)} fusion(bf16[2048,2048]{1,0:T(8,128)(2,1)} %bitcast.79, bf16[1024,1024]{1,0:T(8,128)(2,1)S(1)} %get-tuple-element.76, bf16[1024,1024]{1,0:T(8,128)(2,1)S(1)} %get-tuple-element.75), kind=kOutput, calls=%fused_computation.8 | convolution fusion | flops 8600420352 | bytes 16777216 | tf_op jit(solution)/shard_map/dot_general | solution.py:63
  335.0 2.2 copy-done.2
  337.1 1.0 copy-done.4
  338.2 107.2 %shard_map.204 = (f32[128,2048]{1,0:T(8,128)S(1)}, f32[2,2048]{1,0:T(2,128)S(1)}, bf16[512,2048]{1,0:T(8,128)(2,1)S(1)}, bf16[1024,2048]{1,0:T(8,128)(2,1)S(1)}) custom-call(bf16[1024,2048]{1,0:T(8,128)(2,1)S(1)} %copy-done.2, f32[128,2048]{1,0:T(8,128)S(1)} %get-tuple-element.48.hidden_ref, bf16[128,2048]{1,0:T(8,128)(2,1)S(1)} %bitcast.71, ...), custom_call_target="tpu_custom_call" | custom-call | bytes 150000000 | tf_op jit(solution)/shard_map/pallas_call | solution.py:928
  445.4 1.3 copy-done.5
  446.7 1.0 copy-done.10
  447.7 2.0 copy-done.22
  449.6 6.8 %all-to-all-start = ((bf16[8,64,2048]{2,1,0:T(8,128)(2,1)}), bf16[8,64,2048]{2,1,0:T(8,128)(2,1)}, u32[]{:S(2)}, u32[]{:S(2)}) async-start(bf16[8,64,2048]{2,1,0:T(8,128)(2,1)} %bitcast.72), calls=%async_computation.1 | async-start | bytes 4194304 | tf_op jit(solution)/shard_map/all_to_all | solution.py:1143
  456.5 3.9 convolution_convert_fusion.7.do_ref
  460.4 13.4 %attend_back.1 = bf16[1024,384]{1,0:T(8,128)(2,1)S(1)} custom-call(bf16[1024,256]{1,0:T(8,128)(2,1)S(1)} %copy-done.13, bf16[1024,128]{1,0:T(8,128)(2,1)S(1)} %get-tuple-element.50.kv_ref, bf16[1024,256]{1,0:T(8,128)(2,1)S(1)} %convolution_convert_fusion.7.do_ref, f32[1024,4]{1,0:T(8,128)S(1)} %copy-done.15, f32[1024,128]{1,0:T(8,128)S(1)} %get-tuple-element.88.cos_ref, ...), custom_call_target="tpu_custom_call" | custom-call | tf_op jit(solution)/shard_map/attend_back/pallas_call | solution.py:1264
  473.8 2.4 convolution_convert_fusion.5
  476.2 0.2 copy.74
  476.5 2.4 convolution_convert_fusion.1.x_ref
  478.9 1.3 convolution_convert_fusion.6
  480.1 67.2 %finish_layer.1 = (f32[128,2048]{1,0:T(8,128)S(1)}, f32[8,128]{1,0:T(8,128)S(1)}, f32[64,2048]{1,0:T(8,128)S(1)}, bf16[8,64,384]{2,1,0:T(8,128)(2,1)S(1)}) custom-call(bf16[1024,2048]{1,0:T(8,128)(2,1)S(1)} %convolution_convert_fusion.1.x_ref, bf16[128,2048]{1,0:T(8,128)(2,1)S(1)} %bitcast.70, f32[128,2048]{1,0:T(8,128)S(1)} %copy-done.11, ...), custom_call_target="tpu_custom_call" | custom-call | bytes 150000000 | tf_op jit(solution)/shard_map/finish_layer/pallas_call | solution.py:1108
  547.4 0.8 copy.69
  548.2 0.1 convert_bitcast_fusion.3
  548.3 0.2 copy.64
  548.5 0.8 reshape.106
  549.3 0.2 copy.63
  549.4 0.8 reshape.105
  550.3 0.5 slice_bitcast_fusion
  550.8 2.0 fusion.1
  552.8 2.8 convert_element_type.163
  555.6 2.0 convert_bitcast_fusion
  557.6 1.5 copy.71
  559.0 1.5 copy.70
  560.5 1.0 copy.78
  561.5 0.8 copy.79
  (66 shorter events, 0.7 us)
Async XLA Ops:
  7.2 71.6 %copy-start.3 = (bf16[1,128,2048]{2,1,0:T(8,128)(2,1)S(1)}, bf16[1,128,2048]{2,1,0:T(8,128)(2,1)}, u32[]{:S(2)}) copy-start(bf16[1,128,2048]{2,1,0:T(8,128)(2,1)} %param.14) | copy-start | bytes 1572868
  7.2 72.6 %copy-start.29 = (s32[1,8]{1,0:T(1,128)S(1)}, s32[1,8]{1,0:T(1,128)}, u32[]{:S(2)}) copy-start(s32[1,8]{1,0:T(1,128)} %param.13) | copy-start | bytes 100
  7.2 80.8 %all-gather.4.cloned.1.call-start = ((), (), s32[]{:S(2)}) async-start(), calls=%async_computation.3 | async-start | bytes 1310720 | tf_op jit(solution)/shard_map/all_gather | solution.py:1315
  7.9 271.3 %all-gather.6.cloned.1.call-start = ((), (), s32[]{:S(2)}) async-start(), calls=%async_computation.4 | async-start | bytes 5242880 | tf_op jit(solution)/shard_map/all_gather | solution.py:1316
  8.7 279.9 %all-gather.8.cloned.1.call-start = ((), (), s32[]{:S(2)}) async-start(), calls=%async_computation.5 | async-start | bytes 4718592 | tf_op jit(solution)/shard_map/all_gather | solution.py:1327
  12.6 1.0 copy-start
  75.7 2.0 copy-start.17
  77.7 1.1 copy-start.24
  79.7 471.1 %reduce-scatter.5.cloned.1.call-start = ((), (), s32[]{:S(2)}) async-start(), calls=%async_computation.7 | async-start | bytes 4718592 | tf_op jit(solution)/shard_map/reduce_scatter | solution.py:1345
  80.3 2.8 copy-start.18
  88.0 26.0 %copy-start.1 = (bf16[1,128,2048]{2,1,0:T(8,128)(2,1)S(1)}, bf16[1,128,2048]{2,1,0:T(8,128)(2,1)}, u32[]{:S(2)}) copy-start(bf16[1,128,2048]{2,1,0:T(8,128)(2,1)} %param.12) | copy-start | bytes 1572868
  88.0 1.6 copy-start.6
  89.6 1.3 copy-start.7
  111.7 0.8 copy-start.12
  112.5 0.8 copy-start.14
  113.2 0.8 copy-start.26
  114.0 1.5 copy-start.8
  115.6 1.2 copy-start.9
  262.3 2.1 copy-start.20
  262.3 10.9 %copy-start.16 = (bf16[4,8,64,2048]{3,2,1,0:T(8,128)(2,1)}, bf16[4,8,64,2048]{3,2,1,0:T(8,128)(2,1)S(1)}, u32[]{:S(2)}) copy-start(bf16[4,8,64,2048]{3,2,1,0:T(8,128)(2,1)S(1)} %get-tuple-element.52) | copy-start | bytes 25165828
  273.2 3.3 copy-start.28
  288.6 262.2 %reduce-scatter.3.cloned.1.call-start = ((), (), s32[]{:S(2)}) async-start(), calls=%async_computation.6 | async-start | bytes 5242880 | tf_op jit(solution)/shard_map/reduce_scatter | solution.py:1363
  298.5 12.0 %copy-start.21 = (bf16[1024,2048]{1,0:T(8,128)(2,1)S(1)}, bf16[1024,2048]{1,0:T(8,128)(2,1)}, u32[]{:S(2)}) copy-start(bf16[1024,2048]{1,0:T(8,128)(2,1)} %copy-done.20) | copy-start | bytes 12582916
  335.0 2.2 copy-start.2
  337.1 1.0 copy-start.4
  445.4 1.3 copy-start.5
  446.7 1.0 copy-start.10
  447.7 2.0 copy-start.22
  449.6 101.1 %all-to-all-start = ((bf16[8,64,2048]{2,1,0:T(8,128)(2,1)}), bf16[8,64,2048]{2,1,0:T(8,128)(2,1)}, u32[]{:S(2)}, u32[]{:S(2)}) async-start(bf16[8,64,2048]{2,1,0:T(8,128)(2,1)} %bitcast.72), calls=%async_computation.1 | async-start | bytes 4194304 | tf_op jit(solution)/shard_map/all_to_all | solution.py:1143
  456.5 3.9 copy-start.13
  456.5 3.9 copy-start.15
  460.4 13.4 %copy-start.19 = (bf16[1024,2048]{1,0:T(8,128)(2,1)S(1)}, bf16[1024,2048]{1,0:T(8,128)(2,1)}, u32[]{:S(2)}) copy-start(bf16[1024,2048]{1,0:T(8,128)(2,1)} %copy-done.17) | copy-start | bytes 12582916
  473.8 2.6 copy-start.25
  476.4 2.4 copy-start.23
  476.4 2.4 copy-start.27
  478.8 1.3 copy-start.11
Sparse Core Ops, SparseCore 0:
  9.6 26.1 all-gather.3
  37.3 32.5 all-gather.5
  79.9 108.7 all-gather.7
  288.7 108.8 reduce-scatter.4
  400.0 55.1 reduce-scatter.2

commit v12 on v10

--- a/solution.py
+++ b/solution.py
@@ -1272,6 +1272,49 @@
     )(q, kv, grad_out, lse, *tables)
 
 
+def mlp_kernel(normed_ref, grad_ref, gu_ref, down_ref, activ_ref, out_ref, grad_gu_ref, back_ref):
+    ff = down_ref.shape[0]
+    bf16 = jnp.bfloat16
+    gate_up = dot_plain(normed_ref[...], gu_ref[...])
+    gate, up = gate_up[:, :ff], gate_up[:, ff:]
+    sig = jax.nn.sigmoid(gate)
+    silu = gate * sig
+    activ_ref[...] = (silu * up).astype(bf16)
+    grad_act = dot_back(grad_ref[...], down_ref[...])
+    grad_gu_ref[:, :ff] = (grad_act * up * (sig * (1.0 + gate * (1.0 - sig)))).astype(bf16)
+    grad_gu_ref[:, ff:] = (grad_act * silu).astype(bf16)
+    out_ref[...] = dot_plain(activ_ref[...], down_ref[...]).astype(bf16)
+    back_ref[...] = dot_back(grad_gu_ref[...], gu_ref[...]).astype(bf16)
+
+
+def mlp(normed, grad_out, w_gu, w_down):
+    rows, model = normed.shape
+    ff = w_down.shape[0]
+    block_rows = math.gcd(rows, 256)
+
+    def by_rows(width):
+        return pl.BlockSpec((block_rows, width), lambda i: (i, 0))
+
+    def whole(shape):
+        return pl.BlockSpec(shape, lambda i: (0, 0), pipeline_mode=pl.Buffered(1))
+
+    def like(width):
+        return jax.ShapeDtypeStruct((rows, width), jnp.bfloat16)
+
+    return pl.pallas_call(
+        mlp_kernel,
+        grid=(rows // block_rows,),
+        in_specs=[by_rows(model), by_rows(model), whole(w_gu.shape), whole(w_down.shape)],
+        out_specs=(by_rows(ff), by_rows(model), by_rows(2 * ff), by_rows(model)),
+        out_shape=(like(ff), like(model), like(2 * ff), like(model)),
+        compiler_params=pltpu.CompilerParams(vmem_limit_bytes=44 * 2**20),
+        cost_estimate=pl.CostEstimate(
+            flops=12 * rows * model * ff, bytes_accessed=30_000_000, transcendentals=rows * ff
+        ),
+        name="mlp",
+    )(normed, grad_out, w_gu, w_down)
+
+
 def on_device(
     tokens,
     doc_lengths,
@@ -1291,7 +1334,7 @@
     fsdp_size = lax.axis_size("fsdp")
     length = local_rows * ctx_size
     group_width = (H // KVH) * HD
-    ff_slice = FF // ctx_size
+    ff_slice = w_gate.shape[1] // ctx_size
     held_rows = w_query.shape[0]
     bf16 = jnp.bfloat16
 
@@ -1329,32 +1372,11 @@
     )
     w_gu = rows_of(rows_of(w_gu))
 
-    gate_up = dot_plain(normed2, w_gu)
-    gate_pre, up_pre = gate_up[:, :ff_slice], gate_up[:, ff_slice:]
-    sig_gate = jax.nn.sigmoid(gate_pre)
-    silu_gate = gate_pre * sig_gate
-    activ = (silu_gate * up_pre).astype(bf16)
-    activ, gate_up = lax.optimization_barrier((activ, gate_up))
-    gate_pre, up_pre = gate_up[:, :ff_slice], gate_up[:, ff_slice:]
-    sig_gate = jax.nn.sigmoid(gate_pre)
-    silu_gate = gate_pre * sig_gate
-    out_terms, grad_mlp = lax.optimization_barrier(
-        (dot_plain(activ, wd_mine).astype(bf16), grad_mlp)
-    )
+    activ, out_terms, grad_gu, partial2 = mlp(normed2, grad_mlp, w_gu, wd_mine)
     branch = lax.psum_scatter(out_terms, "ctx", scatter_dimension=0, tiled=True)
-
-    silu_slope = sig_gate * (1.0 + gate_pre * (1.0 - sig_gate))
-    grad_act = dot_back(grad_mlp, wd_mine)
-    grad_gu = jnp.concatenate(
-        [(grad_act * up_pre * silu_slope).astype(bf16), (grad_act * silu_gate).astype(bf16)], axis=1
-    )
-    partial2, gu_terms, wd_terms = lax.optimization_barrier(
-        (
-            dot_back(grad_gu, w_gu).astype(bf16),
-            dot_outer(normed2, grad_gu).astype(bf16),
-            dot_outer(activ, grad_mlp).astype(bf16),
-        )
-    )
+    gu_terms = dot_outer(normed2, grad_gu).astype(bf16)
+    wd_terms = dot_outer(activ, grad_mlp).astype(bf16)
+    partial2, gu_terms, wd_terms = lax.optimization_barrier((partial2, gu_terms, wd_terms))
     grad_hidden, grad_g2, gu_back, grad_attn = mlp_backward(
         partial2, hidden, cotangent[0], gains, gu_terms.reshape(fsdp_size, -1, gu_terms.shape[1])
     )

time: 577 us -> 572 us (level)
  matrix products: 91.4 us -> 40.1 us
  Pallas kernels: 410 us -> 456 us
    pallas_call x0 -> x1, Pallas kernels: none -> 33.7 us  [mlp(): pl.pallas_call(mlp_kernel, grid=(rows // block_rows,), in_specs=[by_rows(...]
    dot_general x4 -> x2, matrix products: 35.7 us -> 6.65 us  [dot_plain(): return jnp.dot(left, right, preferred_element_type=jnp.float32)]
    dot_general x4 -> x2, matrix products: 30.9 us -> 6.28 us  [dot_back(): lax.dot_general(left, right, (((1,), (1,)), ((), ())), preferred_element_...]
    pallas_call x2, Pallas kernels: 259 us -> 271 us  [scatter_gather(): pl.pallas_call(functools.partial(kernel, ctx_size, fsdp_size), out_shape=...]
  transfers between devices with their start and end apart: 6 -> 6, of which waited for: 0 -> 0; matrix products, arithmetic and copies ran while one was open for 19% -> 9% of each run, Pallas kernels for 72% -> 75%
where the time goes in v12:
time: 572 us; the launch traced here: 562 us
  Pallas kernels  456 us (80%)
  matrix products  40.1 us (7%)
  local copies, waits for them, and re-layouts  33.2 us (6%)
  between operations  14.4 us (3%)
  other arithmetic  11.8 us (2%)
    pallas_call x2, Pallas kernels, scatter_gather(): pl.pallas_call(functools.partial(kernel, ctx_size, fsdp_size), out_shape=...  271 us
    pallas_call x1, Pallas kernels, finish_layer(): pl.pallas_call(functools.partial(finish_kernel, ctx_size, fsdp_size), out...  67.2 us
    pallas_call x1, Pallas kernels, start_layer(): pl.pallas_call(functools.partial(start_kernel, ctx_size, fsdp_size), out_...  62 us
    pallas_call x1, Pallas kernels, mlp(): pl.pallas_call(mlp_kernel, grid=(rows // block_rows,), in_specs=[by_rows(...  33.7 us
    dot_general x4, matrix products, dot_outer(): lax.dot_general(left, right, (((0,), (0,)), ((), ())), preferred_element_...  27.1 us
    unnamed x58, local copies, waits for them, and re-layouts  23.7 us
    pallas_call x1, Pallas kernels, attention_backward(): pl.pallas_call(functools.partial(attention_backward_kernel, block_rows),...  13.4 us
  transfers between devices with their start and end apart: 6, of which 0 were waited for; matrix products, arithmetic and copies ran while one was open for 9% of the time, Pallas kernels for 75%

profile of v12, /device:TPU:0, one launch (start us, length us, event | category | flops | bytes accessed | tf_op | source)
XLA Modules:
  0.0 562.0 jit_solution(12635748471825691105)
XLA Ops:
  7.2 0.7 all-gather.4.cloned.1.call-update
  7.9 0.0 all-gather.8.cloned.1.call-start
  8.0 0.7 all-gather.8.cloned.1.call-update
  8.7 0.0 all-gather.6.cloned.1.call-start
  8.7 1.0 reshape.97
  9.8 1.0 reshape.98
  10.8 1.0 copy.66
  11.7 0.7 convert_multiply_fusion.1
  12.4 0.1 select_maximum_fusion.tile_ref
  12.5 0.1 maximum_bitcast_fusion.parts_ref
  12.6 1.0 copy-done
  13.7 62.0 %start_layer.1 = (bf16[1024,2048]{1,0:T(8,128)(2,1)S(1)}, f32[8,2048]{1,0:T(8,128)S(1)}, bf16[32,64,384]{2,1,0:T(8,128)(2,1)S(1)}) custom-call(bf16[128,2048]{1,0:T(8,128)(2,1)S(1)} %bitcast.64, f32[8,128]{1,0:T(8,128)S(1)} %select_maximum_fusion.tile_ref, bf16[8,64,384]{2,1,0:T(8,128)(2,1)S(1)} %maximum_bitcast_fusion.parts_ref), custom_call_target="tpu_custom_call" | custom-call | bytes 150000000 | tf_op jit(solution)/shard_map/start_layer/pallas_call | solution.py:698
  75.7 2.0 copy-done.18
  77.7 1.1 copy-done.24
  78.9 0.9 multiply_convert_fusion
  79.8 0.0 reduce-scatter.5.cloned.1.call-start
  79.9 0.2 reduce-window_clone.1
  80.0 0.1 convert_reduce_fusion
  80.1 0.2 copy.51.doc_col_ref
  80.4 1.9 fusion.1
  82.3 0.9 pad_maximum_fusion
  83.2 3.7 fusion.2.qkv_ref
  86.9 8.2 %attend.1 = (bf16[1024,256]{1,0:T(8,128)(2,1)S(1)}, bf16[1024,128]{1,0:T(8,128)(2,1)S(1)}, bf16[1024,256]{1,0:T(8,128)(2,1)S(1)}, f32[1024,4]{1,0:T(8,128)S(1)}) custom-call(f32[1024,384]{1,0:T(8,128)S(1)} %fusion.2.qkv_ref, f32[1024,128]{1,0:T(8,128)S(1)} %get-tuple-element.84.cos_ref, f32[1024,128]{1,0:T(8,128)S(1)} %get-tuple-element.85.sin_ref, ...), custom_call_target="tpu_custom_call" | custom-call | tf_op jit(solution)/shard_map/attend/pallas_call | solution.py:1244
  95.2 0.8 copy-done.13
  96.0 0.8 copy-done.15
  96.8 2.9 convolution_convert_fusion.2.x_ref
  99.7 155.7 %shard_map.203 = (f32[128,2048]{1,0:T(8,128)S(1)}, bf16[4,8,64,2048]{3,2,1,0:T(8,128)(2,1)S(1)}, bf16[1024,2048]{1,0:T(8,128)(2,1)S(1)}) custom-call(bf16[1024,2048]{1,0:T(8,128)(2,1)S(1)} %convolution_convert_fusion.2.x_ref, bf16[128,2048]{1,0:T(8,128)(2,1)S(1)} %bitcast.65, f32[8,2048]{1,0:T(8,128)S(1)} %get-tuple-element.46.gains_ref, ...), custom_call_target="tpu_custom_call" | custom-call | bytes 150000000 | tf_op jit(solution)/shard_map/pallas_call | solution.py:928
  255.5 3.3 copy-done.17
  258.7 2.0 copy-done.23
  260.7 33.7 %mlp.1 = (bf16[1024,1024]{1,0:T(8,128)(2,1)S(1)}, bf16[1024,2048]{1,0:T(8,128)(2,1)S(1)}, bf16[1024,2048]{1,0:T(8,128)(2,1)}, bf16[1024,2048]{1,0:T(8,128)(2,1)}) custom-call(bf16[1024,2048]{1,0:T(8,128)(2,1)} %copy-done.23, bf16[1024,2048]{1,0:T(8,128)(2,1)} %all-gather.6.cloned.1.call-done.grad_ref, bf16[2048,2048]{1,0:T(8,128)(2,1)} %bitcast.74, ...), custom_call_target="tpu_custom_call" | custom-call | flops 25769803776 | bytes 30000000 | tf_op jit(solution)/shard_map/mlp/pallas_call | solution.py:1304
  294.4 1.9 copy-done.3
  296.3 1.3 copy-done.26
  297.7 0.3 reduce-scatter.3.cloned.1.call-start
  298.0 9.4 %convolution_convert_fusion.3 = bf16[1024,2048]{1,0:T(8,128)(2,1)} fusion(bf16[1024,1024]{1,0:T(8,128)(2,1)} %copy-done.26, bf16[1024,2048]{1,0:T(8,128)(2,1)} %all-gather.6.cloned.1.call-done.grad_ref), kind=kOutput, calls=%fused_computation.3 | convolution fusion | flops 4297064448 | bytes 10485760 | tf_op jit(solution)/shard_map/dot_general | solution.py:69
  307.3 14.1 %convolution_convert_fusion = bf16[2048,2048]{1,0:T(8,128)(2,1)} fusion(bf16[1024,2048]{1,0:T(8,128)(2,1)} %copy-done.23, bf16[1024,2048]{1,0:T(8,128)(2,1)} %get-tuple-element.54), kind=kOutput, calls=%fused_computation | convolution fusion | flops 8594128896 | bytes 16777216 | tf_op jit(solution)/shard_map/dot_general | solution.py:69
  321.5 2.3 copy-done.2
  323.8 1.1 copy-done.5
  324.8 115.6 %shard_map.204 = (f32[128,2048]{1,0:T(8,128)S(1)}, f32[2,2048]{1,0:T(2,128)S(1)}, bf16[512,2048]{1,0:T(8,128)(2,1)S(1)}, bf16[1024,2048]{1,0:T(8,128)(2,1)S(1)}) custom-call(bf16[1024,2048]{1,0:T(8,128)(2,1)S(1)} %copy-done.2, f32[128,2048]{1,0:T(8,128)S(1)} %get-tuple-element.47.hidden_ref, bf16[128,2048]{1,0:T(8,128)(2,1)S(1)} %bitcast.67, ...), custom_call_target="tpu_custom_call" | custom-call | bytes 150000000 | tf_op jit(solution)/shard_map/pallas_call | solution.py:928
  440.4 1.3 copy-done.6
  441.7 1.0 copy-done.11
  442.7 2.0 copy-done.21
  444.6 4.8 all-to-all-start
  449.5 3.9 convolution_convert_fusion.6.do_ref
  453.5 13.4 %attend_back.1 = bf16[1024,384]{1,0:T(8,128)(2,1)S(1)} custom-call(bf16[1024,256]{1,0:T(8,128)(2,1)S(1)} %copy-done.14, bf16[1024,128]{1,0:T(8,128)(2,1)S(1)} %get-tuple-element.49.kv_ref, bf16[1024,256]{1,0:T(8,128)(2,1)S(1)} %convolution_convert_fusion.6.do_ref, f32[1024,4]{1,0:T(8,128)S(1)} %copy-done.16, f32[1024,128]{1,0:T(8,128)S(1)} %get-tuple-element.84.cos_ref, ...), custom_call_target="tpu_custom_call" | custom-call | tf_op jit(solution)/shard_map/attend_back/pallas_call | solution.py:1261
  466.9 2.4 convolution_convert_fusion.4
  469.3 0.2 copy.65
  469.5 2.4 convolution_convert_fusion.1.x_ref
  471.9 1.3 convolution_convert_fusion.5
  473.2 67.2 %finish_layer.1 = (f32[128,2048]{1,0:T(8,128)S(1)}, f32[8,128]{1,0:T(8,128)S(1)}, f32[64,2048]{1,0:T(8,128)S(1)}, bf16[8,64,384]{2,1,0:T(8,128)(2,1)S(1)}) custom-call(bf16[1024,2048]{1,0:T(8,128)(2,1)S(1)} %convolution_convert_fusion.1.x_ref, bf16[128,2048]{1,0:T(8,128)(2,1)S(1)} %bitcast.66, f32[128,2048]{1,0:T(8,128)S(1)} %copy-done.12, ...), custom_call_target="tpu_custom_call" | custom-call | bytes 150000000 | tf_op jit(solution)/shard_map/finish_layer/pallas_call | solution.py:1108
  540.5 0.8 copy.60
  541.3 0.1 convert_bitcast_fusion.3
  541.4 0.2 copy.56
  541.6 0.8 reshape.106
  542.3 0.2 copy.55
  542.5 0.8 reshape.105
  543.3 0.1 slice_select_fusion
  543.3 0.5 slice_bitcast_fusion
  543.9 2.0 fusion
  545.9 2.8 convert_element_type.147
  548.6 2.0 convert_bitcast_fusion
  550.7 1.5 copy.62
  552.1 1.5 copy.61
  553.6 1.0 copy.69
  554.5 0.8 copy.70
  (59 shorter events, 0.3 us)
Async XLA Ops:
  7.2 71.7 %copy-start.4 = (bf16[1,128,2048]{2,1,0:T(8,128)(2,1)S(1)}, bf16[1,128,2048]{2,1,0:T(8,128)(2,1)}, u32[]{:S(2)}) copy-start(bf16[1,128,2048]{2,1,0:T(8,128)(2,1)} %param.14) | copy-start | bytes 1572868
  7.2 72.7 %copy-start.27 = (s32[1,8]{1,0:T(1,128)S(1)}, s32[1,8]{1,0:T(1,128)}, u32[]{:S(2)}) copy-start(s32[1,8]{1,0:T(1,128)} %param.13) | copy-start | bytes 100
  7.2 89.6 %all-gather.4.cloned.1.call-start = ((), (), s32[]{:S(2)}) async-start(), calls=%async_computation.3 | async-start | bytes 1310720 | tf_op jit(solution)/shard_map/all_gather | solution.py:1355
  7.9 252.8 %all-gather.8.cloned.1.call-start = ((), (), s32[]{:S(2)}) async-start(), calls=%async_computation.5 | async-start | bytes 5242880 | tf_op jit(solution)/shard_map/all_gather | solution.py:1356
  8.7 252.0 %all-gather.6.cloned.1.call-start = ((), (), s32[]{:S(2)}) async-start(), calls=%async_computation.4 | async-start | bytes 4718592 | tf_op jit(solution)/shard_map/all_gather | solution.py:1367
  12.6 1.0 copy-start
  75.7 2.0 copy-start.18
  77.7 1.1 copy-start.24
  79.8 464.1 %reduce-scatter.5.cloned.1.call-start = ((), (), s32[]{:S(2)}) async-start(), calls=%async_computation.7 | async-start | bytes 4718592 | tf_op jit(solution)/shard_map/reduce_scatter | solution.py:1376
  80.4 2.8 copy-start.19
  95.2 0.8 copy-start.13
  96.0 0.8 copy-start.15
  96.8 2.9 copy-start.7
  96.8 3.0 copy-start.1
  96.8 3.0 copy-start.9
  96.8 3.0 copy-start.10
  255.4 3.3 copy-start.17
  258.7 2.0 copy-start.23
  294.4 1.9 copy-start.3
  296.3 1.3 copy-start.26
  297.7 246.2 %reduce-scatter.3.cloned.1.call-start = ((), (), s32[]{:S(2)}) async-start(), calls=%async_computation.6 | async-start | bytes 5242880 | tf_op jit(solution)/shard_map/reduce_scatter | solution.py:1384
  321.5 2.3 copy-start.2
  323.8 1.1 copy-start.5
  440.4 1.3 copy-start.6
  441.7 1.0 copy-start.11
  442.7 2.0 copy-start.21
  444.6 99.2 %all-to-all-start = ((bf16[8,64,2048]{2,1,0:T(8,128)(2,1)}), bf16[8,64,2048]{2,1,0:T(8,128)(2,1)}, u32[]{:S(2)}, u32[]{:S(2)}) async-start(bf16[8,64,2048]{2,1,0:T(8,128)(2,1)} %bitcast.68), calls=%async_computation.1 | async-start | bytes 4194304 | tf_op jit(solution)/shard_map/all_to_all | solution.py:1143
  449.5 4.0 copy-start.14
  449.5 4.0 copy-start.16
  453.4 13.4 %copy-start.20 = (bf16[1024,2048]{1,0:T(8,128)(2,1)S(1)}, bf16[1024,2048]{1,0:T(8,128)(2,1)}, u32[]{:S(2)}) copy-start(bf16[1024,2048]{1,0:T(8,128)(2,1)} %copy-done.18) | copy-start | bytes 12582916
  466.9 2.6 copy-start.25
  469.5 2.4 copy-start.8
  469.5 2.4 copy-start.22
  471.9 1.3 copy-start.12
Sparse Core Ops, SparseCore 0:
  9.6 26.1 all-gather.3
  37.3 32.5 all-gather.7
  79.9 132.2 all-gather.5
  297.8 111.9 reduce-scatter.4
  412.1 43.3 reduce-scatter.2
